TPU v7x, 512 devices: a whole 4x4x16 slice. The times are simulated.
512 devices in a mesh: dp: 2 (over core), ctx: 64 (over x, z), head: 4 (over y).
Axes of the slice: x: 4, y: 4, z: 16, core: 2. Of those that a mesh axis runs over, the one named last changes fastest.
Arguments:
- query: bfloat16 [2, 64, 4, 512, 256], P('dp', 'ctx', 'head'), may hold values from -120 to 120
- key: bfloat16 [2, 8192, 4096], P('dp', 'ctx', 'head'), may hold values from -8 to 8
- value: bfloat16 [2, 8192, 4096], P('dp', 'ctx', 'head'), may hold values from -6 to 6
- grad_out: bfloat16 [2, 64, 4, 512, 256], P('dp', 'ctx', 'head'), may hold values from -6 to 6
- chosen: int32 [2, 16, 32, 3], P('dp', None, 'head'), may hold values from 0 to 15, as said below
- placed: int32 [16], replicated, may hold values from 0 to 15, each once
- sink: float32 [32], P('head'), may hold values from -2 to 6
Outputs:
- attended: bfloat16 [2, 64, 4, 512, 256], P('dp', 'ctx', 'head')
- grad_query: bfloat16 [2, 64, 4, 512, 256], P('dp', 'ctx', 'head')
- grad_key: bfloat16 [2, 8192, 4096], P('dp', 'ctx', 'head')
- grad_value: bfloat16 [2, 8192, 4096], P('dp', 'ctx', 'head')
- grad_sink: float32 [32], replicated
Inputs may be any that keep to these rules, and one draw needn't show every extreme that they name: `chosen`: for each sequence, block b and head, the first min(b, 3) entries are distinct blocks before b; the remaining entries are blocks from b to 15. `placed`: every block is held by exactly one slot.
All inputs are finite; a program needn't handle non-finite values.
Results may differ from a plain program's by a relative error of at most 0.025.
Values may be sent and summed in bfloat16 or wider, within the bound.
No kernel may reach another device: no remote copies, remote signals or barrier semaphores. Data moves between devices by JAX's collectives and lax.ppermute only.
A program may use at most 64 MiB of HBM per device.

v0:
```python
import math

import jax
import jax.numpy as jnp
from jax import lax
from jax.sharding import PartitionSpec as P

HEADS = 32
DH = 128


def inner_rows(left, right):
    return lax.dot_general(
        left, right, (((1,), (1,)), ((), ())), preferred_element_type=jnp.float32
    )


def outer_rows(left, right):
    return lax.dot_general(
        left, right, (((0,), (0,)), ((), ())), preferred_element_type=jnp.float32
    )


def attend_block(query_rows, grad_rows, tiles, usable, sink_logit):
    rows, width = query_rows.shape
    scale = 1.0 / math.sqrt(width)
    keys = tiles[:, :, :width].reshape(-1, width)
    vals = tiles[:, :, width:].reshape(-1, width)
    scores = inner_rows(query_rows, keys) * scale
    cols = tiles.shape[0] * rows
    tile_of = jnp.arange(cols) // rows
    offset = jnp.arange(cols) % rows
    own_ok = offset[None, :] <= jnp.arange(rows)[:, None]
    allowed = jnp.where(tile_of[None, :] == 0, own_ok, usable[tile_of][None, :])
    masked = jnp.where(allowed, scores, -jnp.inf)
    top = jnp.maximum(jnp.max(masked, axis=1), sink_logit)
    expo = jnp.exp(masked - top[:, None])
    sink_part = jnp.exp(sink_logit - top)
    total = sink_part + jnp.sum(expo, axis=1)
    prob = expo / total[:, None]
    weights = prob.astype(jnp.bfloat16)
    attended = jnp.dot(weights, vals, preferred_element_type=jnp.float32).astype(jnp.bfloat16)
    stored = lax.optimization_barrier(attended)
    delta = jnp.sum(grad_rows.astype(jnp.float32) * stored.astype(jnp.float32), axis=1)
    dprob = inner_rows(grad_rows, vals)
    dscore = (prob * (dprob - delta[:, None]) * scale).astype(jnp.bfloat16)
    grad_query = jnp.dot(dscore, keys, preferred_element_type=jnp.float32).astype(jnp.bfloat16)
    grad_keys = outer_rows(dscore, query_rows).astype(jnp.bfloat16)
    grad_vals = outer_rows(weights, grad_rows).astype(jnp.bfloat16)
    tiles_grad = jnp.concatenate([grad_keys, grad_vals], axis=1).reshape(tiles.shape)
    sink_grad = -jnp.sum(sink_part / total * delta)
    return (attended, grad_query, tiles_grad, sink_grad)


def body(query, key, value, grad_out, chosen, placed, sink):
    seqs = query.shape[0]
    block = query.shape[3]
    width = DH
    hpd = query.shape[4] // width
    unit = key.shape[1]
    parts_per = block // unit
    n_ctx = lax.axis_size("ctx")
    nblk = n_ctx // parts_per
    place = lax.axis_index("ctx")
    slot = place // parts_per
    position = place % parts_per
    slots = jnp.arange(nblk, dtype=jnp.int32)
    seq_block = jnp.sum(jnp.where(slots == slot, placed, 0))
    slot_of = jnp.sum(jnp.where(placed[None, :] == slots[:, None], slots[None, :], 0), axis=1)
    mine = lax.dynamic_slice_in_dim(chosen, seq_block, 1, 1)[:, 0]
    mine = lax.dynamic_slice_in_dim(mine, position * hpd, hpd, 1)
    usable_pick = mine < seq_block
    mapped = jnp.sum(jnp.where(mine[..., None] == slots, slot_of, 0), axis=-1)
    mapped = jnp.where(usable_pick, mapped, slot)
    lead = jnp.broadcast_to(slot, mine.shape[:2] + (1,))
    picks = jnp.concatenate([lead, mapped], axis=-1)
    kinds = picks.shape[-1]
    usable = jnp.concatenate([jnp.ones(mine.shape[:2] + (1,), bool), usable_pick], axis=-1)
    sink_mine = lax.dynamic_slice_in_dim(sink, position * hpd, hpd)
    paired = jnp.concatenate(
        [
            key.reshape(seqs, unit, parts_per, hpd, width),
            value.reshape(seqs, unit, parts_per, hpd, width),
        ],
        axis=-1,
    )
    paired = jnp.transpose(paired, (2, 0, 3, 1, 4))
    items = seqs * hpd
    frag = unit * 2 * width // n_ctx
    seq_ix = jnp.arange(seqs, dtype=jnp.int32)[None, :, None, None, None]
    head_ix = jnp.arange(hpd, dtype=jnp.int32)[None, None, :, None, None]
    spread = jnp.transpose(paired.reshape(parts_per, seqs, hpd, n_ctx, frag), (3, 0, 1, 2, 4))
    held = lax.all_to_all(spread, "ctx", split_axis=0, concat_axis=0, tiled=True)
    held = jnp.transpose(held, (2, 3, 0, 1, 4)).reshape(seqs, hpd, n_ctx * parts_per, frag)
    match_block = placed[:, None] == slots[None, :]
    chosen_all = jnp.sum(jnp.where(match_block[None, :, :, None, None], chosen[:, None], 0), axis=2)
    before = chosen_all < placed[None, :, None, None]
    mapped_all = jnp.sum(jnp.where(chosen_all[..., None] == slots, slot_of, 0), axis=-1)
    own_slot = slots[None, :, None, None]
    mapped_all = jnp.where(before, mapped_all, own_slot)
    lead_all = jnp.broadcast_to(own_slot, mapped_all.shape[:3] + (1,))
    picks_all = jnp.concatenate([lead_all, mapped_all], axis=-1)
    picks_all = jnp.transpose(
        picks_all.reshape(seqs, nblk, parts_per, hpd, kinds), (1, 2, 0, 3, 4)
    ).reshape(n_ctx, seqs, hpd, kinds)
    dest_group = (jnp.arange(n_ctx, dtype=jnp.int32) % parts_per)[:, None, None, None, None]
    part_ids = jnp.arange(parts_per, dtype=jnp.int32)[None, None, None, None, :]
    route = (picks_all[..., None] * parts_per + part_ids) * parts_per + dest_group
    outgoing = held[seq_ix, head_ix, route]
    fetched = lax.all_to_all(outgoing, "ctx", split_axis=0, concat_axis=0, tiled=True)
    tiles_items = jnp.transpose(fetched, (1, 2, 3, 4, 0, 5)).reshape(
        items, kinds, parts_per * unit, 2 * width
    )
    query_heads = jnp.transpose(query.reshape(seqs, block, hpd, width), (0, 2, 1, 3)).reshape(
        items, block, width
    )
    grad_heads = jnp.transpose(grad_out.reshape(seqs, block, hpd, width), (0, 2, 1, 3)).reshape(
        items, block, width
    )
    sink_items = jnp.tile(sink_mine, seqs)

    def per_head(item):
        q_rows, g_rows, tiles, use_row, sink_logit = item
        return attend_block(q_rows, g_rows, tiles, use_row, sink_logit)

    atts, grads_q, tiles_grad, sink_grads = lax.map(
        per_head, (query_heads, grad_heads, tiles_items, usable.reshape(items, -1), sink_items)
    )
    attended = jnp.transpose(atts.reshape(seqs, hpd, block, width), (0, 2, 1, 3)).reshape(
        seqs, 1, 1, block, hpd * width
    )
    grad_query = jnp.transpose(grads_q.reshape(seqs, hpd, block, width), (0, 2, 1, 3)).reshape(
        seqs, 1, 1, block, hpd * width
    )
    shards = tiles_grad.reshape(seqs, hpd, kinds, parts_per, n_ctx, frag)
    sendback = jnp.transpose(shards, (4, 0, 1, 2, 3, 5))
    landed = lax.all_to_all(sendback, "ctx", split_axis=0, concat_axis=0, tiled=True)
    pooled = (
        jnp.zeros((seqs, hpd, n_ctx * parts_per, frag), jnp.float32)
        .at[seq_ix, head_ix, route]
        .add(landed.astype(jnp.float32))
    )
    pooled = jnp.transpose(pooled.reshape(seqs, hpd, n_ctx, parts_per, frag), (2, 3, 0, 1, 4))
    homed = lax.all_to_all(
        pooled.astype(jnp.bfloat16), "ctx", split_axis=0, concat_axis=0, tiled=True
    ).astype(pooled.dtype)
    totals = jnp.transpose(homed, (1, 2, 3, 0, 4)).reshape(parts_per, seqs, hpd, unit, 2 * width)
    totals = jnp.transpose(totals, (1, 3, 0, 2, 4))
    grad_key = totals[..., :width].reshape(seqs, unit, parts_per * hpd * width).astype(jnp.bfloat16)
    grad_value = (
        totals[..., width:].reshape(seqs, unit, parts_per * hpd * width).astype(jnp.bfloat16)
    )
    sink_local = jnp.sum(sink_grads.reshape(seqs, hpd), axis=0)
    start = lax.axis_index("head") * (parts_per * hpd) + position * hpd
    spread_sink = lax.dynamic_update_slice(jnp.zeros((HEADS,), jnp.float32), sink_local, (start,))
    grad_sink = lax.psum(spread_sink, ("dp", "ctx", "head"))
    return (attended, grad_query, grad_key, grad_value, grad_sink)


def solution(mesh):
    in_specs = (
        P("dp", "ctx", "head", None, None),
        P("dp", "ctx", "head"),
        P("dp", "ctx", "head"),
        P("dp", "ctx", "head", None, None),
        P("dp", None, "head", None),
        P(),
        P("head"),
    )
    out_specs = (
        P("dp", "ctx", "head", None, None),
        P("dp", "ctx", "head", None, None),
        P("dp", "ctx", "head"),
        P("dp", "ctx", "head"),
        P(),
    )
    return jax.shard_map(body, mesh=mesh, in_specs=in_specs, out_specs=out_specs, check_vma=False)
```

profile of v0, /device:TPU:24, one launch (start us, length us, event | category | flops | bytes accessed | tf_op | source)
XLA Modules:
  0.0 482.7 jit_solution(11513940544076405673)
XLA Ops:
  0.7 1.1 reshape.333
  1.8 1.1 reshape.334
  3.3 1.3 copy.152
  4.6 18.6 %all-to-all-start = ((bf16[64,4,1,2,512]{4,3,1,2,0:T(2,128)(2,1)}), bf16[64,4,1,2,512]{4,3,1,2,0:T(2,128)(2,1)S(1)}, u32[]{:S(2)}, u32[]{:S(2)}) async-start(bf16[64,4,1,2,512]{4,3,1,2,0:T(2,128)(2,1)} %copy.152), calls=%async_computation | async-start | bytes 1048576 | tf_op jit(solution)/shard_map/all_to_all | solution.py:93
  23.3 0.9 select_reduce_fusion.2
  24.3 1.0 select_reduce_fusion.1
  26.6 28.3 %all-to-all-done = bf16[64,4,1,2,512]{4,3,1,2,0:T(2,128)(2,1)S(1)} async-done(((bf16[64,4,1,2,512]{4,3,1,2,0:T(2,128)(2,1)}), bf16[64,4,1,2,512]{4,3,1,2,0:T(2,128)(2,1)S(1)}, u32[]{:S(2)}, u32[]{:S(2)}) %all-to-all-start) | async-done | bytes 524320 | tf_op jit(solution)/shard_map/all_to_all | solution.py:93
  54.9 14.1 %gather_fusion = bf16[2048,512]{1,0:T(8,128)(2,1)S(1)} fusion(bf16[1,2,256,512]{3,2,1,0:T(8,128)(2,1)S(1)} %copy.174, s32[2048]{0:T(1024)S(1)} %reshape.369), kind=kCustom, calls=%fused_computation | custom fusion | bytes 4218880 | tf_op jit(solution)/shard_map/gather | solution.py:109
  69.0 2.1 reshape.368
  71.1 7.2 %all-to-all-start.1 = ((bf16[64,1,2,4,4,512]{5,4,3,2,1,0:T(4,128)(2,1)}), bf16[64,1,2,4,4,512]{5,4,3,2,1,0:T(4,128)(2,1)S(1)}, u32[]{:S(2)}, u32[]{:S(2)}) async-start(bf16[64,1,2,4,4,512]{5,4,3,2,1,0:T(4,128)(2,1)} %bitcast.145), calls=%async_computation.1 | async-start | bytes 4194304 | tf_op jit(solution)/shard_map/all_to_all | solution.py:110
  82.3 93.7 %all-to-all-done.1 = bf16[64,1,2,4,4,512]{5,4,3,2,1,0:T(4,128)(2,1)S(1)} async-done(((bf16[64,1,2,4,4,512]{5,4,3,2,1,0:T(4,128)(2,1)}), bf16[64,1,2,4,4,512]{5,4,3,2,1,0:T(4,128)(2,1)S(1)}, u32[]{:S(2)}, u32[]{:S(2)}) %all-to-all-start.1) | async-done | bytes 2097184 | tf_op jit(solution)/shard_map/all_to_all | solution.py:110
  175.9 2.5 copy.159
  178.5 4.1 reshape.337
  182.5 54.9 %while.18 = (s32[]{:T(128)}, bf16[2,512,128]{2,1,0:T(8,128)(2,1)}, bf16[2,512,128]{2,1,0:T(8,128)(2,1)}, bf16[2,4,512,256]{3,2,1,0:T(8,128)(2,1)}, f32[2]{0:T(12...) while((s32[]{:T(128)}, bf16[2,512,128]{2,1,0:T(8,128)(2,1)}, ...), condition=%wide.region_9.10_spmd, body=%wide.region_4.9_spmd.sunk | while | flops 1629425152 | bytes 86695736 | solution.py:126
  183.2 2.6 select_reduce_fusion.5
  185.8 1.3 dynamic-slice_bitcast_fusion.2
  187.1 1.0 fusion.72
  188.1 2.4 fusion.76
  194.0 1.9 copy-done
  195.9 1.4 bitcast_dynamic-update-slice_fusion.2
  197.6 1.3 multiply_reduce_fusion.6
  199.6 3.3 multiply_convert_fusion.2
  203.9 1.3 copy.184
  205.3 2.3 constant_dynamic-update-slice_fusion.2
  207.6 2.4 fusion.80
  210.7 2.6 select_reduce_fusion.5
  213.2 1.3 dynamic-slice_bitcast_fusion.2
  214.5 1.0 fusion.72
  215.6 2.4 fusion.76
  221.5 1.9 copy-done
  223.4 1.4 bitcast_dynamic-update-slice_fusion.2
  225.1 1.3 multiply_reduce_fusion.6
  227.1 3.3 multiply_convert_fusion.2
  231.4 1.3 copy.184
  232.7 2.3 constant_dynamic-update-slice_fusion.2
  235.0 2.4 fusion.80
  237.4 2.7 reshape.344
  240.1 3.0 copy.167
  243.1 7.5 %all-to-all-start.2 = ((bf16[64,1,2,4,4,512]{5,4,3,2,1,0:T(4,128)(2,1)}), bf16[64,1,2,4,4,512]{5,4,3,2,1,0:T(4,128)(2,1)S(1)}, u32[]{:S(2)}, u32[]{:S(2)}) async-start(bf16[64,1,2,4,4,512]{5,4,3,2,1,0:T(4,128)(2,1)} %copy.167), calls=%async_computation.2 | async-start | bytes 4194304 | tf_op jit(solution)/shard_map/all_to_all | solution.py:137
  251.2 96.4 %all-to-all-done.2 = bf16[64,1,2,4,4,512]{5,4,3,2,1,0:T(4,128)(2,1)S(1)} async-done(((bf16[64,1,2,4,4,512]{5,4,3,2,1,0:T(4,128)(2,1)}), bf16[64,1,2,4,4,512]{5,4,3,2,1,0:T(4,128)(2,1)S(1)}, u32[]{:S(2)}, u32[]{:S(2)}) %all-to-all-start.2) | async-done | bytes 2097184 | tf_op jit(solution)/shard_map/all_to_all | solution.py:137
  347.5 2.5 reshape.379
  350.0 13.5 %scatter_custom_fusion = f32[512,512]{1,0:T(8,128)S(1)} fusion(s32[2048]{0:T(1024)S(1)} %reshape.377, f32[2048,512]{1,0:T(8,128)} %reshape.379, f32[]{:T(128)} %constant.166.clone.1), kind=kCustom, calls=%fused_computation.55 | custom fusion | flops 1048576 | bytes 1049088
  363.7 1.0 copy.168
  364.7 8.2 %all-to-all-start.3 = ((bf16[64,4,1,2,512]{4,1,3,2,0:T(4,128)(2,1)}), bf16[64,4,1,2,512]{4,1,3,2,0:T(4,128)(2,1)S(1)}, u32[]{:S(2)}, u32[]{:S(2)}) async-start(bf16[64,4,1,2,512]{4,1,3,2,0:T(4,128)(2,1)} %copy.168), calls=%async_computation.3 | async-start | bytes 1048576 | tf_op jit(solution)/shard_map/all_to_all | solution.py:144
  373.2 103.7 %psum.7 = f32[32]{0:T(128)} all-reduce(f32[32]{0:T(128)S(1)} %dynamic_update_slice.30), channel_id=1, replica_groups=mesh['dp'=2,'ctx'=64,'head'=4] {'dp','ctx','head'}, use_global_device_ids=true, to_apply=%region_11.12 | all-reduce | flops 32 | bytes 256 | tf_op jit(solution)/shard_map/psum | solution.py:156
  476.9 1.2 copy.163
  478.1 0.9 reshape.341
  479.3 0.9 reshape.343
  (118 shorter events, 18.5 us)
Async XLA Ops:
  0.6 25.4 %copy-start.10 = (s32[3]{0:T(128)S(1)}, s32[3]{0:T(128)}, u32[]{:S(2)}) copy-start(s32[3]{0:T(128)} %constant.189) | copy-start | bytes 40
  0.6 22.5 %copy-start.8 = (s32[16]{0:T(128)S(1)}, s32[16]{0:T(128)}, u32[]{:S(2)}) copy-start(s32[16]{0:T(128)} %param.14) | copy-start | bytes 196
  0.7 22.6 %copy-start.7 = (s32[1,16,8,3]{1,2,3,0:T(8,128)S(1)}, s32[1,16,8,3]{1,2,3,0:T(8,128)}, u32[]{:S(2)}) copy-start(s32[1,16,8,3]{1,2,3,0:T(8,128)} %param.13) | copy-start | bytes 4612
  4.6 50.3 %all-to-all-start = ((bf16[64,4,1,2,512]{4,3,1,2,0:T(2,128)(2,1)}), bf16[64,4,1,2,512]{4,3,1,2,0:T(2,128)(2,1)S(1)}, u32[]{:S(2)}, u32[]{:S(2)}) async-start(bf16[64,4,1,2,512]{4,3,1,2,0:T(2,128)(2,1)} %copy.152), calls=%async_computation | async-start | bytes 1048576 | tf_op jit(solution)/shard_map/all_to_all | solution.py:93
  69.0 12.1 %copy-start.11 = (f32[8]{0:T(128)S(1)}, f32[8]{0:T(128)}, u32[]{:S(2)}) copy-start(f32[8]{0:T(128)} %param.15) | copy-start | bytes 100
  69.0 12.2 %copy-start.4 = (bf16[1,1,1,512,256]{4,3,2,1,0:T(8,128)(2,1)S(1)}, bf16[1,1,1,512,256]{4,3,2,1,0:T(8,128)(2,1)}, u32[]{:S(2)}) copy-start(bf16[1,1,1,512,256]{4,3,2,1,0:T(8,128)(2,1)} %param.9) | copy-start | bytes 786436
  71.1 10.3 %copy-start.5 = (bf16[1,1,1,512,256]{4,3,2,1,0:T(8,128)(2,1)S(1)}, bf16[1,1,1,512,256]{4,3,2,1,0:T(8,128)(2,1)}, u32[]{:S(2)}) copy-start(bf16[1,1,1,512,256]{4,3,2,1,0:T(8,128)(2,1)} %param.12) | copy-start | bytes 786436
  71.1 104.8 %all-to-all-start.1 = ((bf16[64,1,2,4,4,512]{5,4,3,2,1,0:T(4,128)(2,1)}), bf16[64,1,2,4,4,512]{5,4,3,2,1,0:T(4,128)(2,1)S(1)}, u32[]{:S(2)}, u32[]{:S(2)}) async-start(bf16[64,1,2,4,4,512]{5,4,3,2,1,0:T(4,128)(2,1)} %bitcast.145), calls=%async_computation.1 | async-start | bytes 4194304 | tf_op jit(solution)/shard_map/all_to_all | solution.py:110
  182.5 14.8 %copy-start.2 = (bf16[2,512,128]{1,2,0:T(8,128)(2,1)}, bf16[2,512,128]{1,2,0:T(8,128)(2,1)S(1)}, u32[]{:S(2)}) copy-start(bf16[2,512,128]{1,2,0:T(8,128)(2,1)S(1)} %get-tuple-element.386) | copy-start | bytes 786436 | tf_op jit(solution)/shard_map/while
  194.0 1.9 copy-start
  199.6 3.7 copy-start.1
  205.2 4.7 copy-start.3
  210.0 14.8 %copy-start.2 = (bf16[2,512,128]{1,2,0:T(8,128)(2,1)}, bf16[2,512,128]{1,2,0:T(8,128)(2,1)S(1)}, u32[]{:S(2)}) copy-start(bf16[2,512,128]{1,2,0:T(8,128)(2,1)S(1)} %get-tuple-element.386) | copy-start | bytes 786436 | tf_op jit(solution)/shard_map/while
  221.5 1.9 copy-start
  227.1 3.7 copy-start.1
  232.7 4.7 copy-start.3
  240.1 10.5 %copy-start.9 = (s32[3]{0:T(128)S(1)}, s32[3]{0:T(128)}, u32[]{:S(2)}) copy-start(s32[3]{0:T(128)} %constant.192) | copy-start | bytes 40
  243.1 104.4 %all-to-all-start.2 = ((bf16[64,1,2,4,4,512]{5,4,3,2,1,0:T(4,128)(2,1)}), bf16[64,1,2,4,4,512]{5,4,3,2,1,0:T(4,128)(2,1)S(1)}, u32[]{:S(2)}, u32[]{:S(2)}) async-start(bf16[64,1,2,4,4,512]{5,4,3,2,1,0:T(4,128)(2,1)} %copy.167), calls=%async_computation.2 | async-start | bytes 4194304 | tf_op jit(solution)/shard_map/all_to_all | solution.py:137
  350.0 129.0 %copy-start.6 = (bf16[2,512,128]{2,1,0:T(8,128)(2,1)S(1)}, bf16[2,512,128]{2,1,0:T(8,128)(2,1)}, u32[]{:S(2)}) copy-start(bf16[2,512,128]{2,1,0:T(8,128)(2,1)} %get-tuple-element.137) | copy-start | bytes 786436
  364.7 115.4 %all-to-all-start.3 = ((bf16[64,4,1,2,512]{4,1,3,2,0:T(4,128)(2,1)}), bf16[64,4,1,2,512]{4,1,3,2,0:T(4,128)(2,1)S(1)}, u32[]{:S(2)}, u32[]{:S(2)}) async-start(bf16[64,4,1,2,512]{4,1,3,2,0:T(4,128)(2,1)} %copy.168), calls=%async_computation.3 | async-start | bytes 1048576 | tf_op jit(solution)/shard_map/all_to_all | solution.py:144
where the time goes:
time: 487 us; the launch traced here: 483 us
  waiting for transfers between devices  218 us (45%)
  blocking collectives  104 us (21%)
  local copies, waits for them, and re-layouts  62.7 us (13%)
  starting transfers between devices  41.5 us (9%)
  other arithmetic  31.3 us (6%)
  matrix products  20.7 us (4%)
    psum x1, blocking collectives, body(): grad_sink = lax.psum(spread_sink, ('dp', 'ctx', 'head'))  104 us
    all_to_all x1, waiting for transfers between devices, body(): lax.all_to_all(sendback, 'ctx', split_axis=0, concat_axis=0, tiled=True)  96.4 us
    all_to_all x1, waiting for transfers between devices, body(): lax.all_to_all(outgoing, 'ctx', split_axis=0, concat_axis=0, tiled=True)  93.7 us
    all_to_all x1, waiting for transfers between devices, body(): lax.all_to_all(spread, 'ctx', split_axis=0, concat_axis=0, tiled=True)  28.3 us
    all_to_all x1, starting transfers between devices, body(): lax.all_to_all(spread, 'ctx', split_axis=0, concat_axis=0, tiled=True)  18.6 us
    gather x2, local copies, waits for them, and re-layouts, body(): outgoing = held[seq_ix, head_ix, route]  16.2 us
    unnamed x4, other arithmetic  13.7 us
    dot_general x4, matrix products, inner_rows(): lax.dot_general(left, right, (((1,), (1,)), ((), ())), preferred_element_...  11.4 us
  transfers between devices with their start and end apart: 4, of which 3 were waited for; matrix products, arithmetic and copies ran while one was open for 2% of the time, Pallas kernels for 0%

commit v1 on v0

v1 whole, which is shorter than its diff:
```python
import math

import jax
import jax.numpy as jnp
from jax import lax
from jax.experimental import pallas as pl
from jax.experimental.pallas import tpu as pltpu
from jax.sharding import PartitionSpec as P

HEADS = 32
DH = 128
BLOCK = 512
SPB = 4
TOPK = 3
HPD = 2
XS = 4
ZG = 4
ZS = ZG * SPB
N_CTX = XS * ZS
FRAG = BLOCK // (XS * SPB)
ROWS = SPB * 2 * FRAG
KINDS = TOPK + 1
LOG2E = math.log2(math.e)
NEG = -1e30

SPREAD_GROUPS = [[x * ZS + g * SPB + r for x in range(XS) for r in range(SPB)] for g in range(ZG)]
X_GROUPS = [[x * ZS + z for x in range(XS)] for z in range(ZS)]


def shift_groups(arr, step):
    pairs = []
    for x in range(XS):
        for z in range(ZS):
            pairs.append((x * ZS + z, x * ZS + (z + step * SPB) % ZS))
    return lax.ppermute(arr, "ctx", pairs)


def swap_spread(arr):
    return lax.all_to_all(arr, "ctx", 0, 0, axis_index_groups=SPREAD_GROUPS, tiled=True)


def swap_x(arr):
    return lax.all_to_all(arr, "ctx", 0, 0, axis_index_groups=X_GROUPS, tiled=True)


def dot(left, right, left_dim, right_dim):
    return lax.dot_general(
        left,
        right,
        (((left_dim,), (right_dim,)), ((), ())),
        preferred_element_type=jnp.float32,
    )


def attend_kernel(use_ref, sink_ref, q_ref, g_ref, own_ref, pick_ref, *rest):
    att_ref, dq_ref, part_ref, sink_out, s_ref = rest[-5:]
    scale = 1.0 / math.sqrt(DH)
    query = q_ref[...]
    grad = g_ref[...]

    def tile(kind, which):
        if kind == 0:
            got = own_ref[:, :, which]
        else:
            got = pick_ref[:, kind - 1, :, which]
        return got.reshape(BLOCK, DH)

    sink = sink_ref[0] * LOG2E
    top = jnp.full((1, BLOCK), sink, jnp.float32)
    for kind in range(KINDS):
        score = dot(tile(kind, 0), query, 1, 1) * (scale * LOG2E)
        if kind == 0:
            row = lax.broadcasted_iota(jnp.int32, (BLOCK, BLOCK), 0)
            col = lax.broadcasted_iota(jnp.int32, (BLOCK, BLOCK), 1)
            quarter = row // (SPB * FRAG)
            part = (row // FRAG) % SPB
            place = part * (XS * FRAG) + quarter * FRAG + row % FRAG
            score = jnp.where(place <= col, score, NEG)
        else:
            score = jnp.where(use_ref[kind - 1] > 0, score, NEG)
        s_ref[kind] = score
        top = jnp.maximum(top, jnp.max(score, axis=0, keepdims=True))
    sink_part = jnp.exp2(sink - top)
    total = sink_part
    for kind in range(KINDS):
        expo = jnp.exp2(s_ref[kind] - top)
        s_ref[kind] = expo
        total = total + jnp.sum(expo, axis=0, keepdims=True)
    inv = 1.0 / total
    att_t = jnp.zeros((DH, BLOCK), jnp.float32)
    for kind in range(KINDS):
        prob = s_ref[kind] * inv
        s_ref[kind] = prob
        weights = prob.astype(jnp.bfloat16)
        att_t = att_t + dot(tile(kind, 1), weights, 0, 0)
        dv = dot(weights, grad, 1, 0).astype(jnp.bfloat16)
        part_ref[:, kind, :, 1] = dv.reshape(XS, SPB, FRAG, DH)
    att = att_t.T.astype(jnp.bfloat16)
    att_ref[...] = att
    both = grad.astype(jnp.float32) * att.astype(jnp.float32)
    delta = jnp.sum(both.T, axis=0, keepdims=True)
    sink_rows = sink_part * inv * delta
    sink_out[...] = jnp.broadcast_to(-jnp.sum(sink_rows, axis=1, keepdims=True), (8, 128))
    dq_t = jnp.zeros((DH, BLOCK), jnp.float32)
    for kind in range(KINDS):
        dprob = dot(tile(kind, 1), grad, 1, 1)
        dscore = (s_ref[kind] * (dprob - delta) * scale).astype(jnp.bfloat16)
        dq_t = dq_t + dot(tile(kind, 0), dscore, 0, 0)
        dk = dot(dscore, query, 1, 0).astype(jnp.bfloat16)
        part_ref[:, kind, :, 0] = dk.reshape(XS, SPB, FRAG, DH)
    dq_ref[...] = dq_t.T.astype(jnp.bfloat16)


def attend(head, use, sink, query, grad, own, picks, earlier):
    lane = pl.BlockSpec((BLOCK, DH), lambda i: (0, head))
    whole = jax.ShapeDtypeStruct((BLOCK, HPD * DH), jnp.bfloat16)
    tile_dims = (SPB, 2, FRAG, DH)
    own = own.reshape((XS,) + tile_dims)
    picks = picks.reshape((XS, TOPK) + tile_dims)
    in_specs = [
        pl.BlockSpec(memory_space=pltpu.SMEM),
        pl.BlockSpec(memory_space=pltpu.SMEM),
        lane,
        lane,
        pl.BlockSpec(own.shape, lambda i: (0,) * own.ndim),
        pl.BlockSpec(picks.shape, lambda i: (0,) * picks.ndim),
    ]
    in_specs += [pl.BlockSpec(memory_space=pl.ANY)] * len(earlier)
    part_shape = (XS, KINDS) + tile_dims
    return pl.pallas_call(
        attend_kernel,
        name="attend_head%d" % head,
        grid=(1,),
        in_specs=in_specs,
        out_specs=(
            lane,
            lane,
            pl.BlockSpec(part_shape, lambda i: (0,) * len(part_shape)),
            pl.BlockSpec((8, 128), lambda i: (0, 0)),
        ),
        out_shape=(
            whole,
            whole,
            jax.ShapeDtypeStruct(part_shape, jnp.bfloat16),
            jax.ShapeDtypeStruct((8, 128), jnp.float32),
        ),
        scratch_shapes=[pltpu.VMEM((KINDS, BLOCK, BLOCK), jnp.float32)],
        input_output_aliases={6 + n: n for n in range(len(earlier))},
        compiler_params=pltpu.CompilerParams(vmem_limit_bytes=40 << 20),
        cost_estimate=pl.CostEstimate(
            flops=20 * KINDS * BLOCK * BLOCK * DH, transcendentals=0, bytes_accessed=8 << 20
        ),
    )(use, sink, query, grad, own, picks, *earlier)


def gather_kernel(index_ref, *refs):
    out_ref, all_ref = refs[-2:]
    for rel in range(ZG):
        all_ref[rel * XS : (rel + 1) * XS] = refs[rel][...]
    for dest in range(XS * TOPK):
        out_ref[dest] = all_ref[index_ref[dest]]


def gather_picks(index, groups):
    return pl.pallas_call(
        gather_kernel,
        name="gather_picks",
        in_specs=[pl.BlockSpec(memory_space=pltpu.SMEM)]
        + [pl.BlockSpec(memory_space=pltpu.VMEM)] * ZG,
        out_specs=pl.BlockSpec(memory_space=pltpu.VMEM),
        out_shape=jax.ShapeDtypeStruct((XS * TOPK, ROWS, DH), jnp.bfloat16),
        scratch_shapes=[pltpu.VMEM((ZG * XS, ROWS, DH), jnp.bfloat16)],
        compiler_params=pltpu.CompilerParams(vmem_limit_bytes=16 << 20),
        cost_estimate=pl.CostEstimate(flops=0, transcendentals=0, bytes_accessed=4 << 20),
    )(index, *groups)


def pool_kernel(index_ref, part_ref, *refs):
    acc_ref = refs[-1]
    for x in range(XS):
        acc_ref[x] = part_ref[x, 0].astype(jnp.float32)
    for slot in range(XS, ZG * XS):
        acc_ref[slot] = jnp.zeros((ROWS, DH), jnp.float32)
    for x in range(XS):
        for pick in range(TOPK):
            slot = index_ref[x * TOPK + pick]
            acc_ref[slot] = acc_ref[slot] + part_ref[x, pick + 1].astype(jnp.float32)
    for rel in range(ZG):
        refs[rel][...] = acc_ref[rel * XS : (rel + 1) * XS].astype(jnp.bfloat16)


def pool_parts(index, parts):
    return pl.pallas_call(
        pool_kernel,
        name="pool_parts",
        in_specs=[
            pl.BlockSpec(memory_space=pltpu.SMEM),
            pl.BlockSpec(memory_space=pltpu.VMEM),
        ],
        out_specs=tuple(pl.BlockSpec(memory_space=pltpu.VMEM) for _ in range(ZG)),
        out_shape=tuple(
            jax.ShapeDtypeStruct((XS, ROWS, DH), jnp.bfloat16) for _ in range(ZG)
        ),
        scratch_shapes=[pltpu.VMEM((ZG * XS, ROWS, DH), jnp.float32)],
        compiler_params=pltpu.CompilerParams(vmem_limit_bytes=16 << 20),
        cost_estimate=pl.CostEstimate(flops=1 << 20, transcendentals=0, bytes_accessed=4 << 20),
    )(index, parts)


def add_rounded(*arrs):
    total = arrs[0].astype(jnp.float32)
    for arr in arrs[1:]:
        total = total + arr.astype(jnp.float32)
    return total.astype(jnp.bfloat16)


def body(query, key, value, grad_out, chosen, placed, sink):
    place = lax.axis_index("ctx")
    group = (place // SPB) % ZG
    row = place // ZS
    position = place % SPB
    nblk = XS * ZG
    slots = jnp.arange(nblk, dtype=jnp.int32)

    def by_head(arr):
        return jnp.transpose(
            arr.reshape(SPB * XS * FRAG // SPB // FRAG, FRAG, SPB, HPD, DH), (3, 0, 2, 1, 4)
        )

    paired = jnp.stack([by_head(key), by_head(value)], axis=3)
    held = [swap_spread(paired[h].reshape(XS * SPB, 2 * FRAG, DH)) for h in range(HPD)]
    held = [arr.reshape(XS, ROWS, DH) for arr in held]

    heads = lax.dynamic_slice_in_dim(chosen[0], position * HPD, HPD, 1)
    slot_of = jnp.sum(jnp.where(placed[None, :] == slots[:, None], slots[None, :], 0), axis=1)
    rows_of = jnp.arange(XS, dtype=jnp.int32)
    mine = rows_of * ZG + group
    blocks = jnp.sum(jnp.where(mine[:, None] == slots, placed, 0), axis=1)
    cand = jnp.sum(
        jnp.where((blocks[:, None] == slots)[:, :, None, None], heads[None], 0), axis=1
    )
    good = cand < blocks[:, None, None]
    slot = jnp.sum(jnp.where(cand[..., None] == slots, slot_of, 0), axis=-1)
    away = (slot % ZG - group + ZG) % ZG
    index = jnp.where(good, away * XS + slot // ZG, rows_of[:, None, None])
    index = jnp.transpose(index, (1, 0, 2)).reshape(HPD, XS * TOPK)
    use = jnp.sum(
        jnp.where((rows_of == row)[:, None, None], good.astype(jnp.int32), 0), axis=0
    )
    sink_mine = lax.dynamic_slice_in_dim(sink, position * HPD, HPD)

    query_rows = query.reshape(BLOCK, HPD * DH)
    grad_rows = grad_out.reshape(BLOCK, HPD * DH)
    own = [swap_x(arr) for arr in held]
    earlier = ()
    pooled = []
    sink_heads = []
    for h in range(HPD):
        below = shift_groups(held[h], 1)
        above = shift_groups(held[h], -1)
        far = shift_groups(below, 1) if h == 0 else shift_groups(above, -1)
        outgoing = gather_picks(index[h], (held[h], above, far, below))
        picks = swap_x(outgoing.reshape(XS, TOPK * ROWS, DH))
        att, dq, part, sink_sum = attend(
            h, use[h], sink_mine[h : h + 1], query_rows, grad_rows, own[h], picks, earlier
        )
        earlier = (att, dq)
        sink_heads.append(sink_sum[0, :1])
        landed = swap_x(part.reshape(XS, KINDS * ROWS, DH)).reshape(XS, KINDS, ROWS, DH)
        here, to_above, to_far, to_below = pool_parts(index[h], landed)
        if h == 0:
            to_above = add_rounded(to_above, shift_groups(to_far, 1))
        else:
            to_below = add_rounded(to_below, shift_groups(to_far, -1))
        pooled.append(
            add_rounded(here, shift_groups(to_above, 1), shift_groups(to_below, -1))
        )
    homed = [swap_spread(arr.reshape(XS * SPB, 2 * FRAG, DH)) for arr in pooled]
    totals = jnp.stack(
        [arr.reshape(XS, SPB, 2, FRAG, DH) for arr in homed], axis=0
    )
    totals = jnp.transpose(totals, (3, 1, 4, 2, 0, 5))
    grad_key = totals[0].reshape(key.shape)
    grad_value = totals[1].reshape(value.shape)
    sink_local = jnp.concatenate(sink_heads)
    sink_ctx = lax.psum(
        lax.dynamic_update_slice(
            jnp.zeros((SPB * HPD,), jnp.float32), sink_local, (position * HPD,)
        ),
        "ctx",
        axis_index_groups=X_GROUPS,
    )
    z_groups = [[x * ZS + z for z in range(ZS)] for x in range(XS)]
    sink_ctx = lax.psum(sink_ctx, "ctx", axis_index_groups=z_groups)
    start = lax.axis_index("head") * (SPB * HPD)
    spread_sink = lax.dynamic_update_slice(jnp.zeros((HEADS,), jnp.float32), sink_ctx, (start,))
    grad_sink = lax.psum(spread_sink, ("dp", "head"))
    return (att.reshape(query.shape), dq.reshape(query.shape), grad_key, grad_value, grad_sink)


def solution(mesh):
    in_specs = (
        P("dp", "ctx", "head", None, None),
        P("dp", "ctx", "head"),
        P("dp", "ctx", "head"),
        P("dp", "ctx", "head", None, None),
        P("dp", None, "head", None),
        P(),
        P("head"),
    )
    out_specs = (
        P("dp", "ctx", "head", None, None),
        P("dp", "ctx", "head", None, None),
        P("dp", "ctx", "head"),
        P("dp", "ctx", "head"),
        P(),
    )
    return jax.shard_map(body, mesh=mesh, in_specs=in_specs, out_specs=out_specs, check_vma=False)
```

time: 487 us -> 326 us (0.67)
  waiting for transfers between devices: 218 us -> 64.1 us
  starting transfers between devices: 41.5 us -> 168 us
  local copies, waits for them, and re-layouts: 62.7 us -> 9.51 us
  blocking collectives: 104 us -> 53.3 us
  other arithmetic: 31.3 us -> 6.33 us
  matrix products: 20.7 us -> 0 us
  Pallas kernels: 0 us -> 18.7 us
    all_to_all x4 -> x10, waiting for transfers between devices: 218 us -> 26.2 us  [the longest x6 16 us: swap_x(): lax.all_to_all(arr, 'ctx', 0, 0, axis_index_groups=X_GROUPS, tiled=True)]
    all_to_all x4 -> x10, starting transfers between devices: 41.5 us -> 105 us  [the longest x4 80.6 us: swap_spread(): lax.all_to_all(arr, 'ctx', 0, 0, axis_index_groups=SPREAD_GROUPS, tiled=T...]
    ppermute x0 -> x12, starting transfers between devices: none -> 63.1 us  [shift_groups(): return lax.ppermute(arr, 'ctx', pairs)]
    psum x1 -> x3, blocking collectives: 104 us -> 53.3 us  [the longest x1 29.2 us: body(): sink_ctx = lax.psum(sink_ctx, 'ctx', axis_index_groups=z_groups)]
    ppermute x0 -> x12, waiting for transfers between devices: none -> 38 us  [shift_groups(): return lax.ppermute(arr, 'ctx', pairs)]
    dot_general x12 -> x0, matrix products: 20.7 us -> none  [the longest x4 11.4 us: inner_rows(): lax.dot_general(left, right, (((1,), (1,)), ((), ())), preferred_element_...]
    pallas_call x0 -> x6, Pallas kernels: none -> 18.7 us  [the longest x2 13 us: attend(): pl.pallas_call(attend_kernel, name='attend_head%d' % head, grid=(1,), in_...]
    gather x4 -> x0, local copies, waits for them, and re-layouts: 17.5 us -> none  [the longest x2 16.2 us: body(): outgoing = held[seq_ix, head_ix, route]]
  transfers between devices with their start and end apart: 4 -> 22, of which waited for: 3 -> 12; matrix products, arithmetic and copies ran while one was open for 2% -> 2% of each run, Pallas kernels for 0% -> 6%
where the time goes in v1:
time: 326 us; the launch traced here: 321 us
  starting transfers between devices  168 us (52%)
  waiting for transfers between devices  64.1 us (20%)
  blocking collectives  53.3 us (16%)
  Pallas kernels  18.7 us (6%)
  local copies, waits for them, and re-layouts  9.51 us (3%)
  other arithmetic  6.33 us (2%)
    all_to_all x4, starting transfers between devices, swap_spread(): lax.all_to_all(arr, 'ctx', 0, 0, axis_index_groups=SPREAD_GROUPS, tiled=T...  80.6 us
    ppermute x12, starting transfers between devices, shift_groups(): return lax.ppermute(arr, 'ctx', pairs)  63.1 us
    ppermute x12, waiting for transfers between devices, shift_groups(): return lax.ppermute(arr, 'ctx', pairs)  38 us
    psum x1, blocking collectives, body(): sink_ctx = lax.psum(sink_ctx, 'ctx', axis_index_groups=z_groups)  29.2 us
    all_to_all x6, starting transfers between devices, swap_x(): lax.all_to_all(arr, 'ctx', 0, 0, axis_index_groups=X_GROUPS, tiled=True)  24.2 us
    all_to_all x6, waiting for transfers between devices, swap_x(): lax.all_to_all(arr, 'ctx', 0, 0, axis_index_groups=X_GROUPS, tiled=True)  16 us
    psum x1, blocking collectives, body(): grad_sink = lax.psum(spread_sink, ('dp', 'head'))  13.3 us
    pallas_call x2, Pallas kernels, attend(): pl.pallas_call(attend_kernel, name='attend_head%d' % head, grid=(1,), in_...  13 us
  transfers between devices with their start and end apart: 22, of which 12 were waited for; matrix products, arithmetic and copies ran while one was open for 2% of the time, Pallas kernels for 6%

profile of v1, /device:TPU:24, one launch (start us, length us, event | category | flops | bytes accessed | tf_op | source)
XLA Modules:
  0.0 321.0 jit_solution(17041667830046352138)
XLA Ops:
  0.7 1.2 reshape.112
  2.0 0.9 pad_maximum_fusion
  3.7 8.5 %all-to-all-start.3 = ((bf16[16,64,128]{2,1,0:T(8,128)(2,1)}), bf16[16,64,128]{2,1,0:T(8,128)(2,1)}, u32[]{:S(2)}, u32[]{:S(2)}) async-start(bf16[16,64,128]{2,1,0:T(8,128)(2,1)} %bitcast.16), calls=%async_computation.3 | async-start | bytes 524288 | tf_op jit(solution)/shard_map/all_to_all | solution.py:39
  13.0 10.2 %all-to-all-done.3 = bf16[16,64,128]{2,1,0:T(8,128)(2,1)} async-done(((bf16[16,64,128]{2,1,0:T(8,128)(2,1)}), bf16[16,64,128]{2,1,0:T(8,128)(2,1)}, u32[]{:S(2)}, u32[]{:S(2)}) %all-to-all-start.3) | async-done | bytes 262176 | tf_op jit(solution)/shard_map/all_to_all | solution.py:39
  23.2 4.2 %all-to-all-start = ((bf16[16,64,128]{2,1,0:T(8,128)(2,1)}), bf16[16,64,128]{2,1,0:T(8,128)(2,1)}, u32[]{:S(2)}, u32[]{:S(2)}) async-start(bf16[16,64,128]{2,1,0:T(8,128)(2,1)} %bitcast.8), calls=%async_computation | async-start | bytes 524288 | tf_op jit(solution)/shard_map/all_to_all | solution.py:39
  28.5 9.1 %collective-permute-start.4 = (bf16[4,256,128]{2,1,0:T(8,128)(2,1)}, bf16[4,256,128]{2,1,0:T(8,128)(2,1)S(1)}, u32[]{:S(2)}, u32[]{:S(2)}) collective-permute-start(bf16[4,256,128]{2,1,0:T(8,128)(2,1)} %bitcast.17.refs_0_), channel_id=1, source_target_pairs={{0,16},{4,20},{8,24},{12,28},{16,32},{20,36},{24,40},{28,44},{32,4... | collective-permute-start | bytes 786440 | tf_op jit(solution)/shard_map/ppermute | solution.py:35
  38.0 2.9 collective-permute-start.3
  40.9 4.2 %collective-permute-done.4.refs_3_ = bf16[4,256,128]{2,1,0:T(8,128)(2,1)S(1)} collective-permute-done((bf16[4,256,128]{2,1,0:T(8,128)(2,1)}, bf16[4,256,128]{2,1,0:T(8,128)(2,1)S(1)}, u32[]{:S(2)}, u32[]{:S(2)}) %collective-permute-start.4) | collective-permute-done | bytes 262176 | tf_op jit(solution)/shard_map/ppermute | solution.py:35
  45.1 6.7 %collective-permute-start.5 = (bf16[4,256,128]{2,1,0:T(8,128)(2,1)S(1)}, bf16[4,256,128]{2,1,0:T(8,128)(2,1)S(1)}, u32[]{:S(2)}, u32[]{:S(2)}) collective-permute-start(bf16[4,256,128]{2,1,0:T(8,128)(2,1)S(1)} %collective-permute-done.4.refs_3_), channel_id=1, source_target_pairs={{0,16},{4,20},{8,24},{12,28},{16,32},{20,36},{24,40},{28,44},{32,4... | collective-permute-start | bytes 786440 | tf_op jit(solution)/shard_map/ppermute | solution.py:35
  51.8 4.5 %all-to-all-start.4 = ((bf16[4,256,128]{2,1,0:T(8,128)(2,1)}), bf16[4,256,128]{2,1,0:T(8,128)(2,1)S(1)}, u32[]{:S(2)}, u32[]{:S(2)}) async-start(bf16[4,256,128]{2,1,0:T(8,128)(2,1)} %bitcast.17.refs_0_), calls=%async_computation.4 | async-start | bytes 524288 | tf_op jit(solution)/shard_map/all_to_all | solution.py:43
  56.3 6.7 %all-to-all-done.4 = bf16[4,256,128]{2,1,0:T(8,128)(2,1)S(1)} async-done(((bf16[4,256,128]{2,1,0:T(8,128)(2,1)}), bf16[4,256,128]{2,1,0:T(8,128)(2,1)S(1)}, u32[]{:S(2)}, u32[]{:S(2)}) %all-to-all-start.4) | async-done | bytes 262176 | tf_op jit(solution)/shard_map/all_to_all | solution.py:43
  63.0 3.4 %all-to-all-start.1 = ((bf16[4,256,128]{2,1,0:T(8,128)(2,1)}), bf16[4,256,128]{2,1,0:T(8,128)(2,1)S(1)}, u32[]{:S(2)}, u32[]{:S(2)}) async-start(bf16[4,256,128]{2,1,0:T(8,128)(2,1)} %bitcast.9.refs_0_), calls=%async_computation.1 | async-start | bytes 524288 | tf_op jit(solution)/shard_map/all_to_all | solution.py:43
  66.6 4.8 %collective-permute-done.5.refs_2_ = bf16[4,256,128]{2,1,0:T(8,128)(2,1)S(1)} collective-permute-done((bf16[4,256,128]{2,1,0:T(8,128)(2,1)S(1)}, bf16[4,256,128]{2,1,0:T(8,128)(2,1)S(1)}, u32[]{:S(2)}, u32[]{:S(2)}) %collective-permute-start.5) | collective-permute-done | bytes 262176 | tf_op jit(solution)/shard_map/ppermute | solution.py:35
  71.4 2.0 gather_picks.3
  73.3 4.2 %all-to-all-start.5 = ((bf16[4,768,128]{2,1,0:T(8,128)(2,1)}), bf16[4,768,128]{2,1,0:T(8,128)(2,1)S(1)}, u32[]{:S(2)}, u32[]{:S(2)}) async-start(bf16[4,768,128]{2,1,0:T(8,128)(2,1)} %bitcast.19), calls=%async_computation.5 | async-start | bytes 1572864 | tf_op jit(solution)/shard_map/all_to_all | solution.py:43
  77.5 5.5 %collective-permute-start = (bf16[4,256,128]{2,1,0:T(8,128)(2,1)}, bf16[4,256,128]{2,1,0:T(8,128)(2,1)S(1)}, u32[]{:S(2)}, u32[]{:S(2)}) collective-permute-start(bf16[4,256,128]{2,1,0:T(8,128)(2,1)} %bitcast.9.refs_0_), channel_id=1, source_target_pairs={{0,48},{4,52},{8,56},{12,60},{16,0},{20,4},{24,8},{28,12},{32,16},... | collective-permute-start | bytes 786440 | tf_op jit(solution)/shard_map/ppermute | solution.py:35
  83.0 4.3 %collective-permute-start.2 = (bf16[4,256,128]{2,1,0:T(8,128)(2,1)}, bf16[4,256,128]{2,1,0:T(8,128)(2,1)S(1)}, u32[]{:S(2)}, u32[]{:S(2)}) collective-permute-start(bf16[4,256,128]{2,1,0:T(8,128)(2,1)} %bitcast.9.refs_0_), channel_id=1, source_target_pairs={{0,16},{4,20},{8,24},{12,28},{16,32},{20,36},{24,40},{28,44},{32,4... | collective-permute-start | bytes 786440 | tf_op jit(solution)/shard_map/ppermute | solution.py:35
  87.3 4.2 %collective-permute-done.refs_1_ = bf16[4,256,128]{2,1,0:T(8,128)(2,1)S(1)} collective-permute-done((bf16[4,256,128]{2,1,0:T(8,128)(2,1)}, bf16[4,256,128]{2,1,0:T(8,128)(2,1)S(1)}, u32[]{:S(2)}, u32[]{:S(2)}) %collective-permute-start) | collective-permute-done | bytes 262176 | tf_op jit(solution)/shard_map/ppermute | solution.py:35
  91.4 5.5 %collective-permute-start.1 = (bf16[4,256,128]{2,1,0:T(8,128)(2,1)S(1)}, bf16[4,256,128]{2,1,0:T(8,128)(2,1)S(1)}, u32[]{:S(2)}, u32[]{:S(2)}) collective-permute-start(bf16[4,256,128]{2,1,0:T(8,128)(2,1)S(1)} %collective-permute-done.refs_1_), channel_id=1, source_target_pairs={{0,48},{4,52},{8,56},{12,60},{16,0},{20,4},{24,8},{28,12},{32,16},... | collective-permute-start | bytes 786440 | tf_op jit(solution)/shard_map/ppermute | solution.py:35
  98.4 6.1 %collective-permute-done.1.refs_2_ = bf16[4,256,128]{2,1,0:T(8,128)(2,1)S(1)} collective-permute-done((bf16[4,256,128]{2,1,0:T(8,128)(2,1)S(1)}, bf16[4,256,128]{2,1,0:T(8,128)(2,1)S(1)}, u32[]{:S(2)}, u32[]{:S(2)}) %collective-permute-start.1) | collective-permute-done | bytes 262176 | tf_op jit(solution)/shard_map/ppermute | solution.py:35
  104.5 2.0 gather_picks.2
  106.5 4.9 %all-to-all-start.2 = ((bf16[4,768,128]{2,1,0:T(8,128)(2,1)}), bf16[4,768,128]{2,1,0:T(8,128)(2,1)S(1)}, u32[]{:S(2)}, u32[]{:S(2)}) async-start(bf16[4,768,128]{2,1,0:T(8,128)(2,1)} %bitcast.13), calls=%async_computation.2 | async-start | bytes 1572864 | tf_op jit(solution)/shard_map/all_to_all | solution.py:43
  111.7 6.5 %attend_head0.1 = (bf16[512,256]{1,0:T(8,128)(2,1)}, bf16[512,256]{1,0:T(8,128)(2,1)}, bf16[4,4,4,2,32,128]{5,4,3,2,1,0:T(8,128)(2,1)}, f32[8,128]{1,0:T(8,128)S(1)}) custom-call(s32[3]{0:T(128)S(1)} %get-tuple-element.45.use_ref, f32[1]{0:T(128)} %get-tuple-element.47.sink_ref, bf16[512,256]{1,0:T(8,128)(2,1)S(1)} %bitcast.62, ...), custom_call_target="tpu_custom_call" | custom-call | flops 2684354560 | bytes 8388608 | tf_op jit(solution)/shard_map/attend_head0/pallas_call | solution.py:130
  118.2 3.8 %all-to-all-done.2 = bf16[4,768,128]{2,1,0:T(8,128)(2,1)S(1)} async-done(((bf16[4,768,128]{2,1,0:T(8,128)(2,1)}), bf16[4,768,128]{2,1,0:T(8,128)(2,1)S(1)}, u32[]{:S(2)}, u32[]{:S(2)}) %all-to-all-start.2) | async-done | bytes 786464 | tf_op jit(solution)/shard_map/all_to_all | solution.py:43
  121.9 3.5 %all-to-all-start.6 = ((bf16[4,1024,128]{2,1,0:T(8,128)(2,1)}), bf16[4,1024,128]{2,1,0:T(8,128)(2,1)S(1)}, u32[]{:S(2)}, u32[]{:S(2)}) async-start(bf16[4,1024,128]{2,1,0:T(8,128)(2,1)} %bitcast.23), calls=%async_computation.6 | async-start | bytes 2097152 | tf_op jit(solution)/shard_map/all_to_all | solution.py:43
  125.5 6.5 %attend_head1.1 = (bf16[512,256]{1,0:T(8,128)(2,1)}, bf16[512,256]{1,0:T(8,128)(2,1)}, bf16[4,4,4,2,32,128]{5,4,3,2,1,0:T(8,128)(2,1)}, f32[8,128]{1,0:T(8,128)S(1)}) custom-call(s32[3]{0:T(128)S(1)} %get-tuple-element.46.use_ref, f32[1]{0:T(128)} %get-tuple-element.48.sink_ref, ...), custom_call_target="tpu_custom_call", output_to_operand_aliasing={{0}: (6, {}), {1}: (7, {})} | custom-call | flops 2684354560 | bytes 8388608 | tf_op jit(solution)/shard_map/attend_head1/pallas_call | solution.py:130
  131.9 5.5 %all-to-all-done.6 = bf16[4,1024,128]{2,1,0:T(8,128)(2,1)S(1)} async-done(((bf16[4,1024,128]{2,1,0:T(8,128)(2,1)}), bf16[4,1024,128]{2,1,0:T(8,128)(2,1)S(1)}, u32[]{:S(2)}, u32[]{:S(2)}) %all-to-all-start.6) | async-done | bytes 1048608 | tf_op jit(solution)/shard_map/all_to_all | solution.py:43
  137.5 3.7 %all-to-all-start.8 = ((bf16[4,1024,128]{2,1,0:T(8,128)(2,1)}), bf16[4,1024,128]{2,1,0:T(8,128)(2,1)S(1)}, u32[]{:S(2)}, u32[]{:S(2)}) async-start(bf16[4,1024,128]{2,1,0:T(8,128)(2,1)} %bitcast.27), calls=%async_computation.8 | async-start | bytes 2097152 | tf_op jit(solution)/shard_map/all_to_all | solution.py:43
  141.2 0.9 pool_parts.2
  142.1 7.0 %collective-permute-start.6 = (bf16[4,256,128]{2,1,0:T(8,128)(2,1)S(1)}, bf16[4,256,128]{2,1,0:T(8,128)(2,1)S(1)}, u32[]{:S(2)}, u32[]{:S(2)}) collective-permute-start(bf16[4,256,128]{2,1,0:T(8,128)(2,1)S(1)} %get-tuple-element.28), channel_id=1, source_target_pairs={{0,16},{4,20},{8,24},{12,28},{16,32},{20,36},{24,40},{28,44},{32,4... | collective-permute-start | bytes 786440 | tf_op jit(solution)/shard_map/ppermute | solution.py:35
  149.1 2.8 collective-permute-start.8
  151.9 2.4 collective-permute-done.6
  154.4 7.0 %collective-permute-start.7 = (bf16[4,256,128]{2,1,0:T(8,128)(2,1)S(1)}, bf16[4,256,128]{2,1,0:T(8,128)(2,1)S(1)}, u32[]{:S(2)}, u32[]{:S(2)}) collective-permute-start(bf16[4,256,128]{2,1,0:T(8,128)(2,1)S(1)} %add_convert_fusion.3), channel_id=1, source_target_pairs={{0,16},{4,20},{8,24},{12,28},{16,32},{20,36},{24,40},{28,44},{32,4... | collective-permute-start | bytes 786440 | tf_op jit(solution)/shard_map/ppermute | solution.py:35
  161.3 0.9 pool_parts.3
  162.3 2.8 collective-permute-start.10
  165.1 1.5 collective-permute-done.7
  167.3 50.7 %all-to-all-start.7 = ((bf16[16,64,128]{2,1,0:T(8,128)(2,1)}), bf16[16,64,128]{2,1,0:T(8,128)(2,1)S(1)}, u32[]{:S(2)}, u32[]{:S(2)}) async-start(bf16[16,64,128]{2,1,0:T(8,128)(2,1)} %bitcast.25), calls=%async_computation.7 | async-start | bytes 524288 | tf_op jit(solution)/shard_map/all_to_all | solution.py:39
  218.1 5.7 %collective-permute-start.9 = (bf16[4,256,128]{2,1,0:T(8,128)(2,1)S(1)}, bf16[4,256,128]{2,1,0:T(8,128)(2,1)S(1)}, u32[]{:S(2)}, u32[]{:S(2)}) collective-permute-start(bf16[4,256,128]{2,1,0:T(8,128)(2,1)S(1)} %get-tuple-element.32), channel_id=1, source_target_pairs={{0,16},{4,20},{8,24},{12,28},{16,32},{20,36},{24,40},{28,44},{32,4... | collective-permute-start | bytes 786440 | tf_op jit(solution)/shard_map/ppermute | solution.py:35
  223.8 4.1 %collective-permute-start.11 = (bf16[4,256,128]{2,1,0:T(8,128)(2,1)S(1)}, bf16[4,256,128]{2,1,0:T(8,128)(2,1)S(1)}, u32[]{:S(2)}, u32[]{:S(2)}) collective-permute-start(bf16[4,256,128]{2,1,0:T(8,128)(2,1)S(1)} %add_convert_fusion.1), channel_id=1, source_target_pairs={{0,48},{4,52},{8,56},{12,60},{16,0},{20,4},{24,8},{28,12},{32,16},... | collective-permute-start | bytes 786440 | tf_op jit(solution)/shard_map/ppermute | solution.py:35
  227.9 3.3 %collective-permute-done.9 = bf16[4,256,128]{2,1,0:T(8,128)(2,1)S(1)} collective-permute-done((bf16[4,256,128]{2,1,0:T(8,128)(2,1)S(1)}, bf16[4,256,128]{2,1,0:T(8,128)(2,1)S(1)}, u32[]{:S(2)}, u32[]{:S(2)}) %collective-permute-start.9) | collective-permute-done | bytes 262176 | tf_op jit(solution)/shard_map/ppermute | solution.py:35
  231.2 11.5 %collective-permute-done.11 = bf16[4,256,128]{2,1,0:T(8,128)(2,1)S(1)} collective-permute-done((bf16[4,256,128]{2,1,0:T(8,128)(2,1)S(1)}, bf16[4,256,128]{2,1,0:T(8,128)(2,1)S(1)}, u32[]{:S(2)}, u32[]{:S(2)}) %collective-permute-start.11) | collective-permute-done | bytes 262176 | tf_op jit(solution)/shard_map/ppermute | solution.py:35
  243.5 17.1 %all-to-all-start.9 = ((bf16[16,64,128]{2,1,0:T(8,128)(2,1)}), bf16[16,64,128]{2,1,0:T(8,128)(2,1)S(1)}, u32[]{:S(2)}, u32[]{:S(2)}) async-start(bf16[16,64,128]{2,1,0:T(8,128)(2,1)} %bitcast.29), calls=%async_computation.9 | async-start | bytes 524288 | tf_op jit(solution)/shard_map/all_to_all | solution.py:39
  261.7 1.5 maximum_dynamic-update-slice_fusion
  263.2 10.8 %psum.21 = f32[8]{0:T(128)S(1)} all-reduce(f32[8]{0:T(128)S(1)} %maximum_dynamic-update-slice_fusion), channel_id=1, replica_groups={{0,64,128,192},{4,68,132,196},{8,72,136,200},{12,76,140,204},{16,80,144..., use_global_device_ids=true, to_apply=%region_5.6 | all-reduce | flops 8 | bytes 64 | tf_op jit(solution)/shard_map/psum | solution.py:286
  274.0 29.2 %psum.22 = f32[8]{0:T(128)S(1)} all-reduce(f32[8]{0:T(128)S(1)} %psum.21), channel_id=1, replica_groups={{0,4,8,12,16,20,24,28,32,36,40,44,48,52,56,60},{64,68,72,76,80,84,88,92..., use_global_device_ids=true, to_apply=%region_6.7 | all-reduce | flops 8 | bytes 64 | tf_op jit(solution)/shard_map/psum | solution.py:294
  303.4 13.3 %psum.23 = f32[32]{0:T(128)} all-reduce(f32[32]{0:T(128)S(1)} %dynamic_update_slice.7), channel_id=1, replica_groups=mesh['dp'=2,'ctx'=64,'head'=4] {'dp','head'}, use_global_device_ids=true, to_apply=%region_7.8 | all-reduce | flops 32 | bytes 256 | tf_op jit(solution)/shard_map/psum | solution.py:297
  317.7 1.2 maximum_bitcast_fusion
  319.2 0.9 reshape_squeeze.14
  (57 shorter events, 10.2 us)
Async XLA Ops:
  0.6 36.9 %copy-start = (s32[1,16,8,3]{1,2,3,0:T(8,128)S(1)}, s32[1,16,8,3]{1,2,3,0:T(8,128)}, u32[]{:S(2)}) copy-start(s32[1,16,8,3]{1,2,3,0:T(8,128)} %param.11) | copy-start | bytes 4612
  0.6 1.2 copy-start.3
  3.7 19.5 %all-to-all-start.3 = ((bf16[16,64,128]{2,1,0:T(8,128)(2,1)}), bf16[16,64,128]{2,1,0:T(8,128)(2,1)}, u32[]{:S(2)}, u32[]{:S(2)}) async-start(bf16[16,64,128]{2,1,0:T(8,128)(2,1)} %bitcast.16), calls=%async_computation.3 | async-start | bytes 524288 | tf_op jit(solution)/shard_map/all_to_all | solution.py:39
  23.2 28.7 %all-to-all-start = ((bf16[16,64,128]{2,1,0:T(8,128)(2,1)}), bf16[16,64,128]{2,1,0:T(8,128)(2,1)}, u32[]{:S(2)}, u32[]{:S(2)}) async-start(bf16[16,64,128]{2,1,0:T(8,128)(2,1)} %bitcast.8), calls=%async_computation | async-start | bytes 524288 | tf_op jit(solution)/shard_map/all_to_all | solution.py:39
  27.4 0.7 copy-start.4
  28.5 16.6 %collective-permute-start.4 = (bf16[4,256,128]{2,1,0:T(8,128)(2,1)}, bf16[4,256,128]{2,1,0:T(8,128)(2,1)S(1)}, u32[]{:S(2)}, u32[]{:S(2)}) collective-permute-start(bf16[4,256,128]{2,1,0:T(8,128)(2,1)} %bitcast.17.refs_0_), channel_id=1, source_target_pairs={{0,16},{4,20},{8,24},{12,28},{16,32},{20,36},{24,40},{28,44},{32,4... | collective-permute-start | bytes 786440 | tf_op jit(solution)/shard_map/ppermute | solution.py:35
  38.0 28.6 %collective-permute-start.3 = (bf16[4,256,128]{2,1,0:T(8,128)(2,1)}, bf16[4,256,128]{2,1,0:T(8,128)(2,1)S(1)}, u32[]{:S(2)}, u32[]{:S(2)}) collective-permute-start(bf16[4,256,128]{2,1,0:T(8,128)(2,1)} %bitcast.17.refs_0_), channel_id=1, source_target_pairs={{0,48},{4,52},{8,56},{12,60},{16,0},{20,4},{24,8},{28,12},{32,16},... | collective-permute-start | bytes 786440 | tf_op jit(solution)/shard_map/ppermute | solution.py:35
  45.1 26.3 %collective-permute-start.5 = (bf16[4,256,128]{2,1,0:T(8,128)(2,1)S(1)}, bf16[4,256,128]{2,1,0:T(8,128)(2,1)S(1)}, u32[]{:S(2)}, u32[]{:S(2)}) collective-permute-start(bf16[4,256,128]{2,1,0:T(8,128)(2,1)S(1)} %collective-permute-done.4.refs_3_), channel_id=1, source_target_pairs={{0,16},{4,20},{8,24},{12,28},{16,32},{20,36},{24,40},{28,44},{32,4... | collective-permute-start | bytes 786440 | tf_op jit(solution)/shard_map/ppermute | solution.py:35
  51.8 11.1 %all-to-all-start.4 = ((bf16[4,256,128]{2,1,0:T(8,128)(2,1)}), bf16[4,256,128]{2,1,0:T(8,128)(2,1)S(1)}, u32[]{:S(2)}, u32[]{:S(2)}) async-start(bf16[4,256,128]{2,1,0:T(8,128)(2,1)} %bitcast.17.refs_0_), calls=%async_computation.4 | async-start | bytes 524288 | tf_op jit(solution)/shard_map/all_to_all | solution.py:43
  63.0 10.4 %all-to-all-start.1 = ((bf16[4,256,128]{2,1,0:T(8,128)(2,1)}), bf16[4,256,128]{2,1,0:T(8,128)(2,1)S(1)}, u32[]{:S(2)}, u32[]{:S(2)}) async-start(bf16[4,256,128]{2,1,0:T(8,128)(2,1)} %bitcast.9.refs_0_), calls=%async_computation.1 | async-start | bytes 524288 | tf_op jit(solution)/shard_map/all_to_all | solution.py:43
  73.3 33.2 %all-to-all-start.5 = ((bf16[4,768,128]{2,1,0:T(8,128)(2,1)}), bf16[4,768,128]{2,1,0:T(8,128)(2,1)S(1)}, u32[]{:S(2)}, u32[]{:S(2)}) async-start(bf16[4,768,128]{2,1,0:T(8,128)(2,1)} %bitcast.19), calls=%async_computation.5 | async-start | bytes 1572864 | tf_op jit(solution)/shard_map/all_to_all | solution.py:43
  77.5 13.9 %collective-permute-start = (bf16[4,256,128]{2,1,0:T(8,128)(2,1)}, bf16[4,256,128]{2,1,0:T(8,128)(2,1)S(1)}, u32[]{:S(2)}, u32[]{:S(2)}) collective-permute-start(bf16[4,256,128]{2,1,0:T(8,128)(2,1)} %bitcast.9.refs_0_), channel_id=1, source_target_pairs={{0,48},{4,52},{8,56},{12,60},{16,0},{20,4},{24,8},{28,12},{32,16},... | collective-permute-start | bytes 786440 | tf_op jit(solution)/shard_map/ppermute | solution.py:35
  83.0 15.4 %collective-permute-start.2 = (bf16[4,256,128]{2,1,0:T(8,128)(2,1)}, bf16[4,256,128]{2,1,0:T(8,128)(2,1)S(1)}, u32[]{:S(2)}, u32[]{:S(2)}) collective-permute-start(bf16[4,256,128]{2,1,0:T(8,128)(2,1)} %bitcast.9.refs_0_), channel_id=1, source_target_pairs={{0,16},{4,20},{8,24},{12,28},{16,32},{20,36},{24,40},{28,44},{32,4... | collective-permute-start | bytes 786440 | tf_op jit(solution)/shard_map/ppermute | solution.py:35
  91.4 13.1 %collective-permute-start.1 = (bf16[4,256,128]{2,1,0:T(8,128)(2,1)S(1)}, bf16[4,256,128]{2,1,0:T(8,128)(2,1)S(1)}, u32[]{:S(2)}, u32[]{:S(2)}) collective-permute-start(bf16[4,256,128]{2,1,0:T(8,128)(2,1)S(1)} %collective-permute-done.refs_1_), channel_id=1, source_target_pairs={{0,48},{4,52},{8,56},{12,60},{16,0},{20,4},{24,8},{28,12},{32,16},... | collective-permute-start | bytes 786440 | tf_op jit(solution)/shard_map/ppermute | solution.py:35
  96.9 0.7 copy-start.5
  106.5 5.1 %copy-start.1 = (bf16[1,1,1,512,256]{4,3,2,1,0:T(8,128)(2,1)S(1)}, bf16[1,1,1,512,256]{4,3,2,1,0:T(8,128)(2,1)}, u32[]{:S(2)}) copy-start(bf16[1,1,1,512,256]{4,3,2,1,0:T(8,128)(2,1)} %param.7) | copy-start | bytes 786436
  106.5 5.1 %copy-start.2 = (bf16[1,1,1,512,256]{4,3,2,1,0:T(8,128)(2,1)S(1)}, bf16[1,1,1,512,256]{4,3,2,1,0:T(8,128)(2,1)}, u32[]{:S(2)}) copy-start(bf16[1,1,1,512,256]{4,3,2,1,0:T(8,128)(2,1)} %param.10) | copy-start | bytes 786436
  106.5 15.4 %all-to-all-start.2 = ((bf16[4,768,128]{2,1,0:T(8,128)(2,1)}), bf16[4,768,128]{2,1,0:T(8,128)(2,1)S(1)}, u32[]{:S(2)}, u32[]{:S(2)}) async-start(bf16[4,768,128]{2,1,0:T(8,128)(2,1)} %bitcast.13), calls=%async_computation.2 | async-start | bytes 1572864 | tf_op jit(solution)/shard_map/all_to_all | solution.py:43
  121.9 15.5 %all-to-all-start.6 = ((bf16[4,1024,128]{2,1,0:T(8,128)(2,1)}), bf16[4,1024,128]{2,1,0:T(8,128)(2,1)S(1)}, u32[]{:S(2)}, u32[]{:S(2)}) async-start(bf16[4,1024,128]{2,1,0:T(8,128)(2,1)} %bitcast.23), calls=%async_computation.6 | async-start | bytes 2097152 | tf_op jit(solution)/shard_map/all_to_all | solution.py:43
  137.5 23.8 %all-to-all-start.8 = ((bf16[4,1024,128]{2,1,0:T(8,128)(2,1)}), bf16[4,1024,128]{2,1,0:T(8,128)(2,1)S(1)}, u32[]{:S(2)}, u32[]{:S(2)}) async-start(bf16[4,1024,128]{2,1,0:T(8,128)(2,1)} %bitcast.27), calls=%async_computation.8 | async-start | bytes 2097152 | tf_op jit(solution)/shard_map/all_to_all | solution.py:43
  142.1 12.2 %collective-permute-start.6 = (bf16[4,256,128]{2,1,0:T(8,128)(2,1)S(1)}, bf16[4,256,128]{2,1,0:T(8,128)(2,1)S(1)}, u32[]{:S(2)}, u32[]{:S(2)}) collective-permute-start(bf16[4,256,128]{2,1,0:T(8,128)(2,1)S(1)} %get-tuple-element.28), channel_id=1, source_target_pairs={{0,16},{4,20},{8,24},{12,28},{16,32},{20,36},{24,40},{28,44},{32,4... | collective-permute-start | bytes 786440 | tf_op jit(solution)/shard_map/ppermute | solution.py:35
  149.1 16.0 %collective-permute-start.8 = (bf16[4,256,128]{2,1,0:T(8,128)(2,1)S(1)}, bf16[4,256,128]{2,1,0:T(8,128)(2,1)S(1)}, u32[]{:S(2)}, u32[]{:S(2)}) collective-permute-start(bf16[4,256,128]{2,1,0:T(8,128)(2,1)S(1)} %get-tuple-element.29), channel_id=1, source_target_pairs={{0,48},{4,52},{8,56},{12,60},{16,0},{20,4},{24,8},{28,12},{32,16},... | collective-permute-start | bytes 786440 | tf_op jit(solution)/shard_map/ppermute | solution.py:35
  154.4 12.2 %collective-permute-start.7 = (bf16[4,256,128]{2,1,0:T(8,128)(2,1)S(1)}, bf16[4,256,128]{2,1,0:T(8,128)(2,1)S(1)}, u32[]{:S(2)}, u32[]{:S(2)}) collective-permute-start(bf16[4,256,128]{2,1,0:T(8,128)(2,1)S(1)} %add_convert_fusion.3), channel_id=1, source_target_pairs={{0,16},{4,20},{8,24},{12,28},{16,32},{20,36},{24,40},{28,44},{32,4... | collective-permute-start | bytes 786440 | tf_op jit(solution)/shard_map/ppermute | solution.py:35
  162.3 61.5 %collective-permute-start.10 = (bf16[4,256,128]{2,1,0:T(8,128)(2,1)S(1)}, bf16[4,256,128]{2,1,0:T(8,128)(2,1)S(1)}, u32[]{:S(2)}, u32[]{:S(2)}) collective-permute-start(bf16[4,256,128]{2,1,0:T(8,128)(2,1)S(1)} %get-tuple-element.34), channel_id=1, source_target_pairs={{0,48},{4,52},{8,56},{12,60},{16,0},{20,4},{24,8},{28,12},{32,16},... | collective-permute-start | bytes 786440 | tf_op jit(solution)/shard_map/ppermute | solution.py:35
  167.3 76.2 %all-to-all-start.7 = ((bf16[16,64,128]{2,1,0:T(8,128)(2,1)}), bf16[16,64,128]{2,1,0:T(8,128)(2,1)S(1)}, u32[]{:S(2)}, u32[]{:S(2)}) async-start(bf16[16,64,128]{2,1,0:T(8,128)(2,1)} %bitcast.25), calls=%async_computation.7 | async-start | bytes 524288 | tf_op jit(solution)/shard_map/all_to_all | solution.py:39
  218.1 13.2 %collective-permute-start.9 = (bf16[4,256,128]{2,1,0:T(8,128)(2,1)S(1)}, bf16[4,256,128]{2,1,0:T(8,128)(2,1)S(1)}, u32[]{:S(2)}, u32[]{:S(2)}) collective-permute-start(bf16[4,256,128]{2,1,0:T(8,128)(2,1)S(1)} %get-tuple-element.32), channel_id=1, source_target_pairs={{0,16},{4,20},{8,24},{12,28},{16,32},{20,36},{24,40},{28,44},{32,4... | collective-permute-start | bytes 786440 | tf_op jit(solution)/shard_map/ppermute | solution.py:35
  223.8 18.9 %collective-permute-start.11 = (bf16[4,256,128]{2,1,0:T(8,128)(2,1)S(1)}, bf16[4,256,128]{2,1,0:T(8,128)(2,1)S(1)}, u32[]{:S(2)}, u32[]{:S(2)}) collective-permute-start(bf16[4,256,128]{2,1,0:T(8,128)(2,1)S(1)} %add_convert_fusion.1), channel_id=1, source_target_pairs={{0,48},{4,52},{8,56},{12,60},{16,0},{20,4},{24,8},{28,12},{32,16},... | collective-permute-start | bytes 786440 | tf_op jit(solution)/shard_map/ppermute | solution.py:35
  243.5 73.6 %all-to-all-start.9 = ((bf16[16,64,128]{2,1,0:T(8,128)(2,1)}), bf16[16,64,128]{2,1,0:T(8,128)(2,1)S(1)}, u32[]{:S(2)}, u32[]{:S(2)}) async-start(bf16[16,64,128]{2,1,0:T(8,128)(2,1)} %bitcast.29), calls=%async_computation.9 | async-start | bytes 524288 | tf_op jit(solution)/shard_map/all_to_all | solution.py:39

commit v2 on v1

--- a/solution.py
+++ b/solution.py
@@ -223,13 +223,12 @@
     slots = jnp.arange(nblk, dtype=jnp.int32)
 
     def by_head(arr):
-        return jnp.transpose(
-            arr.reshape(SPB * XS * FRAG // SPB // FRAG, FRAG, SPB, HPD, DH), (3, 0, 2, 1, 4)
-        )
+        return jnp.transpose(arr.reshape(XS, FRAG, SPB, HPD, DH), (0, 2, 3, 1, 4))
 
     paired = jnp.stack([by_head(key), by_head(value)], axis=3)
-    held = [swap_spread(paired[h].reshape(XS * SPB, 2 * FRAG, DH)) for h in range(HPD)]
-    held = [arr.reshape(XS, ROWS, DH) for arr in held]
+    landed = swap_spread(paired.reshape(XS * SPB, HPD * 2 * FRAG, DH))
+    landed = jnp.transpose(landed.reshape(XS, SPB, HPD, 2 * FRAG, DH), (2, 0, 1, 3, 4))
+    held = [landed[h].reshape(XS, ROWS, DH) for h in range(HPD)]
 
     heads = lax.dynamic_slice_in_dim(chosen[0], position * HPD, HPD, 1)
     slot_of = jnp.sum(jnp.where(placed[None, :] == slots[:, None], slots[None, :], 0), axis=1)
@@ -252,49 +251,42 @@
     query_rows = query.reshape(BLOCK, HPD * DH)
     grad_rows = grad_out.reshape(BLOCK, HPD * DH)
     own = [swap_x(arr) for arr in held]
+    below = [shift_groups(arr, 1) for arr in held]
+    above = [shift_groups(arr, -1) for arr in held]
+    far = [shift_groups(below[0], 1), shift_groups(above[1], -1)]
+    ready, below[1], above[1] = lax.optimization_barrier((held[0], below[1], above[1]))
+    first = gather_picks(index[0], (ready, above[0], far[0], below[0]))
+    second = gather_picks(index[1], (held[1], above[1], far[1], below[1]))
+    picks = [swap_x(arr.reshape(XS, TOPK * ROWS, DH)) for arr in (first, second)]
     earlier = ()
-    pooled = []
     sink_heads = []
+    pools = []
     for h in range(HPD):
-        below = shift_groups(held[h], 1)
-        above = shift_groups(held[h], -1)
-        far = shift_groups(below, 1) if h == 0 else shift_groups(above, -1)
-        outgoing = gather_picks(index[h], (held[h], above, far, below))
-        picks = swap_x(outgoing.reshape(XS, TOPK * ROWS, DH))
         att, dq, part, sink_sum = attend(
-            h, use[h], sink_mine[h : h + 1], query_rows, grad_rows, own[h], picks, earlier
+            h, use[h], sink_mine[h : h + 1], query_rows, grad_rows, own[h], picks[h], earlier
         )
         earlier = (att, dq)
-        sink_heads.append(sink_sum[0, :1])
-        landed = swap_x(part.reshape(XS, KINDS * ROWS, DH)).reshape(XS, KINDS, ROWS, DH)
-        here, to_above, to_far, to_below = pool_parts(index[h], landed)
-        if h == 0:
-            to_above = add_rounded(to_above, shift_groups(to_far, 1))
-        else:
-            to_below = add_rounded(to_below, shift_groups(to_far, -1))
-        pooled.append(
-            add_rounded(here, shift_groups(to_above, 1), shift_groups(to_below, -1))
-        )
-    homed = [swap_spread(arr.reshape(XS * SPB, 2 * FRAG, DH)) for arr in pooled]
-    totals = jnp.stack(
-        [arr.reshape(XS, SPB, 2, FRAG, DH) for arr in homed], axis=0
-    )
-    totals = jnp.transpose(totals, (3, 1, 4, 2, 0, 5))
+        sink_heads.append(sink_sum)
+        back = swap_x(part.reshape(XS, KINDS * ROWS, DH)).reshape(XS, KINDS, ROWS, DH)
+        pools.append(list(pool_parts(index[h], back)))
+    lane = lax.broadcasted_iota(jnp.int32, (8, 128), 1)
+    sink_local = jnp.where(lane == 0, sink_heads[0], sink_heads[1])
+    sink_local, pools[0][0] = lax.optimization_barrier((sink_local, pools[0][0]))
+    sink_all = lax.all_gather(sink_local, ("dp", "ctx", "head"))[:, 0, :HPD]
+    up_far = shift_groups(pools[0][2], 1)
+    down_near = shift_groups(pools[0][3], -1)
+    down_far = shift_groups(pools[1][2], -1)
+    up_near = shift_groups(pools[1][1], 1)
+    up = [shift_groups(add_rounded(pools[0][1], up_far), 1), up_near]
+    down = [down_near, shift_groups(add_rounded(pools[1][3], down_far), -1)]
+    pooled = [add_rounded(pools[h][0], up[h], down[h]) for h in range(HPD)]
+    pooled = jnp.stack([arr.reshape(XS, SPB, 2 * FRAG, DH) for arr in pooled], axis=2)
+    homed = swap_spread(pooled.reshape(XS * SPB, HPD * 2 * FRAG, DH))
+    totals = jnp.transpose(homed.reshape(XS, SPB, HPD, 2, FRAG, DH), (3, 0, 4, 1, 2, 5))
     grad_key = totals[0].reshape(key.shape)
     grad_value = totals[1].reshape(value.shape)
-    sink_local = jnp.concatenate(sink_heads)
-    sink_ctx = lax.psum(
-        lax.dynamic_update_slice(
-            jnp.zeros((SPB * HPD,), jnp.float32), sink_local, (position * HPD,)
-        ),
-        "ctx",
-        axis_index_groups=X_GROUPS,
-    )
-    z_groups = [[x * ZS + z for z in range(ZS)] for x in range(XS)]
-    sink_ctx = lax.psum(sink_ctx, "ctx", axis_index_groups=z_groups)
-    start = lax.axis_index("head") * (SPB * HPD)
-    spread_sink = lax.dynamic_update_slice(jnp.zeros((HEADS,), jnp.float32), sink_ctx, (start,))
-    grad_sink = lax.psum(spread_sink, ("dp", "head"))
+    sink_all = sink_all.reshape(-1, nblk, SPB, HEADS // (SPB * HPD), HPD)
+    grad_sink = jnp.transpose(jnp.sum(sink_all, axis=(0, 1)), (1, 0, 2)).reshape(HEADS)
     return (att.reshape(query.shape), dq.reshape(query.shape), grad_key, grad_value, grad_sink)
 
 

time: 326 us -> 414 us (1.27)
  waiting for transfers between devices: 64.1 us -> 236 us
  starting transfers between devices: 168 us -> 95.5 us
  blocking collectives: 53.3 us -> 33.3 us
  between operations: 1.09 us -> 14.4 us
    all_gather x0 -> x1, waiting for transfers between devices: none -> 129 us  [body(): sink_all = lax.all_gather(sink_local, ('dp', 'ctx', 'head'))[:, 0, :HPD]]
    all_to_all x4 -> x1, starting transfers between devices: 80.6 us -> 8.47 us  [swap_spread(): lax.all_to_all(arr, 'ctx', 0, 0, axis_index_groups=SPREAD_GROUPS, tiled=T...]
    psum x3 -> x0, blocking collectives: 53.3 us -> none  [the longest x1 29.2 us: body(): sink_ctx = lax.psum(sink_ctx, 'ctx', axis_index_groups=z_groups)]
    ppermute x12, waiting for transfers between devices: 38 us -> 72.3 us  [shift_groups(): return lax.ppermute(arr, 'ctx', pairs)]
    all_to_all x0 -> x1, blocking collectives: none -> 33.3 us  [swap_spread(): lax.all_to_all(arr, 'ctx', 0, 0, axis_index_groups=SPREAD_GROUPS, tiled=T...]
    all_to_all x4 -> x1, waiting for transfers between devices: 10.2 us -> 16.1 us  [swap_spread(): lax.all_to_all(arr, 'ctx', 0, 0, axis_index_groups=SPREAD_GROUPS, tiled=T...]
  transfers between devices with their start and end apart: 22 -> 20, of which waited for: 12 -> 14; matrix products, arithmetic and copies ran while one was open for 2% -> 1% of each run, Pallas kernels for 6% -> 4%
where the time goes in v2:
time: 414 us; the launch traced here: 411 us
  waiting for transfers between devices  236 us (57%)
  starting transfers between devices  95.5 us (23%)
  blocking collectives  33.3 us (8%)
  Pallas kernels  18.8 us (5%)
  between operations  14.4 us (3%)
  local copies, waits for them, and re-layouts  9.61 us (2%)
    all_gather x1, waiting for transfers between devices, body(): sink_all = lax.all_gather(sink_local, ('dp', 'ctx', 'head'))[:, 0, :HPD]  129 us
    ppermute x12, waiting for transfers between devices, shift_groups(): return lax.ppermute(arr, 'ctx', pairs)  72.3 us
    ppermute x12, starting transfers between devices, shift_groups(): return lax.ppermute(arr, 'ctx', pairs)  62.9 us
    all_to_all x1, blocking collectives, swap_spread(): lax.all_to_all(arr, 'ctx', 0, 0, axis_index_groups=SPREAD_GROUPS, tiled=T...  33.3 us
    all_to_all x6, starting transfers between devices, swap_x(): lax.all_to_all(arr, 'ctx', 0, 0, axis_index_groups=X_GROUPS, tiled=True)  23.8 us
    all_to_all x6, waiting for transfers between devices, swap_x(): lax.all_to_all(arr, 'ctx', 0, 0, axis_index_groups=X_GROUPS, tiled=True)  18.9 us
    all_to_all x1, waiting for transfers between devices, swap_spread(): lax.all_to_all(arr, 'ctx', 0, 0, axis_index_groups=SPREAD_GROUPS, tiled=T...  16.1 us
    pallas_call x2, Pallas kernels, attend(): pl.pallas_call(attend_kernel, name='attend_head%d' % head, grid=(1,), in_...  13 us
  transfers between devices with their start and end apart: 20, of which 14 were waited for; matrix products, arithmetic and copies ran while one was open for 1% of the time, Pallas kernels for 4%

profile of v2, /device:TPU:24, one launch (start us, length us, event | category | flops | bytes accessed | tf_op | source)
XLA Modules:
  0.0 410.8 jit_solution(1627214755859246693)
XLA Ops:
  7.2 1.1 reshape.115
  8.3 1.1 reshape.116
  9.4 0.7 pad_maximum_fusion
  10.2 0.9 copy.36
  11.1 8.5 %all-to-all-start = ((bf16[16,128,128]{2,1,0:T(8,128)(2,1)}), bf16[16,128,128]{2,1,0:T(8,128)(2,1)S(1)}, u32[]{:S(2)}, u32[]{:S(2)}) async-start(bf16[16,128,128]{2,1,0:T(8,128)(2,1)} %bitcast.8), calls=%async_computation | async-start | bytes 1048576 | tf_op jit(solution)/shard_map/all_to_all | solution.py:39
  20.0 16.1 %all-to-all-done = bf16[16,128,128]{2,1,0:T(8,128)(2,1)S(1)} async-done(((bf16[16,128,128]{2,1,0:T(8,128)(2,1)}), bf16[16,128,128]{2,1,0:T(8,128)(2,1)S(1)}, u32[]{:S(2)}, u32[]{:S(2)}) %all-to-all-start) | async-done | bytes 524320 | tf_op jit(solution)/shard_map/all_to_all | solution.py:39
  36.1 0.8 fusion.10
  36.9 9.1 %collective-permute-start.4 = (bf16[4,256,128]{2,1,0:T(8,128)(2,1)}, bf16[4,256,128]{2,1,0:T(8,128)(2,1)S(1)}, u32[]{:S(2)}, u32[]{:S(2)}) collective-permute-start(bf16[4,256,128]{2,1,0:T(8,128)(2,1)} %bitcast.16.refs_0_), channel_id=1, source_target_pairs={{0,16},{4,20},{8,24},{12,28},{16,32},{20,36},{24,40},{28,44},{32,4... | collective-permute-start | bytes 786440 | tf_op jit(solution)/shard_map/ppermute | solution.py:35
  46.5 2.9 collective-permute-start.1
  49.4 6.9 %collective-permute-start = (bf16[4,256,128]{2,1,0:T(8,128)(2,1)}, bf16[4,256,128]{2,1,0:T(8,128)(2,1)S(1)}, u32[]{:S(2)}, u32[]{:S(2)}) collective-permute-start(bf16[4,256,128]{2,1,0:T(8,128)(2,1)} %bitcast.11.refs_0_), channel_id=1, source_target_pairs={{0,16},{4,20},{8,24},{12,28},{16,32},{20,36},{24,40},{28,44},{32,4... | collective-permute-start | bytes 786440 | tf_op jit(solution)/shard_map/ppermute | solution.py:35
  56.3 2.9 collective-permute-start.3
  59.1 3.4 all-to-all-start.3
  62.6 24.5 %collective-permute-done.4.refs_3_ = bf16[4,256,128]{2,1,0:T(8,128)(2,1)S(1)} collective-permute-done((bf16[4,256,128]{2,1,0:T(8,128)(2,1)}, bf16[4,256,128]{2,1,0:T(8,128)(2,1)S(1)}, u32[]{:S(2)}, u32[]{:S(2)}) %collective-permute-start.4) | collective-permute-done | bytes 262176 | tf_op jit(solution)/shard_map/ppermute | solution.py:35
  87.1 7.2 %collective-permute-start.5 = (bf16[4,256,128]{2,1,0:T(8,128)(2,1)S(1)}, bf16[4,256,128]{2,1,0:T(8,128)(2,1)S(1)}, u32[]{:S(2)}, u32[]{:S(2)}) collective-permute-start(bf16[4,256,128]{2,1,0:T(8,128)(2,1)S(1)} %collective-permute-done.4.refs_3_), channel_id=1, source_target_pairs={{0,16},{4,20},{8,24},{12,28},{16,32},{20,36},{24,40},{28,44},{32,4... | collective-permute-start | bytes 786440 | tf_op jit(solution)/shard_map/ppermute | solution.py:35
  94.3 3.4 all-to-all-start.1
  97.9 12.5 %collective-permute-done.refs_3_ = bf16[4,256,128]{2,1,0:T(8,128)(2,1)S(1)} collective-permute-done((bf16[4,256,128]{2,1,0:T(8,128)(2,1)}, bf16[4,256,128]{2,1,0:T(8,128)(2,1)S(1)}, u32[]{:S(2)}, u32[]{:S(2)}) %collective-permute-start) | collective-permute-done | bytes 262176 | tf_op jit(solution)/shard_map/ppermute | solution.py:35
  110.5 3.9 collective-permute-done.5.refs_2_
  114.4 2.0 gather_picks.3
  116.3 5.4 %all-to-all-start.4 = ((bf16[4,768,128]{2,1,0:T(8,128)(2,1)}), bf16[4,768,128]{2,1,0:T(8,128)(2,1)S(1)}, u32[]{:S(2)}, u32[]{:S(2)}) async-start(bf16[4,768,128]{2,1,0:T(8,128)(2,1)} %bitcast.21), calls=%async_computation.4 | async-start | bytes 1572864 | tf_op jit(solution)/shard_map/all_to_all | solution.py:43
  121.8 5.4 %collective-permute-start.2 = (bf16[4,256,128]{2,1,0:T(8,128)(2,1)S(1)}, bf16[4,256,128]{2,1,0:T(8,128)(2,1)S(1)}, u32[]{:S(2)}, u32[]{:S(2)}) collective-permute-start(bf16[4,256,128]{2,1,0:T(8,128)(2,1)S(1)} %collective-permute-done.1.refs_1_), channel_id=1, source_target_pairs={{0,48},{4,52},{8,56},{12,60},{16,0},{20,4},{24,8},{28,12},{32,16},... | collective-permute-start | bytes 786440 | tf_op jit(solution)/shard_map/ppermute | solution.py:35
  128.0 7.8 %collective-permute-done.2.refs_2_ = bf16[4,256,128]{2,1,0:T(8,128)(2,1)S(1)} collective-permute-done((bf16[4,256,128]{2,1,0:T(8,128)(2,1)S(1)}, bf16[4,256,128]{2,1,0:T(8,128)(2,1)S(1)}, u32[]{:S(2)}, u32[]{:S(2)}) %collective-permute-start.2) | collective-permute-done | bytes 262176 | tf_op jit(solution)/shard_map/ppermute | solution.py:35
  135.8 2.0 gather_picks.2
  137.8 4.5 %all-to-all-start.2 = ((bf16[4,768,128]{2,1,0:T(8,128)(2,1)}), bf16[4,768,128]{2,1,0:T(8,128)(2,1)S(1)}, u32[]{:S(2)}, u32[]{:S(2)}) async-start(bf16[4,768,128]{2,1,0:T(8,128)(2,1)} %bitcast.17), calls=%async_computation.2 | async-start | bytes 1572864 | tf_op jit(solution)/shard_map/all_to_all | solution.py:43
  142.5 6.5 %attend_head0.1 = (bf16[512,256]{1,0:T(8,128)(2,1)}, bf16[512,256]{1,0:T(8,128)(2,1)}, bf16[4,4,4,2,32,128]{5,4,3,2,1,0:T(8,128)(2,1)}, f32[8,128]{1,0:T(8,128)S(1)}) custom-call(s32[3]{0:T(128)S(1)} %get-tuple-element.55.use_ref, f32[1]{0:T(128)} %get-tuple-element.57.sink_ref, bf16[512,256]{1,0:T(8,128)(2,1)S(1)} %bitcast.69, ...), custom_call_target="tpu_custom_call" | custom-call | flops 2684354560 | bytes 8388608 | tf_op jit(solution)/shard_map/attend_head0/pallas_call | solution.py:130
  149.0 4.3 %all-to-all-done.2 = bf16[4,768,128]{2,1,0:T(8,128)(2,1)S(1)} async-done(((bf16[4,768,128]{2,1,0:T(8,128)(2,1)}), bf16[4,768,128]{2,1,0:T(8,128)(2,1)S(1)}, u32[]{:S(2)}, u32[]{:S(2)}) %all-to-all-start.2) | async-done | bytes 786464 | tf_op jit(solution)/shard_map/all_to_all | solution.py:43
  153.3 3.5 all-to-all-start.5
  157.0 6.5 %attend_head1.1 = (bf16[512,256]{1,0:T(8,128)(2,1)}, bf16[512,256]{1,0:T(8,128)(2,1)}, bf16[4,4,4,2,32,128]{5,4,3,2,1,0:T(8,128)(2,1)}, f32[8,128]{1,0:T(8,128)S(1)}) custom-call(s32[3]{0:T(128)S(1)} %get-tuple-element.56.use_ref, f32[1]{0:T(128)} %get-tuple-element.58.sink_ref, ...), custom_call_target="tpu_custom_call", output_to_operand_aliasing={{0}: (6, {}), {1}: (7, {})} | custom-call | flops 2684354560 | bytes 8388608 | tf_op jit(solution)/shard_map/attend_head1/pallas_call | solution.py:130
  164.1 5.2 %all-to-all-done.5 = bf16[4,1024,128]{2,1,0:T(8,128)(2,1)S(1)} async-done(((bf16[4,1024,128]{2,1,0:T(8,128)(2,1)}), bf16[4,1024,128]{2,1,0:T(8,128)(2,1)S(1)}, u32[]{:S(2)}, u32[]{:S(2)}) %all-to-all-start.5) | async-done | bytes 1048608 | tf_op jit(solution)/shard_map/all_to_all | solution.py:43
  169.3 0.9 pool_parts.2
  170.2 3.5 all-to-all-start.6
  173.8 1.9 collective-permute-start.6
  175.7 9.4 %all-to-all-done.6 = bf16[4,1024,128]{2,1,0:T(8,128)(2,1)S(1)} async-done(((bf16[4,1024,128]{2,1,0:T(8,128)(2,1)}), bf16[4,1024,128]{2,1,0:T(8,128)(2,1)S(1)}, u32[]{:S(2)}, u32[]{:S(2)}) %all-to-all-start.6) | async-done | bytes 1048608 | tf_op jit(solution)/shard_map/all_to_all | solution.py:43
  185.1 0.9 pool_parts.3
  186.0 5.3 %collective-permute-start.10 = (bf16[4,256,128]{2,1,0:T(8,128)(2,1)S(1)}, bf16[4,256,128]{2,1,0:T(8,128)(2,1)S(1)}, u32[]{:S(2)}, u32[]{:S(2)}) collective-permute-start(bf16[4,256,128]{2,1,0:T(8,128)(2,1)S(1)} %get-tuple-element.45), channel_id=1, source_target_pairs={{0,48},{4,52},{8,56},{12,60},{16,0},{20,4},{24,8},{28,12},{32,16},... | collective-permute-start | bytes 786440 | tf_op jit(solution)/shard_map/ppermute | solution.py:35
  191.4 2.5 collective-permute-start.8
  193.9 7.3 %collective-permute-start.7 = (bf16[4,256,128]{2,1,0:T(8,128)(2,1)S(1)}, bf16[4,256,128]{2,1,0:T(8,128)(2,1)S(1)}, u32[]{:S(2)}, u32[]{:S(2)}) collective-permute-start(bf16[4,256,128]{2,1,0:T(8,128)(2,1)S(1)} %add_convert_fusion.3), channel_id=1, source_target_pairs={{0,16},{4,20},{8,24},{12,28},{16,32},{20,36},{24,40},{28,44},{32,4... | collective-permute-start | bytes 786440 | tf_op jit(solution)/shard_map/ppermute | solution.py:35
  201.2 4.4 %collective-permute-start.9 = (bf16[4,256,128]{2,1,0:T(8,128)(2,1)S(1)}, bf16[4,256,128]{2,1,0:T(8,128)(2,1)S(1)}, u32[]{:S(2)}, u32[]{:S(2)}) collective-permute-start(bf16[4,256,128]{2,1,0:T(8,128)(2,1)S(1)} %get-tuple-element.43), channel_id=1, source_target_pairs={{0,16},{4,20},{8,24},{12,28},{16,32},{20,36},{24,40},{28,44},{32,4... | collective-permute-start | bytes 786440 | tf_op jit(solution)/shard_map/ppermute | solution.py:35
  205.6 8.7 %collective-permute-done.10 = bf16[4,256,128]{2,1,0:T(8,128)(2,1)S(1)} collective-permute-done((bf16[4,256,128]{2,1,0:T(8,128)(2,1)S(1)}, bf16[4,256,128]{2,1,0:T(8,128)(2,1)S(1)}, u32[]{:S(2)}, u32[]{:S(2)}) %collective-permute-start.10) | collective-permute-done | bytes 262176 | tf_op jit(solution)/shard_map/ppermute | solution.py:35
  214.4 7.3 %collective-permute-start.11 = (bf16[4,256,128]{2,1,0:T(8,128)(2,1)S(1)}, bf16[4,256,128]{2,1,0:T(8,128)(2,1)S(1)}, u32[]{:S(2)}, u32[]{:S(2)}) collective-permute-start(bf16[4,256,128]{2,1,0:T(8,128)(2,1)S(1)} %add_convert_fusion.1), channel_id=1, source_target_pairs={{0,48},{4,52},{8,56},{12,60},{16,0},{20,4},{24,8},{28,12},{32,16},... | collective-permute-start | bytes 786440 | tf_op jit(solution)/shard_map/ppermute | solution.py:35
  222.0 1.2 collective-permute-done.7
  223.3 5.4 %collective-permute-done.9 = bf16[4,256,128]{2,1,0:T(8,128)(2,1)S(1)} collective-permute-done((bf16[4,256,128]{2,1,0:T(8,128)(2,1)S(1)}, bf16[4,256,128]{2,1,0:T(8,128)(2,1)S(1)}, u32[]{:S(2)}, u32[]{:S(2)}) %collective-permute-start.9) | collective-permute-done | bytes 262176 | tf_op jit(solution)/shard_map/ppermute | solution.py:35
  228.8 7.9 %collective-permute-done.11 = bf16[4,256,128]{2,1,0:T(8,128)(2,1)S(1)} collective-permute-done((bf16[4,256,128]{2,1,0:T(8,128)(2,1)S(1)}, bf16[4,256,128]{2,1,0:T(8,128)(2,1)S(1)}, u32[]{:S(2)}, u32[]{:S(2)}) %collective-permute-start.11) | collective-permute-done | bytes 262176 | tf_op jit(solution)/shard_map/ppermute | solution.py:35
  236.9 33.3 %all_to_all.40 = bf16[16,128,128]{2,1,0:T(8,128)(2,1)S(1)} all-to-all(bf16[16,128,128]{2,1,0:T(8,128)(2,1)S(1)} %bitcast.75), channel_id=1, replica_groups={{0,4,8,12,64,68,72,76,128,132,136,140,192,196,200,204},{16,20,24,28,80,..., dimensions={0} | all-to-all | bytes 1048576 | tf_op jit(solution)/shard_map/all_to_all | solution.py:39
  270.5 0.9 reshape_squeeze.17
  271.5 0.9 reshape_squeeze.18
  272.4 129.2 %all-gather.3.cloned.1.call-done = f32[4096,128]{1,0:T(8,128)} async-done(((f32[8,128]{1,0:T(8,128)}), f32[4096,128]{1,0:T(8,128)}) %all-gather.3.cloned.1.call-update) | async-done | bytes 2097168 | tf_op jit(solution)/shard_map/all_gather | solution.py:275
  401.6 1.7 slice.54
  403.4 0.6 reshape.133
  (50 shorter events, 4.1 us)
Async XLA Ops:
  7.2 38.9 %copy-start = (s32[1,16,8,3]{1,2,3,0:T(8,128)S(1)}, s32[1,16,8,3]{1,2,3,0:T(8,128)}, u32[]{:S(2)}) copy-start(s32[1,16,8,3]{1,2,3,0:T(8,128)} %param.11) | copy-start | bytes 4612
  7.2 12.5 %copy-start.3 = (s32[16]{0:T(128)S(1)}, s32[16]{0:T(128)}, u32[]{:S(2)}) copy-start(s32[16]{0:T(128)} %param.12) | copy-start | bytes 196
  11.1 25.0 %all-to-all-start = ((bf16[16,128,128]{2,1,0:T(8,128)(2,1)}), bf16[16,128,128]{2,1,0:T(8,128)(2,1)S(1)}, u32[]{:S(2)}, u32[]{:S(2)}) async-start(bf16[16,128,128]{2,1,0:T(8,128)(2,1)} %bitcast.8), calls=%async_computation | async-start | bytes 1048576 | tf_op jit(solution)/shard_map/all_to_all | solution.py:39
  36.9 50.2 %collective-permute-start.4 = (bf16[4,256,128]{2,1,0:T(8,128)(2,1)}, bf16[4,256,128]{2,1,0:T(8,128)(2,1)S(1)}, u32[]{:S(2)}, u32[]{:S(2)}) collective-permute-start(bf16[4,256,128]{2,1,0:T(8,128)(2,1)} %bitcast.16.refs_0_), channel_id=1, source_target_pairs={{0,16},{4,20},{8,24},{12,28},{16,32},{20,36},{24,40},{28,44},{32,4... | collective-permute-start | bytes 786440 | tf_op jit(solution)/shard_map/ppermute | solution.py:35
  46.5 51.4 %collective-permute-start.1 = (bf16[4,256,128]{2,1,0:T(8,128)(2,1)}, bf16[4,256,128]{2,1,0:T(8,128)(2,1)S(1)}, u32[]{:S(2)}, u32[]{:S(2)}) collective-permute-start(bf16[4,256,128]{2,1,0:T(8,128)(2,1)} %bitcast.11.refs_0_), channel_id=1, source_target_pairs={{0,48},{4,52},{8,56},{12,60},{16,0},{20,4},{24,8},{28,12},{32,16},... | collective-permute-start | bytes 786440 | tf_op jit(solution)/shard_map/ppermute | solution.py:35
  49.4 61.1 %collective-permute-start = (bf16[4,256,128]{2,1,0:T(8,128)(2,1)}, bf16[4,256,128]{2,1,0:T(8,128)(2,1)S(1)}, u32[]{:S(2)}, u32[]{:S(2)}) collective-permute-start(bf16[4,256,128]{2,1,0:T(8,128)(2,1)} %bitcast.11.refs_0_), channel_id=1, source_target_pairs={{0,16},{4,20},{8,24},{12,28},{16,32},{20,36},{24,40},{28,44},{32,4... | collective-permute-start | bytes 786440 | tf_op jit(solution)/shard_map/ppermute | solution.py:35
  56.3 54.2 %collective-permute-start.3 = (bf16[4,256,128]{2,1,0:T(8,128)(2,1)}, bf16[4,256,128]{2,1,0:T(8,128)(2,1)S(1)}, u32[]{:S(2)}, u32[]{:S(2)}) collective-permute-start(bf16[4,256,128]{2,1,0:T(8,128)(2,1)} %bitcast.16.refs_0_), channel_id=1, source_target_pairs={{0,48},{4,52},{8,56},{12,60},{16,0},{20,4},{24,8},{28,12},{32,16},... | collective-permute-start | bytes 786440 | tf_op jit(solution)/shard_map/ppermute | solution.py:35
  59.1 35.2 %all-to-all-start.3 = ((bf16[4,256,128]{2,1,0:T(8,128)(2,1)}), bf16[4,256,128]{2,1,0:T(8,128)(2,1)S(1)}, u32[]{:S(2)}, u32[]{:S(2)}) async-start(bf16[4,256,128]{2,1,0:T(8,128)(2,1)} %bitcast.16.refs_0_), calls=%async_computation.3 | async-start | bytes 524288 | tf_op jit(solution)/shard_map/all_to_all | solution.py:43
  62.6 64.6 %copy-start.4 = (f32[8]{0:T(128)S(1)}, f32[8]{0:T(128)}, u32[]{:S(2)}) copy-start(f32[8]{0:T(128)} %param.13) | copy-start | bytes 100
  87.1 27.3 %collective-permute-start.5 = (bf16[4,256,128]{2,1,0:T(8,128)(2,1)S(1)}, bf16[4,256,128]{2,1,0:T(8,128)(2,1)S(1)}, u32[]{:S(2)}, u32[]{:S(2)}) collective-permute-start(bf16[4,256,128]{2,1,0:T(8,128)(2,1)S(1)} %collective-permute-done.4.refs_3_), channel_id=1, source_target_pairs={{0,16},{4,20},{8,24},{12,28},{16,32},{20,36},{24,40},{28,44},{32,4... | collective-permute-start | bytes 786440 | tf_op jit(solution)/shard_map/ppermute | solution.py:35
  94.3 22.0 %all-to-all-start.1 = ((bf16[4,256,128]{2,1,0:T(8,128)(2,1)}), bf16[4,256,128]{2,1,0:T(8,128)(2,1)S(1)}, u32[]{:S(2)}, u32[]{:S(2)}) async-start(bf16[4,256,128]{2,1,0:T(8,128)(2,1)} %bitcast.11.refs_0_), calls=%async_computation.1 | async-start | bytes 524288 | tf_op jit(solution)/shard_map/all_to_all | solution.py:43
  116.3 21.4 %all-to-all-start.4 = ((bf16[4,768,128]{2,1,0:T(8,128)(2,1)}), bf16[4,768,128]{2,1,0:T(8,128)(2,1)S(1)}, u32[]{:S(2)}, u32[]{:S(2)}) async-start(bf16[4,768,128]{2,1,0:T(8,128)(2,1)} %bitcast.21), calls=%async_computation.4 | async-start | bytes 1572864 | tf_op jit(solution)/shard_map/all_to_all | solution.py:43
  121.8 20.7 %copy-start.1 = (bf16[1,1,1,512,256]{4,3,2,1,0:T(8,128)(2,1)S(1)}, bf16[1,1,1,512,256]{4,3,2,1,0:T(8,128)(2,1)}, u32[]{:S(2)}) copy-start(bf16[1,1,1,512,256]{4,3,2,1,0:T(8,128)(2,1)} %param.7) | copy-start | bytes 786436
  121.8 20.7 %copy-start.2 = (bf16[1,1,1,512,256]{4,3,2,1,0:T(8,128)(2,1)S(1)}, bf16[1,1,1,512,256]{4,3,2,1,0:T(8,128)(2,1)}, u32[]{:S(2)}) copy-start(bf16[1,1,1,512,256]{4,3,2,1,0:T(8,128)(2,1)} %param.10) | copy-start | bytes 786436
  121.8 14.0 %collective-permute-start.2 = (bf16[4,256,128]{2,1,0:T(8,128)(2,1)S(1)}, bf16[4,256,128]{2,1,0:T(8,128)(2,1)S(1)}, u32[]{:S(2)}, u32[]{:S(2)}) collective-permute-start(bf16[4,256,128]{2,1,0:T(8,128)(2,1)S(1)} %collective-permute-done.1.refs_1_), channel_id=1, source_target_pairs={{0,48},{4,52},{8,56},{12,60},{16,0},{20,4},{24,8},{28,12},{32,16},... | collective-permute-start | bytes 786440 | tf_op jit(solution)/shard_map/ppermute | solution.py:35
  137.8 15.5 %all-to-all-start.2 = ((bf16[4,768,128]{2,1,0:T(8,128)(2,1)}), bf16[4,768,128]{2,1,0:T(8,128)(2,1)S(1)}, u32[]{:S(2)}, u32[]{:S(2)}) async-start(bf16[4,768,128]{2,1,0:T(8,128)(2,1)} %bitcast.17), calls=%async_computation.2 | async-start | bytes 1572864 | tf_op jit(solution)/shard_map/all_to_all | solution.py:43
  153.3 16.1 %all-to-all-start.5 = ((bf16[4,1024,128]{2,1,0:T(8,128)(2,1)}), bf16[4,1024,128]{2,1,0:T(8,128)(2,1)S(1)}, u32[]{:S(2)}, u32[]{:S(2)}) async-start(bf16[4,1024,128]{2,1,0:T(8,128)(2,1)} %bitcast.25), calls=%async_computation.5 | async-start | bytes 2097152 | tf_op jit(solution)/shard_map/all_to_all | solution.py:43
  156.8 244.8 %all-gather.3.cloned.1.call-start = ((), (), s32[]{:S(2)}) async-start(), calls=%async_computation.8 | async-start | bytes 2101248 | tf_op jit(solution)/shard_map/all_gather | solution.py:275
  170.2 14.8 %all-to-all-start.6 = ((bf16[4,1024,128]{2,1,0:T(8,128)(2,1)}), bf16[4,1024,128]{2,1,0:T(8,128)(2,1)S(1)}, u32[]{:S(2)}, u32[]{:S(2)}) async-start(bf16[4,1024,128]{2,1,0:T(8,128)(2,1)} %bitcast.29), calls=%async_computation.6 | async-start | bytes 2097152 | tf_op jit(solution)/shard_map/all_to_all | solution.py:43
  173.8 20.1 %collective-permute-start.6 = (bf16[4,256,128]{2,1,0:T(8,128)(2,1)S(1)}, bf16[4,256,128]{2,1,0:T(8,128)(2,1)S(1)}, u32[]{:S(2)}, u32[]{:S(2)}) collective-permute-start(bf16[4,256,128]{2,1,0:T(8,128)(2,1)S(1)} %get-tuple-element.39), channel_id=1, source_target_pairs={{0,16},{4,20},{8,24},{12,28},{16,32},{20,36},{24,40},{28,44},{32,4... | collective-permute-start | bytes 786440 | tf_op jit(solution)/shard_map/ppermute | solution.py:35
  186.0 28.3 %collective-permute-start.10 = (bf16[4,256,128]{2,1,0:T(8,128)(2,1)S(1)}, bf16[4,256,128]{2,1,0:T(8,128)(2,1)S(1)}, u32[]{:S(2)}, u32[]{:S(2)}) collective-permute-start(bf16[4,256,128]{2,1,0:T(8,128)(2,1)S(1)} %get-tuple-element.45), channel_id=1, source_target_pairs={{0,48},{4,52},{8,56},{12,60},{16,0},{20,4},{24,8},{28,12},{32,16},... | collective-permute-start | bytes 786440 | tf_op jit(solution)/shard_map/ppermute | solution.py:35
  191.4 30.7 %collective-permute-start.8 = (bf16[4,256,128]{2,1,0:T(8,128)(2,1)S(1)}, bf16[4,256,128]{2,1,0:T(8,128)(2,1)S(1)}, u32[]{:S(2)}, u32[]{:S(2)}) collective-permute-start(bf16[4,256,128]{2,1,0:T(8,128)(2,1)S(1)} %get-tuple-element.40), channel_id=1, source_target_pairs={{0,48},{4,52},{8,56},{12,60},{16,0},{20,4},{24,8},{28,12},{32,16},... | collective-permute-start | bytes 786440 | tf_op jit(solution)/shard_map/ppermute | solution.py:35
  193.9 29.3 %collective-permute-start.7 = (bf16[4,256,128]{2,1,0:T(8,128)(2,1)S(1)}, bf16[4,256,128]{2,1,0:T(8,128)(2,1)S(1)}, u32[]{:S(2)}, u32[]{:S(2)}) collective-permute-start(bf16[4,256,128]{2,1,0:T(8,128)(2,1)S(1)} %add_convert_fusion.3), channel_id=1, source_target_pairs={{0,16},{4,20},{8,24},{12,28},{16,32},{20,36},{24,40},{28,44},{32,4... | collective-permute-start | bytes 786440 | tf_op jit(solution)/shard_map/ppermute | solution.py:35
  201.2 27.6 %collective-permute-start.9 = (bf16[4,256,128]{2,1,0:T(8,128)(2,1)S(1)}, bf16[4,256,128]{2,1,0:T(8,128)(2,1)S(1)}, u32[]{:S(2)}, u32[]{:S(2)}) collective-permute-start(bf16[4,256,128]{2,1,0:T(8,128)(2,1)S(1)} %get-tuple-element.43), channel_id=1, source_target_pairs={{0,16},{4,20},{8,24},{12,28},{16,32},{20,36},{24,40},{28,44},{32,4... | collective-permute-start | bytes 786440 | tf_op jit(solution)/shard_map/ppermute | solution.py:35
  214.4 22.3 %collective-permute-start.11 = (bf16[4,256,128]{2,1,0:T(8,128)(2,1)S(1)}, bf16[4,256,128]{2,1,0:T(8,128)(2,1)S(1)}, u32[]{:S(2)}, u32[]{:S(2)}) collective-permute-start(bf16[4,256,128]{2,1,0:T(8,128)(2,1)S(1)} %add_convert_fusion.1), channel_id=1, source_target_pairs={{0,48},{4,52},{8,56},{12,60},{16,0},{20,4},{24,8},{28,12},{32,16},... | collective-permute-start | bytes 786440 | tf_op jit(solution)/shard_map/ppermute | solution.py:35
Sparse Core Ops, SparseCore 0:
  170.4 231.1 all-gather.2

commit v3 on v2

--- a/solution.py
+++ b/solution.py
@@ -24,6 +24,7 @@
 NEG = -1e30
 
 SPREAD_GROUPS = [[x * ZS + g * SPB + r for x in range(XS) for r in range(SPB)] for g in range(ZG)]
+Z_GROUPS = [[x * ZS + z for z in range(ZS)] for x in range(XS)]
 X_GROUPS = [[x * ZS + z for x in range(XS)] for z in range(ZS)]
 
 
@@ -41,6 +42,16 @@
 
 def swap_x(arr):
     return lax.all_to_all(arr, "ctx", 0, 0, axis_index_groups=X_GROUPS, tiled=True)
+
+
+def swap_sink(vals, axes, groups, after=None):
+    count = 8 if groups is None else len(groups[0])
+    vals = vals.reshape(1, -1)
+    size = vals.shape[1]
+    rows = jnp.broadcast_to(jnp.pad(vals, ((0, 0), (0, 128 - size))), (count, 128))
+    if after is not None:
+        rows, _ = lax.optimization_barrier((rows, after))
+    return lax.all_to_all(rows, axes, 0, 0, axis_index_groups=groups, tiled=True)[:, :size]
 
 
 def dot(left, right, left_dim, right_dim):
@@ -254,7 +265,9 @@
     below = [shift_groups(arr, 1) for arr in held]
     above = [shift_groups(arr, -1) for arr in held]
     far = [shift_groups(below[0], 1), shift_groups(above[1], -1)]
-    ready, below[1], above[1] = lax.optimization_barrier((held[0], below[1], above[1]))
+    ready, below[1], above[1], far[1] = lax.optimization_barrier(
+        (held[0], below[1], above[1], far[1])
+    )
     first = gather_picks(index[0], (ready, above[0], far[0], below[0]))
     second = gather_picks(index[1], (held[1], above[1], far[1], below[1]))
     picks = [swap_x(arr.reshape(XS, TOPK * ROWS, DH)) for arr in (first, second)]
@@ -266,27 +279,27 @@
             h, use[h], sink_mine[h : h + 1], query_rows, grad_rows, own[h], picks[h], earlier
         )
         earlier = (att, dq)
-        sink_heads.append(sink_sum)
+        sink_heads.append(sink_sum[0, 0])
         back = swap_x(part.reshape(XS, KINDS * ROWS, DH)).reshape(XS, KINDS, ROWS, DH)
         pools.append(list(pool_parts(index[h], back)))
-    lane = lax.broadcasted_iota(jnp.int32, (8, 128), 1)
-    sink_local = jnp.where(lane == 0, sink_heads[0], sink_heads[1])
-    sink_local, pools[0][0] = lax.optimization_barrier((sink_local, pools[0][0]))
-    sink_all = lax.all_gather(sink_local, ("dp", "ctx", "head"))[:, 0, :HPD]
     up_far = shift_groups(pools[0][2], 1)
     down_near = shift_groups(pools[0][3], -1)
     down_far = shift_groups(pools[1][2], -1)
     up_near = shift_groups(pools[1][1], 1)
+    sink_all = swap_sink(jnp.stack(sink_heads), "ctx", Z_GROUPS, after=up_far)
+    sink_all = jnp.sum(sink_all.reshape(ZG, SPB, HPD), axis=0)
+    sink_all = jnp.sum(swap_sink(sink_all, "ctx", X_GROUPS), axis=0)
+    sink_all = swap_sink(sink_all, ("dp", "head"), None)
+    grad_sink = jnp.sum(sink_all.reshape(-1, HEADS), axis=0)
     up = [shift_groups(add_rounded(pools[0][1], up_far), 1), up_near]
     down = [down_near, shift_groups(add_rounded(pools[1][3], down_far), -1)]
     pooled = [add_rounded(pools[h][0], up[h], down[h]) for h in range(HPD)]
+    pooled[0], grad_sink = lax.optimization_barrier((pooled[0], grad_sink))
     pooled = jnp.stack([arr.reshape(XS, SPB, 2 * FRAG, DH) for arr in pooled], axis=2)
     homed = swap_spread(pooled.reshape(XS * SPB, HPD * 2 * FRAG, DH))
     totals = jnp.transpose(homed.reshape(XS, SPB, HPD, 2, FRAG, DH), (3, 0, 4, 1, 2, 5))
     grad_key = totals[0].reshape(key.shape)
     grad_value = totals[1].reshape(value.shape)
-    sink_all = sink_all.reshape(-1, nblk, SPB, HEADS // (SPB * HPD), HPD)
-    grad_sink = jnp.transpose(jnp.sum(sink_all, axis=(0, 1)), (1, 0, 2)).reshape(HEADS)
     return (att.reshape(query.shape), dq.reshape(query.shape), grad_key, grad_value, grad_sink)
 
 

time: 414 us -> 282 us (0.68)
  waiting for transfers between devices: 236 us -> 99.5 us
  starting transfers between devices: 95.5 us -> 111 us
  between operations: 14.4 us -> 1.1 us
    all_gather x1 -> x0, waiting for transfers between devices: 129 us -> none  [body(): sink_all = lax.all_gather(sink_local, ('dp', 'ctx', 'head'))[:, 0, :HPD]]
    ppermute x12, waiting for transfers between devices: 72.3 us -> 57.4 us  [shift_groups(): return lax.ppermute(arr, 'ctx', pairs)]
    all_to_all x0 -> x2, starting transfers between devices: none -> 12.3 us  [swap_sink(): lax.all_to_all(rows, axes, 0, 0, axis_index_groups=groups, tiled=True)]
    all_to_all x0 -> x1, blocking collectives: none -> 7.69 us  [swap_sink(): lax.all_to_all(rows, axes, 0, 0, axis_index_groups=groups, tiled=True)]
    ppermute x12, starting transfers between devices: 62.9 us -> 69.3 us  [shift_groups(): return lax.ppermute(arr, 'ctx', pairs)]
    all_to_all x1, blocking collectives: 33.3 us -> 27.5 us  [swap_spread(): lax.all_to_all(arr, 'ctx', 0, 0, axis_index_groups=SPREAD_GROUPS, tiled=T...]
    all_to_all x0 -> x2, waiting for transfers between devices: none -> 5.05 us  [swap_sink(): lax.all_to_all(rows, axes, 0, 0, axis_index_groups=groups, tiled=True)]
  transfers between devices with their start and end apart: 20 -> 21, of which waited for: 14 -> 11; matrix products, arithmetic and copies ran while one was open for 1% -> 3% of each run, Pallas kernels for 4% -> 7%
where the time goes in v3:
time: 282 us; the launch traced here: 281 us
  starting transfers between devices  111 us (39%)
  waiting for transfers between devices  99.5 us (35%)
  blocking collectives  35.2 us (12%)
  Pallas kernels  18.8 us (7%)
  local copies, waits for them, and re-layouts  10 us (4%)
  other arithmetic  5.02 us (2%)
    ppermute x12, starting transfers between devices, shift_groups(): return lax.ppermute(arr, 'ctx', pairs)  69.3 us
    ppermute x12, waiting for transfers between devices, shift_groups(): return lax.ppermute(arr, 'ctx', pairs)  57.4 us
    all_to_all x1, blocking collectives, swap_spread(): lax.all_to_all(arr, 'ctx', 0, 0, axis_index_groups=SPREAD_GROUPS, tiled=T...  27.5 us
    all_to_all x6, waiting for transfers between devices, swap_x(): lax.all_to_all(arr, 'ctx', 0, 0, axis_index_groups=X_GROUPS, tiled=True)  21.7 us
    all_to_all x6, starting transfers between devices, swap_x(): lax.all_to_all(arr, 'ctx', 0, 0, axis_index_groups=X_GROUPS, tiled=True)  21.2 us
    all_to_all x1, waiting for transfers between devices, swap_spread(): lax.all_to_all(arr, 'ctx', 0, 0, axis_index_groups=SPREAD_GROUPS, tiled=T...  15.4 us
    pallas_call x2, Pallas kernels, attend(): pl.pallas_call(attend_kernel, name='attend_head%d' % head, grid=(1,), in_...  13 us
    all_to_all x2, starting transfers between devices, swap_sink(): lax.all_to_all(rows, axes, 0, 0, axis_index_groups=groups, tiled=True)  12.3 us
  transfers between devices with their start and end apart: 21, of which 11 were waited for; matrix products, arithmetic and copies ran while one was open for 3% of the time, Pallas kernels for 7%

profile of v3, /device:TPU:24, one launch (start us, length us, event | category | flops | bytes accessed | tf_op | source)
XLA Modules:
  0.0 280.8 jit_solution(5872894567514167305)
XLA Ops:
  0.7 1.2 reshape.141
  2.0 0.7 pad_maximum_fusion
  2.8 0.9 copy.47
  3.7 8.5 %all-to-all-start = ((bf16[16,128,128]{2,1,0:T(8,128)(2,1)}), bf16[16,128,128]{2,1,0:T(8,128)(2,1)S(1)}, u32[]{:S(2)}, u32[]{:S(2)}) async-start(bf16[16,128,128]{2,1,0:T(8,128)(2,1)} %bitcast.8), calls=%async_computation | async-start | bytes 1048576 | tf_op jit(solution)/shard_map/all_to_all | solution.py:40
  13.2 15.4 %all-to-all-done = bf16[16,128,128]{2,1,0:T(8,128)(2,1)S(1)} async-done(((bf16[16,128,128]{2,1,0:T(8,128)(2,1)}), bf16[16,128,128]{2,1,0:T(8,128)(2,1)S(1)}, u32[]{:S(2)}, u32[]{:S(2)}) %all-to-all-start) | async-done | bytes 524320 | tf_op jit(solution)/shard_map/all_to_all | solution.py:40
  28.7 0.8 fusion.10
  29.5 10.0 %collective-permute-start.1 = (bf16[4,256,128]{2,1,0:T(8,128)(2,1)}, bf16[4,256,128]{2,1,0:T(8,128)(2,1)S(1)}, u32[]{:S(2)}, u32[]{:S(2)}) collective-permute-start(bf16[4,256,128]{2,1,0:T(8,128)(2,1)} %bitcast.11.refs_0_), channel_id=1, source_target_pairs={{0,48},{4,52},{8,56},{12,60},{16,0},{20,4},{24,8},{28,12},{32,16},... | collective-permute-start | bytes 786440 | tf_op jit(solution)/shard_map/ppermute | solution.py:36
  39.5 1.9 collective-permute-start.4
  41.9 3.4 %all-to-all-start.1 = ((bf16[4,256,128]{2,1,0:T(8,128)(2,1)}), bf16[4,256,128]{2,1,0:T(8,128)(2,1)S(1)}, u32[]{:S(2)}, u32[]{:S(2)}) async-start(bf16[4,256,128]{2,1,0:T(8,128)(2,1)} %bitcast.11.refs_0_), calls=%async_computation.1 | async-start | bytes 524288 | tf_op jit(solution)/shard_map/all_to_all | solution.py:44
  45.4 6.9 %collective-permute-start = (bf16[4,256,128]{2,1,0:T(8,128)(2,1)}, bf16[4,256,128]{2,1,0:T(8,128)(2,1)S(1)}, u32[]{:S(2)}, u32[]{:S(2)}) collective-permute-start(bf16[4,256,128]{2,1,0:T(8,128)(2,1)} %bitcast.11.refs_0_), channel_id=1, source_target_pairs={{0,16},{4,20},{8,24},{12,28},{16,32},{20,36},{24,40},{28,44},{32,4... | collective-permute-start | bytes 786440 | tf_op jit(solution)/shard_map/ppermute | solution.py:36
  52.3 2.9 %collective-permute-start.3 = (bf16[4,256,128]{2,1,0:T(8,128)(2,1)}, bf16[4,256,128]{2,1,0:T(8,128)(2,1)S(1)}, u32[]{:S(2)}, u32[]{:S(2)}) collective-permute-start(bf16[4,256,128]{2,1,0:T(8,128)(2,1)} %bitcast.16.refs_0_), channel_id=1, source_target_pairs={{0,48},{4,52},{8,56},{12,60},{16,0},{20,4},{24,8},{28,12},{32,16},... | collective-permute-start | bytes 786440 | tf_op jit(solution)/shard_map/ppermute | solution.py:36
  55.1 7.7 %collective-permute-done.1.refs_1_ = bf16[4,256,128]{2,1,0:T(8,128)(2,1)S(1)} collective-permute-done((bf16[4,256,128]{2,1,0:T(8,128)(2,1)}, bf16[4,256,128]{2,1,0:T(8,128)(2,1)S(1)}, u32[]{:S(2)}, u32[]{:S(2)}) %collective-permute-start.1) | collective-permute-done | bytes 262176 | tf_op jit(solution)/shard_map/ppermute | solution.py:36
  62.8 7.5 %collective-permute-start.2 = (bf16[4,256,128]{2,1,0:T(8,128)(2,1)S(1)}, bf16[4,256,128]{2,1,0:T(8,128)(2,1)S(1)}, u32[]{:S(2)}, u32[]{:S(2)}) collective-permute-start(bf16[4,256,128]{2,1,0:T(8,128)(2,1)S(1)} %collective-permute-done.1.refs_1_), channel_id=1, source_target_pairs={{0,48},{4,52},{8,56},{12,60},{16,0},{20,4},{24,8},{28,12},{32,16},... | collective-permute-start | bytes 786440 | tf_op jit(solution)/shard_map/ppermute | solution.py:36
  70.3 10.8 %collective-permute-done.4.refs_3_ = bf16[4,256,128]{2,1,0:T(8,128)(2,1)S(1)} collective-permute-done((bf16[4,256,128]{2,1,0:T(8,128)(2,1)}, bf16[4,256,128]{2,1,0:T(8,128)(2,1)S(1)}, u32[]{:S(2)}, u32[]{:S(2)}) %collective-permute-start.4) | collective-permute-done | bytes 262176 | tf_op jit(solution)/shard_map/ppermute | solution.py:36
  81.1 7.4 %collective-permute-start.5 = (bf16[4,256,128]{2,1,0:T(8,128)(2,1)S(1)}, bf16[4,256,128]{2,1,0:T(8,128)(2,1)S(1)}, u32[]{:S(2)}, u32[]{:S(2)}) collective-permute-start(bf16[4,256,128]{2,1,0:T(8,128)(2,1)S(1)} %collective-permute-done.4.refs_3_), channel_id=1, source_target_pairs={{0,16},{4,20},{8,24},{12,28},{16,32},{20,36},{24,40},{28,44},{32,4... | collective-permute-start | bytes 786440 | tf_op jit(solution)/shard_map/ppermute | solution.py:36
  88.6 3.4 %all-to-all-start.3 = ((bf16[4,256,128]{2,1,0:T(8,128)(2,1)}), bf16[4,256,128]{2,1,0:T(8,128)(2,1)S(1)}, u32[]{:S(2)}, u32[]{:S(2)}) async-start(bf16[4,256,128]{2,1,0:T(8,128)(2,1)} %bitcast.16.refs_0_), calls=%async_computation.3 | async-start | bytes 524288 | tf_op jit(solution)/shard_map/all_to_all | solution.py:44
  92.2 12.4 %collective-permute-done.refs_3_ = bf16[4,256,128]{2,1,0:T(8,128)(2,1)S(1)} collective-permute-done((bf16[4,256,128]{2,1,0:T(8,128)(2,1)}, bf16[4,256,128]{2,1,0:T(8,128)(2,1)S(1)}, u32[]{:S(2)}, u32[]{:S(2)}) %collective-permute-start) | collective-permute-done | bytes 262176 | tf_op jit(solution)/shard_map/ppermute | solution.py:36
  104.6 8.5 %collective-permute-done.5.refs_2_ = bf16[4,256,128]{2,1,0:T(8,128)(2,1)S(1)} collective-permute-done((bf16[4,256,128]{2,1,0:T(8,128)(2,1)S(1)}, bf16[4,256,128]{2,1,0:T(8,128)(2,1)S(1)}, u32[]{:S(2)}, u32[]{:S(2)}) %collective-permute-start.5) | collective-permute-done | bytes 262176 | tf_op jit(solution)/shard_map/ppermute | solution.py:36
  113.1 2.0 gather_picks.3
  115.1 3.5 %all-to-all-start.4 = ((bf16[4,768,128]{2,1,0:T(8,128)(2,1)}), bf16[4,768,128]{2,1,0:T(8,128)(2,1)S(1)}, u32[]{:S(2)}, u32[]{:S(2)}) async-start(bf16[4,768,128]{2,1,0:T(8,128)(2,1)} %bitcast.21), calls=%async_computation.4 | async-start | bytes 1572864 | tf_op jit(solution)/shard_map/all_to_all | solution.py:44
  120.1 2.0 gather_picks.2
  122.1 9.2 %all-to-all-done.4 = bf16[4,768,128]{2,1,0:T(8,128)(2,1)S(1)} async-done(((bf16[4,768,128]{2,1,0:T(8,128)(2,1)}), bf16[4,768,128]{2,1,0:T(8,128)(2,1)S(1)}, u32[]{:S(2)}, u32[]{:S(2)}) %all-to-all-start.4) | async-done | bytes 786464 | tf_op jit(solution)/shard_map/all_to_all | solution.py:44
  131.3 3.6 %all-to-all-start.2 = ((bf16[4,768,128]{2,1,0:T(8,128)(2,1)}), bf16[4,768,128]{2,1,0:T(8,128)(2,1)S(1)}, u32[]{:S(2)}, u32[]{:S(2)}) async-start(bf16[4,768,128]{2,1,0:T(8,128)(2,1)} %bitcast.17), calls=%async_computation.2 | async-start | bytes 1572864 | tf_op jit(solution)/shard_map/all_to_all | solution.py:44
  135.1 6.5 %attend_head0.1 = (bf16[512,256]{1,0:T(8,128)(2,1)}, bf16[512,256]{1,0:T(8,128)(2,1)}, bf16[4,4,4,2,32,128]{5,4,3,2,1,0:T(8,128)(2,1)}, f32[8,128]{1,0:T(8,128)S(1)}) custom-call(s32[3]{0:T(128)S(1)} %get-tuple-element.59.use_ref, f32[1]{0:T(128)} %get-tuple-element.61.sink_ref, bf16[512,256]{1,0:T(8,128)(2,1)S(1)} %bitcast.84, ...), custom_call_target="tpu_custom_call" | custom-call | flops 2684354560 | bytes 8388608 | tf_op jit(solution)/shard_map/attend_head0/pallas_call | solution.py:141
  141.7 5.2 %all-to-all-done.2 = bf16[4,768,128]{2,1,0:T(8,128)(2,1)S(1)} async-done(((bf16[4,768,128]{2,1,0:T(8,128)(2,1)}), bf16[4,768,128]{2,1,0:T(8,128)(2,1)S(1)}, u32[]{:S(2)}, u32[]{:S(2)}) %all-to-all-start.2) | async-done | bytes 786464 | tf_op jit(solution)/shard_map/all_to_all | solution.py:44
  146.8 3.5 %all-to-all-start.5 = ((bf16[4,1024,128]{2,1,0:T(8,128)(2,1)}), bf16[4,1024,128]{2,1,0:T(8,128)(2,1)S(1)}, u32[]{:S(2)}, u32[]{:S(2)}) async-start(bf16[4,1024,128]{2,1,0:T(8,128)(2,1)} %bitcast.25), calls=%async_computation.5 | async-start | bytes 2097152 | tf_op jit(solution)/shard_map/all_to_all | solution.py:44
  150.4 6.5 %attend_head1.1 = (bf16[512,256]{1,0:T(8,128)(2,1)}, bf16[512,256]{1,0:T(8,128)(2,1)}, bf16[4,4,4,2,32,128]{5,4,3,2,1,0:T(8,128)(2,1)}, f32[8,128]{1,0:T(8,128)S(1)}) custom-call(s32[3]{0:T(128)S(1)} %get-tuple-element.60.use_ref, f32[1]{0:T(128)} %get-tuple-element.62.sink_ref, ...), custom_call_target="tpu_custom_call", output_to_operand_aliasing={{0}: (6, {}), {1}: (7, {})} | custom-call | flops 2684354560 | bytes 8388608 | tf_op jit(solution)/shard_map/attend_head1/pallas_call | solution.py:141
  156.8 7.3 %all-to-all-done.5 = bf16[4,1024,128]{2,1,0:T(8,128)(2,1)S(1)} async-done(((bf16[4,1024,128]{2,1,0:T(8,128)(2,1)}), bf16[4,1024,128]{2,1,0:T(8,128)(2,1)S(1)}, u32[]{:S(2)}, u32[]{:S(2)}) %all-to-all-start.5) | async-done | bytes 1048608 | tf_op jit(solution)/shard_map/all_to_all | solution.py:44
  164.1 3.7 %all-to-all-start.9 = ((bf16[4,1024,128]{2,1,0:T(8,128)(2,1)}), bf16[4,1024,128]{2,1,0:T(8,128)(2,1)S(1)}, u32[]{:S(2)}, u32[]{:S(2)}) async-start(bf16[4,1024,128]{2,1,0:T(8,128)(2,1)} %bitcast.41), calls=%async_computation.9 | async-start | bytes 2097152 | tf_op jit(solution)/shard_map/all_to_all | solution.py:44
  167.8 0.9 pool_parts.2
  168.7 1.9 collective-permute-start.6
  171.7 1.4 maximum_bitcast_fusion
  173.1 7.8 %collective-permute-start.8 = (bf16[4,256,128]{2,1,0:T(8,128)(2,1)S(1)}, bf16[4,256,128]{2,1,0:T(8,128)(2,1)}, u32[]{:S(2)}, u32[]{:S(2)}) collective-permute-start(bf16[4,256,128]{2,1,0:T(8,128)(2,1)S(1)} %get-tuple-element.40), channel_id=1, source_target_pairs={{0,48},{4,52},{8,56},{12,60},{16,0},{20,4},{24,8},{28,12},{32,16},... | collective-permute-start | bytes 786440 | tf_op jit(solution)/shard_map/ppermute | solution.py:36
  180.9 0.9 pool_parts.3
  181.8 1.9 collective-permute-start.9
  183.8 7.8 %collective-permute-start.10 = (bf16[4,256,128]{2,1,0:T(8,128)(2,1)S(1)}, bf16[4,256,128]{2,1,0:T(8,128)(2,1)S(1)}, u32[]{:S(2)}, u32[]{:S(2)}) collective-permute-start(bf16[4,256,128]{2,1,0:T(8,128)(2,1)S(1)} %get-tuple-element.49), channel_id=1, source_target_pairs={{0,48},{4,52},{8,56},{12,60},{16,0},{20,4},{24,8},{28,12},{32,16},... | collective-permute-start | bytes 786440 | tf_op jit(solution)/shard_map/ppermute | solution.py:36
  191.6 12.7 %collective-permute-done.6 = bf16[4,256,128]{2,1,0:T(8,128)(2,1)S(1)} collective-permute-done((bf16[4,256,128]{2,1,0:T(8,128)(2,1)S(1)}, bf16[4,256,128]{2,1,0:T(8,128)(2,1)S(1)}, u32[]{:S(2)}, u32[]{:S(2)}) %collective-permute-start.6) | collective-permute-done | bytes 262176 | tf_op jit(solution)/shard_map/ppermute | solution.py:36
  204.9 8.1 %all-to-all-start.6 = ((f32[16,1,128]{2,1,0:T(1,128)}), f32[16,1,128]{2,1,0:T(1,128)S(1)}, u32[]{:S(2)}, u32[]{:S(2)}) async-start(f32[16,1,128]{2,1,0:T(1,128)} %bitcast.31), calls=%async_computation.6 | async-start | bytes 16384 | tf_op jit(solution)/shard_map/all_to_all | solution.py:54
  213.2 7.7 %collective-permute-start.7 = (bf16[4,256,128]{2,1,0:T(8,128)(2,1)S(1)}, bf16[4,256,128]{2,1,0:T(8,128)(2,1)S(1)}, u32[]{:S(2)}, u32[]{:S(2)}) collective-permute-start(bf16[4,256,128]{2,1,0:T(8,128)(2,1)S(1)} %add_convert_fusion.3), channel_id=1, source_target_pairs={{0,16},{4,20},{8,24},{12,28},{16,32},{20,36},{24,40},{28,44},{32,4... | collective-permute-start | bytes 786440 | tf_op jit(solution)/shard_map/ppermute | solution.py:36
  220.9 5.0 %all-to-all-done.6 = f32[16,1,128]{2,1,0:T(1,128)S(1)} async-done(((f32[16,1,128]{2,1,0:T(1,128)}), f32[16,1,128]{2,1,0:T(1,128)S(1)}, u32[]{:S(2)}, u32[]{:S(2)}) %all-to-all-start.6) | async-done | bytes 8224 | tf_op jit(solution)/shard_map/all_to_all | solution.py:54
  226.6 4.1 %all-to-all-start.7 = ((f32[4,1,128]{2,1,0:T(1,128)}), f32[4,1,128]{2,1,0:T(1,128)S(1)}, u32[]{:S(2)}, u32[]{:S(2)}) async-start(f32[4,1,128]{2,1,0:T(1,128)} %broadcast_in_dim.116), calls=%async_computation.7 | async-start | bytes 4096 | tf_op jit(solution)/shard_map/all_to_all | solution.py:54
  230.8 5.4 %collective-permute-start.11 = (bf16[4,256,128]{2,1,0:T(8,128)(2,1)S(1)}, bf16[4,256,128]{2,1,0:T(8,128)(2,1)S(1)}, u32[]{:S(2)}, u32[]{:S(2)}) collective-permute-start(bf16[4,256,128]{2,1,0:T(8,128)(2,1)S(1)} %add_convert_fusion.1), channel_id=1, source_target_pairs={{0,48},{4,52},{8,56},{12,60},{16,0},{20,4},{24,8},{28,12},{32,16},... | collective-permute-start | bytes 786440 | tf_op jit(solution)/shard_map/ppermute | solution.py:36
  236.3 7.7 %all_to_all.70 = f32[8,1,128]{2,1,0:T(1,128)S(1)} all-to-all(f32[8,1,128]{2,1,0:T(1,128)S(1)} %broadcast_in_dim.117), channel_id=1, replica_groups=mesh['dp'=2,'ctx'=64,'head'=4] {'dp','head'}, dimensions={0} | all-to-all | bytes 8192 | tf_op jit(solution)/shard_map/all_to_all | solution.py:54
  244.6 1.1 add_convert_fusion.2
  245.7 5.2 %collective-permute-done.11 = bf16[4,256,128]{2,1,0:T(8,128)(2,1)S(1)} collective-permute-done((bf16[4,256,128]{2,1,0:T(8,128)(2,1)S(1)}, bf16[4,256,128]{2,1,0:T(8,128)(2,1)S(1)}, u32[]{:S(2)}, u32[]{:S(2)}) %collective-permute-start.11) | collective-permute-done | bytes 262176 | tf_op jit(solution)/shard_map/ppermute | solution.py:36
  251.1 27.5 %all_to_all.71 = bf16[16,128,128]{2,1,0:T(8,128)(2,1)S(1)} all-to-all(bf16[16,128,128]{2,1,0:T(8,128)(2,1)S(1)} %bitcast.90), channel_id=1, replica_groups={{0,4,8,12,64,68,72,76,128,132,136,140,192,196,200,204},{16,20,24,28,80,..., dimensions={0} | all-to-all | bytes 1048576 | tf_op jit(solution)/shard_map/all_to_all | solution.py:40
  278.9 0.9 reshape_squeeze.15
  279.9 0.9 reshape_squeeze.14
  (62 shorter events, 7.2 us)
Async XLA Ops:
  0.6 40.8 %copy-start = (s32[1,16,8,3]{1,2,3,0:T(8,128)S(1)}, s32[1,16,8,3]{1,2,3,0:T(8,128)}, u32[]{:S(2)}) copy-start(s32[1,16,8,3]{1,2,3,0:T(8,128)} %param.11) | copy-start | bytes 4612
  0.6 1.2 copy-start.3
  3.7 25.0 %all-to-all-start = ((bf16[16,128,128]{2,1,0:T(8,128)(2,1)}), bf16[16,128,128]{2,1,0:T(8,128)(2,1)S(1)}, u32[]{:S(2)}, u32[]{:S(2)}) async-start(bf16[16,128,128]{2,1,0:T(8,128)(2,1)} %bitcast.8), calls=%async_computation | async-start | bytes 1048576 | tf_op jit(solution)/shard_map/all_to_all | solution.py:40
  12.2 0.7 copy-start.4
  29.5 33.3 %collective-permute-start.1 = (bf16[4,256,128]{2,1,0:T(8,128)(2,1)}, bf16[4,256,128]{2,1,0:T(8,128)(2,1)S(1)}, u32[]{:S(2)}, u32[]{:S(2)}) collective-permute-start(bf16[4,256,128]{2,1,0:T(8,128)(2,1)} %bitcast.11.refs_0_), channel_id=1, source_target_pairs={{0,48},{4,52},{8,56},{12,60},{16,0},{20,4},{24,8},{28,12},{32,16},... | collective-permute-start | bytes 786440 | tf_op jit(solution)/shard_map/ppermute | solution.py:36
  39.5 41.6 %collective-permute-start.4 = (bf16[4,256,128]{2,1,0:T(8,128)(2,1)}, bf16[4,256,128]{2,1,0:T(8,128)(2,1)S(1)}, u32[]{:S(2)}, u32[]{:S(2)}) collective-permute-start(bf16[4,256,128]{2,1,0:T(8,128)(2,1)} %bitcast.16.refs_0_), channel_id=1, source_target_pairs={{0,16},{4,20},{8,24},{12,28},{16,32},{20,36},{24,40},{28,44},{32,4... | collective-permute-start | bytes 786440 | tf_op jit(solution)/shard_map/ppermute | solution.py:36
  41.9 46.6 %all-to-all-start.1 = ((bf16[4,256,128]{2,1,0:T(8,128)(2,1)}), bf16[4,256,128]{2,1,0:T(8,128)(2,1)S(1)}, u32[]{:S(2)}, u32[]{:S(2)}) async-start(bf16[4,256,128]{2,1,0:T(8,128)(2,1)} %bitcast.11.refs_0_), calls=%async_computation.1 | async-start | bytes 524288 | tf_op jit(solution)/shard_map/all_to_all | solution.py:44
  45.4 59.2 %collective-permute-start = (bf16[4,256,128]{2,1,0:T(8,128)(2,1)}, bf16[4,256,128]{2,1,0:T(8,128)(2,1)S(1)}, u32[]{:S(2)}, u32[]{:S(2)}) collective-permute-start(bf16[4,256,128]{2,1,0:T(8,128)(2,1)} %bitcast.11.refs_0_), channel_id=1, source_target_pairs={{0,16},{4,20},{8,24},{12,28},{16,32},{20,36},{24,40},{28,44},{32,4... | collective-permute-start | bytes 786440 | tf_op jit(solution)/shard_map/ppermute | solution.py:36
  52.3 52.4 %collective-permute-start.3 = (bf16[4,256,128]{2,1,0:T(8,128)(2,1)}, bf16[4,256,128]{2,1,0:T(8,128)(2,1)S(1)}, u32[]{:S(2)}, u32[]{:S(2)}) collective-permute-start(bf16[4,256,128]{2,1,0:T(8,128)(2,1)} %bitcast.16.refs_0_), channel_id=1, source_target_pairs={{0,48},{4,52},{8,56},{12,60},{16,0},{20,4},{24,8},{28,12},{32,16},... | collective-permute-start | bytes 786440 | tf_op jit(solution)/shard_map/ppermute | solution.py:36
  62.8 41.8 %collective-permute-start.2 = (bf16[4,256,128]{2,1,0:T(8,128)(2,1)S(1)}, bf16[4,256,128]{2,1,0:T(8,128)(2,1)S(1)}, u32[]{:S(2)}, u32[]{:S(2)}) collective-permute-start(bf16[4,256,128]{2,1,0:T(8,128)(2,1)S(1)} %collective-permute-done.1.refs_1_), channel_id=1, source_target_pairs={{0,48},{4,52},{8,56},{12,60},{16,0},{20,4},{24,8},{28,12},{32,16},... | collective-permute-start | bytes 786440 | tf_op jit(solution)/shard_map/ppermute | solution.py:36
  81.1 32.0 %collective-permute-start.5 = (bf16[4,256,128]{2,1,0:T(8,128)(2,1)S(1)}, bf16[4,256,128]{2,1,0:T(8,128)(2,1)S(1)}, u32[]{:S(2)}, u32[]{:S(2)}) collective-permute-start(bf16[4,256,128]{2,1,0:T(8,128)(2,1)S(1)} %collective-permute-done.4.refs_3_), channel_id=1, source_target_pairs={{0,16},{4,20},{8,24},{12,28},{16,32},{20,36},{24,40},{28,44},{32,4... | collective-permute-start | bytes 786440 | tf_op jit(solution)/shard_map/ppermute | solution.py:36
  88.6 26.5 %all-to-all-start.3 = ((bf16[4,256,128]{2,1,0:T(8,128)(2,1)}), bf16[4,256,128]{2,1,0:T(8,128)(2,1)S(1)}, u32[]{:S(2)}, u32[]{:S(2)}) async-start(bf16[4,256,128]{2,1,0:T(8,128)(2,1)} %bitcast.16.refs_0_), calls=%async_computation.3 | async-start | bytes 524288 | tf_op jit(solution)/shard_map/all_to_all | solution.py:44
  115.1 16.2 %all-to-all-start.4 = ((bf16[4,768,128]{2,1,0:T(8,128)(2,1)}), bf16[4,768,128]{2,1,0:T(8,128)(2,1)S(1)}, u32[]{:S(2)}, u32[]{:S(2)}) async-start(bf16[4,768,128]{2,1,0:T(8,128)(2,1)} %bitcast.21), calls=%async_computation.4 | async-start | bytes 1572864 | tf_op jit(solution)/shard_map/all_to_all | solution.py:44
  118.6 0.7 copy-start.5
  131.3 3.8 %copy-start.1 = (bf16[1,1,1,512,256]{4,3,2,1,0:T(8,128)(2,1)S(1)}, bf16[1,1,1,512,256]{4,3,2,1,0:T(8,128)(2,1)}, u32[]{:S(2)}) copy-start(bf16[1,1,1,512,256]{4,3,2,1,0:T(8,128)(2,1)} %param.7) | copy-start | bytes 786436
  131.3 3.8 %copy-start.2 = (bf16[1,1,1,512,256]{4,3,2,1,0:T(8,128)(2,1)S(1)}, bf16[1,1,1,512,256]{4,3,2,1,0:T(8,128)(2,1)}, u32[]{:S(2)}) copy-start(bf16[1,1,1,512,256]{4,3,2,1,0:T(8,128)(2,1)} %param.10) | copy-start | bytes 786436
  131.3 15.5 %all-to-all-start.2 = ((bf16[4,768,128]{2,1,0:T(8,128)(2,1)}), bf16[4,768,128]{2,1,0:T(8,128)(2,1)S(1)}, u32[]{:S(2)}, u32[]{:S(2)}) async-start(bf16[4,768,128]{2,1,0:T(8,128)(2,1)} %bitcast.17), calls=%async_computation.2 | async-start | bytes 1572864 | tf_op jit(solution)/shard_map/all_to_all | solution.py:44
  146.8 17.3 %all-to-all-start.5 = ((bf16[4,1024,128]{2,1,0:T(8,128)(2,1)}), bf16[4,1024,128]{2,1,0:T(8,128)(2,1)S(1)}, u32[]{:S(2)}, u32[]{:S(2)}) async-start(bf16[4,1024,128]{2,1,0:T(8,128)(2,1)} %bitcast.25), calls=%async_computation.5 | async-start | bytes 2097152 | tf_op jit(solution)/shard_map/all_to_all | solution.py:44
  164.1 16.8 %all-to-all-start.9 = ((bf16[4,1024,128]{2,1,0:T(8,128)(2,1)}), bf16[4,1024,128]{2,1,0:T(8,128)(2,1)S(1)}, u32[]{:S(2)}, u32[]{:S(2)}) async-start(bf16[4,1024,128]{2,1,0:T(8,128)(2,1)} %bitcast.41), calls=%async_computation.9 | async-start | bytes 2097152 | tf_op jit(solution)/shard_map/all_to_all | solution.py:44
  168.7 35.6 %collective-permute-start.6 = (bf16[4,256,128]{2,1,0:T(8,128)(2,1)S(1)}, bf16[4,256,128]{2,1,0:T(8,128)(2,1)S(1)}, u32[]{:S(2)}, u32[]{:S(2)}) collective-permute-start(bf16[4,256,128]{2,1,0:T(8,128)(2,1)S(1)} %get-tuple-element.39), channel_id=1, source_target_pairs={{0,16},{4,20},{8,24},{12,28},{16,32},{20,36},{24,40},{28,44},{32,4... | collective-permute-start | bytes 786440 | tf_op jit(solution)/shard_map/ppermute | solution.py:36
  173.1 71.6 %collective-permute-start.8 = (bf16[4,256,128]{2,1,0:T(8,128)(2,1)S(1)}, bf16[4,256,128]{2,1,0:T(8,128)(2,1)}, u32[]{:S(2)}, u32[]{:S(2)}) collective-permute-start(bf16[4,256,128]{2,1,0:T(8,128)(2,1)S(1)} %get-tuple-element.40), channel_id=1, source_target_pairs={{0,48},{4,52},{8,56},{12,60},{16,0},{20,4},{24,8},{28,12},{32,16},... | collective-permute-start | bytes 786440 | tf_op jit(solution)/shard_map/ppermute | solution.py:36
  181.8 63.9 %collective-permute-start.9 = (bf16[4,256,128]{2,1,0:T(8,128)(2,1)S(1)}, bf16[4,256,128]{2,1,0:T(8,128)(2,1)S(1)}, u32[]{:S(2)}, u32[]{:S(2)}) collective-permute-start(bf16[4,256,128]{2,1,0:T(8,128)(2,1)S(1)} %get-tuple-element.47), channel_id=1, source_target_pairs={{0,16},{4,20},{8,24},{12,28},{16,32},{20,36},{24,40},{28,44},{32,4... | collective-permute-start | bytes 786440 | tf_op jit(solution)/shard_map/ppermute | solution.py:36
  183.8 47.0 %collective-permute-start.10 = (bf16[4,256,128]{2,1,0:T(8,128)(2,1)S(1)}, bf16[4,256,128]{2,1,0:T(8,128)(2,1)S(1)}, u32[]{:S(2)}, u32[]{:S(2)}) collective-permute-start(bf16[4,256,128]{2,1,0:T(8,128)(2,1)S(1)} %get-tuple-element.49), channel_id=1, source_target_pairs={{0,48},{4,52},{8,56},{12,60},{16,0},{20,4},{24,8},{28,12},{32,16},... | collective-permute-start | bytes 786440 | tf_op jit(solution)/shard_map/ppermute | solution.py:36
  204.9 21.0 %all-to-all-start.6 = ((f32[16,1,128]{2,1,0:T(1,128)}), f32[16,1,128]{2,1,0:T(1,128)S(1)}, u32[]{:S(2)}, u32[]{:S(2)}) async-start(f32[16,1,128]{2,1,0:T(1,128)} %bitcast.31), calls=%async_computation.6 | async-start | bytes 16384 | tf_op jit(solution)/shard_map/all_to_all | solution.py:54
  213.2 31.5 %collective-permute-start.7 = (bf16[4,256,128]{2,1,0:T(8,128)(2,1)S(1)}, bf16[4,256,128]{2,1,0:T(8,128)(2,1)S(1)}, u32[]{:S(2)}, u32[]{:S(2)}) collective-permute-start(bf16[4,256,128]{2,1,0:T(8,128)(2,1)S(1)} %add_convert_fusion.3), channel_id=1, source_target_pairs={{0,16},{4,20},{8,24},{12,28},{16,32},{20,36},{24,40},{28,44},{32,4... | collective-permute-start | bytes 786440 | tf_op jit(solution)/shard_map/ppermute | solution.py:36
  226.6 9.6 %all-to-all-start.7 = ((f32[4,1,128]{2,1,0:T(1,128)}), f32[4,1,128]{2,1,0:T(1,128)S(1)}, u32[]{:S(2)}, u32[]{:S(2)}) async-start(f32[4,1,128]{2,1,0:T(1,128)} %broadcast_in_dim.116), calls=%async_computation.7 | async-start | bytes 4096 | tf_op jit(solution)/shard_map/all_to_all | solution.py:54
  230.8 20.1 %collective-permute-start.11 = (bf16[4,256,128]{2,1,0:T(8,128)(2,1)S(1)}, bf16[4,256,128]{2,1,0:T(8,128)(2,1)S(1)}, u32[]{:S(2)}, u32[]{:S(2)}) collective-permute-start(bf16[4,256,128]{2,1,0:T(8,128)(2,1)S(1)} %add_convert_fusion.1), channel_id=1, source_target_pairs={{0,48},{4,52},{8,56},{12,60},{16,0},{20,4},{24,8},{28,12},{32,16},... | collective-permute-start | bytes 786440 | tf_op jit(solution)/shard_map/ppermute | solution.py:36

commit v4 on v3

--- a/solution.py
+++ b/solution.py
@@ -262,36 +262,48 @@
     query_rows = query.reshape(BLOCK, HPD * DH)
     grad_rows = grad_out.reshape(BLOCK, HPD * DH)
     own = [swap_x(arr) for arr in held]
-    below = [shift_groups(arr, 1) for arr in held]
-    above = [shift_groups(arr, -1) for arr in held]
-    far = [shift_groups(below[0], 1), shift_groups(above[1], -1)]
-    ready, below[1], above[1], far[1] = lax.optimization_barrier(
-        (held[0], below[1], above[1], far[1])
-    )
-    first = gather_picks(index[0], (ready, above[0], far[0], below[0]))
-    second = gather_picks(index[1], (held[1], above[1], far[1], below[1]))
-    picks = [swap_x(arr.reshape(XS, TOPK * ROWS, DH)) for arr in (first, second)]
+    below = [shift_groups(held[0], 1), None]
+    above = [shift_groups(held[0], -1), None]
+    down, _ = lax.optimization_barrier((held[1], below[0]))
+    above[1] = shift_groups(down, -1)
+    far = [shift_groups(below[0], 1), None]
+    up, far[0] = lax.optimization_barrier((held[1], far[0]))
+    below[1] = shift_groups(up, 1)
+    far[1] = shift_groups(above[1], -1)
+    ready, above[1], own = lax.optimization_barrier((held[0], above[1], own))
+    sources = [(ready, above[0], far[0], below[0]), None]
     earlier = ()
     sink_heads = []
     pools = []
     for h in range(HPD):
+        picks = swap_x(gather_picks(index[h], sources[h]).reshape(XS, TOPK * ROWS, DH))
         att, dq, part, sink_sum = attend(
-            h, use[h], sink_mine[h : h + 1], query_rows, grad_rows, own[h], picks[h], earlier
+            h, use[h], sink_mine[h : h + 1], query_rows, grad_rows, own[h], picks, earlier
         )
         earlier = (att, dq)
         sink_heads.append(sink_sum[0, 0])
+        if h == 0:
+            part, below[1], far[1] = lax.optimization_barrier((part, below[1], far[1]))
+        else:
+            part, up_far, down_near = lax.optimization_barrier((part, up_far, down_near))
         back = swap_x(part.reshape(XS, KINDS * ROWS, DH)).reshape(XS, KINDS, ROWS, DH)
-        pools.append(list(pool_parts(index[h], back)))
-    up_far = shift_groups(pools[0][2], 1)
-    down_near = shift_groups(pools[0][3], -1)
+        if h > 0:
+            up_first = shift_groups(add_rounded(pools[0][1], up_far), 1)
+            back, up_first = lax.optimization_barrier((back, up_first))
+        pools.append(pool_parts(index[h], back))
+        if h == 0:
+            up_far = shift_groups(pools[0][2], 1)
+            down_near = shift_groups(pools[0][3], -1)
+            late, _ = lax.optimization_barrier((held[1], pools[0]))
+            sources[1] = (late, above[1], far[1], below[1])
     down_far = shift_groups(pools[1][2], -1)
     up_near = shift_groups(pools[1][1], 1)
-    sink_all = swap_sink(jnp.stack(sink_heads), "ctx", Z_GROUPS, after=up_far)
+    sink_all = swap_sink(jnp.stack(sink_heads), "ctx", Z_GROUPS, after=down_far)
     sink_all = jnp.sum(sink_all.reshape(ZG, SPB, HPD), axis=0)
     sink_all = jnp.sum(swap_sink(sink_all, "ctx", X_GROUPS), axis=0)
     sink_all = swap_sink(sink_all, ("dp", "head"), None)
     grad_sink = jnp.sum(sink_all.reshape(-1, HEADS), axis=0)
-    up = [shift_groups(add_rounded(pools[0][1], up_far), 1), up_near]
+    up = [up_first, up_near]
     down = [down_near, shift_groups(add_rounded(pools[1][3], down_far), -1)]
     pooled = [add_rounded(pools[h][0], up[h], down[h]) for h in range(HPD)]
     pooled[0], grad_sink = lax.optimization_barrier((pooled[0], grad_sink))

time: 282 us -> 289 us (1.025)
  blocking collectives: 35.2 us -> 17.4 us
  starting transfers between devices: 111 us -> 127 us
  waiting for transfers between devices: 99.5 us -> 107 us
    all_to_all x1, blocking collectives: 27.5 us -> 17.4 us  [swap_spread(): lax.all_to_all(arr, 'ctx', 0, 0, axis_index_groups=SPREAD_GROUPS, tiled=T...]
    all_to_all x1 -> x0, blocking collectives: 7.69 us -> none  [swap_sink(): lax.all_to_all(rows, axes, 0, 0, axis_index_groups=groups, tiled=True)]
    ppermute x12, starting transfers between devices: 69.3 us -> 76.9 us  [shift_groups(): return lax.ppermute(arr, 'ctx', pairs)]
    all_to_all x2 -> x3, waiting for transfers between devices: 5.05 us -> 11.6 us  [swap_sink(): lax.all_to_all(rows, axes, 0, 0, axis_index_groups=groups, tiled=True)]
    all_to_all x2 -> x3, starting transfers between devices: 12.3 us -> 18 us  [swap_sink(): lax.all_to_all(rows, axes, 0, 0, axis_index_groups=groups, tiled=True)]
    ppermute x12, waiting for transfers between devices: 57.4 us -> 61 us  [shift_groups(): return lax.ppermute(arr, 'ctx', pairs)]
    all_to_all x6, waiting for transfers between devices: 21.7 us -> 18.6 us  [swap_x(): lax.all_to_all(arr, 'ctx', 0, 0, axis_index_groups=X_GROUPS, tiled=True)]
  transfers between devices with their start and end apart: 21 -> 22, of which waited for: 11 -> 16; matrix products, arithmetic and copies ran while one was open for 3% -> 2% of each run, Pallas kernels for 7% -> 5%
where the time goes in v4:
time: 289 us; the launch traced here: 287 us
  starting transfers between devices  127 us (44%)
  waiting for transfers between devices  107 us (37%)
  Pallas kernels  18.8 us (7%)
  blocking collectives  17.4 us (6%)
  local copies, waits for them, and re-layouts  11.4 us (4%)
  other arithmetic  4.08 us (1%)
    ppermute x12, starting transfers between devices, shift_groups(): return lax.ppermute(arr, 'ctx', pairs)  76.9 us
    ppermute x12, waiting for transfers between devices, shift_groups(): return lax.ppermute(arr, 'ctx', pairs)  61 us
    all_to_all x6, starting transfers between devices, swap_x(): lax.all_to_all(arr, 'ctx', 0, 0, axis_index_groups=X_GROUPS, tiled=True)  23.7 us
    all_to_all x6, waiting for transfers between devices, swap_x(): lax.all_to_all(arr, 'ctx', 0, 0, axis_index_groups=X_GROUPS, tiled=True)  18.6 us
    all_to_all x3, starting transfers between devices, swap_sink(): lax.all_to_all(rows, axes, 0, 0, axis_index_groups=groups, tiled=True)  18 us
    all_to_all x1, blocking collectives, swap_spread(): lax.all_to_all(arr, 'ctx', 0, 0, axis_index_groups=SPREAD_GROUPS, tiled=T...  17.4 us
    all_to_all x1, waiting for transfers between devices, swap_spread(): lax.all_to_all(arr, 'ctx', 0, 0, axis_index_groups=SPREAD_GROUPS, tiled=T...  15.4 us
    pallas_call x2, Pallas kernels, attend(): pl.pallas_call(attend_kernel, name='attend_head%d' % head, grid=(1,), in_...  13 us
  transfers between devices with their start and end apart: 22, of which 16 were waited for; matrix products, arithmetic and copies ran while one was open for 2% of the time, Pallas kernels for 5%

profile of v4, /device:TPU:24, one launch (start us, length us, event | category | flops | bytes accessed | tf_op | source)
XLA Modules:
  0.0 286.5 jit_solution(438266643543741358)
XLA Ops:
  0.7 1.2 reshape.141
  2.8 0.9 copy.47
  3.7 8.5 %all-to-all-start = ((bf16[16,128,128]{2,1,0:T(8,128)(2,1)}), bf16[16,128,128]{2,1,0:T(8,128)(2,1)S(1)}, u32[]{:S(2)}, u32[]{:S(2)}) async-start(bf16[16,128,128]{2,1,0:T(8,128)(2,1)} %bitcast.8), calls=%async_computation | async-start | bytes 1048576 | tf_op jit(solution)/shard_map/all_to_all | solution.py:40
  13.2 15.4 %all-to-all-done = bf16[16,128,128]{2,1,0:T(8,128)(2,1)S(1)} async-done(((bf16[16,128,128]{2,1,0:T(8,128)(2,1)}), bf16[16,128,128]{2,1,0:T(8,128)(2,1)S(1)}, u32[]{:S(2)}, u32[]{:S(2)}) %all-to-all-start) | async-done | bytes 524320 | tf_op jit(solution)/shard_map/all_to_all | solution.py:40
  29.5 9.1 %collective-permute-start = (bf16[4,256,128]{2,1,0:T(8,128)(2,1)}, bf16[4,256,128]{2,1,0:T(8,128)(2,1)S(1)}, u32[]{:S(2)}, u32[]{:S(2)}) collective-permute-start(bf16[4,256,128]{2,1,0:T(8,128)(2,1)} %bitcast.11.refs_0_), channel_id=1, source_target_pairs={{0,16},{4,20},{8,24},{12,28},{16,32},{20,36},{24,40},{28,44},{32,4... | collective-permute-start | bytes 786440 | tf_op jit(solution)/shard_map/ppermute | solution.py:36
  39.1 3.4 %all-to-all-start.1 = ((bf16[4,256,128]{2,1,0:T(8,128)(2,1)}), bf16[4,256,128]{2,1,0:T(8,128)(2,1)S(1)}, u32[]{:S(2)}, u32[]{:S(2)}) async-start(bf16[4,256,128]{2,1,0:T(8,128)(2,1)} %bitcast.11.refs_0_), calls=%async_computation.1 | async-start | bytes 524288 | tf_op jit(solution)/shard_map/all_to_all | solution.py:44
  42.5 2.9 collective-permute-start.2
  45.4 16.7 %collective-permute-done.refs_3_ = bf16[4,256,128]{2,1,0:T(8,128)(2,1)S(1)} collective-permute-done((bf16[4,256,128]{2,1,0:T(8,128)(2,1)}, bf16[4,256,128]{2,1,0:T(8,128)(2,1)S(1)}, u32[]{:S(2)}, u32[]{:S(2)}) %collective-permute-start) | collective-permute-done | bytes 262176 | tf_op jit(solution)/shard_map/ppermute | solution.py:36
  62.0 6.9 %collective-permute-start.1 = (bf16[4,256,128]{2,1,0:T(8,128)(2,1)}, bf16[4,256,128]{2,1,0:T(8,128)(2,1)S(1)}, u32[]{:S(2)}, u32[]{:S(2)}) collective-permute-start(bf16[4,256,128]{2,1,0:T(8,128)(2,1)} %bitcast.13.refs_0_), channel_id=1, source_target_pairs={{0,48},{4,52},{8,56},{12,60},{16,0},{20,4},{24,8},{28,12},{32,16},... | collective-permute-start | bytes 786440 | tf_op jit(solution)/shard_map/ppermute | solution.py:36
  68.9 2.9 %collective-permute-start.3 = (bf16[4,256,128]{2,1,0:T(8,128)(2,1)S(1)}, bf16[4,256,128]{2,1,0:T(8,128)(2,1)S(1)}, u32[]{:S(2)}, u32[]{:S(2)}) collective-permute-start(bf16[4,256,128]{2,1,0:T(8,128)(2,1)S(1)} %collective-permute-done.refs_3_), channel_id=1, source_target_pairs={{0,16},{4,20},{8,24},{12,28},{16,32},{20,36},{24,40},{28,44},{32,4... | collective-permute-start | bytes 786440 | tf_op jit(solution)/shard_map/ppermute | solution.py:36
  71.8 3.4 %all-to-all-start.2 = ((bf16[4,256,128]{2,1,0:T(8,128)(2,1)}), bf16[4,256,128]{2,1,0:T(8,128)(2,1)S(1)}, u32[]{:S(2)}, u32[]{:S(2)}) async-start(bf16[4,256,128]{2,1,0:T(8,128)(2,1)} %bitcast.13.refs_0_), calls=%async_computation.2 | async-start | bytes 524288 | tf_op jit(solution)/shard_map/all_to_all | solution.py:44
  75.5 6.5 %all-to-all-done.2 = bf16[4,256,128]{2,1,0:T(8,128)(2,1)S(1)} async-done(((bf16[4,256,128]{2,1,0:T(8,128)(2,1)}), bf16[4,256,128]{2,1,0:T(8,128)(2,1)S(1)}, u32[]{:S(2)}, u32[]{:S(2)}) %all-to-all-start.2) | async-done | bytes 262176 | tf_op jit(solution)/shard_map/all_to_all | solution.py:44
  81.9 5.9 %collective-permute-done.1.refs_1_ = bf16[4,256,128]{2,1,0:T(8,128)(2,1)S(1)} collective-permute-done((bf16[4,256,128]{2,1,0:T(8,128)(2,1)}, bf16[4,256,128]{2,1,0:T(8,128)(2,1)S(1)}, u32[]{:S(2)}, u32[]{:S(2)}) %collective-permute-start.1) | collective-permute-done | bytes 262176 | tf_op jit(solution)/shard_map/ppermute | solution.py:36
  87.8 2.3 collective-permute-done.3.refs_2_
  90.1 2.0 gather_picks.2
  92.1 3.6 %all-to-all-start.3 = ((bf16[4,768,128]{2,1,0:T(8,128)(2,1)}), bf16[4,768,128]{2,1,0:T(8,128)(2,1)S(1)}, u32[]{:S(2)}, u32[]{:S(2)}) async-start(bf16[4,768,128]{2,1,0:T(8,128)(2,1)} %bitcast.19), calls=%async_computation.3 | async-start | bytes 1572864 | tf_op jit(solution)/shard_map/all_to_all | solution.py:44
  96.6 4.4 %collective-permute-start.4 = (bf16[4,256,128]{2,1,0:T(8,128)(2,1)}, bf16[4,256,128]{2,1,0:T(8,128)(2,1)S(1)}, u32[]{:S(2)}, u32[]{:S(2)}) collective-permute-start(bf16[4,256,128]{2,1,0:T(8,128)(2,1)} %bitcast.13.refs_0_), channel_id=1, source_target_pairs={{0,16},{4,20},{8,24},{12,28},{16,32},{20,36},{24,40},{28,44},{32,4... | collective-permute-start | bytes 786440 | tf_op jit(solution)/shard_map/ppermute | solution.py:36
  101.0 5.4 %collective-permute-start.5 = (bf16[4,256,128]{2,1,0:T(8,128)(2,1)S(1)}, bf16[4,256,128]{2,1,0:T(8,128)(2,1)S(1)}, u32[]{:S(2)}, u32[]{:S(2)}) collective-permute-start(bf16[4,256,128]{2,1,0:T(8,128)(2,1)S(1)} %collective-permute-done.1.refs_1_), channel_id=1, source_target_pairs={{0,48},{4,52},{8,56},{12,60},{16,0},{20,4},{24,8},{28,12},{32,16},... | collective-permute-start | bytes 786440 | tf_op jit(solution)/shard_map/ppermute | solution.py:36
  107.0 1.4 all-to-all-done.3
  108.5 6.5 %attend_head0.1 = (bf16[512,256]{1,0:T(8,128)(2,1)}, bf16[512,256]{1,0:T(8,128)(2,1)}, bf16[4,4,4,2,32,128]{5,4,3,2,1,0:T(8,128)(2,1)}, f32[8,128]{1,0:T(8,128)S(1)}) custom-call(s32[3]{0:T(128)S(1)} %get-tuple-element.83.use_ref, f32[1]{0:T(128)} %get-tuple-element.85.sink_ref, bf16[512,256]{1,0:T(8,128)(2,1)S(1)} %bitcast.84, ...), custom_call_target="tpu_custom_call" | custom-call | flops 2684354560 | bytes 8388608 | tf_op jit(solution)/shard_map/attend_head0/pallas_call | solution.py:141
  115.0 4.9 %collective-permute-done.5.refs_2_ = bf16[4,256,128]{2,1,0:T(8,128)(2,1)S(1)} collective-permute-done((bf16[4,256,128]{2,1,0:T(8,128)(2,1)S(1)}, bf16[4,256,128]{2,1,0:T(8,128)(2,1)S(1)}, u32[]{:S(2)}, u32[]{:S(2)}) %collective-permute-start.5) | collective-permute-done | bytes 262176 | tf_op jit(solution)/shard_map/ppermute | solution.py:36
  119.9 5.1 %all-to-all-start.4 = ((bf16[4,1024,128]{2,1,0:T(8,128)(2,1)}), bf16[4,1024,128]{2,1,0:T(8,128)(2,1)S(1)}, u32[]{:S(2)}, u32[]{:S(2)}) async-start(bf16[4,1024,128]{2,1,0:T(8,128)(2,1)} %bitcast.21), calls=%async_computation.4 | async-start | bytes 2097152 | tf_op jit(solution)/shard_map/all_to_all | solution.py:44
  125.1 10.7 %all-to-all-done.4 = bf16[4,1024,128]{2,1,0:T(8,128)(2,1)S(1)} async-done(((bf16[4,1024,128]{2,1,0:T(8,128)(2,1)}), bf16[4,1024,128]{2,1,0:T(8,128)(2,1)S(1)}, u32[]{:S(2)}, u32[]{:S(2)}) %all-to-all-start.4) | async-done | bytes 1048608 | tf_op jit(solution)/shard_map/all_to_all | solution.py:44
  135.9 0.9 pool_parts.2
  137.5 2.0 gather_picks.3
  139.5 3.6 %all-to-all-start.5 = ((bf16[4,768,128]{2,1,0:T(8,128)(2,1)}), bf16[4,768,128]{2,1,0:T(8,128)(2,1)S(1)}, u32[]{:S(2)}, u32[]{:S(2)}) async-start(bf16[4,768,128]{2,1,0:T(8,128)(2,1)} %bitcast.23), calls=%async_computation.5 | async-start | bytes 1572864 | tf_op jit(solution)/shard_map/all_to_all | solution.py:44
  143.1 16.6 %collective-permute-start.6 = (bf16[4,256,128]{2,1,0:T(8,128)(2,1)S(1)}, bf16[4,256,128]{2,1,0:T(8,128)(2,1)S(1)}, u32[]{:S(2)}, u32[]{:S(2)}) collective-permute-start(bf16[4,256,128]{2,1,0:T(8,128)(2,1)S(1)} %copy-done.4), channel_id=1, source_target_pairs={{0,16},{4,20},{8,24},{12,28},{16,32},{20,36},{24,40},{28,44},{32,4... | collective-permute-start | bytes 786440 | tf_op jit(solution)/shard_map/ppermute | solution.py:36
  159.7 2.1 collective-permute-start.7
  161.8 6.5 %attend_head1.1 = (bf16[512,256]{1,0:T(8,128)(2,1)}, bf16[512,256]{1,0:T(8,128)(2,1)}, bf16[4,4,4,2,32,128]{5,4,3,2,1,0:T(8,128)(2,1)}, f32[8,128]{1,0:T(8,128)S(1)}) custom-call(s32[3]{0:T(128)S(1)} %get-tuple-element.84.use_ref, f32[1]{0:T(128)} %get-tuple-element.86.sink_ref, ...), custom_call_target="tpu_custom_call", output_to_operand_aliasing={{0}: (6, {}), {1}: (7, {})} | custom-call | flops 2684354560 | bytes 8388608 | tf_op jit(solution)/shard_map/attend_head1/pallas_call | solution.py:141
  168.3 6.8 %collective-permute-done.6 = bf16[4,256,128]{2,1,0:T(8,128)(2,1)S(1)} collective-permute-done((bf16[4,256,128]{2,1,0:T(8,128)(2,1)S(1)}, bf16[4,256,128]{2,1,0:T(8,128)(2,1)S(1)}, u32[]{:S(2)}, u32[]{:S(2)}) %collective-permute-start.6) | collective-permute-done | bytes 262176 | tf_op jit(solution)/shard_map/ppermute | solution.py:36
  175.1 2.7 collective-permute-done.7
  177.7 4.6 %all-to-all-start.6 = ((bf16[4,1024,128]{2,1,0:T(8,128)(2,1)}), bf16[4,1024,128]{2,1,0:T(8,128)(2,1)S(1)}, u32[]{:S(2)}, u32[]{:S(2)}) async-start(bf16[4,1024,128]{2,1,0:T(8,128)(2,1)} %bitcast.27), calls=%async_computation.6 | async-start | bytes 2097152 | tf_op jit(solution)/shard_map/all_to_all | solution.py:44
  182.4 6.6 %collective-permute-start.8 = (bf16[4,256,128]{2,1,0:T(8,128)(2,1)S(1)}, bf16[4,256,128]{2,1,0:T(8,128)(2,1)S(1)}, u32[]{:S(2)}, u32[]{:S(2)}) collective-permute-start(bf16[4,256,128]{2,1,0:T(8,128)(2,1)S(1)} %add_convert_fusion.3), channel_id=1, source_target_pairs={{0,16},{4,20},{8,24},{12,28},{16,32},{20,36},{24,40},{28,44},{32,4... | collective-permute-start | bytes 786440 | tf_op jit(solution)/shard_map/ppermute | solution.py:36
  188.9 7.0 %collective-permute-done.8 = bf16[4,256,128]{2,1,0:T(8,128)(2,1)S(1)} collective-permute-done((bf16[4,256,128]{2,1,0:T(8,128)(2,1)S(1)}, bf16[4,256,128]{2,1,0:T(8,128)(2,1)S(1)}, u32[]{:S(2)}, u32[]{:S(2)}) %collective-permute-start.8) | collective-permute-done | bytes 262176 | tf_op jit(solution)/shard_map/ppermute | solution.py:36
  195.9 0.9 pool_parts.3
  196.8 8.6 %collective-permute-start.9 = (bf16[4,256,128]{2,1,0:T(8,128)(2,1)S(1)}, bf16[4,256,128]{2,1,0:T(8,128)(2,1)S(1)}, u32[]{:S(2)}, u32[]{:S(2)}) collective-permute-start(bf16[4,256,128]{2,1,0:T(8,128)(2,1)S(1)} %get-tuple-element.68), channel_id=1, source_target_pairs={{0,48},{4,52},{8,56},{12,60},{16,0},{20,4},{24,8},{28,12},{32,16},... | collective-permute-start | bytes 786440 | tf_op jit(solution)/shard_map/ppermute | solution.py:36
  206.4 1.4 maximum_bitcast_fusion
  207.8 8.5 %collective-permute-done.9 = bf16[4,256,128]{2,1,0:T(8,128)(2,1)S(1)} collective-permute-done((bf16[4,256,128]{2,1,0:T(8,128)(2,1)S(1)}, bf16[4,256,128]{2,1,0:T(8,128)(2,1)S(1)}, u32[]{:S(2)}, u32[]{:S(2)}) %collective-permute-start.9) | collective-permute-done | bytes 262176 | tf_op jit(solution)/shard_map/ppermute | solution.py:36
  216.9 8.8 %all-to-all-start.7 = ((f32[16,1,128]{2,1,0:T(1,128)}), f32[16,1,128]{2,1,0:T(1,128)S(1)}, u32[]{:S(2)}, u32[]{:S(2)}) async-start(f32[16,1,128]{2,1,0:T(1,128)} %bitcast.33), calls=%async_computation.7 | async-start | bytes 16384 | tf_op jit(solution)/shard_map/all_to_all | solution.py:54
  225.7 7.7 %collective-permute-start.10 = (bf16[4,256,128]{2,1,0:T(8,128)(2,1)S(1)}, bf16[4,256,128]{2,1,0:T(8,128)(2,1)S(1)}, u32[]{:S(2)}, u32[]{:S(2)}) collective-permute-start(bf16[4,256,128]{2,1,0:T(8,128)(2,1)S(1)} %get-tuple-element.72), channel_id=1, source_target_pairs={{0,16},{4,20},{8,24},{12,28},{16,32},{20,36},{24,40},{28,44},{32,4... | collective-permute-start | bytes 786440 | tf_op jit(solution)/shard_map/ppermute | solution.py:36
  233.4 7.5 %all-to-all-done.7 = f32[16,1,128]{2,1,0:T(1,128)S(1)} async-done(((f32[16,1,128]{2,1,0:T(1,128)}), f32[16,1,128]{2,1,0:T(1,128)S(1)}, u32[]{:S(2)}, u32[]{:S(2)}) %all-to-all-start.7) | async-done | bytes 8224 | tf_op jit(solution)/shard_map/all_to_all | solution.py:54
  241.6 4.5 %all-to-all-start.8 = ((f32[4,1,128]{2,1,0:T(1,128)}), f32[4,1,128]{2,1,0:T(1,128)S(1)}, u32[]{:S(2)}, u32[]{:S(2)}) async-start(f32[4,1,128]{2,1,0:T(1,128)} %broadcast_in_dim.116), calls=%async_computation.8 | async-start | bytes 4096 | tf_op jit(solution)/shard_map/all_to_all | solution.py:54
  246.2 3.9 %collective-permute-start.11 = (bf16[4,256,128]{2,1,0:T(8,128)(2,1)S(1)}, bf16[4,256,128]{2,1,0:T(8,128)(2,1)S(1)}, u32[]{:S(2)}, u32[]{:S(2)}) collective-permute-start(bf16[4,256,128]{2,1,0:T(8,128)(2,1)S(1)} %add_convert_fusion.1), channel_id=1, source_target_pairs={{0,48},{4,52},{8,56},{12,60},{16,0},{20,4},{24,8},{28,12},{32,16},... | collective-permute-start | bytes 786440 | tf_op jit(solution)/shard_map/ppermute | solution.py:36
  250.2 1.2 all-to-all-done.8
  251.9 4.7 %all-to-all-start.9 = ((f32[8,1,128]{2,1,0:T(1,128)}), f32[8,1,128]{2,1,0:T(1,128)S(1)}, u32[]{:S(2)}, u32[]{:S(2)}) async-start(f32[8,1,128]{2,1,0:T(1,128)} %broadcast_in_dim.117), calls=%async_computation.9 | async-start | bytes 8192 | tf_op jit(solution)/shard_map/all_to_all | solution.py:54
  256.7 3.0 %all-to-all-done.9 = f32[8,1,128]{2,1,0:T(1,128)S(1)} async-done(((f32[8,1,128]{2,1,0:T(1,128)}), f32[8,1,128]{2,1,0:T(1,128)S(1)}, u32[]{:S(2)}, u32[]{:S(2)}) %all-to-all-start.9) | async-done | bytes 4128 | tf_op jit(solution)/shard_map/all_to_all | solution.py:54
  260.4 6.3 %collective-permute-done.11 = bf16[4,256,128]{2,1,0:T(8,128)(2,1)S(1)} collective-permute-done((bf16[4,256,128]{2,1,0:T(8,128)(2,1)S(1)}, bf16[4,256,128]{2,1,0:T(8,128)(2,1)S(1)}, u32[]{:S(2)}, u32[]{:S(2)}) %collective-permute-start.11) | collective-permute-done | bytes 262176 | tf_op jit(solution)/shard_map/ppermute | solution.py:36
  266.9 17.4 %all_to_all.70 = bf16[16,128,128]{2,1,0:T(8,128)(2,1)S(1)} all-to-all(bf16[16,128,128]{2,1,0:T(8,128)(2,1)S(1)} %bitcast.90), channel_id=1, replica_groups={{0,4,8,12,64,68,72,76,128,132,136,140,192,196,200,204},{16,20,24,28,80,..., dimensions={0} | all-to-all | bytes 1048576 | tf_op jit(solution)/shard_map/all_to_all | solution.py:40
  (67 shorter events, 12.0 us)
Async XLA Ops:
  0.6 38.0 %copy-start = (s32[1,16,8,3]{1,2,3,0:T(8,128)S(1)}, s32[1,16,8,3]{1,2,3,0:T(8,128)}, u32[]{:S(2)}) copy-start(s32[1,16,8,3]{1,2,3,0:T(8,128)} %param.11) | copy-start | bytes 4612
  0.6 1.2 copy-start.5
  3.7 25.0 %all-to-all-start = ((bf16[16,128,128]{2,1,0:T(8,128)(2,1)}), bf16[16,128,128]{2,1,0:T(8,128)(2,1)S(1)}, u32[]{:S(2)}, u32[]{:S(2)}) async-start(bf16[16,128,128]{2,1,0:T(8,128)(2,1)} %bitcast.8), calls=%async_computation | async-start | bytes 1048576 | tf_op jit(solution)/shard_map/all_to_all | solution.py:40
  12.2 0.7 copy-start.6
  29.5 32.5 %collective-permute-start = (bf16[4,256,128]{2,1,0:T(8,128)(2,1)}, bf16[4,256,128]{2,1,0:T(8,128)(2,1)S(1)}, u32[]{:S(2)}, u32[]{:S(2)}) collective-permute-start(bf16[4,256,128]{2,1,0:T(8,128)(2,1)} %bitcast.11.refs_0_), channel_id=1, source_target_pairs={{0,16},{4,20},{8,24},{12,28},{16,32},{20,36},{24,40},{28,44},{32,4... | collective-permute-start | bytes 786440 | tf_op jit(solution)/shard_map/ppermute | solution.py:36
  39.1 32.8 %all-to-all-start.1 = ((bf16[4,256,128]{2,1,0:T(8,128)(2,1)}), bf16[4,256,128]{2,1,0:T(8,128)(2,1)S(1)}, u32[]{:S(2)}, u32[]{:S(2)}) async-start(bf16[4,256,128]{2,1,0:T(8,128)(2,1)} %bitcast.11.refs_0_), calls=%async_computation.1 | async-start | bytes 524288 | tf_op jit(solution)/shard_map/all_to_all | solution.py:44
  42.5 47.6 %collective-permute-start.2 = (bf16[4,256,128]{2,1,0:T(8,128)(2,1)}, bf16[4,256,128]{2,1,0:T(8,128)(2,1)S(1)}, u32[]{:S(2)}, u32[]{:S(2)}) collective-permute-start(bf16[4,256,128]{2,1,0:T(8,128)(2,1)} %bitcast.11.refs_0_), channel_id=1, source_target_pairs={{0,48},{4,52},{8,56},{12,60},{16,0},{20,4},{24,8},{28,12},{32,16},... | collective-permute-start | bytes 786440 | tf_op jit(solution)/shard_map/ppermute | solution.py:36
  62.0 25.8 %collective-permute-start.1 = (bf16[4,256,128]{2,1,0:T(8,128)(2,1)}, bf16[4,256,128]{2,1,0:T(8,128)(2,1)S(1)}, u32[]{:S(2)}, u32[]{:S(2)}) collective-permute-start(bf16[4,256,128]{2,1,0:T(8,128)(2,1)} %bitcast.13.refs_0_), channel_id=1, source_target_pairs={{0,48},{4,52},{8,56},{12,60},{16,0},{20,4},{24,8},{28,12},{32,16},... | collective-permute-start | bytes 786440 | tf_op jit(solution)/shard_map/ppermute | solution.py:36
  68.9 21.2 %collective-permute-start.3 = (bf16[4,256,128]{2,1,0:T(8,128)(2,1)S(1)}, bf16[4,256,128]{2,1,0:T(8,128)(2,1)S(1)}, u32[]{:S(2)}, u32[]{:S(2)}) collective-permute-start(bf16[4,256,128]{2,1,0:T(8,128)(2,1)S(1)} %collective-permute-done.refs_3_), channel_id=1, source_target_pairs={{0,16},{4,20},{8,24},{12,28},{16,32},{20,36},{24,40},{28,44},{32,4... | collective-permute-start | bytes 786440 | tf_op jit(solution)/shard_map/ppermute | solution.py:36
  71.8 10.1 %all-to-all-start.2 = ((bf16[4,256,128]{2,1,0:T(8,128)(2,1)}), bf16[4,256,128]{2,1,0:T(8,128)(2,1)S(1)}, u32[]{:S(2)}, u32[]{:S(2)}) async-start(bf16[4,256,128]{2,1,0:T(8,128)(2,1)} %bitcast.13.refs_0_), calls=%async_computation.2 | async-start | bytes 524288 | tf_op jit(solution)/shard_map/all_to_all | solution.py:44
  92.1 16.4 %copy-start.1 = (bf16[1,1,1,512,256]{4,3,2,1,0:T(8,128)(2,1)S(1)}, bf16[1,1,1,512,256]{4,3,2,1,0:T(8,128)(2,1)}, u32[]{:S(2)}) copy-start(bf16[1,1,1,512,256]{4,3,2,1,0:T(8,128)(2,1)} %param.7) | copy-start | bytes 786436
  92.1 16.4 %copy-start.2 = (bf16[1,1,1,512,256]{4,3,2,1,0:T(8,128)(2,1)S(1)}, bf16[1,1,1,512,256]{4,3,2,1,0:T(8,128)(2,1)}, u32[]{:S(2)}) copy-start(bf16[1,1,1,512,256]{4,3,2,1,0:T(8,128)(2,1)} %param.10) | copy-start | bytes 786436
  92.1 16.3 %all-to-all-start.3 = ((bf16[4,768,128]{2,1,0:T(8,128)(2,1)}), bf16[4,768,128]{2,1,0:T(8,128)(2,1)S(1)}, u32[]{:S(2)}, u32[]{:S(2)}) async-start(bf16[4,768,128]{2,1,0:T(8,128)(2,1)} %bitcast.19), calls=%async_computation.3 | async-start | bytes 1572864 | tf_op jit(solution)/shard_map/all_to_all | solution.py:44
  95.7 0.7 copy-start.7
  96.6 23.2 %collective-permute-start.4 = (bf16[4,256,128]{2,1,0:T(8,128)(2,1)}, bf16[4,256,128]{2,1,0:T(8,128)(2,1)S(1)}, u32[]{:S(2)}, u32[]{:S(2)}) collective-permute-start(bf16[4,256,128]{2,1,0:T(8,128)(2,1)} %bitcast.13.refs_0_), channel_id=1, source_target_pairs={{0,16},{4,20},{8,24},{12,28},{16,32},{20,36},{24,40},{28,44},{32,4... | collective-permute-start | bytes 786440 | tf_op jit(solution)/shard_map/ppermute | solution.py:36
  101.0 18.9 %collective-permute-start.5 = (bf16[4,256,128]{2,1,0:T(8,128)(2,1)S(1)}, bf16[4,256,128]{2,1,0:T(8,128)(2,1)S(1)}, u32[]{:S(2)}, u32[]{:S(2)}) collective-permute-start(bf16[4,256,128]{2,1,0:T(8,128)(2,1)S(1)} %collective-permute-done.1.refs_1_), channel_id=1, source_target_pairs={{0,48},{4,52},{8,56},{12,60},{16,0},{20,4},{24,8},{28,12},{32,16},... | collective-permute-start | bytes 786440 | tf_op jit(solution)/shard_map/ppermute | solution.py:36
  119.9 16.0 %all-to-all-start.4 = ((bf16[4,1024,128]{2,1,0:T(8,128)(2,1)}), bf16[4,1024,128]{2,1,0:T(8,128)(2,1)S(1)}, u32[]{:S(2)}, u32[]{:S(2)}) async-start(bf16[4,1024,128]{2,1,0:T(8,128)(2,1)} %bitcast.21), calls=%async_computation.4 | async-start | bytes 2097152 | tf_op jit(solution)/shard_map/all_to_all | solution.py:44
  136.8 0.7 copy-start.3
  139.5 3.6 %copy-start.4 = (bf16[4,256,128]{2,1,0:T(8,128)(2,1)S(1)}, bf16[4,256,128]{2,1,0:T(8,128)(2,1)}, u32[]{:S(2)}) copy-start(bf16[4,256,128]{2,1,0:T(8,128)(2,1)} %copy-done.3) | copy-start | bytes 786436
  139.5 22.3 %all-to-all-start.5 = ((bf16[4,768,128]{2,1,0:T(8,128)(2,1)}), bf16[4,768,128]{2,1,0:T(8,128)(2,1)S(1)}, u32[]{:S(2)}, u32[]{:S(2)}) async-start(bf16[4,768,128]{2,1,0:T(8,128)(2,1)} %bitcast.23), calls=%async_computation.5 | async-start | bytes 1572864 | tf_op jit(solution)/shard_map/all_to_all | solution.py:44
  143.1 31.9 %collective-permute-start.6 = (bf16[4,256,128]{2,1,0:T(8,128)(2,1)S(1)}, bf16[4,256,128]{2,1,0:T(8,128)(2,1)S(1)}, u32[]{:S(2)}, u32[]{:S(2)}) collective-permute-start(bf16[4,256,128]{2,1,0:T(8,128)(2,1)S(1)} %copy-done.4), channel_id=1, source_target_pairs={{0,16},{4,20},{8,24},{12,28},{16,32},{20,36},{24,40},{28,44},{32,4... | collective-permute-start | bytes 786440 | tf_op jit(solution)/shard_map/ppermute | solution.py:36
  159.7 18.0 %collective-permute-start.7 = (bf16[4,256,128]{2,1,0:T(8,128)(2,1)S(1)}, bf16[4,256,128]{2,1,0:T(8,128)(2,1)S(1)}, u32[]{:S(2)}, u32[]{:S(2)}) collective-permute-start(bf16[4,256,128]{2,1,0:T(8,128)(2,1)S(1)} %get-tuple-element.51), channel_id=1, source_target_pairs={{0,48},{4,52},{8,56},{12,60},{16,0},{20,4},{24,8},{28,12},{32,16},... | collective-permute-start | bytes 786440 | tf_op jit(solution)/shard_map/ppermute | solution.py:36
  177.7 18.2 %all-to-all-start.6 = ((bf16[4,1024,128]{2,1,0:T(8,128)(2,1)}), bf16[4,1024,128]{2,1,0:T(8,128)(2,1)S(1)}, u32[]{:S(2)}, u32[]{:S(2)}) async-start(bf16[4,1024,128]{2,1,0:T(8,128)(2,1)} %bitcast.27), calls=%async_computation.6 | async-start | bytes 2097152 | tf_op jit(solution)/shard_map/all_to_all | solution.py:44
  182.4 13.6 %collective-permute-start.8 = (bf16[4,256,128]{2,1,0:T(8,128)(2,1)S(1)}, bf16[4,256,128]{2,1,0:T(8,128)(2,1)S(1)}, u32[]{:S(2)}, u32[]{:S(2)}) collective-permute-start(bf16[4,256,128]{2,1,0:T(8,128)(2,1)S(1)} %add_convert_fusion.3), channel_id=1, source_target_pairs={{0,16},{4,20},{8,24},{12,28},{16,32},{20,36},{24,40},{28,44},{32,4... | collective-permute-start | bytes 786440 | tf_op jit(solution)/shard_map/ppermute | solution.py:36
  196.8 19.5 %collective-permute-start.9 = (bf16[4,256,128]{2,1,0:T(8,128)(2,1)S(1)}, bf16[4,256,128]{2,1,0:T(8,128)(2,1)S(1)}, u32[]{:S(2)}, u32[]{:S(2)}) collective-permute-start(bf16[4,256,128]{2,1,0:T(8,128)(2,1)S(1)} %get-tuple-element.68), channel_id=1, source_target_pairs={{0,48},{4,52},{8,56},{12,60},{16,0},{20,4},{24,8},{28,12},{32,16},... | collective-permute-start | bytes 786440 | tf_op jit(solution)/shard_map/ppermute | solution.py:36
  216.9 24.0 %all-to-all-start.7 = ((f32[16,1,128]{2,1,0:T(1,128)}), f32[16,1,128]{2,1,0:T(1,128)S(1)}, u32[]{:S(2)}, u32[]{:S(2)}) async-start(f32[16,1,128]{2,1,0:T(1,128)} %bitcast.33), calls=%async_computation.7 | async-start | bytes 16384 | tf_op jit(solution)/shard_map/all_to_all | solution.py:54
  225.7 34.7 %collective-permute-start.10 = (bf16[4,256,128]{2,1,0:T(8,128)(2,1)S(1)}, bf16[4,256,128]{2,1,0:T(8,128)(2,1)S(1)}, u32[]{:S(2)}, u32[]{:S(2)}) collective-permute-start(bf16[4,256,128]{2,1,0:T(8,128)(2,1)S(1)} %get-tuple-element.72), channel_id=1, source_target_pairs={{0,16},{4,20},{8,24},{12,28},{16,32},{20,36},{24,40},{28,44},{32,4... | collective-permute-start | bytes 786440 | tf_op jit(solution)/shard_map/ppermute | solution.py:36
  241.6 9.7 %all-to-all-start.8 = ((f32[4,1,128]{2,1,0:T(1,128)}), f32[4,1,128]{2,1,0:T(1,128)S(1)}, u32[]{:S(2)}, u32[]{:S(2)}) async-start(f32[4,1,128]{2,1,0:T(1,128)} %broadcast_in_dim.116), calls=%async_computation.8 | async-start | bytes 4096 | tf_op jit(solution)/shard_map/all_to_all | solution.py:54
  246.2 20.5 %collective-permute-start.11 = (bf16[4,256,128]{2,1,0:T(8,128)(2,1)S(1)}, bf16[4,256,128]{2,1,0:T(8,128)(2,1)S(1)}, u32[]{:S(2)}, u32[]{:S(2)}) collective-permute-start(bf16[4,256,128]{2,1,0:T(8,128)(2,1)S(1)} %add_convert_fusion.1), channel_id=1, source_target_pairs={{0,48},{4,52},{8,56},{12,60},{16,0},{20,4},{24,8},{28,12},{32,16},... | collective-permute-start | bytes 786440 | tf_op jit(solution)/shard_map/ppermute | solution.py:36
  251.9 7.8 %all-to-all-start.9 = ((f32[8,1,128]{2,1,0:T(1,128)}), f32[8,1,128]{2,1,0:T(1,128)S(1)}, u32[]{:S(2)}, u32[]{:S(2)}) async-start(f32[8,1,128]{2,1,0:T(1,128)} %broadcast_in_dim.117), calls=%async_computation.9 | async-start | bytes 8192 | tf_op jit(solution)/shard_map/all_to_all | solution.py:54

commit v5 on v1

v5 whole, which is shorter than its diff:
```python
import math

import jax
import jax.numpy as jnp
from jax import lax
from jax.experimental import pallas as pl
from jax.experimental.pallas import tpu as pltpu
from jax.sharding import PartitionSpec as P

HEADS = 32
DH = 128
BLOCK = 512
SPB = 4
TOPK = 3
HPD = 2
XS = 4
ZG = 4
ZS = ZG * SPB
N_CTX = XS * ZS
FRAG = BLOCK // (XS * SPB)
ROWS = SPB * 2 * FRAG
KINDS = TOPK + 1
LOG2E = math.log2(math.e)
NEG = -1e30

Z_GROUPS = [[x * ZS + z for z in range(ZS)] for x in range(XS)]
X_GROUPS = [[x * ZS + z for x in range(XS)] for z in range(ZS)]


def shift_x(arr, step):
    pairs = []
    for x in range(XS):
        for z in range(ZS):
            pairs.append((x * ZS + z, (x + step) % XS * ZS + z))
    return lax.ppermute(arr, "ctx", pairs)


def swap_all(arr):
    return lax.all_to_all(arr, "ctx", 0, 0, tiled=True)


def dot(left, right, left_dim, right_dim):
    return lax.dot_general(
        left,
        right,
        (((left_dim,), (right_dim,)), ((), ())),
        preferred_element_type=jnp.float32,
    )


def attend_kernel(use_ref, row_ref, sink_ref, q_ref, g_ref, *rest):
    tile_refs = rest[:XS]
    att_ref, dq_ref = rest[-XS - 4 : -XS - 2]
    part_refs = rest[-XS - 2 : -2]
    sink_out, s_ref = rest[-2:]
    scale = 1.0 / math.sqrt(DH)
    query = q_ref[...]
    grad = g_ref[...]

    def tile(kind, which):
        got = [ref[kind, :, which].reshape(SPB * FRAG, DH) for ref in tile_refs]
        return jnp.concatenate(got, axis=0)

    def put(kind, which, grads):
        got = grads.astype(jnp.bfloat16).reshape(XS, SPB, FRAG, DH)
        for step in range(XS):
            part_refs[step][kind, :, which] = got[step]

    sink = sink_ref[0] * LOG2E
    top = jnp.full((1, BLOCK), sink, jnp.float32)
    for kind in range(KINDS):
        score = dot(tile(kind, 0), query, 1, 1) * (scale * LOG2E)
        if kind == 0:
            row = lax.broadcasted_iota(jnp.int32, (BLOCK, BLOCK), 0)
            col = lax.broadcasted_iota(jnp.int32, (BLOCK, BLOCK), 1)
            quarter = (row_ref[0] - row // (SPB * FRAG) + XS) % XS
            part = (row // FRAG) % SPB
            place = part * (XS * FRAG) + quarter * FRAG + row % FRAG
            score = jnp.where(place <= col, score, NEG)
        else:
            score = jnp.where(use_ref[kind - 1] > 0, score, NEG)
        s_ref[kind] = score
        top = jnp.maximum(top, jnp.max(score, axis=0, keepdims=True))
    sink_part = jnp.exp2(sink - top)
    total = sink_part
    for kind in range(KINDS):
        expo = jnp.exp2(s_ref[kind] - top)
        s_ref[kind] = expo
        total = total + jnp.sum(expo, axis=0, keepdims=True)
    inv = 1.0 / total
    att_t = jnp.zeros((DH, BLOCK), jnp.float32)
    for kind in range(KINDS):
        prob = s_ref[kind] * inv
        s_ref[kind] = prob
        weights = prob.astype(jnp.bfloat16)
        att_t = att_t + dot(tile(kind, 1), weights, 0, 0)
        put(kind, 1, dot(weights, grad, 1, 0))
    att = att_t.T.astype(jnp.bfloat16)
    att_ref[...] = att
    both = grad.astype(jnp.float32) * att.astype(jnp.float32)
    delta = jnp.sum(both.T, axis=0, keepdims=True)
    sink_rows = sink_part * inv * delta
    sink_out[...] = jnp.broadcast_to(-jnp.sum(sink_rows, axis=1, keepdims=True), (8, 128))
    dq_t = jnp.zeros((DH, BLOCK), jnp.float32)
    for kind in range(KINDS):
        dprob = dot(tile(kind, 1), grad, 1, 1)
        dscore = (s_ref[kind] * (dprob - delta) * scale).astype(jnp.bfloat16)
        dq_t = dq_t + dot(tile(kind, 0), dscore, 0, 0)
        put(kind, 0, dot(dscore, query, 1, 0))
    dq_ref[...] = dq_t.T.astype(jnp.bfloat16)


def attend(head, use, row, sink, query, grad, tiles, earlier):
    lane = pl.BlockSpec((BLOCK, DH), lambda i: (0, head))
    whole = jax.ShapeDtypeStruct((BLOCK, HPD * DH), jnp.bfloat16)
    dims = (KINDS, SPB, 2, FRAG, DH)
    tile = pl.BlockSpec(dims, lambda i: (0,) * len(dims))
    in_specs = [pl.BlockSpec(memory_space=pltpu.SMEM)] * 3 + [lane, lane] + [tile] * XS
    in_specs += [pl.BlockSpec(memory_space=pl.ANY)] * len(earlier)
    outs = pl.pallas_call(
        attend_kernel,
        name="attend_head%d" % head,
        grid=(1,),
        in_specs=in_specs,
        out_specs=[lane, lane] + [tile] * XS + [pl.BlockSpec((8, 128), lambda i: (0, 0))],
        out_shape=[whole, whole]
        + [jax.ShapeDtypeStruct(dims, jnp.bfloat16)] * XS
        + [jax.ShapeDtypeStruct((8, 128), jnp.float32)],
        scratch_shapes=[pltpu.VMEM((KINDS, BLOCK, BLOCK), jnp.float32)],
        input_output_aliases={5 + XS + n: n for n in range(len(earlier))},
        compiler_params=pltpu.CompilerParams(vmem_limit_bytes=40 << 20),
        cost_estimate=pl.CostEstimate(
            flops=20 * KINDS * BLOCK * BLOCK * DH, transcendentals=0, bytes_accessed=8 << 20
        ),
    )(use, row, sink, query, grad, *[arr.reshape(dims) for arr in tiles], *earlier)
    return outs[:2], outs[2:-1], outs[-1]


def gather_kernel(index_ref, all_ref, *out_refs):
    for step in range(XS):
        for kind in range(KINDS):
            out_refs[step][kind] = all_ref[index_ref[step * KINDS + kind]]


def gather_picks(index, shares):
    return pl.pallas_call(
        gather_kernel,
        name="gather_picks",
        in_specs=[
            pl.BlockSpec(memory_space=pltpu.SMEM),
            pl.BlockSpec(memory_space=pltpu.VMEM),
        ],
        out_specs=[pl.BlockSpec(memory_space=pltpu.VMEM)] * XS,
        out_shape=[jax.ShapeDtypeStruct((KINDS, ROWS, DH), jnp.bfloat16)] * XS,
        compiler_params=pltpu.CompilerParams(vmem_limit_bytes=16 << 20),
        cost_estimate=pl.CostEstimate(flops=0, transcendentals=0, bytes_accessed=4 << 20),
    )(index, shares)


def pool_kernel(index_ref, *refs):
    part_refs = refs[:XS]
    out_ref, acc_ref = refs[XS:]
    acc_ref[...] = jnp.zeros(acc_ref.shape, jnp.float32)
    for step in range(XS):
        for kind in range(KINDS):
            slot = index_ref[step * KINDS + kind]
            acc_ref[slot] = acc_ref[slot] + part_refs[step][kind].astype(jnp.float32)
    out_ref[...] = acc_ref[...].astype(jnp.bfloat16)


def pool_parts(index, parts):
    shape = (ZG * XS, ROWS, DH)
    return pl.pallas_call(
        pool_kernel,
        name="pool_parts",
        in_specs=[pl.BlockSpec(memory_space=pltpu.SMEM)]
        + [pl.BlockSpec(memory_space=pltpu.VMEM)] * XS,
        out_specs=pl.BlockSpec(memory_space=pltpu.VMEM),
        out_shape=jax.ShapeDtypeStruct(shape, jnp.bfloat16),
        scratch_shapes=[pltpu.VMEM(shape, jnp.float32)],
        compiler_params=pltpu.CompilerParams(vmem_limit_bytes=16 << 20),
        cost_estimate=pl.CostEstimate(flops=1 << 20, transcendentals=0, bytes_accessed=4 << 20),
    )(index, *[arr.reshape(KINDS, ROWS, DH) for arr in parts])


def body(query, key, value, grad_out, chosen, placed, sink):
    place = lax.axis_index("ctx")
    group = (place // SPB) % ZG
    row = place // ZS
    position = place % SPB
    nblk = XS * ZG
    slots = jnp.arange(nblk, dtype=jnp.int32)

    def by_head(arr):
        return jnp.transpose(arr.reshape(XS, FRAG, SPB, HPD, DH), (0, 2, 3, 1, 4))

    paired = jnp.stack([by_head(key), by_head(value)], axis=3)
    paired = jnp.broadcast_to(
        jnp.transpose(paired, (2, 0, 1, 3, 4, 5))[:, :, None],
        (HPD, XS, ZG, SPB, 2, FRAG, DH),
    ).reshape(HPD, N_CTX, 2 * FRAG, DH)

    heads = lax.dynamic_slice_in_dim(chosen[0], position * HPD, HPD, 1)
    slot_of = jnp.sum(jnp.where(placed[None, :] == slots[:, None], slots[None, :], 0), axis=1)
    mine = (row + jnp.arange(XS, dtype=jnp.int32)) % XS * ZG + group
    blocks = jnp.sum(jnp.where(mine[:, None] == slots, placed, 0), axis=1)
    cand = jnp.sum(
        jnp.where((blocks[:, None] == slots)[:, :, None, None], heads[None], 0), axis=1
    )
    good = cand < blocks[:, None, None]
    slot = jnp.sum(jnp.where(cand[..., None] == slots, slot_of, 0), axis=-1)
    index = jnp.where(good, slot, mine[:, None, None])
    lead = jnp.broadcast_to(mine[:, None, None], (XS, HPD, 1))
    index = jnp.concatenate([lead, index], axis=2)
    index = jnp.transpose(index, (1, 0, 2)).reshape(HPD, XS * KINDS)
    use = good[0].astype(jnp.int32)
    sink_mine = lax.dynamic_slice_in_dim(sink, position * HPD, HPD)

    query_rows = query.reshape(BLOCK, HPD * DH)
    grad_rows = grad_out.reshape(BLOCK, HPD * DH)
    shares = [swap_all(paired[h]).reshape(nblk, ROWS, DH) for h in range(HPD)]
    earlier = ()
    sink_heads = []
    pools = []
    for h in range(HPD):
        if h > 0:
            shares[h], pools[0] = lax.optimization_barrier((shares[h], pools[0]))
        outgoing = gather_picks(index[h], shares[h])
        tiles = [outgoing[0]] + [shift_x(outgoing[step], step) for step in range(1, XS)]
        earlier, parts, sink_sum = attend(
            h, use[h], row.reshape(1), sink_mine[h : h + 1], query_rows, grad_rows, tiles, earlier
        )
        sink_heads.append(sink_sum[0, :1])
        back = [parts[0]] + [shift_x(parts[step], -step) for step in range(1, XS)]
        pools.append(pool_parts(index[h], back))
    att, dq = earlier
    homed = [swap_all(arr.reshape(N_CTX, 2 * FRAG, DH)) for arr in pools]
    grads = []
    for arr in homed:
        summed = jnp.sum(
            arr.reshape(XS, ZG, SPB, 2, FRAG, DH).astype(jnp.float32), axis=1
        )
        grads.append(summed.astype(jnp.bfloat16))
    totals = jnp.transpose(jnp.stack(grads, axis=2), (3, 0, 4, 1, 2, 5))
    grad_key = totals[0].reshape(key.shape)
    grad_value = totals[1].reshape(value.shape)
    sink_local = jnp.concatenate(sink_heads)
    sink_local, _ = lax.optimization_barrier((sink_local, pools[1]))
    sink_ctx = lax.psum(
        lax.dynamic_update_slice(
            jnp.zeros((SPB * HPD,), jnp.float32), sink_local, (position * HPD,)
        ),
        "ctx",
        axis_index_groups=X_GROUPS,
    )
    sink_ctx = lax.psum(sink_ctx, "ctx", axis_index_groups=Z_GROUPS)
    start = lax.axis_index("head") * (SPB * HPD)
    spread_sink = lax.dynamic_update_slice(jnp.zeros((HEADS,), jnp.float32), sink_ctx, (start,))
    grad_sink = lax.psum(spread_sink, ("dp", "head"))
    return (att.reshape(query.shape), dq.reshape(query.shape), grad_key, grad_value, grad_sink)


def solution(mesh):
    in_specs = (
        P("dp", "ctx", "head", None, None),
        P("dp", "ctx", "head"),
        P("dp", "ctx", "head"),
        P("dp", "ctx", "head", None, None),
        P("dp", None, "head", None),
        P(),
        P("head"),
    )
    out_specs = (
        P("dp", "ctx", "head", None, None),
        P("dp", "ctx", "head", None, None),
        P("dp", "ctx", "head"),
        P("dp", "ctx", "head"),
        P(),
    )
    return jax.shard_map(body, mesh=mesh, in_specs=in_specs, out_specs=out_specs, check_vma=False)
```

time: 326 us -> 313 us (0.960)
  blocking collectives: 53.3 us -> 154 us
  starting transfers between devices: 168 us -> 75.7 us
  waiting for transfers between devices: 64.1 us -> 46.3 us
    all_to_all x10 -> x3, starting transfers between devices: 105 us -> 32.3 us  [swap_all(): return lax.all_to_all(arr, 'ctx', 0, 0, tiled=True)]
    all_to_all x0 -> x1, blocking collectives: none -> 72.2 us  [swap_all(): return lax.all_to_all(arr, 'ctx', 0, 0, tiled=True)]
    psum x1, blocking collectives: 29.2 us -> 57.3 us  [body(): sink_ctx = lax.psum(sink_ctx, 'ctx', axis_index_groups=Z_GROUPS)]
    all_to_all x10 -> x3, waiting for transfers between devices: 26.2 us -> 0.01 us  [swap_all(): return lax.all_to_all(arr, 'ctx', 0, 0, tiled=True)]
    ppermute x12, starting transfers between devices: 63.1 us -> 43.4 us  [shift_x(): return lax.ppermute(arr, 'ctx', pairs)]
    ppermute x12, waiting for transfers between devices: 38 us -> 46.3 us  [shift_x(): return lax.ppermute(arr, 'ctx', pairs)]
  transfers between devices with their start and end apart: 22 -> 15, of which waited for: 12 -> 11; matrix products, arithmetic and copies ran while one was open for 2% -> 2% of each run, Pallas kernels for 6% -> 6%
where the time goes in v5:
time: 313 us; the launch traced here: 309 us
  blocking collectives  154 us (49%)
  starting transfers between devices  75.7 us (24%)
  waiting for transfers between devices  46.3 us (15%)
  Pallas kernels  17.4 us (6%)
  local copies, waits for them, and re-layouts  10.2 us (3%)
  other arithmetic  4.64 us (1%)
    all_to_all x1, blocking collectives, swap_all(): return lax.all_to_all(arr, 'ctx', 0, 0, tiled=True)  72.2 us
    psum x1, blocking collectives, body(): sink_ctx = lax.psum(sink_ctx, 'ctx', axis_index_groups=Z_GROUPS)  57.3 us
    ppermute x12, waiting for transfers between devices, shift_x(): return lax.ppermute(arr, 'ctx', pairs)  46.3 us
    ppermute x12, starting transfers between devices, shift_x(): return lax.ppermute(arr, 'ctx', pairs)  43.4 us
    all_to_all x3, starting transfers between devices, swap_all(): return lax.all_to_all(arr, 'ctx', 0, 0, tiled=True)  32.3 us
    psum x1, blocking collectives, body(): grad_sink = lax.psum(spread_sink, ('dp', 'head'))  13.3 us
    pallas_call x2, Pallas kernels, attend(): pl.pallas_call(attend_kernel, name='attend_head%d' % head, grid=(1,), in_...  12.3 us
    psum x1, blocking collectives, body(): lax.psum(lax.dynamic_update_slice(jnp.zeros((SPB * HPD,), jnp.float32), s...  10.7 us
  transfers between devices with their start and end apart: 15, of which 11 were waited for; matrix products, arithmetic and copies ran while one was open for 2% of the time, Pallas kernels for 6%

profile of v5, /device:TPU:24, one launch (start us, length us, event | category | flops | bytes accessed | tf_op | source)
XLA Modules:
  0.0 308.7 jit_solution(11360981639493941032)
XLA Ops:
  0.7 1.2 reshape.168
  2.0 0.7 maximum_bitcast_fusion
  2.8 0.9 fusion.4
  4.1 72.2 %all_to_all.20 = bf16[64,64,128]{2,1,0:T(8,128)(2,1)S(1)} all-to-all(bf16[64,64,128]{2,1,0:T(8,128)(2,1)S(1)} %bitcast.73), channel_id=1, replica_groups=mesh['dp'=2,'ctx'=64,'head'=4] {'ctx'}, dimensions={0} | all-to-all | bytes 2097152 | tf_op jit(solution)/shard_map/all_to_all | solution.py:39
  76.3 1.3 broadcast_in_dim.104
  77.6 6.8 %all-to-all-start = ((bf16[64,64,128]{2,1,0:T(8,128)(2,1)}), bf16[64,64,128]{2,1,0:T(8,128)(2,1)S(1)}, u32[]{:S(2)}, u32[]{:S(2)}) async-start(bf16[64,64,128]{2,1,0:T(8,128)(2,1)} %bitcast.11), calls=%async_computation | async-start | bytes 2097152 | tf_op jit(solution)/shard_map/all_to_all | solution.py:39
  84.5 0.6 copy-done.4
  86.2 0.6 gather_picks.2
  86.8 3.5 %collective-permute-start = (bf16[4,256,128]{2,1,0:T(8,128)(2,1)S(1)}, bf16[4,256,128]{2,1,0:T(8,128)(2,1)S(1)}, u32[]{:S(2)}, u32[]{:S(2)}) collective-permute-start(bf16[4,256,128]{2,1,0:T(8,128)(2,1)S(1)} %get-tuple-element.31), channel_id=1, source_target_pairs={{0,64},{4,68},{8,72},{12,76},{16,80},{20,84},{24,88},{28,92},{32,9... | collective-permute-start | bytes 786440 | tf_op jit(solution)/shard_map/ppermute | solution.py:35
  90.3 4.8 %collective-permute-start.1 = (bf16[4,256,128]{2,1,0:T(8,128)(2,1)S(1)}, bf16[4,256,128]{2,1,0:T(8,128)(2,1)S(1)}, u32[]{:S(2)}, u32[]{:S(2)}) collective-permute-start(bf16[4,256,128]{2,1,0:T(8,128)(2,1)S(1)} %get-tuple-element.32), channel_id=1, source_target_pairs={{0,128},{4,132},{8,136},{12,140},{16,144},{20,148},{24,152},{28,15... | collective-permute-start | bytes 786440 | tf_op jit(solution)/shard_map/ppermute | solution.py:35
  95.1 3.3 %collective-permute-start.2 = (bf16[4,256,128]{2,1,0:T(8,128)(2,1)S(1)}, bf16[4,256,128]{2,1,0:T(8,128)(2,1)S(1)}, u32[]{:S(2)}, u32[]{:S(2)}) collective-permute-start(bf16[4,256,128]{2,1,0:T(8,128)(2,1)S(1)} %get-tuple-element.33), channel_id=1, source_target_pairs={{0,192},{4,196},{8,200},{12,204},{16,208},{20,212},{24,216},{28,22... | collective-permute-start | bytes 786440 | tf_op jit(solution)/shard_map/ppermute | solution.py:35
  98.4 0.6 copy-done.5
  99.1 0.6 fusion.6
  100.2 6.9 %collective-permute-done.1 = bf16[4,256,128]{2,1,0:T(8,128)(2,1)S(1)} collective-permute-done((bf16[4,256,128]{2,1,0:T(8,128)(2,1)S(1)}, bf16[4,256,128]{2,1,0:T(8,128)(2,1)S(1)}, u32[]{:S(2)}, u32[]{:S(2)}) %collective-permute-start.1) | collective-permute-done | bytes 262176 | tf_op jit(solution)/shard_map/ppermute | solution.py:35
  107.2 0.7 collective-permute-done.2
  107.9 6.1 %attend_head0.1 = (bf16[512,256]{1,0:T(8,128)(2,1)}, bf16[512,256]{1,0:T(8,128)(2,1)}, bf16[4,4,2,32,128]{4,3,2,1,0:T(8,128)(2,1)S(1)}, bf16[4,4,2,32,128]{4,3,2...) custom-call(s32[3]{0:T(128)S(1)} %get-tuple-element.55.use_ref, ...), custom_call_target="tpu_custom_call" | custom-call | flops 2684354560 | bytes 8388608 | tf_op jit(solution)/shard_map/attend_head0/pallas_call | solution.py:120
  114.0 4.7 %collective-permute-start.3 = (bf16[4,4,2,32,128]{4,3,2,1,0:T(8,128)(2,1)S(1)}, bf16[4,4,2,32,128]{4,3,2,1,0:T(8,128)(2,1)S(1)}, u32[]{:S(2)}, u32[]{:S(2)}) collective-permute-start(bf16[4,4,2,32,128]{4,3,2,1,0:T(8,128)(2,1)S(1)} %get-tuple-element.35), channel_id=1, source_target_pairs={{0,192},{4,196},{8,200},{12,204},{16,208},{20,212},{24,216},{28,22... | collective-permute-start | bytes 786440 | tf_op jit(solution)/shard_map/ppermute | solution.py:35
  118.7 3.6 %collective-permute-start.4 = (bf16[4,4,2,32,128]{4,3,2,1,0:T(8,128)(2,1)S(1)}, bf16[4,4,2,32,128]{4,3,2,1,0:T(8,128)(2,1)S(1)}, u32[]{:S(2)}, u32[]{:S(2)}) collective-permute-start(bf16[4,4,2,32,128]{4,3,2,1,0:T(8,128)(2,1)S(1)} %get-tuple-element.36), channel_id=1, source_target_pairs={{0,128},{4,132},{8,136},{12,140},{16,144},{20,148},{24,152},{28,15... | collective-permute-start | bytes 786440 | tf_op jit(solution)/shard_map/ppermute | solution.py:35
  122.2 1.9 collective-permute-start.5
  124.2 3.9 %collective-permute-done.3 = bf16[4,4,2,32,128]{4,3,2,1,0:T(8,128)(2,1)S(1)} collective-permute-done((bf16[4,4,2,32,128]{4,3,2,1,0:T(8,128)(2,1)S(1)}, bf16[4,4,2,32,128]{4,3,2,1,0:T(8,128)(2,1)S(1)}, u32[]{:S(2)}, u32[]{:S(2)}) %collective-permute-start.3) | collective-permute-done | bytes 262176 | tf_op jit(solution)/shard_map/ppermute | solution.py:35
  128.0 5.0 %collective-permute-done.4 = bf16[4,4,2,32,128]{4,3,2,1,0:T(8,128)(2,1)S(1)} collective-permute-done((bf16[4,4,2,32,128]{4,3,2,1,0:T(8,128)(2,1)S(1)}, bf16[4,4,2,32,128]{4,3,2,1,0:T(8,128)(2,1)S(1)}, u32[]{:S(2)}, u32[]{:S(2)}) %collective-permute-start.4) | collective-permute-done | bytes 262176 | tf_op jit(solution)/shard_map/ppermute | solution.py:35
  133.0 5.0 %collective-permute-done.5 = bf16[4,4,2,32,128]{4,3,2,1,0:T(8,128)(2,1)S(1)} collective-permute-done((bf16[4,4,2,32,128]{4,3,2,1,0:T(8,128)(2,1)S(1)}, bf16[4,4,2,32,128]{4,3,2,1,0:T(8,128)(2,1)S(1)}, u32[]{:S(2)}, u32[]{:S(2)}) %collective-permute-start.5) | collective-permute-done | bytes 262176 | tf_op jit(solution)/shard_map/ppermute | solution.py:35
  138.0 1.9 pool_parts.2
  140.0 13.2 %all-to-all-start.2 = ((bf16[64,64,128]{2,1,0:T(8,128)(2,1)}), bf16[64,64,128]{2,1,0:T(8,128)(2,1)}, u32[]{:S(2)}, u32[]{:S(2)}) async-start(bf16[64,64,128]{2,1,0:T(8,128)(2,1)} %bitcast.30), calls=%async_computation.2 | async-start | bytes 2097152 | tf_op jit(solution)/shard_map/all_to_all | solution.py:39
  153.4 0.6 gather_picks.3
  154.0 3.4 %collective-permute-start.6 = (bf16[4,256,128]{2,1,0:T(8,128)(2,1)S(1)}, bf16[4,256,128]{2,1,0:T(8,128)(2,1)S(1)}, u32[]{:S(2)}, u32[]{:S(2)}) collective-permute-start(bf16[4,256,128]{2,1,0:T(8,128)(2,1)S(1)} %get-tuple-element.40), channel_id=1, source_target_pairs={{0,64},{4,68},{8,72},{12,76},{16,80},{20,84},{24,88},{28,92},{32,9... | collective-permute-start | bytes 786440 | tf_op jit(solution)/shard_map/ppermute | solution.py:35
  157.4 4.8 %collective-permute-start.7 = (bf16[4,256,128]{2,1,0:T(8,128)(2,1)S(1)}, bf16[4,256,128]{2,1,0:T(8,128)(2,1)S(1)}, u32[]{:S(2)}, u32[]{:S(2)}) collective-permute-start(bf16[4,256,128]{2,1,0:T(8,128)(2,1)S(1)} %get-tuple-element.41), channel_id=1, source_target_pairs={{0,128},{4,132},{8,136},{12,140},{16,144},{20,148},{24,152},{28,15... | collective-permute-start | bytes 786440 | tf_op jit(solution)/shard_map/ppermute | solution.py:35
  162.2 3.4 %collective-permute-start.8 = (bf16[4,256,128]{2,1,0:T(8,128)(2,1)S(1)}, bf16[4,256,128]{2,1,0:T(8,128)(2,1)S(1)}, u32[]{:S(2)}, u32[]{:S(2)}) collective-permute-start(bf16[4,256,128]{2,1,0:T(8,128)(2,1)S(1)} %get-tuple-element.42), channel_id=1, source_target_pairs={{0,192},{4,196},{8,200},{12,204},{16,208},{20,212},{24,216},{28,22... | collective-permute-start | bytes 786440 | tf_op jit(solution)/shard_map/ppermute | solution.py:35
  165.7 0.8 collective-permute-done.6
  166.5 8.0 %collective-permute-done.7 = bf16[4,256,128]{2,1,0:T(8,128)(2,1)S(1)} collective-permute-done((bf16[4,256,128]{2,1,0:T(8,128)(2,1)S(1)}, bf16[4,256,128]{2,1,0:T(8,128)(2,1)S(1)}, u32[]{:S(2)}, u32[]{:S(2)}) %collective-permute-start.7) | collective-permute-done | bytes 262176 | tf_op jit(solution)/shard_map/ppermute | solution.py:35
  174.5 1.1 collective-permute-done.8
  175.6 6.1 %attend_head1.1 = (bf16[512,256]{1,0:T(8,128)(2,1)}, bf16[512,256]{1,0:T(8,128)(2,1)}, bf16[4,4,2,32,128]{4,3,2,1,0:T(8,128)(2,1)S(1)}, bf16[4,4,2,32,128]{4,3,2...) custom-call(s32[3]{0:T(128)S(1)} %get-tuple-element.56.use_ref, ...), custom_call_target="tpu_custom_call", output_to_operand_aliasing={{0}: (9, {}), {1}: (10, {})} | custom-call | flops 2684354560 | bytes 8388608 | tf_op jit(solution)/shard_map/attend_head1/pallas_call | solution.py:120
  181.7 4.6 %collective-permute-start.9 = (bf16[4,4,2,32,128]{4,3,2,1,0:T(8,128)(2,1)S(1)}, bf16[4,4,2,32,128]{4,3,2,1,0:T(8,128)(2,1)S(1)}, u32[]{:S(2)}, u32[]{:S(2)}) collective-permute-start(bf16[4,4,2,32,128]{4,3,2,1,0:T(8,128)(2,1)S(1)} %get-tuple-element.49), channel_id=1, source_target_pairs={{0,192},{4,196},{8,200},{12,204},{16,208},{20,212},{24,216},{28,22... | collective-permute-start | bytes 786440 | tf_op jit(solution)/shard_map/ppermute | solution.py:35
  186.3 3.6 %collective-permute-start.10 = (bf16[4,4,2,32,128]{4,3,2,1,0:T(8,128)(2,1)S(1)}, bf16[4,4,2,32,128]{4,3,2,1,0:T(8,128)(2,1)S(1)}, u32[]{:S(2)}, u32[]{:S(2)}) collective-permute-start(bf16[4,4,2,32,128]{4,3,2,1,0:T(8,128)(2,1)S(1)} %get-tuple-element.50), channel_id=1, source_target_pairs={{0,128},{4,132},{8,136},{12,140},{16,144},{20,148},{24,152},{28,15... | collective-permute-start | bytes 786440 | tf_op jit(solution)/shard_map/ppermute | solution.py:35
  189.9 1.9 collective-permute-start.11
  191.8 10.0 %collective-permute-done.9 = bf16[4,4,2,32,128]{4,3,2,1,0:T(8,128)(2,1)S(1)} collective-permute-done((bf16[4,4,2,32,128]{4,3,2,1,0:T(8,128)(2,1)S(1)}, bf16[4,4,2,32,128]{4,3,2,1,0:T(8,128)(2,1)S(1)}, u32[]{:S(2)}, u32[]{:S(2)}) %collective-permute-start.9) | collective-permute-done | bytes 262176 | tf_op jit(solution)/shard_map/ppermute | solution.py:35
  201.8 4.5 %collective-permute-done.11 = bf16[4,4,2,32,128]{4,3,2,1,0:T(8,128)(2,1)S(1)} collective-permute-done((bf16[4,4,2,32,128]{4,3,2,1,0:T(8,128)(2,1)S(1)}, bf16[4,4,2,32,128]{4,3,2,1,0:T(8,128)(2,1)S(1)}, u32[]{:S(2)}, u32[]{:S(2)}) %collective-permute-start.11) | collective-permute-done | bytes 262176 | tf_op jit(solution)/shard_map/ppermute | solution.py:35
  206.3 2.0 pool_parts.3
  208.2 12.3 %all-to-all-start.3 = ((bf16[64,64,128]{2,1,0:T(8,128)(2,1)}), bf16[64,64,128]{2,1,0:T(8,128)(2,1)S(1)}, u32[]{:S(2)}, u32[]{:S(2)}) async-start(bf16[64,64,128]{2,1,0:T(8,128)(2,1)} %bitcast.37), calls=%async_computation.3 | async-start | bytes 2097152 | tf_op jit(solution)/shard_map/all_to_all | solution.py:39
  220.6 0.5 slice.66
  221.1 0.5 slice.67
  221.6 1.4 pad_maximum_fusion
  223.2 10.7 %psum.21 = f32[8]{0:T(128)S(1)} all-reduce(f32[8]{0:T(128)S(1)} %dynamic_update_slice.6), channel_id=1, replica_groups={{0,64,128,192},{4,68,132,196},{8,72,136,200},{12,76,140,204},{16,80,144..., use_global_device_ids=true, to_apply=%region_6.7 | all-reduce | flops 8 | bytes 64 | tf_op jit(solution)/shard_map/psum | solution.py:249
  233.8 57.3 %psum.22 = f32[8]{0:T(128)S(1)} all-reduce(f32[8]{0:T(128)S(1)} %psum.21), channel_id=1, replica_groups={{0,4,8,12,16,20,24,28,32,36,40,44,48,52,56,60},{64,68,72,76,80,84,88,92..., use_global_device_ids=true, to_apply=%region_7.8 | all-reduce | flops 8 | bytes 64 | tf_op jit(solution)/shard_map/psum | solution.py:256
  291.4 13.3 %psum.23 = f32[32]{0:T(128)} all-reduce(f32[32]{0:T(128)S(1)} %dynamic_update_slice.7), channel_id=1, replica_groups=mesh['dp'=2,'ctx'=64,'head'=4] {'dp','head'}, use_global_device_ids=true, to_apply=%region_8.9 | all-reduce | flops 32 | bytes 256 | tf_op jit(solution)/shard_map/psum | solution.py:259
  304.7 1.4 reduce_sum.64
  306.7 0.9 reshape_squeeze.7
  307.9 0.9 reshape_squeeze.6
  (46 shorter events, 3.7 us)
Async XLA Ops:
  0.6 83.8 %copy-start = (s32[1,16,8,3]{1,2,3,0:T(8,128)S(1)}, s32[1,16,8,3]{1,2,3,0:T(8,128)}, u32[]{:S(2)}) copy-start(s32[1,16,8,3]{1,2,3,0:T(8,128)} %param.11) | copy-start | bytes 4612
  0.6 1.2 copy-start.3
  77.6 62.4 %all-to-all-start = ((bf16[64,64,128]{2,1,0:T(8,128)(2,1)}), bf16[64,64,128]{2,1,0:T(8,128)(2,1)S(1)}, u32[]{:S(2)}, u32[]{:S(2)}) async-start(bf16[64,64,128]{2,1,0:T(8,128)(2,1)} %bitcast.11), calls=%async_computation | async-start | bytes 2097152 | tf_op jit(solution)/shard_map/all_to_all | solution.py:39
  84.5 0.7 copy-start.4
  86.2 21.7 %copy-start.1 = (bf16[1,1,1,512,256]{4,3,2,1,0:T(8,128)(2,1)S(1)}, bf16[1,1,1,512,256]{4,3,2,1,0:T(8,128)(2,1)}, u32[]{:S(2)}) copy-start(bf16[1,1,1,512,256]{4,3,2,1,0:T(8,128)(2,1)} %param.7) | copy-start | bytes 786436
  86.2 21.7 %copy-start.2 = (bf16[1,1,1,512,256]{4,3,2,1,0:T(8,128)(2,1)S(1)}, bf16[1,1,1,512,256]{4,3,2,1,0:T(8,128)(2,1)}, u32[]{:S(2)}) copy-start(bf16[1,1,1,512,256]{4,3,2,1,0:T(8,128)(2,1)} %param.10) | copy-start | bytes 786436
  86.8 13.4 %collective-permute-start = (bf16[4,256,128]{2,1,0:T(8,128)(2,1)S(1)}, bf16[4,256,128]{2,1,0:T(8,128)(2,1)S(1)}, u32[]{:S(2)}, u32[]{:S(2)}) collective-permute-start(bf16[4,256,128]{2,1,0:T(8,128)(2,1)S(1)} %get-tuple-element.31), channel_id=1, source_target_pairs={{0,64},{4,68},{8,72},{12,76},{16,80},{20,84},{24,88},{28,92},{32,9... | collective-permute-start | bytes 786440 | tf_op jit(solution)/shard_map/ppermute | solution.py:35
  90.3 16.8 %collective-permute-start.1 = (bf16[4,256,128]{2,1,0:T(8,128)(2,1)S(1)}, bf16[4,256,128]{2,1,0:T(8,128)(2,1)S(1)}, u32[]{:S(2)}, u32[]{:S(2)}) collective-permute-start(bf16[4,256,128]{2,1,0:T(8,128)(2,1)S(1)} %get-tuple-element.32), channel_id=1, source_target_pairs={{0,128},{4,132},{8,136},{12,140},{16,144},{20,148},{24,152},{28,15... | collective-permute-start | bytes 786440 | tf_op jit(solution)/shard_map/ppermute | solution.py:35
  95.1 12.8 %collective-permute-start.2 = (bf16[4,256,128]{2,1,0:T(8,128)(2,1)S(1)}, bf16[4,256,128]{2,1,0:T(8,128)(2,1)S(1)}, u32[]{:S(2)}, u32[]{:S(2)}) collective-permute-start(bf16[4,256,128]{2,1,0:T(8,128)(2,1)S(1)} %get-tuple-element.33), channel_id=1, source_target_pairs={{0,192},{4,196},{8,200},{12,204},{16,208},{20,212},{24,216},{28,22... | collective-permute-start | bytes 786440 | tf_op jit(solution)/shard_map/ppermute | solution.py:35
  98.4 0.7 copy-start.5
  114.0 14.0 %collective-permute-start.3 = (bf16[4,4,2,32,128]{4,3,2,1,0:T(8,128)(2,1)S(1)}, bf16[4,4,2,32,128]{4,3,2,1,0:T(8,128)(2,1)S(1)}, u32[]{:S(2)}, u32[]{:S(2)}) collective-permute-start(bf16[4,4,2,32,128]{4,3,2,1,0:T(8,128)(2,1)S(1)} %get-tuple-element.35), channel_id=1, source_target_pairs={{0,192},{4,196},{8,200},{12,204},{16,208},{20,212},{24,216},{28,22... | collective-permute-start | bytes 786440 | tf_op jit(solution)/shard_map/ppermute | solution.py:35
  118.7 14.3 %collective-permute-start.4 = (bf16[4,4,2,32,128]{4,3,2,1,0:T(8,128)(2,1)S(1)}, bf16[4,4,2,32,128]{4,3,2,1,0:T(8,128)(2,1)S(1)}, u32[]{:S(2)}, u32[]{:S(2)}) collective-permute-start(bf16[4,4,2,32,128]{4,3,2,1,0:T(8,128)(2,1)S(1)} %get-tuple-element.36), channel_id=1, source_target_pairs={{0,128},{4,132},{8,136},{12,140},{16,144},{20,148},{24,152},{28,15... | collective-permute-start | bytes 786440 | tf_op jit(solution)/shard_map/ppermute | solution.py:35
  122.2 15.8 %collective-permute-start.5 = (bf16[4,4,2,32,128]{4,3,2,1,0:T(8,128)(2,1)S(1)}, bf16[4,4,2,32,128]{4,3,2,1,0:T(8,128)(2,1)S(1)}, u32[]{:S(2)}, u32[]{:S(2)}) collective-permute-start(bf16[4,4,2,32,128]{4,3,2,1,0:T(8,128)(2,1)S(1)} %get-tuple-element.37), channel_id=1, source_target_pairs={{0,64},{4,68},{8,72},{12,76},{16,80},{20,84},{24,88},{28,92},{32,9... | collective-permute-start | bytes 786440 | tf_op jit(solution)/shard_map/ppermute | solution.py:35
  140.0 68.3 %all-to-all-start.2 = ((bf16[64,64,128]{2,1,0:T(8,128)(2,1)}), bf16[64,64,128]{2,1,0:T(8,128)(2,1)}, u32[]{:S(2)}, u32[]{:S(2)}) async-start(bf16[64,64,128]{2,1,0:T(8,128)(2,1)} %bitcast.30), calls=%async_computation.2 | async-start | bytes 2097152 | tf_op jit(solution)/shard_map/all_to_all | solution.py:39
  154.0 12.5 %collective-permute-start.6 = (bf16[4,256,128]{2,1,0:T(8,128)(2,1)S(1)}, bf16[4,256,128]{2,1,0:T(8,128)(2,1)S(1)}, u32[]{:S(2)}, u32[]{:S(2)}) collective-permute-start(bf16[4,256,128]{2,1,0:T(8,128)(2,1)S(1)} %get-tuple-element.40), channel_id=1, source_target_pairs={{0,64},{4,68},{8,72},{12,76},{16,80},{20,84},{24,88},{28,92},{32,9... | collective-permute-start | bytes 786440 | tf_op jit(solution)/shard_map/ppermute | solution.py:35
  157.4 17.1 %collective-permute-start.7 = (bf16[4,256,128]{2,1,0:T(8,128)(2,1)S(1)}, bf16[4,256,128]{2,1,0:T(8,128)(2,1)S(1)}, u32[]{:S(2)}, u32[]{:S(2)}) collective-permute-start(bf16[4,256,128]{2,1,0:T(8,128)(2,1)S(1)} %get-tuple-element.41), channel_id=1, source_target_pairs={{0,128},{4,132},{8,136},{12,140},{16,144},{20,148},{24,152},{28,15... | collective-permute-start | bytes 786440 | tf_op jit(solution)/shard_map/ppermute | solution.py:35
  162.2 13.4 %collective-permute-start.8 = (bf16[4,256,128]{2,1,0:T(8,128)(2,1)S(1)}, bf16[4,256,128]{2,1,0:T(8,128)(2,1)S(1)}, u32[]{:S(2)}, u32[]{:S(2)}) collective-permute-start(bf16[4,256,128]{2,1,0:T(8,128)(2,1)S(1)} %get-tuple-element.42), channel_id=1, source_target_pairs={{0,192},{4,196},{8,200},{12,204},{16,208},{20,212},{24,216},{28,22... | collective-permute-start | bytes 786440 | tf_op jit(solution)/shard_map/ppermute | solution.py:35
  181.7 20.1 %collective-permute-start.9 = (bf16[4,4,2,32,128]{4,3,2,1,0:T(8,128)(2,1)S(1)}, bf16[4,4,2,32,128]{4,3,2,1,0:T(8,128)(2,1)S(1)}, u32[]{:S(2)}, u32[]{:S(2)}) collective-permute-start(bf16[4,4,2,32,128]{4,3,2,1,0:T(8,128)(2,1)S(1)} %get-tuple-element.49), channel_id=1, source_target_pairs={{0,192},{4,196},{8,200},{12,204},{16,208},{20,212},{24,216},{28,22... | collective-permute-start | bytes 786440 | tf_op jit(solution)/shard_map/ppermute | solution.py:35
  186.3 15.5 %collective-permute-start.10 = (bf16[4,4,2,32,128]{4,3,2,1,0:T(8,128)(2,1)S(1)}, bf16[4,4,2,32,128]{4,3,2,1,0:T(8,128)(2,1)S(1)}, u32[]{:S(2)}, u32[]{:S(2)}) collective-permute-start(bf16[4,4,2,32,128]{4,3,2,1,0:T(8,128)(2,1)S(1)} %get-tuple-element.50), channel_id=1, source_target_pairs={{0,128},{4,132},{8,136},{12,140},{16,144},{20,148},{24,152},{28,15... | collective-permute-start | bytes 786440 | tf_op jit(solution)/shard_map/ppermute | solution.py:35
  189.9 16.4 %collective-permute-start.11 = (bf16[4,4,2,32,128]{4,3,2,1,0:T(8,128)(2,1)S(1)}, bf16[4,4,2,32,128]{4,3,2,1,0:T(8,128)(2,1)S(1)}, u32[]{:S(2)}, u32[]{:S(2)}) collective-permute-start(bf16[4,4,2,32,128]{4,3,2,1,0:T(8,128)(2,1)S(1)} %get-tuple-element.51), channel_id=1, source_target_pairs={{0,64},{4,68},{8,72},{12,76},{16,80},{20,84},{24,88},{28,92},{32,9... | collective-permute-start | bytes 786440 | tf_op jit(solution)/shard_map/ppermute | solution.py:35
  208.2 97.9 %all-to-all-start.3 = ((bf16[64,64,128]{2,1,0:T(8,128)(2,1)}), bf16[64,64,128]{2,1,0:T(8,128)(2,1)S(1)}, u32[]{:S(2)}, u32[]{:S(2)}) async-start(bf16[64,64,128]{2,1,0:T(8,128)(2,1)} %bitcast.37), calls=%async_computation.3 | async-start | bytes 2097152 | tf_op jit(solution)/shard_map/all_to_all | solution.py:39

commit v6 on v5

--- a/solution.py
+++ b/solution.py
@@ -20,6 +20,8 @@
 FRAG = BLOCK // (XS * SPB)
 ROWS = SPB * 2 * FRAG
 KINDS = TOPK + 1
+EXTRA = 8
+STEPS = (2, 1, 3)
 LOG2E = math.log2(math.e)
 NEG = -1e30
 
@@ -159,28 +161,42 @@
 
 def pool_kernel(index_ref, *refs):
     part_refs = refs[:XS]
-    out_ref, acc_ref = refs[XS:]
+    out_ref, acc_ref = refs[-2:]
     acc_ref[...] = jnp.zeros(acc_ref.shape, jnp.float32)
     for step in range(XS):
         for kind in range(KINDS):
             slot = index_ref[step * KINDS + kind]
             acc_ref[slot] = acc_ref[slot] + part_refs[step][kind].astype(jnp.float32)
-    out_ref[...] = acc_ref[...].astype(jnp.bfloat16)
-
-
-def pool_parts(index, parts):
-    shape = (ZG * XS, ROWS, DH)
+    for slot in range(ZG * XS):
+        pooled = acc_ref[slot].astype(jnp.bfloat16).reshape(SPB, 2 * FRAG, DH)
+        out_ref[slot * SPB : (slot + 1) * SPB, : 2 * FRAG] = pooled
+    if len(refs) > XS + 2:
+        left = refs[XS][...]
+        lane = lax.broadcasted_iota(jnp.int32, left.shape, 1)
+        terms = jnp.zeros(left.shape, jnp.float32)
+        for term in range(3):
+            rounded = left.astype(jnp.bfloat16).astype(jnp.float32)
+            terms = jnp.where(lane // HEADS == term, rounded, terms)
+            left = left - rounded
+        out_ref[:, 2 * FRAG :] = jnp.broadcast_to(
+            terms.astype(jnp.bfloat16)[None], (N_CTX,) + left.shape
+        )
+
+
+def pool_parts(index, parts, sink_sum=None):
+    extra = [] if sink_sum is None else [jnp.tile(sink_sum[None], (EXTRA, 128 // HEADS))]
+    shape = (N_CTX, 2 * FRAG + EXTRA * len(extra), DH)
     return pl.pallas_call(
         pool_kernel,
         name="pool_parts",
         in_specs=[pl.BlockSpec(memory_space=pltpu.SMEM)]
-        + [pl.BlockSpec(memory_space=pltpu.VMEM)] * XS,
+        + [pl.BlockSpec(memory_space=pltpu.VMEM)] * (XS + len(extra)),
         out_specs=pl.BlockSpec(memory_space=pltpu.VMEM),
         out_shape=jax.ShapeDtypeStruct(shape, jnp.bfloat16),
-        scratch_shapes=[pltpu.VMEM(shape, jnp.float32)],
+        scratch_shapes=[pltpu.VMEM((ZG * XS, ROWS, DH), jnp.float32)],
         compiler_params=pltpu.CompilerParams(vmem_limit_bytes=16 << 20),
         cost_estimate=pl.CostEstimate(flops=1 << 20, transcendentals=0, bytes_accessed=4 << 20),
-    )(index, *[arr.reshape(KINDS, ROWS, DH) for arr in parts])
+    )(index, *[arr.reshape(KINDS, ROWS, DH) for arr in parts], *extra)
 
 
 def body(query, key, value, grad_out, chosen, placed, sink):
@@ -226,37 +242,36 @@
         if h > 0:
             shares[h], pools[0] = lax.optimization_barrier((shares[h], pools[0]))
         outgoing = gather_picks(index[h], shares[h])
-        tiles = [outgoing[0]] + [shift_x(outgoing[step], step) for step in range(1, XS)]
+        tiles = list(outgoing)
+        for step in STEPS:
+            tiles[step] = shift_x(outgoing[step], step)
         earlier, parts, sink_sum = attend(
             h, use[h], row.reshape(1), sink_mine[h : h + 1], query_rows, grad_rows, tiles, earlier
         )
         sink_heads.append(sink_sum[0, :1])
-        back = [parts[0]] + [shift_x(parts[step], -step) for step in range(1, XS)]
-        pools.append(pool_parts(index[h], back))
+        back = list(parts)
+        for step in STEPS:
+            back[step] = shift_x(parts[step], -step)
+        sink_sum = None
+        if h == HPD - 1:
+            start = lax.axis_index("head") * (SPB * HPD) + position * HPD
+            sink_sum = lax.dynamic_update_slice(
+                jnp.zeros((HEADS,), jnp.float32), jnp.concatenate(sink_heads), (start,)
+            )
+            sink_sum = lax.psum(sink_sum, ("dp", "head"))
+        pools.append(pool_parts(index[h], back, sink_sum))
     att, dq = earlier
-    homed = [swap_all(arr.reshape(N_CTX, 2 * FRAG, DH)) for arr in pools]
+    homed = [swap_all(arr) for arr in pools]
+    terms = homed[-1][:, 2 * FRAG, : 3 * HEADS].astype(jnp.float32)
+    grad_sink = jnp.sum(terms.reshape(N_CTX * 3, HEADS), axis=0)
     grads = []
     for arr in homed:
-        summed = jnp.sum(
-            arr.reshape(XS, ZG, SPB, 2, FRAG, DH).astype(jnp.float32), axis=1
-        )
+        arr = arr[:, : 2 * FRAG].reshape(XS, ZG, SPB, 2, FRAG, DH)
+        summed = jnp.sum(arr.astype(jnp.float32), axis=1)
         grads.append(summed.astype(jnp.bfloat16))
     totals = jnp.transpose(jnp.stack(grads, axis=2), (3, 0, 4, 1, 2, 5))
     grad_key = totals[0].reshape(key.shape)
     grad_value = totals[1].reshape(value.shape)
-    sink_local = jnp.concatenate(sink_heads)
-    sink_local, _ = lax.optimization_barrier((sink_local, pools[1]))
-    sink_ctx = lax.psum(
-        lax.dynamic_update_slice(
-            jnp.zeros((SPB * HPD,), jnp.float32), sink_local, (position * HPD,)
-        ),
-        "ctx",
-        axis_index_groups=X_GROUPS,
-    )
-    sink_ctx = lax.psum(sink_ctx, "ctx", axis_index_groups=Z_GROUPS)
-    start = lax.axis_index("head") * (SPB * HPD)
-    spread_sink = lax.dynamic_update_slice(jnp.zeros((HEADS,), jnp.float32), sink_ctx, (start,))
-    grad_sink = lax.psum(spread_sink, ("dp", "head"))
     return (att.reshape(query.shape), dq.reshape(query.shape), grad_key, grad_value, grad_sink)
 
 

time: 313 us -> 291 us (0.930)
  blocking collectives: 154 us -> 85.3 us
  waiting for transfers between devices: 46.3 us -> 90.2 us
    psum x3 -> x1, blocking collectives: 81.3 us -> 13.1 us  [body(): sink_sum = lax.psum(sink_sum, ('dp', 'head'))]
    all_to_all x3, waiting for transfers between devices: 0.01 us -> 57.9 us  [swap_all(): return lax.all_to_all(arr, 'ctx', 0, 0, tiled=True)]
    ppermute x12, waiting for transfers between devices: 46.3 us -> 32.2 us  [shift_x(): return lax.ppermute(arr, 'ctx', pairs)]
  transfers between devices with their start and end apart: 15 -> 15, of which waited for: 11 -> 10; matrix products, arithmetic and copies ran while one was open for 2% -> 2% of each run, Pallas kernels for 6% -> 6%
where the time goes in v6:
time: 291 us; the launch traced here: 287 us
  waiting for transfers between devices  90.2 us (31%)
  blocking collectives  85.3 us (29%)
  starting transfers between devices  78.8 us (27%)
  Pallas kernels  17.5 us (6%)
  local copies, waits for them, and re-layouts  9.67 us (3%)
  other arithmetic  4.16 us (1%)
    all_to_all x1, blocking collectives, swap_all(): return lax.all_to_all(arr, 'ctx', 0, 0, tiled=True)  72.2 us
    all_to_all x3, waiting for transfers between devices, swap_all(): return lax.all_to_all(arr, 'ctx', 0, 0, tiled=True)  57.9 us
    ppermute x12, starting transfers between devices, shift_x(): return lax.ppermute(arr, 'ctx', pairs)  43.5 us
    all_to_all x3, starting transfers between devices, swap_all(): return lax.all_to_all(arr, 'ctx', 0, 0, tiled=True)  35.2 us
    ppermute x12, waiting for transfers between devices, shift_x(): return lax.ppermute(arr, 'ctx', pairs)  32.2 us
    psum x1, blocking collectives, body(): sink_sum = lax.psum(sink_sum, ('dp', 'head'))  13.1 us
    pallas_call x2, Pallas kernels, attend(): pl.pallas_call(attend_kernel, name='attend_head%d' % head, grid=(1,), in_...  12.3 us
  transfers between devices with their start and end apart: 15, of which 10 were waited for; matrix products, arithmetic and copies ran while one was open for 2% of the time, Pallas kernels for 6%

profile of v6, /device:TPU:24, one launch (start us, length us, event | category | flops | bytes accessed | tf_op | source)
XLA Modules:
  0.0 286.6 jit_solution(4807639799055417208)
XLA Ops:
  0.6 1.1 reshape.170
  1.8 1.1 reshape.171
  2.9 0.7 maximum_bitcast_fusion
  3.6 0.9 fusion.5
  5.0 72.2 %all_to_all.20 = bf16[64,64,128]{2,1,0:T(8,128)(2,1)S(1)} all-to-all(bf16[64,64,128]{2,1,0:T(8,128)(2,1)S(1)} %bitcast.72), channel_id=1, replica_groups=mesh['dp'=2,'ctx'=64,'head'=4] {'ctx'}, dimensions={0} | all-to-all | bytes 2097152 | tf_op jit(solution)/shard_map/all_to_all | solution.py:41
  77.2 1.2 broadcast_in_dim.104
  78.4 6.9 %all-to-all-start = ((bf16[64,64,128]{2,1,0:T(8,128)(2,1)}), bf16[64,64,128]{2,1,0:T(8,128)(2,1)S(1)}, u32[]{:S(2)}, u32[]{:S(2)}) async-start(bf16[64,64,128]{2,1,0:T(8,128)(2,1)} %bitcast.71), calls=%async_computation | async-start | bytes 2097152 | tf_op jit(solution)/shard_map/all_to_all | solution.py:41
  86.1 0.3 select_reduce_fusion
  86.6 0.6 gather_picks.2
  87.2 3.5 %collective-permute-start = (bf16[4,256,128]{2,1,0:T(8,128)(2,1)S(1)}, bf16[4,256,128]{2,1,0:T(8,128)(2,1)S(1)}, u32[]{:S(2)}, u32[]{:S(2)}) collective-permute-start(bf16[4,256,128]{2,1,0:T(8,128)(2,1)S(1)} %get-tuple-element.30), channel_id=1, source_target_pairs={{0,64},{4,68},{8,72},{12,76},{16,80},{20,84},{24,88},{28,92},{32,9... | collective-permute-start | bytes 786440 | tf_op jit(solution)/shard_map/ppermute | solution.py:37
  90.7 4.8 %collective-permute-start.1 = (bf16[4,256,128]{2,1,0:T(8,128)(2,1)S(1)}, bf16[4,256,128]{2,1,0:T(8,128)(2,1)S(1)}, u32[]{:S(2)}, u32[]{:S(2)}) collective-permute-start(bf16[4,256,128]{2,1,0:T(8,128)(2,1)S(1)} %get-tuple-element.31), channel_id=1, source_target_pairs={{0,128},{4,132},{8,136},{12,140},{16,144},{20,148},{24,152},{28,15... | collective-permute-start | bytes 786440 | tf_op jit(solution)/shard_map/ppermute | solution.py:37
  95.5 3.3 %collective-permute-start.2 = (bf16[4,256,128]{2,1,0:T(8,128)(2,1)S(1)}, bf16[4,256,128]{2,1,0:T(8,128)(2,1)S(1)}, u32[]{:S(2)}, u32[]{:S(2)}) collective-permute-start(bf16[4,256,128]{2,1,0:T(8,128)(2,1)S(1)} %get-tuple-element.32), channel_id=1, source_target_pairs={{0,192},{4,196},{8,200},{12,204},{16,208},{20,212},{24,216},{28,22... | collective-permute-start | bytes 786440 | tf_op jit(solution)/shard_map/ppermute | solution.py:37
  98.8 0.6 fusion.7
  99.6 0.6 collective-permute-done
  100.1 7.5 %collective-permute-done.1 = bf16[4,256,128]{2,1,0:T(8,128)(2,1)S(1)} collective-permute-done((bf16[4,256,128]{2,1,0:T(8,128)(2,1)S(1)}, bf16[4,256,128]{2,1,0:T(8,128)(2,1)S(1)}, u32[]{:S(2)}, u32[]{:S(2)}) %collective-permute-start.1) | collective-permute-done | bytes 262176 | tf_op jit(solution)/shard_map/ppermute | solution.py:37
  107.6 0.6 collective-permute-done.2
  108.2 6.1 %attend_head0.1 = (bf16[512,256]{1,0:T(8,128)(2,1)}, bf16[512,256]{1,0:T(8,128)(2,1)}, bf16[4,4,2,32,128]{4,3,2,1,0:T(8,128)(2,1)S(1)}, bf16[4,4,2,32,128]{4,3,2...) custom-call(s32[3]{0:T(128)S(1)} %get-tuple-element.53.use_ref, ...), custom_call_target="tpu_custom_call" | custom-call | flops 2684354560 | bytes 8388608 | tf_op jit(solution)/shard_map/attend_head0/pallas_call | solution.py:122
  114.3 4.7 %collective-permute-start.3 = (bf16[4,4,2,32,128]{4,3,2,1,0:T(8,128)(2,1)S(1)}, bf16[4,4,2,32,128]{4,3,2,1,0:T(8,128)(2,1)S(1)}, u32[]{:S(2)}, u32[]{:S(2)}) collective-permute-start(bf16[4,4,2,32,128]{4,3,2,1,0:T(8,128)(2,1)S(1)} %get-tuple-element.34), channel_id=1, source_target_pairs={{0,192},{4,196},{8,200},{12,204},{16,208},{20,212},{24,216},{28,22... | collective-permute-start | bytes 786440 | tf_op jit(solution)/shard_map/ppermute | solution.py:37
  119.0 3.6 %collective-permute-start.4 = (bf16[4,4,2,32,128]{4,3,2,1,0:T(8,128)(2,1)S(1)}, bf16[4,4,2,32,128]{4,3,2,1,0:T(8,128)(2,1)S(1)}, u32[]{:S(2)}, u32[]{:S(2)}) collective-permute-start(bf16[4,4,2,32,128]{4,3,2,1,0:T(8,128)(2,1)S(1)} %get-tuple-element.35), channel_id=1, source_target_pairs={{0,128},{4,132},{8,136},{12,140},{16,144},{20,148},{24,152},{28,15... | collective-permute-start | bytes 786440 | tf_op jit(solution)/shard_map/ppermute | solution.py:37
  122.6 1.9 collective-permute-start.5
  124.5 4.0 %collective-permute-done.3 = bf16[4,4,2,32,128]{4,3,2,1,0:T(8,128)(2,1)S(1)} collective-permute-done((bf16[4,4,2,32,128]{4,3,2,1,0:T(8,128)(2,1)S(1)}, bf16[4,4,2,32,128]{4,3,2,1,0:T(8,128)(2,1)S(1)}, u32[]{:S(2)}, u32[]{:S(2)}) %collective-permute-start.3) | collective-permute-done | bytes 262176 | tf_op jit(solution)/shard_map/ppermute | solution.py:37
  128.5 5.0 %collective-permute-done.4 = bf16[4,4,2,32,128]{4,3,2,1,0:T(8,128)(2,1)S(1)} collective-permute-done((bf16[4,4,2,32,128]{4,3,2,1,0:T(8,128)(2,1)S(1)}, bf16[4,4,2,32,128]{4,3,2,1,0:T(8,128)(2,1)S(1)}, u32[]{:S(2)}, u32[]{:S(2)}) %collective-permute-start.4) | collective-permute-done | bytes 262176 | tf_op jit(solution)/shard_map/ppermute | solution.py:37
  133.5 4.7 %collective-permute-done.5 = bf16[4,4,2,32,128]{4,3,2,1,0:T(8,128)(2,1)S(1)} collective-permute-done((bf16[4,4,2,32,128]{4,3,2,1,0:T(8,128)(2,1)S(1)}, bf16[4,4,2,32,128]{4,3,2,1,0:T(8,128)(2,1)S(1)}, u32[]{:S(2)}, u32[]{:S(2)}) %collective-permute-start.5) | collective-permute-done | bytes 262176 | tf_op jit(solution)/shard_map/ppermute | solution.py:37
  138.2 2.0 pool_parts.2
  140.2 13.1 %all-to-all-start.2 = ((bf16[64,64,128]{2,1,0:T(8,128)(2,1)}), bf16[64,64,128]{2,1,0:T(8,128)(2,1)S(1)}, u32[]{:S(2)}, u32[]{:S(2)}) async-start(bf16[64,64,128]{2,1,0:T(8,128)(2,1)} %pool_parts.2), calls=%async_computation.2 | async-start | bytes 2097152 | tf_op jit(solution)/shard_map/all_to_all | solution.py:41
  153.4 0.6 gather_picks.3
  154.1 3.5 %collective-permute-start.6 = (bf16[4,256,128]{2,1,0:T(8,128)(2,1)S(1)}, bf16[4,256,128]{2,1,0:T(8,128)(2,1)S(1)}, u32[]{:S(2)}, u32[]{:S(2)}) collective-permute-start(bf16[4,256,128]{2,1,0:T(8,128)(2,1)S(1)} %get-tuple-element.39), channel_id=1, source_target_pairs={{0,64},{4,68},{8,72},{12,76},{16,80},{20,84},{24,88},{28,92},{32,9... | collective-permute-start | bytes 786440 | tf_op jit(solution)/shard_map/ppermute | solution.py:37
  157.6 4.8 %collective-permute-start.7 = (bf16[4,256,128]{2,1,0:T(8,128)(2,1)S(1)}, bf16[4,256,128]{2,1,0:T(8,128)(2,1)S(1)}, u32[]{:S(2)}, u32[]{:S(2)}) collective-permute-start(bf16[4,256,128]{2,1,0:T(8,128)(2,1)S(1)} %get-tuple-element.40), channel_id=1, source_target_pairs={{0,128},{4,132},{8,136},{12,140},{16,144},{20,148},{24,152},{28,15... | collective-permute-start | bytes 786440 | tf_op jit(solution)/shard_map/ppermute | solution.py:37
  162.3 3.4 %collective-permute-start.8 = (bf16[4,256,128]{2,1,0:T(8,128)(2,1)S(1)}, bf16[4,256,128]{2,1,0:T(8,128)(2,1)S(1)}, u32[]{:S(2)}, u32[]{:S(2)}) collective-permute-start(bf16[4,256,128]{2,1,0:T(8,128)(2,1)S(1)} %get-tuple-element.41), channel_id=1, source_target_pairs={{0,192},{4,196},{8,200},{12,204},{16,208},{20,212},{24,216},{28,22... | collective-permute-start | bytes 786440 | tf_op jit(solution)/shard_map/ppermute | solution.py:37
  165.8 0.7 collective-permute-done.6
  166.5 8.1 %collective-permute-done.7 = bf16[4,256,128]{2,1,0:T(8,128)(2,1)S(1)} collective-permute-done((bf16[4,256,128]{2,1,0:T(8,128)(2,1)S(1)}, bf16[4,256,128]{2,1,0:T(8,128)(2,1)S(1)}, u32[]{:S(2)}, u32[]{:S(2)}) %collective-permute-start.7) | collective-permute-done | bytes 262176 | tf_op jit(solution)/shard_map/ppermute | solution.py:37
  174.6 1.1 collective-permute-done.8
  175.7 6.1 %attend_head1.1 = (bf16[512,256]{1,0:T(8,128)(2,1)}, bf16[512,256]{1,0:T(8,128)(2,1)}, bf16[4,4,2,32,128]{4,3,2,1,0:T(8,128)(2,1)S(1)}, bf16[4,4,2,32,128]{4,3,2...) custom-call(s32[3]{0:T(128)S(1)} %get-tuple-element.54.use_ref, ...), custom_call_target="tpu_custom_call", output_to_operand_aliasing={{0}: (9, {}), {1}: (10, {})} | custom-call | flops 2684354560 | bytes 8388608 | tf_op jit(solution)/shard_map/attend_head1/pallas_call | solution.py:122
  181.9 4.6 %collective-permute-start.9 = (bf16[4,4,2,32,128]{4,3,2,1,0:T(8,128)(2,1)S(1)}, bf16[4,4,2,32,128]{4,3,2,1,0:T(8,128)(2,1)S(1)}, u32[]{:S(2)}, u32[]{:S(2)}) collective-permute-start(bf16[4,4,2,32,128]{4,3,2,1,0:T(8,128)(2,1)S(1)} %get-tuple-element.48), channel_id=1, source_target_pairs={{0,192},{4,196},{8,200},{12,204},{16,208},{20,212},{24,216},{28,22... | collective-permute-start | bytes 786440 | tf_op jit(solution)/shard_map/ppermute | solution.py:37
  186.5 3.6 %collective-permute-start.10 = (bf16[4,4,2,32,128]{4,3,2,1,0:T(8,128)(2,1)S(1)}, bf16[4,4,2,32,128]{4,3,2,1,0:T(8,128)(2,1)S(1)}, u32[]{:S(2)}, u32[]{:S(2)}) collective-permute-start(bf16[4,4,2,32,128]{4,3,2,1,0:T(8,128)(2,1)S(1)} %get-tuple-element.49), channel_id=1, source_target_pairs={{0,128},{4,132},{8,136},{12,140},{16,144},{20,148},{24,152},{28,15... | collective-permute-start | bytes 786440 | tf_op jit(solution)/shard_map/ppermute | solution.py:37
  190.1 1.9 collective-permute-start.11
  192.0 0.5 slice.70
  192.5 0.5 slice.71
  193.0 1.5 maximum_dynamic-update-slice_fusion
  194.5 13.1 %psum.7 = f32[32]{0:T(128)S(1)} all-reduce(f32[32]{0:T(128)S(1)} %maximum_dynamic-update-slice_fusion), channel_id=1, replica_groups=mesh['dp'=2,'ctx'=64,'head'=4] {'dp','head'}, use_global_device_ids=true, to_apply=%region_5.6 | all-reduce | flops 32 | bytes 256 | tf_op jit(solution)/shard_map/psum | solution.py:261
  207.7 2.0 pool_parts.3
  209.7 15.2 %all-to-all-start.3 = ((bf16[64,72,128]{2,1,0:T(8,128)(2,1)}), bf16[64,72,128]{2,1,0:T(8,128)(2,1)S(1)}, u32[]{:S(2)}, u32[]{:S(2)}) async-start(bf16[64,72,128]{2,1,0:T(8,128)(2,1)} %pool_parts.3), calls=%async_computation.3 | async-start | bytes 2359296 | tf_op jit(solution)/shard_map/all_to_all | solution.py:41
  225.2 57.9 %all-to-all-done.3 = bf16[64,72,128]{2,1,0:T(8,128)(2,1)S(1)} async-done(((bf16[64,72,128]{2,1,0:T(8,128)(2,1)}), bf16[64,72,128]{2,1,0:T(8,128)(2,1)S(1)}, u32[]{:S(2)}, u32[]{:S(2)}) %all-to-all-start.3) | async-done | bytes 1179680 | tf_op jit(solution)/shard_map/all_to_all | solution.py:41
  283.6 0.3 copy.36
  283.8 0.9 reshape_squeeze.7
  284.9 0.6 reduce_sum.75
  285.5 0.3 copy.35
  285.7 0.9 reshape_squeeze.6
  (46 shorter events, 2.5 us)
Async XLA Ops:
  0.6 84.8 %copy-start = (s32[1,16,8,3]{1,2,3,0:T(8,128)S(1)}, s32[1,16,8,3]{1,2,3,0:T(8,128)}, u32[]{:S(2)}) copy-start(s32[1,16,8,3]{1,2,3,0:T(8,128)} %param.11) | copy-start | bytes 4612
  78.4 7.1 %copy-start.3 = (s32[16]{0:T(128)S(1)}, s32[16]{0:T(128)}, u32[]{:S(2)}) copy-start(s32[16]{0:T(128)} %param.12) | copy-start | bytes 196
  78.4 20.3 %copy-start.4 = (f32[8]{0:T(128)S(1)}, f32[8]{0:T(128)}, u32[]{:S(2)}) copy-start(f32[8]{0:T(128)} %param.13) | copy-start | bytes 100
  78.4 29.7 %copy-start.1 = (bf16[1,1,1,512,256]{4,3,2,1,0:T(8,128)(2,1)S(1)}, bf16[1,1,1,512,256]{4,3,2,1,0:T(8,128)(2,1)}, u32[]{:S(2)}) copy-start(bf16[1,1,1,512,256]{4,3,2,1,0:T(8,128)(2,1)} %param.7) | copy-start | bytes 786436
  78.4 29.7 %copy-start.2 = (bf16[1,1,1,512,256]{4,3,2,1,0:T(8,128)(2,1)S(1)}, bf16[1,1,1,512,256]{4,3,2,1,0:T(8,128)(2,1)}, u32[]{:S(2)}) copy-start(bf16[1,1,1,512,256]{4,3,2,1,0:T(8,128)(2,1)} %param.10) | copy-start | bytes 786436
  78.4 61.7 %all-to-all-start = ((bf16[64,64,128]{2,1,0:T(8,128)(2,1)}), bf16[64,64,128]{2,1,0:T(8,128)(2,1)S(1)}, u32[]{:S(2)}, u32[]{:S(2)}) async-start(bf16[64,64,128]{2,1,0:T(8,128)(2,1)} %bitcast.71), calls=%async_computation | async-start | bytes 2097152 | tf_op jit(solution)/shard_map/all_to_all | solution.py:41
  87.2 13.0 %collective-permute-start = (bf16[4,256,128]{2,1,0:T(8,128)(2,1)S(1)}, bf16[4,256,128]{2,1,0:T(8,128)(2,1)S(1)}, u32[]{:S(2)}, u32[]{:S(2)}) collective-permute-start(bf16[4,256,128]{2,1,0:T(8,128)(2,1)S(1)} %get-tuple-element.30), channel_id=1, source_target_pairs={{0,64},{4,68},{8,72},{12,76},{16,80},{20,84},{24,88},{28,92},{32,9... | collective-permute-start | bytes 786440 | tf_op jit(solution)/shard_map/ppermute | solution.py:37
  90.7 16.9 %collective-permute-start.1 = (bf16[4,256,128]{2,1,0:T(8,128)(2,1)S(1)}, bf16[4,256,128]{2,1,0:T(8,128)(2,1)S(1)}, u32[]{:S(2)}, u32[]{:S(2)}) collective-permute-start(bf16[4,256,128]{2,1,0:T(8,128)(2,1)S(1)} %get-tuple-element.31), channel_id=1, source_target_pairs={{0,128},{4,132},{8,136},{12,140},{16,144},{20,148},{24,152},{28,15... | collective-permute-start | bytes 786440 | tf_op jit(solution)/shard_map/ppermute | solution.py:37
  95.5 12.7 %collective-permute-start.2 = (bf16[4,256,128]{2,1,0:T(8,128)(2,1)S(1)}, bf16[4,256,128]{2,1,0:T(8,128)(2,1)S(1)}, u32[]{:S(2)}, u32[]{:S(2)}) collective-permute-start(bf16[4,256,128]{2,1,0:T(8,128)(2,1)S(1)} %get-tuple-element.32), channel_id=1, source_target_pairs={{0,192},{4,196},{8,200},{12,204},{16,208},{20,212},{24,216},{28,22... | collective-permute-start | bytes 786440 | tf_op jit(solution)/shard_map/ppermute | solution.py:37
  114.3 14.2 %collective-permute-start.3 = (bf16[4,4,2,32,128]{4,3,2,1,0:T(8,128)(2,1)S(1)}, bf16[4,4,2,32,128]{4,3,2,1,0:T(8,128)(2,1)S(1)}, u32[]{:S(2)}, u32[]{:S(2)}) collective-permute-start(bf16[4,4,2,32,128]{4,3,2,1,0:T(8,128)(2,1)S(1)} %get-tuple-element.34), channel_id=1, source_target_pairs={{0,192},{4,196},{8,200},{12,204},{16,208},{20,212},{24,216},{28,22... | collective-permute-start | bytes 786440 | tf_op jit(solution)/shard_map/ppermute | solution.py:37
  119.0 14.5 %collective-permute-start.4 = (bf16[4,4,2,32,128]{4,3,2,1,0:T(8,128)(2,1)S(1)}, bf16[4,4,2,32,128]{4,3,2,1,0:T(8,128)(2,1)S(1)}, u32[]{:S(2)}, u32[]{:S(2)}) collective-permute-start(bf16[4,4,2,32,128]{4,3,2,1,0:T(8,128)(2,1)S(1)} %get-tuple-element.35), channel_id=1, source_target_pairs={{0,128},{4,132},{8,136},{12,140},{16,144},{20,148},{24,152},{28,15... | collective-permute-start | bytes 786440 | tf_op jit(solution)/shard_map/ppermute | solution.py:37
  122.6 15.6 %collective-permute-start.5 = (bf16[4,4,2,32,128]{4,3,2,1,0:T(8,128)(2,1)S(1)}, bf16[4,4,2,32,128]{4,3,2,1,0:T(8,128)(2,1)S(1)}, u32[]{:S(2)}, u32[]{:S(2)}) collective-permute-start(bf16[4,4,2,32,128]{4,3,2,1,0:T(8,128)(2,1)S(1)} %get-tuple-element.36), channel_id=1, source_target_pairs={{0,64},{4,68},{8,72},{12,76},{16,80},{20,84},{24,88},{28,92},{32,9... | collective-permute-start | bytes 786440 | tf_op jit(solution)/shard_map/ppermute | solution.py:37
  140.2 69.6 %all-to-all-start.2 = ((bf16[64,64,128]{2,1,0:T(8,128)(2,1)}), bf16[64,64,128]{2,1,0:T(8,128)(2,1)S(1)}, u32[]{:S(2)}, u32[]{:S(2)}) async-start(bf16[64,64,128]{2,1,0:T(8,128)(2,1)} %pool_parts.2), calls=%async_computation.2 | async-start | bytes 2097152 | tf_op jit(solution)/shard_map/all_to_all | solution.py:41
  154.1 12.5 %collective-permute-start.6 = (bf16[4,256,128]{2,1,0:T(8,128)(2,1)S(1)}, bf16[4,256,128]{2,1,0:T(8,128)(2,1)S(1)}, u32[]{:S(2)}, u32[]{:S(2)}) collective-permute-start(bf16[4,256,128]{2,1,0:T(8,128)(2,1)S(1)} %get-tuple-element.39), channel_id=1, source_target_pairs={{0,64},{4,68},{8,72},{12,76},{16,80},{20,84},{24,88},{28,92},{32,9... | collective-permute-start | bytes 786440 | tf_op jit(solution)/shard_map/ppermute | solution.py:37
  157.6 17.1 %collective-permute-start.7 = (bf16[4,256,128]{2,1,0:T(8,128)(2,1)S(1)}, bf16[4,256,128]{2,1,0:T(8,128)(2,1)S(1)}, u32[]{:S(2)}, u32[]{:S(2)}) collective-permute-start(bf16[4,256,128]{2,1,0:T(8,128)(2,1)S(1)} %get-tuple-element.40), channel_id=1, source_target_pairs={{0,128},{4,132},{8,136},{12,140},{16,144},{20,148},{24,152},{28,15... | collective-permute-start | bytes 786440 | tf_op jit(solution)/shard_map/ppermute | solution.py:37
  162.3 13.4 %collective-permute-start.8 = (bf16[4,256,128]{2,1,0:T(8,128)(2,1)S(1)}, bf16[4,256,128]{2,1,0:T(8,128)(2,1)S(1)}, u32[]{:S(2)}, u32[]{:S(2)}) collective-permute-start(bf16[4,256,128]{2,1,0:T(8,128)(2,1)S(1)} %get-tuple-element.41), channel_id=1, source_target_pairs={{0,192},{4,196},{8,200},{12,204},{16,208},{20,212},{24,216},{28,22... | collective-permute-start | bytes 786440 | tf_op jit(solution)/shard_map/ppermute | solution.py:37
  181.9 25.8 %collective-permute-start.9 = (bf16[4,4,2,32,128]{4,3,2,1,0:T(8,128)(2,1)S(1)}, bf16[4,4,2,32,128]{4,3,2,1,0:T(8,128)(2,1)S(1)}, u32[]{:S(2)}, u32[]{:S(2)}) collective-permute-start(bf16[4,4,2,32,128]{4,3,2,1,0:T(8,128)(2,1)S(1)} %get-tuple-element.48), channel_id=1, source_target_pairs={{0,192},{4,196},{8,200},{12,204},{16,208},{20,212},{24,216},{28,22... | collective-permute-start | bytes 786440 | tf_op jit(solution)/shard_map/ppermute | solution.py:37
  186.5 21.2 %collective-permute-start.10 = (bf16[4,4,2,32,128]{4,3,2,1,0:T(8,128)(2,1)S(1)}, bf16[4,4,2,32,128]{4,3,2,1,0:T(8,128)(2,1)S(1)}, u32[]{:S(2)}, u32[]{:S(2)}) collective-permute-start(bf16[4,4,2,32,128]{4,3,2,1,0:T(8,128)(2,1)S(1)} %get-tuple-element.49), channel_id=1, source_target_pairs={{0,128},{4,132},{8,136},{12,140},{16,144},{20,148},{24,152},{28,15... | collective-permute-start | bytes 786440 | tf_op jit(solution)/shard_map/ppermute | solution.py:37
  190.1 17.6 %collective-permute-start.11 = (bf16[4,4,2,32,128]{4,3,2,1,0:T(8,128)(2,1)S(1)}, bf16[4,4,2,32,128]{4,3,2,1,0:T(8,128)(2,1)S(1)}, u32[]{:S(2)}, u32[]{:S(2)}) collective-permute-start(bf16[4,4,2,32,128]{4,3,2,1,0:T(8,128)(2,1)S(1)} %get-tuple-element.50), channel_id=1, source_target_pairs={{0,64},{4,68},{8,72},{12,76},{16,80},{20,84},{24,88},{28,92},{32,9... | collective-permute-start | bytes 786440 | tf_op jit(solution)/shard_map/ppermute | solution.py:37
  209.7 73.4 %all-to-all-start.3 = ((bf16[64,72,128]{2,1,0:T(8,128)(2,1)}), bf16[64,72,128]{2,1,0:T(8,128)(2,1)S(1)}, u32[]{:S(2)}, u32[]{:S(2)}) async-start(bf16[64,72,128]{2,1,0:T(8,128)(2,1)} %pool_parts.3), calls=%async_computation.3 | async-start | bytes 2359296 | tf_op jit(solution)/shard_map/all_to_all | solution.py:41

commit v7 on v4

--- a/solution.py
+++ b/solution.py
@@ -20,11 +20,11 @@
 FRAG = BLOCK // (XS * SPB)
 ROWS = SPB * 2 * FRAG
 KINDS = TOPK + 1
+EXTRA = 8
 LOG2E = math.log2(math.e)
 NEG = -1e30
 
 SPREAD_GROUPS = [[x * ZS + g * SPB + r for x in range(XS) for r in range(SPB)] for g in range(ZG)]
-Z_GROUPS = [[x * ZS + z for z in range(ZS)] for x in range(XS)]
 X_GROUPS = [[x * ZS + z for x in range(XS)] for z in range(ZS)]
 
 
@@ -42,16 +42,6 @@
 
 def swap_x(arr):
     return lax.all_to_all(arr, "ctx", 0, 0, axis_index_groups=X_GROUPS, tiled=True)
-
-
-def swap_sink(vals, axes, groups, after=None):
-    count = 8 if groups is None else len(groups[0])
-    vals = vals.reshape(1, -1)
-    size = vals.shape[1]
-    rows = jnp.broadcast_to(jnp.pad(vals, ((0, 0), (0, 128 - size))), (count, 128))
-    if after is not None:
-        rows, _ = lax.optimization_barrier((rows, after))
-    return lax.all_to_all(rows, axes, 0, 0, axis_index_groups=groups, tiled=True)[:, :size]
 
 
 def dot(left, right, left_dim, right_dim):
@@ -188,6 +178,7 @@
 
 def pool_kernel(index_ref, part_ref, *refs):
     acc_ref = refs[-1]
+    out_refs = refs[-1 - ZG : -1]
     for x in range(XS):
         acc_ref[x] = part_ref[x, 0].astype(jnp.float32)
     for slot in range(XS, ZG * XS):
@@ -196,26 +187,35 @@
         for pick in range(TOPK):
             slot = index_ref[x * TOPK + pick]
             acc_ref[slot] = acc_ref[slot] + part_ref[x, pick + 1].astype(jnp.float32)
-    for rel in range(ZG):
-        refs[rel][...] = acc_ref[rel * XS : (rel + 1) * XS].astype(jnp.bfloat16)
-
-
-def pool_parts(index, parts):
+    for slot in range(ZG * XS):
+        at = slot % XS * ROWS
+        out_refs[slot // XS][at : at + ROWS] = acc_ref[slot].astype(jnp.bfloat16)
+    if len(refs) > ZG + 1:
+        left = refs[0][...]
+        lane = lax.broadcasted_iota(jnp.int32, left.shape, 1)
+        terms = jnp.zeros(left.shape, jnp.float32)
+        for term in range(3):
+            rounded = left.astype(jnp.bfloat16).astype(jnp.float32)
+            terms = jnp.where(lane // HEADS == term, rounded, terms)
+            left = left - rounded
+        for ref in out_refs:
+            ref[XS * ROWS :] = terms.astype(jnp.bfloat16)
+
+
+def pool_parts(index, parts, sink_sum=None):
+    extra = [] if sink_sum is None else [jnp.tile(sink_sum[None], (EXTRA, 128 // HEADS))]
+    shape = (XS * ROWS + EXTRA * len(extra), DH)
     return pl.pallas_call(
         pool_kernel,
         name="pool_parts",
-        in_specs=[
-            pl.BlockSpec(memory_space=pltpu.SMEM),
-            pl.BlockSpec(memory_space=pltpu.VMEM),
-        ],
+        in_specs=[pl.BlockSpec(memory_space=pltpu.SMEM)]
+        + [pl.BlockSpec(memory_space=pltpu.VMEM)] * (1 + len(extra)),
         out_specs=tuple(pl.BlockSpec(memory_space=pltpu.VMEM) for _ in range(ZG)),
-        out_shape=tuple(
-            jax.ShapeDtypeStruct((XS, ROWS, DH), jnp.bfloat16) for _ in range(ZG)
-        ),
+        out_shape=tuple(jax.ShapeDtypeStruct(shape, jnp.bfloat16) for _ in range(ZG)),
         scratch_shapes=[pltpu.VMEM((ZG * XS, ROWS, DH), jnp.float32)],
         compiler_params=pltpu.CompilerParams(vmem_limit_bytes=16 << 20),
         cost_estimate=pl.CostEstimate(flops=1 << 20, transcendentals=0, bytes_accessed=4 << 20),
-    )(index, parts)
+    )(index, parts, *extra)
 
 
 def add_rounded(*arrs):
@@ -281,7 +281,8 @@
             h, use[h], sink_mine[h : h + 1], query_rows, grad_rows, own[h], picks, earlier
         )
         earlier = (att, dq)
-        sink_heads.append(sink_sum[0, 0])
+        sink_heads.append(sink_sum[0, :1])
+        sink_sum = None
         if h == 0:
             part, below[1], far[1] = lax.optimization_barrier((part, below[1], far[1]))
         else:
@@ -290,25 +291,35 @@
         if h > 0:
             up_first = shift_groups(add_rounded(pools[0][1], up_far), 1)
             back, up_first = lax.optimization_barrier((back, up_first))
-        pools.append(pool_parts(index[h], back))
+            start = lax.axis_index("head") * (SPB * HPD) + position * HPD
+            sink_sum = lax.dynamic_update_slice(
+                jnp.zeros((HEADS,), jnp.float32), jnp.concatenate(sink_heads), (start,)
+            )
+            sink_sum = lax.psum(sink_sum, ("dp", "head"))
+        pools.append(pool_parts(index[h], back, sink_sum))
         if h == 0:
             up_far = shift_groups(pools[0][2], 1)
             down_near = shift_groups(pools[0][3], -1)
             late, _ = lax.optimization_barrier((held[1], pools[0]))
             sources[1] = (late, above[1], far[1], below[1])
+    main = XS * ROWS
     down_far = shift_groups(pools[1][2], -1)
     up_near = shift_groups(pools[1][1], 1)
-    sink_all = swap_sink(jnp.stack(sink_heads), "ctx", Z_GROUPS, after=down_far)
-    sink_all = jnp.sum(sink_all.reshape(ZG, SPB, HPD), axis=0)
-    sink_all = jnp.sum(swap_sink(sink_all, "ctx", X_GROUPS), axis=0)
-    sink_all = swap_sink(sink_all, ("dp", "head"), None)
-    grad_sink = jnp.sum(sink_all.reshape(-1, HEADS), axis=0)
-    up = [up_first, up_near]
-    down = [down_near, shift_groups(add_rounded(pools[1][3], down_far), -1)]
-    pooled = [add_rounded(pools[h][0], up[h], down[h]) for h in range(HPD)]
-    pooled[0], grad_sink = lax.optimization_barrier((pooled[0], grad_sink))
-    pooled = jnp.stack([arr.reshape(XS, SPB, 2 * FRAG, DH) for arr in pooled], axis=2)
-    homed = swap_spread(pooled.reshape(XS * SPB, HPD * 2 * FRAG, DH))
+    onward = jnp.concatenate([add_rounded(pools[1][3][:main], down_far[:main]), down_far[main:]])
+    down_last = shift_groups(onward, -1)
+    first = add_rounded(pools[0][0], up_first, down_near)
+    second = add_rounded(pools[1][0][:main], up_near[:main], down_last[:main])
+    terms = [arr[main : main + 1] for arr in (pools[1][0], up_near, down_far, down_last)]
+    terms = jnp.concatenate(terms + [jnp.zeros((EXTRA - ZG, DH), jnp.bfloat16)])
+    pooled = jnp.concatenate(
+        [arr.reshape(XS * SPB, 2 * FRAG, DH) for arr in (first, second)]
+        + [jnp.broadcast_to(terms[None], (XS * SPB, EXTRA, DH))],
+        axis=1,
+    )
+    homed = swap_spread(pooled)
+    terms = homed[:, HPD * 2 * FRAG :, : 3 * HEADS].astype(jnp.float32)
+    grad_sink = jnp.sum(terms.reshape(-1, HEADS), axis=0)
+    homed = homed[:, : HPD * 2 * FRAG]
     totals = jnp.transpose(homed.reshape(XS, SPB, HPD, 2, FRAG, DH), (3, 0, 4, 1, 2, 5))
     grad_key = totals[0].reshape(key.shape)
     grad_value = totals[1].reshape(value.shape)

time: 289 us -> 288 us (level)
  blocking collectives: 17.4 us -> 49.1 us
  starting transfers between devices: 127 us -> 104 us
  waiting for transfers between devices: 107 us -> 95.8 us
    all_to_all x1, blocking collectives: 17.4 us -> 36.3 us  [swap_spread(): lax.all_to_all(arr, 'ctx', 0, 0, axis_index_groups=SPREAD_GROUPS, tiled=T...]
    all_to_all x3 -> x0, starting transfers between devices: 18 us -> none  [swap_sink(): lax.all_to_all(rows, axes, 0, 0, axis_index_groups=groups, tiled=True)]
    psum x0 -> x1, blocking collectives: none -> 12.8 us  [body(): sink_sum = lax.psum(sink_sum, ('dp', 'head'))]
    all_to_all x3 -> x0, waiting for transfers between devices: 11.6 us -> none  [swap_sink(): lax.all_to_all(rows, axes, 0, 0, axis_index_groups=groups, tiled=True)]
    ppermute x12, starting transfers between devices: 76.9 us -> 71.4 us  [shift_groups(): return lax.ppermute(arr, 'ctx', pairs)]
  transfers between devices with their start and end apart: 22 -> 19, of which waited for: 16 -> 12; matrix products, arithmetic and copies ran while one was open for 2% -> 2% of each run, Pallas kernels for 5% -> 5%
where the time goes in v7:
time: 288 us; the launch traced here: 283 us
  starting transfers between devices  104 us (36%)
  waiting for transfers between devices  95.8 us (33%)
  blocking collectives  49.1 us (17%)
  Pallas kernels  18.7 us (6%)
  local copies, waits for them, and re-layouts  10.5 us (4%)
  other arithmetic  4.19 us (1%)
    ppermute x12, starting transfers between devices, shift_groups(): return lax.ppermute(arr, 'ctx', pairs)  71.4 us
    ppermute x12, waiting for transfers between devices, shift_groups(): return lax.ppermute(arr, 'ctx', pairs)  60.6 us
    all_to_all x1, blocking collectives, swap_spread(): lax.all_to_all(arr, 'ctx', 0, 0, axis_index_groups=SPREAD_GROUPS, tiled=T...  36.3 us
    all_to_all x6, starting transfers between devices, swap_x(): lax.all_to_all(arr, 'ctx', 0, 0, axis_index_groups=X_GROUPS, tiled=True)  24 us
    all_to_all x6, waiting for transfers between devices, swap_x(): lax.all_to_all(arr, 'ctx', 0, 0, axis_index_groups=X_GROUPS, tiled=True)  19.2 us
    all_to_all x1, waiting for transfers between devices, swap_spread(): lax.all_to_all(arr, 'ctx', 0, 0, axis_index_groups=SPREAD_GROUPS, tiled=T...  16.1 us
    pallas_call x2, Pallas kernels, attend(): pl.pallas_call(attend_kernel, name='attend_head%d' % head, grid=(1,), in_...  13 us
    psum x1, blocking collectives, body(): sink_sum = lax.psum(sink_sum, ('dp', 'head'))  12.8 us
  transfers between devices with their start and end apart: 19, of which 12 were waited for; matrix products, arithmetic and copies ran while one was open for 2% of the time, Pallas kernels for 5%

profile of v7, /device:TPU:24, one launch (start us, length us, event | category | flops | bytes accessed | tf_op | source)
XLA Modules:
  0.0 283.4 jit_solution(8309284578221657968)
XLA Ops:
  0.6 1.1 reshape.126
  1.8 1.1 reshape.127
  2.9 0.7 pad_maximum_fusion.1
  3.7 0.9 copy.25
  4.6 8.5 %all-to-all-start = ((bf16[16,128,128]{2,1,0:T(8,128)(2,1)}), bf16[16,128,128]{2,1,0:T(8,128)(2,1)S(1)}, u32[]{:S(2)}, u32[]{:S(2)}) async-start(bf16[16,128,128]{2,1,0:T(8,128)(2,1)} %bitcast.8), calls=%async_computation | async-start | bytes 1048576 | tf_op jit(solution)/shard_map/all_to_all | solution.py:40
  13.5 16.1 %all-to-all-done = bf16[16,128,128]{2,1,0:T(8,128)(2,1)S(1)} async-done(((bf16[16,128,128]{2,1,0:T(8,128)(2,1)}), bf16[16,128,128]{2,1,0:T(8,128)(2,1)S(1)}, u32[]{:S(2)}, u32[]{:S(2)}) %all-to-all-start) | async-done | bytes 524320 | tf_op jit(solution)/shard_map/all_to_all | solution.py:40
  29.6 0.8 fusion.10
  30.4 9.1 %collective-permute-start = (bf16[4,256,128]{2,1,0:T(8,128)(2,1)}, bf16[4,256,128]{2,1,0:T(8,128)(2,1)S(1)}, u32[]{:S(2)}, u32[]{:S(2)}) collective-permute-start(bf16[4,256,128]{2,1,0:T(8,128)(2,1)} %bitcast.11.refs_0_), channel_id=1, source_target_pairs={{0,16},{4,20},{8,24},{12,28},{16,32},{20,36},{24,40},{28,44},{32,4... | collective-permute-start | bytes 786440 | tf_op jit(solution)/shard_map/ppermute | solution.py:36
  40.0 3.4 %all-to-all-start.1 = ((bf16[4,256,128]{2,1,0:T(8,128)(2,1)}), bf16[4,256,128]{2,1,0:T(8,128)(2,1)S(1)}, u32[]{:S(2)}, u32[]{:S(2)}) async-start(bf16[4,256,128]{2,1,0:T(8,128)(2,1)} %bitcast.11.refs_0_), calls=%async_computation.1 | async-start | bytes 524288 | tf_op jit(solution)/shard_map/all_to_all | solution.py:44
  43.4 2.9 %collective-permute-start.2 = (bf16[4,256,128]{2,1,0:T(8,128)(2,1)}, bf16[4,256,128]{2,1,0:T(8,128)(2,1)S(1)}, u32[]{:S(2)}, u32[]{:S(2)}) collective-permute-start(bf16[4,256,128]{2,1,0:T(8,128)(2,1)} %bitcast.11.refs_0_), channel_id=1, source_target_pairs={{0,48},{4,52},{8,56},{12,60},{16,0},{20,4},{24,8},{28,12},{32,16},... | collective-permute-start | bytes 786440 | tf_op jit(solution)/shard_map/ppermute | solution.py:36
  46.3 16.7 %collective-permute-done.refs_3_ = bf16[4,256,128]{2,1,0:T(8,128)(2,1)S(1)} collective-permute-done((bf16[4,256,128]{2,1,0:T(8,128)(2,1)}, bf16[4,256,128]{2,1,0:T(8,128)(2,1)S(1)}, u32[]{:S(2)}, u32[]{:S(2)}) %collective-permute-start) | collective-permute-done | bytes 262176 | tf_op jit(solution)/shard_map/ppermute | solution.py:36
  63.0 6.9 %collective-permute-start.1 = (bf16[4,256,128]{2,1,0:T(8,128)(2,1)}, bf16[4,256,128]{2,1,0:T(8,128)(2,1)S(1)}, u32[]{:S(2)}, u32[]{:S(2)}) collective-permute-start(bf16[4,256,128]{2,1,0:T(8,128)(2,1)} %bitcast.13.refs_0_), channel_id=1, source_target_pairs={{0,48},{4,52},{8,56},{12,60},{16,0},{20,4},{24,8},{28,12},{32,16},... | collective-permute-start | bytes 786440 | tf_op jit(solution)/shard_map/ppermute | solution.py:36
  69.8 2.9 %collective-permute-start.3 = (bf16[4,256,128]{2,1,0:T(8,128)(2,1)S(1)}, bf16[4,256,128]{2,1,0:T(8,128)(2,1)S(1)}, u32[]{:S(2)}, u32[]{:S(2)}) collective-permute-start(bf16[4,256,128]{2,1,0:T(8,128)(2,1)S(1)} %collective-permute-done.refs_3_), channel_id=1, source_target_pairs={{0,16},{4,20},{8,24},{12,28},{16,32},{20,36},{24,40},{28,44},{32,4... | collective-permute-start | bytes 786440 | tf_op jit(solution)/shard_map/ppermute | solution.py:36
  72.7 3.4 %all-to-all-start.2 = ((bf16[4,256,128]{2,1,0:T(8,128)(2,1)}), bf16[4,256,128]{2,1,0:T(8,128)(2,1)S(1)}, u32[]{:S(2)}, u32[]{:S(2)}) async-start(bf16[4,256,128]{2,1,0:T(8,128)(2,1)} %bitcast.13.refs_0_), calls=%async_computation.2 | async-start | bytes 524288 | tf_op jit(solution)/shard_map/all_to_all | solution.py:44
  76.4 6.5 %all-to-all-done.2 = bf16[4,256,128]{2,1,0:T(8,128)(2,1)S(1)} async-done(((bf16[4,256,128]{2,1,0:T(8,128)(2,1)}), bf16[4,256,128]{2,1,0:T(8,128)(2,1)S(1)}, u32[]{:S(2)}, u32[]{:S(2)}) %all-to-all-start.2) | async-done | bytes 262176 | tf_op jit(solution)/shard_map/all_to_all | solution.py:44
  82.8 5.9 %collective-permute-done.1.refs_1_ = bf16[4,256,128]{2,1,0:T(8,128)(2,1)S(1)} collective-permute-done((bf16[4,256,128]{2,1,0:T(8,128)(2,1)}, bf16[4,256,128]{2,1,0:T(8,128)(2,1)S(1)}, u32[]{:S(2)}, u32[]{:S(2)}) %collective-permute-start.1) | collective-permute-done | bytes 262176 | tf_op jit(solution)/shard_map/ppermute | solution.py:36
  88.7 2.3 collective-permute-done.3.refs_2_
  91.1 2.0 gather_picks.2
  93.0 3.6 %all-to-all-start.3 = ((bf16[4,768,128]{2,1,0:T(8,128)(2,1)}), bf16[4,768,128]{2,1,0:T(8,128)(2,1)S(1)}, u32[]{:S(2)}, u32[]{:S(2)}) async-start(bf16[4,768,128]{2,1,0:T(8,128)(2,1)} %bitcast.19), calls=%async_computation.3 | async-start | bytes 1572864 | tf_op jit(solution)/shard_map/all_to_all | solution.py:44
  96.9 4.3 %collective-permute-start.4 = (bf16[4,256,128]{2,1,0:T(8,128)(2,1)}, bf16[4,256,128]{2,1,0:T(8,128)(2,1)S(1)}, u32[]{:S(2)}, u32[]{:S(2)}) collective-permute-start(bf16[4,256,128]{2,1,0:T(8,128)(2,1)} %bitcast.13.refs_0_), channel_id=1, source_target_pairs={{0,16},{4,20},{8,24},{12,28},{16,32},{20,36},{24,40},{28,44},{32,4... | collective-permute-start | bytes 786440 | tf_op jit(solution)/shard_map/ppermute | solution.py:36
  101.3 5.4 %collective-permute-start.5 = (bf16[4,256,128]{2,1,0:T(8,128)(2,1)S(1)}, bf16[4,256,128]{2,1,0:T(8,128)(2,1)S(1)}, u32[]{:S(2)}, u32[]{:S(2)}) collective-permute-start(bf16[4,256,128]{2,1,0:T(8,128)(2,1)S(1)} %collective-permute-done.1.refs_1_), channel_id=1, source_target_pairs={{0,48},{4,52},{8,56},{12,60},{16,0},{20,4},{24,8},{28,12},{32,16},... | collective-permute-start | bytes 786440 | tf_op jit(solution)/shard_map/ppermute | solution.py:36
  107.4 2.0 all-to-all-done.3
  109.4 6.5 %attend_head0.1 = (bf16[512,256]{1,0:T(8,128)(2,1)}, bf16[512,256]{1,0:T(8,128)(2,1)}, bf16[4,4,4,2,32,128]{5,4,3,2,1,0:T(8,128)(2,1)}, f32[8,128]{1,0:T(8,128)S(1)}) custom-call(s32[3]{0:T(128)S(1)} %get-tuple-element.77.use_ref, f32[1]{0:T(128)} %get-tuple-element.79.sink_ref, bf16[512,256]{1,0:T(8,128)(2,1)S(1)} %bitcast.64, ...), custom_call_target="tpu_custom_call" | custom-call | flops 2684354560 | bytes 8388608 | tf_op jit(solution)/shard_map/attend_head0/pallas_call | solution.py:131
  115.9 4.3 %collective-permute-done.5.refs_2_ = bf16[4,256,128]{2,1,0:T(8,128)(2,1)S(1)} collective-permute-done((bf16[4,256,128]{2,1,0:T(8,128)(2,1)S(1)}, bf16[4,256,128]{2,1,0:T(8,128)(2,1)S(1)}, u32[]{:S(2)}, u32[]{:S(2)}) %collective-permute-start.5) | collective-permute-done | bytes 262176 | tf_op jit(solution)/shard_map/ppermute | solution.py:36
  120.1 5.1 %all-to-all-start.4 = ((bf16[4,1024,128]{2,1,0:T(8,128)(2,1)}), bf16[4,1024,128]{2,1,0:T(8,128)(2,1)S(1)}, u32[]{:S(2)}, u32[]{:S(2)}) async-start(bf16[4,1024,128]{2,1,0:T(8,128)(2,1)} %bitcast.21), calls=%async_computation.4 | async-start | bytes 2097152 | tf_op jit(solution)/shard_map/all_to_all | solution.py:44
  125.4 10.7 %all-to-all-done.4 = bf16[4,1024,128]{2,1,0:T(8,128)(2,1)S(1)} async-done(((bf16[4,1024,128]{2,1,0:T(8,128)(2,1)}), bf16[4,1024,128]{2,1,0:T(8,128)(2,1)S(1)}, u32[]{:S(2)}, u32[]{:S(2)}) %all-to-all-start.4) | async-done | bytes 1048608 | tf_op jit(solution)/shard_map/all_to_all | solution.py:44
  136.1 0.9 pool_parts.2
  137.7 2.0 gather_picks.3
  139.7 3.6 %all-to-all-start.5 = ((bf16[4,768,128]{2,1,0:T(8,128)(2,1)}), bf16[4,768,128]{2,1,0:T(8,128)(2,1)S(1)}, u32[]{:S(2)}, u32[]{:S(2)}) async-start(bf16[4,768,128]{2,1,0:T(8,128)(2,1)} %bitcast.23), calls=%async_computation.5 | async-start | bytes 1572864 | tf_op jit(solution)/shard_map/all_to_all | solution.py:44
  143.3 16.9 %collective-permute-start.6 = (bf16[1024,128]{1,0:T(8,128)(2,1)S(1)}, bf16[1024,128]{1,0:T(8,128)(2,1)S(1)}, u32[]{:S(2)}, u32[]{:S(2)}) collective-permute-start(bf16[1024,128]{1,0:T(8,128)(2,1)S(1)} %copy-done.4), channel_id=1, source_target_pairs={{0,16},{4,20},{8,24},{12,28},{16,32},{20,36},{24,40},{28,44},{32,4... | collective-permute-start | bytes 786440 | tf_op jit(solution)/shard_map/ppermute | solution.py:36
  160.3 2.1 collective-permute-start.7
  162.4 6.5 %attend_head1.1 = (bf16[512,256]{1,0:T(8,128)(2,1)}, bf16[512,256]{1,0:T(8,128)(2,1)}, bf16[4,4,4,2,32,128]{5,4,3,2,1,0:T(8,128)(2,1)}, f32[8,128]{1,0:T(8,128)S(1)}) custom-call(s32[3]{0:T(128)S(1)} %get-tuple-element.78.use_ref, f32[1]{0:T(128)} %get-tuple-element.80.sink_ref, ...), custom_call_target="tpu_custom_call", output_to_operand_aliasing={{0}: (6, {}), {1}: (7, {})} | custom-call | flops 2684354560 | bytes 8388608 | tf_op jit(solution)/shard_map/attend_head1/pallas_call | solution.py:131
  168.9 6.8 %collective-permute-done.6 = bf16[1024,128]{1,0:T(8,128)(2,1)S(1)} collective-permute-done((bf16[1024,128]{1,0:T(8,128)(2,1)S(1)}, bf16[1024,128]{1,0:T(8,128)(2,1)S(1)}, u32[]{:S(2)}, u32[]{:S(2)}) %collective-permute-start.6) | collective-permute-done | bytes 262176 | tf_op jit(solution)/shard_map/ppermute | solution.py:36
  175.7 0.7 copy-done.5
  176.4 4.8 %all-to-all-start.6 = ((bf16[4,1024,128]{2,1,0:T(8,128)(2,1)}), bf16[4,1024,128]{2,1,0:T(8,128)(2,1)S(1)}, u32[]{:S(2)}, u32[]{:S(2)}) async-start(bf16[4,1024,128]{2,1,0:T(8,128)(2,1)} %bitcast.27), calls=%async_computation.6 | async-start | bytes 2097152 | tf_op jit(solution)/shard_map/all_to_all | solution.py:44
  181.3 8.3 %collective-permute-start.8 = (bf16[1024,128]{1,0:T(8,128)(2,1)S(1)}, bf16[1024,128]{1,0:T(8,128)(2,1)S(1)}, u32[]{:S(2)}, u32[]{:S(2)}) collective-permute-start(bf16[1024,128]{1,0:T(8,128)(2,1)S(1)} %add_convert_fusion.3), channel_id=1, source_target_pairs={{0,16},{4,20},{8,24},{12,28},{16,32},{20,36},{24,40},{28,44},{32,4... | collective-permute-start | bytes 786440 | tf_op jit(solution)/shard_map/ppermute | solution.py:36
  190.6 1.5 maximum_dynamic-update-slice_fusion
  192.1 12.8 %psum.7 = f32[32]{0:T(128)S(1)} all-reduce(f32[32]{0:T(128)S(1)} %maximum_dynamic-update-slice_fusion), channel_id=1, replica_groups=mesh['dp'=2,'ctx'=64,'head'=4] {'dp','head'}, use_global_device_ids=true, to_apply=%region_5.6 | all-reduce | flops 32 | bytes 256 | tf_op jit(solution)/shard_map/psum | solution.py:298
  205.0 0.9 pool_parts.3
  205.9 1.9 collective-permute-start.10
  207.9 7.8 %collective-permute-start.9 = (bf16[1032,128]{1,0:T(8,128)(2,1)S(1)}, bf16[1032,128]{1,0:T(8,128)(2,1)S(1)}, u32[]{:S(2)}, u32[]{:S(2)}) collective-permute-start(bf16[1032,128]{1,0:T(8,128)(2,1)S(1)} %get-tuple-element.66), channel_id=1, source_target_pairs={{0,16},{4,20},{8,24},{12,28},{16,32},{20,36},{24,40},{28,44},{32,4... | collective-permute-start | bytes 792584 | tf_op jit(solution)/shard_map/ppermute | solution.py:36
  215.7 11.4 %collective-permute-done.10 = bf16[1032,128]{1,0:T(8,128)(2,1)S(1)} collective-permute-done((bf16[1032,128]{1,0:T(8,128)(2,1)S(1)}, bf16[1032,128]{1,0:T(8,128)(2,1)S(1)}, u32[]{:S(2)}, u32[]{:S(2)}) %collective-permute-start.10) | collective-permute-done | bytes 264224 | tf_op jit(solution)/shard_map/ppermute | solution.py:36
  227.2 2.9 %collective-permute-start.11 = (bf16[1032,128]{1,0:T(8,128)(2,1)S(1)}, bf16[1032,128]{1,0:T(8,128)(2,1)S(1)}, u32[]{:S(2)}, u32[]{:S(2)}) collective-permute-start(bf16[1032,128]{1,0:T(8,128)(2,1)S(1)} %pad_maximum_fusion.2), channel_id=1, source_target_pairs={{0,48},{4,52},{8,56},{12,60},{16,0},{20,4},{24,8},{28,12},{32,16},... | collective-permute-start | bytes 792584 | tf_op jit(solution)/shard_map/ppermute | solution.py:36
  230.3 5.4 %collective-permute-done.9 = bf16[1032,128]{1,0:T(8,128)(2,1)S(1)} collective-permute-done((bf16[1032,128]{1,0:T(8,128)(2,1)S(1)}, bf16[1032,128]{1,0:T(8,128)(2,1)S(1)}, u32[]{:S(2)}, u32[]{:S(2)}) %collective-permute-start.9) | collective-permute-done | bytes 264224 | tf_op jit(solution)/shard_map/ppermute | solution.py:36
  235.7 7.8 %collective-permute-done.11 = bf16[1032,128]{1,0:T(8,128)(2,1)S(1)} collective-permute-done((bf16[1032,128]{1,0:T(8,128)(2,1)S(1)}, bf16[1032,128]{1,0:T(8,128)(2,1)S(1)}, u32[]{:S(2)}, u32[]{:S(2)}) %collective-permute-start.11) | collective-permute-done | bytes 264224 | tf_op jit(solution)/shard_map/ppermute | solution.py:36
  243.7 36.3 %all_to_all.40 = bf16[16,136,128]{2,1,0:T(8,128)(2,1)S(1)} all-to-all(bf16[16,136,128]{2,1,0:T(8,128)(2,1)S(1)} %pad_maximum_fusion), channel_id=1, replica_groups={{0,4,8,12,64,68,72,76,128,132,136,140,192,196,200,204},{16,20,24,28,80,..., dimensions={0} | all-to-all | bytes 1114112 | tf_op jit(solution)/shard_map/all_to_all | solution.py:40
  281.0 0.9 reshape_squeeze.15
  282.5 0.9 reshape_squeeze.14
  (69 shorter events, 6.1 us)
Async XLA Ops:
  0.6 38.9 %copy-start = (s32[1,16,8,3]{1,2,3,0:T(8,128)S(1)}, s32[1,16,8,3]{1,2,3,0:T(8,128)}, u32[]{:S(2)}) copy-start(s32[1,16,8,3]{1,2,3,0:T(8,128)} %param.11) | copy-start | bytes 4612
  3.6 9.5 %copy-start.7 = (s32[16]{0:T(128)S(1)}, s32[16]{0:T(128)}, u32[]{:S(2)}) copy-start(s32[16]{0:T(128)} %param.12) | copy-start | bytes 196
  4.6 25.0 %all-to-all-start = ((bf16[16,128,128]{2,1,0:T(8,128)(2,1)}), bf16[16,128,128]{2,1,0:T(8,128)(2,1)S(1)}, u32[]{:S(2)}, u32[]{:S(2)}) async-start(bf16[16,128,128]{2,1,0:T(8,128)(2,1)} %bitcast.8), calls=%async_computation | async-start | bytes 1048576 | tf_op jit(solution)/shard_map/all_to_all | solution.py:40
  30.4 32.5 %collective-permute-start = (bf16[4,256,128]{2,1,0:T(8,128)(2,1)}, bf16[4,256,128]{2,1,0:T(8,128)(2,1)S(1)}, u32[]{:S(2)}, u32[]{:S(2)}) collective-permute-start(bf16[4,256,128]{2,1,0:T(8,128)(2,1)} %bitcast.11.refs_0_), channel_id=1, source_target_pairs={{0,16},{4,20},{8,24},{12,28},{16,32},{20,36},{24,40},{28,44},{32,4... | collective-permute-start | bytes 786440 | tf_op jit(solution)/shard_map/ppermute | solution.py:36
  40.0 32.8 %all-to-all-start.1 = ((bf16[4,256,128]{2,1,0:T(8,128)(2,1)}), bf16[4,256,128]{2,1,0:T(8,128)(2,1)S(1)}, u32[]{:S(2)}, u32[]{:S(2)}) async-start(bf16[4,256,128]{2,1,0:T(8,128)(2,1)} %bitcast.11.refs_0_), calls=%async_computation.1 | async-start | bytes 524288 | tf_op jit(solution)/shard_map/all_to_all | solution.py:44
  43.4 47.7 %collective-permute-start.2 = (bf16[4,256,128]{2,1,0:T(8,128)(2,1)}, bf16[4,256,128]{2,1,0:T(8,128)(2,1)S(1)}, u32[]{:S(2)}, u32[]{:S(2)}) collective-permute-start(bf16[4,256,128]{2,1,0:T(8,128)(2,1)} %bitcast.11.refs_0_), channel_id=1, source_target_pairs={{0,48},{4,52},{8,56},{12,60},{16,0},{20,4},{24,8},{28,12},{32,16},... | collective-permute-start | bytes 786440 | tf_op jit(solution)/shard_map/ppermute | solution.py:36
  63.0 25.8 %collective-permute-start.1 = (bf16[4,256,128]{2,1,0:T(8,128)(2,1)}, bf16[4,256,128]{2,1,0:T(8,128)(2,1)S(1)}, u32[]{:S(2)}, u32[]{:S(2)}) collective-permute-start(bf16[4,256,128]{2,1,0:T(8,128)(2,1)} %bitcast.13.refs_0_), channel_id=1, source_target_pairs={{0,48},{4,52},{8,56},{12,60},{16,0},{20,4},{24,8},{28,12},{32,16},... | collective-permute-start | bytes 786440 | tf_op jit(solution)/shard_map/ppermute | solution.py:36
  69.8 21.3 %collective-permute-start.3 = (bf16[4,256,128]{2,1,0:T(8,128)(2,1)S(1)}, bf16[4,256,128]{2,1,0:T(8,128)(2,1)S(1)}, u32[]{:S(2)}, u32[]{:S(2)}) collective-permute-start(bf16[4,256,128]{2,1,0:T(8,128)(2,1)S(1)} %collective-permute-done.refs_3_), channel_id=1, source_target_pairs={{0,16},{4,20},{8,24},{12,28},{16,32},{20,36},{24,40},{28,44},{32,4... | collective-permute-start | bytes 786440 | tf_op jit(solution)/shard_map/ppermute | solution.py:36
  72.7 10.1 %all-to-all-start.2 = ((bf16[4,256,128]{2,1,0:T(8,128)(2,1)}), bf16[4,256,128]{2,1,0:T(8,128)(2,1)S(1)}, u32[]{:S(2)}, u32[]{:S(2)}) async-start(bf16[4,256,128]{2,1,0:T(8,128)(2,1)} %bitcast.13.refs_0_), calls=%async_computation.2 | async-start | bytes 524288 | tf_op jit(solution)/shard_map/all_to_all | solution.py:44
  93.0 3.7 %copy-start.8 = (f32[8]{0:T(128)S(1)}, f32[8]{0:T(128)}, u32[]{:S(2)}) copy-start(f32[8]{0:T(128)} %param.13) | copy-start | bytes 100
  93.0 16.3 %copy-start.1 = (bf16[1,1,1,512,256]{4,3,2,1,0:T(8,128)(2,1)S(1)}, bf16[1,1,1,512,256]{4,3,2,1,0:T(8,128)(2,1)}, u32[]{:S(2)}) copy-start(bf16[1,1,1,512,256]{4,3,2,1,0:T(8,128)(2,1)} %param.7) | copy-start | bytes 786436
  93.0 16.3 %copy-start.2 = (bf16[1,1,1,512,256]{4,3,2,1,0:T(8,128)(2,1)S(1)}, bf16[1,1,1,512,256]{4,3,2,1,0:T(8,128)(2,1)}, u32[]{:S(2)}) copy-start(bf16[1,1,1,512,256]{4,3,2,1,0:T(8,128)(2,1)} %param.10) | copy-start | bytes 786436
  93.0 16.3 %all-to-all-start.3 = ((bf16[4,768,128]{2,1,0:T(8,128)(2,1)}), bf16[4,768,128]{2,1,0:T(8,128)(2,1)S(1)}, u32[]{:S(2)}, u32[]{:S(2)}) async-start(bf16[4,768,128]{2,1,0:T(8,128)(2,1)} %bitcast.19), calls=%async_computation.3 | async-start | bytes 1572864 | tf_op jit(solution)/shard_map/all_to_all | solution.py:44
  96.9 23.2 %collective-permute-start.4 = (bf16[4,256,128]{2,1,0:T(8,128)(2,1)}, bf16[4,256,128]{2,1,0:T(8,128)(2,1)S(1)}, u32[]{:S(2)}, u32[]{:S(2)}) collective-permute-start(bf16[4,256,128]{2,1,0:T(8,128)(2,1)} %bitcast.13.refs_0_), channel_id=1, source_target_pairs={{0,16},{4,20},{8,24},{12,28},{16,32},{20,36},{24,40},{28,44},{32,4... | collective-permute-start | bytes 786440 | tf_op jit(solution)/shard_map/ppermute | solution.py:36
  101.3 18.9 %collective-permute-start.5 = (bf16[4,256,128]{2,1,0:T(8,128)(2,1)S(1)}, bf16[4,256,128]{2,1,0:T(8,128)(2,1)S(1)}, u32[]{:S(2)}, u32[]{:S(2)}) collective-permute-start(bf16[4,256,128]{2,1,0:T(8,128)(2,1)S(1)} %collective-permute-done.1.refs_1_), channel_id=1, source_target_pairs={{0,48},{4,52},{8,56},{12,60},{16,0},{20,4},{24,8},{28,12},{32,16},... | collective-permute-start | bytes 786440 | tf_op jit(solution)/shard_map/ppermute | solution.py:36
  120.1 16.0 %all-to-all-start.4 = ((bf16[4,1024,128]{2,1,0:T(8,128)(2,1)}), bf16[4,1024,128]{2,1,0:T(8,128)(2,1)S(1)}, u32[]{:S(2)}, u32[]{:S(2)}) async-start(bf16[4,1024,128]{2,1,0:T(8,128)(2,1)} %bitcast.21), calls=%async_computation.4 | async-start | bytes 2097152 | tf_op jit(solution)/shard_map/all_to_all | solution.py:44
  137.0 0.7 copy-start.3
  139.7 3.6 %copy-start.4 = (bf16[1024,128]{1,0:T(8,128)(2,1)S(1)}, bf16[1024,128]{1,0:T(8,128)(2,1)}, u32[]{:S(2)}) copy-start(bf16[1024,128]{1,0:T(8,128)(2,1)} %copy-done.3) | copy-start | bytes 786436
  139.7 22.7 %all-to-all-start.5 = ((bf16[4,768,128]{2,1,0:T(8,128)(2,1)}), bf16[4,768,128]{2,1,0:T(8,128)(2,1)S(1)}, u32[]{:S(2)}, u32[]{:S(2)}) async-start(bf16[4,768,128]{2,1,0:T(8,128)(2,1)} %bitcast.23), calls=%async_computation.5 | async-start | bytes 1572864 | tf_op jit(solution)/shard_map/all_to_all | solution.py:44
  143.3 32.3 %collective-permute-start.6 = (bf16[1024,128]{1,0:T(8,128)(2,1)S(1)}, bf16[1024,128]{1,0:T(8,128)(2,1)S(1)}, u32[]{:S(2)}, u32[]{:S(2)}) collective-permute-start(bf16[1024,128]{1,0:T(8,128)(2,1)S(1)} %copy-done.4), channel_id=1, source_target_pairs={{0,16},{4,20},{8,24},{12,28},{16,32},{20,36},{24,40},{28,44},{32,4... | collective-permute-start | bytes 786440 | tf_op jit(solution)/shard_map/ppermute | solution.py:36
  160.3 15.4 %collective-permute-start.7 = (bf16[1024,128]{1,0:T(8,128)(2,1)S(1)}, bf16[1024,128]{1,0:T(8,128)(2,1)S(1)}, u32[]{:S(2)}, u32[]{:S(2)}) collective-permute-start(bf16[1024,128]{1,0:T(8,128)(2,1)S(1)} %get-tuple-element.48), channel_id=1, source_target_pairs={{0,48},{4,52},{8,56},{12,60},{16,0},{20,4},{24,8},{28,12},{32,16},... | collective-permute-start | bytes 786440 | tf_op jit(solution)/shard_map/ppermute | solution.py:36
  175.7 0.7 copy-start.5
  176.4 28.6 %all-to-all-start.6 = ((bf16[4,1024,128]{2,1,0:T(8,128)(2,1)}), bf16[4,1024,128]{2,1,0:T(8,128)(2,1)S(1)}, u32[]{:S(2)}, u32[]{:S(2)}) async-start(bf16[4,1024,128]{2,1,0:T(8,128)(2,1)} %bitcast.27), calls=%async_computation.6 | async-start | bytes 2097152 | tf_op jit(solution)/shard_map/all_to_all | solution.py:44
  181.3 23.7 %collective-permute-start.8 = (bf16[1024,128]{1,0:T(8,128)(2,1)S(1)}, bf16[1024,128]{1,0:T(8,128)(2,1)S(1)}, u32[]{:S(2)}, u32[]{:S(2)}) collective-permute-start(bf16[1024,128]{1,0:T(8,128)(2,1)S(1)} %add_convert_fusion.3), channel_id=1, source_target_pairs={{0,16},{4,20},{8,24},{12,28},{16,32},{20,36},{24,40},{28,44},{32,4... | collective-permute-start | bytes 786440 | tf_op jit(solution)/shard_map/ppermute | solution.py:36
  205.0 25.1 %copy-start.6 = (bf16[1024,128]{1,0:T(8,128)(2,1)S(1)}, bf16[1024,128]{1,0:T(8,128)(2,1)}, u32[]{:S(2)}) copy-start(bf16[1024,128]{1,0:T(8,128)(2,1)} %copy-done.5) | copy-start | bytes 786436
  205.9 21.2 %collective-permute-start.10 = (bf16[1032,128]{1,0:T(8,128)(2,1)S(1)}, bf16[1032,128]{1,0:T(8,128)(2,1)S(1)}, u32[]{:S(2)}, u32[]{:S(2)}) collective-permute-start(bf16[1032,128]{1,0:T(8,128)(2,1)S(1)} %get-tuple-element.68), channel_id=1, source_target_pairs={{0,48},{4,52},{8,56},{12,60},{16,0},{20,4},{24,8},{28,12},{32,16},... | collective-permute-start | bytes 792584 | tf_op jit(solution)/shard_map/ppermute | solution.py:36
  207.9 27.8 %collective-permute-start.9 = (bf16[1032,128]{1,0:T(8,128)(2,1)S(1)}, bf16[1032,128]{1,0:T(8,128)(2,1)S(1)}, u32[]{:S(2)}, u32[]{:S(2)}) collective-permute-start(bf16[1032,128]{1,0:T(8,128)(2,1)S(1)} %get-tuple-element.66), channel_id=1, source_target_pairs={{0,16},{4,20},{8,24},{12,28},{16,32},{20,36},{24,40},{28,44},{32,4... | collective-permute-start | bytes 792584 | tf_op jit(solution)/shard_map/ppermute | solution.py:36
  227.2 16.2 %collective-permute-start.11 = (bf16[1032,128]{1,0:T(8,128)(2,1)S(1)}, bf16[1032,128]{1,0:T(8,128)(2,1)S(1)}, u32[]{:S(2)}, u32[]{:S(2)}) collective-permute-start(bf16[1032,128]{1,0:T(8,128)(2,1)S(1)} %pad_maximum_fusion.2), channel_id=1, source_target_pairs={{0,48},{4,52},{8,56},{12,60},{16,0},{20,4},{24,8},{28,12},{32,16},... | collective-permute-start | bytes 792584 | tf_op jit(solution)/shard_map/ppermute | solution.py:36

commit v8 on v7

--- a/solution.py
+++ b/solution.py
@@ -25,6 +25,7 @@
 NEG = -1e30
 
 SPREAD_GROUPS = [[x * ZS + g * SPB + r for x in range(XS) for r in range(SPB)] for g in range(ZG)]
+PART_GROUPS = [[s * SPB + r for r in range(SPB)] for s in range(XS * ZG)]
 X_GROUPS = [[x * ZS + z for x in range(XS)] for z in range(ZS)]
 
 
@@ -53,6 +54,16 @@
     )
 
 
+def split_terms(left):
+    lane = lax.broadcasted_iota(jnp.int32, left.shape, 1)
+    terms = jnp.zeros(left.shape, jnp.float32)
+    for term in range(3):
+        rounded = left.astype(jnp.bfloat16).astype(jnp.float32)
+        terms = jnp.where(lane // HEADS == term, rounded, terms)
+        left = left - rounded
+    return terms.astype(jnp.bfloat16)
+
+
 def attend_kernel(use_ref, sink_ref, q_ref, g_ref, own_ref, pick_ref, *rest):
     att_ref, dq_ref, part_ref, sink_out, s_ref = rest[-5:]
     scale = 1.0 / math.sqrt(DH)
@@ -65,6 +76,12 @@
         else:
             got = pick_ref[:, kind - 1, :, which]
         return got.reshape(BLOCK, DH)
+
+    def put(kind, which, grads):
+        got = grads.astype(jnp.bfloat16).reshape(XS, SPB, FRAG, DH)
+        for i in range(SPB):
+            at = kind * ROWS + (i * 2 + which) * FRAG
+            part_ref[:, at : at + FRAG] = got[:, i]
 
     sink = sink_ref[0] * LOG2E
     top = jnp.full((1, BLOCK), sink, jnp.float32)
@@ -94,21 +111,28 @@
         s_ref[kind] = prob
         weights = prob.astype(jnp.bfloat16)
         att_t = att_t + dot(tile(kind, 1), weights, 0, 0)
-        dv = dot(weights, grad, 1, 0).astype(jnp.bfloat16)
-        part_ref[:, kind, :, 1] = dv.reshape(XS, SPB, FRAG, DH)
+        put(kind, 1, dot(weights, grad, 1, 0))
     att = att_t.T.astype(jnp.bfloat16)
     att_ref[...] = att
     both = grad.astype(jnp.float32) * att.astype(jnp.float32)
     delta = jnp.sum(both.T, axis=0, keepdims=True)
     sink_rows = sink_part * inv * delta
-    sink_out[...] = jnp.broadcast_to(-jnp.sum(sink_rows, axis=1, keepdims=True), (8, 128))
+    sink_sum = jnp.broadcast_to(-jnp.sum(sink_rows, axis=1, keepdims=True), (EXTRA, 128))
+    lane = lax.broadcasted_iota(jnp.int32, sink_sum.shape, 1)
+    sink_sum = jnp.where(lane % HEADS == use_ref[TOPK], sink_sum, 0.0)
+    if len(rest) > 5:
+        sink_sum = sink_sum + rest[2][...]
+    sink_out[...] = sink_sum
+    if part_ref.shape[1] > KINDS * ROWS:
+        part_ref[:, KINDS * ROWS :] = jnp.broadcast_to(
+            split_terms(sink_sum)[None], (XS, EXTRA, 128)
+        )
     dq_t = jnp.zeros((DH, BLOCK), jnp.float32)
     for kind in range(KINDS):
         dprob = dot(tile(kind, 1), grad, 1, 1)
         dscore = (s_ref[kind] * (dprob - delta) * scale).astype(jnp.bfloat16)
         dq_t = dq_t + dot(tile(kind, 0), dscore, 0, 0)
-        dk = dot(dscore, query, 1, 0).astype(jnp.bfloat16)
-        part_ref[:, kind, :, 0] = dk.reshape(XS, SPB, FRAG, DH)
+        put(kind, 0, dot(dscore, query, 1, 0))
     dq_ref[...] = dq_t.T.astype(jnp.bfloat16)
 
 
@@ -126,8 +150,9 @@
         pl.BlockSpec(own.shape, lambda i: (0,) * own.ndim),
         pl.BlockSpec(picks.shape, lambda i: (0,) * picks.ndim),
     ]
-    in_specs += [pl.BlockSpec(memory_space=pl.ANY)] * len(earlier)
-    part_shape = (XS, KINDS) + tile_dims
+    in_specs += [pl.BlockSpec(memory_space=pl.ANY)] * len(earlier[:2])
+    in_specs += [pl.BlockSpec((EXTRA, 128), lambda i: (0, 0))] * len(earlier[2:])
+    part_shape = (XS, KINDS * ROWS + EXTRA * len(earlier[2:]), DH)
     return pl.pallas_call(
         attend_kernel,
         name="attend_head%d" % head,
@@ -146,7 +171,7 @@
             jax.ShapeDtypeStruct((8, 128), jnp.float32),
         ),
         scratch_shapes=[pltpu.VMEM((KINDS, BLOCK, BLOCK), jnp.float32)],
-        input_output_aliases={6 + n: n for n in range(len(earlier))},
+        input_output_aliases={6 + n: n for n in range(len(earlier[:2]))},
         compiler_params=pltpu.CompilerParams(vmem_limit_bytes=40 << 20),
         cost_estimate=pl.CostEstimate(
             flops=20 * KINDS * BLOCK * BLOCK * DH, transcendentals=0, bytes_accessed=8 << 20
@@ -178,44 +203,42 @@
 
 def pool_kernel(index_ref, part_ref, *refs):
     acc_ref = refs[-1]
-    out_refs = refs[-1 - ZG : -1]
+    out_refs = refs[:ZG]
     for x in range(XS):
-        acc_ref[x] = part_ref[x, 0].astype(jnp.float32)
+        acc_ref[x] = part_ref[x, :ROWS].astype(jnp.float32)
     for slot in range(XS, ZG * XS):
         acc_ref[slot] = jnp.zeros((ROWS, DH), jnp.float32)
     for x in range(XS):
         for pick in range(TOPK):
             slot = index_ref[x * TOPK + pick]
-            acc_ref[slot] = acc_ref[slot] + part_ref[x, pick + 1].astype(jnp.float32)
+            at = (pick + 1) * ROWS
+            acc_ref[slot] = acc_ref[slot] + part_ref[x, at : at + ROWS].astype(jnp.float32)
     for slot in range(ZG * XS):
         at = slot % XS * ROWS
         out_refs[slot // XS][at : at + ROWS] = acc_ref[slot].astype(jnp.bfloat16)
-    if len(refs) > ZG + 1:
-        left = refs[0][...]
-        lane = lax.broadcasted_iota(jnp.int32, left.shape, 1)
-        terms = jnp.zeros(left.shape, jnp.float32)
-        for term in range(3):
-            rounded = left.astype(jnp.bfloat16).astype(jnp.float32)
-            terms = jnp.where(lane // HEADS == term, rounded, terms)
-            left = left - rounded
+    if part_ref.shape[1] > KINDS * ROWS:
+        terms = part_ref[0, KINDS * ROWS :].astype(jnp.float32)
+        for x in range(1, XS):
+            terms = terms + part_ref[x, KINDS * ROWS :].astype(jnp.float32)
+        total = terms
+        for term in range(1, 4):
+            total = total + pltpu.roll(terms, term * HEADS, 1)
         for ref in out_refs:
-            ref[XS * ROWS :] = terms.astype(jnp.bfloat16)
-
-
-def pool_parts(index, parts, sink_sum=None):
-    extra = [] if sink_sum is None else [jnp.tile(sink_sum[None], (EXTRA, 128 // HEADS))]
-    shape = (XS * ROWS + EXTRA * len(extra), DH)
+            ref[XS * ROWS :] = split_terms(total)
+
+
+def pool_parts(index, parts):
+    shape = (XS * ROWS + parts.shape[1] - KINDS * ROWS, DH)
     return pl.pallas_call(
         pool_kernel,
         name="pool_parts",
-        in_specs=[pl.BlockSpec(memory_space=pltpu.SMEM)]
-        + [pl.BlockSpec(memory_space=pltpu.VMEM)] * (1 + len(extra)),
+        in_specs=[pl.BlockSpec(memory_space=pltpu.SMEM), pl.BlockSpec(memory_space=pltpu.VMEM)],
         out_specs=tuple(pl.BlockSpec(memory_space=pltpu.VMEM) for _ in range(ZG)),
         out_shape=tuple(jax.ShapeDtypeStruct(shape, jnp.bfloat16) for _ in range(ZG)),
         scratch_shapes=[pltpu.VMEM((ZG * XS, ROWS, DH), jnp.float32)],
         compiler_params=pltpu.CompilerParams(vmem_limit_bytes=16 << 20),
         cost_estimate=pl.CostEstimate(flops=1 << 20, transcendentals=0, bytes_accessed=4 << 20),
-    )(index, parts, *extra)
+    )(index, parts)
 
 
 def add_rounded(*arrs):
@@ -272,31 +295,24 @@
     far[1] = shift_groups(above[1], -1)
     ready, above[1], own = lax.optimization_barrier((held[0], above[1], own))
     sources = [(ready, above[0], far[0], below[0]), None]
+    start = lax.axis_index("head") * (SPB * HPD) + position * HPD
     earlier = ()
-    sink_heads = []
     pools = []
     for h in range(HPD):
         picks = swap_x(gather_picks(index[h], sources[h]).reshape(XS, TOPK * ROWS, DH))
         att, dq, part, sink_sum = attend(
-            h, use[h], sink_mine[h : h + 1], query_rows, grad_rows, own[h], picks, earlier
+            h, jnp.append(use[h], start + h), sink_mine[h : h + 1], query_rows, grad_rows, own[h], picks, earlier
         )
-        earlier = (att, dq)
-        sink_heads.append(sink_sum[0, :1])
-        sink_sum = None
+        earlier = (att, dq, sink_sum)
         if h == 0:
             part, below[1], far[1] = lax.optimization_barrier((part, below[1], far[1]))
         else:
             part, up_far, down_near = lax.optimization_barrier((part, up_far, down_near))
-        back = swap_x(part.reshape(XS, KINDS * ROWS, DH)).reshape(XS, KINDS, ROWS, DH)
+        back = swap_x(part)
         if h > 0:
             up_first = shift_groups(add_rounded(pools[0][1], up_far), 1)
             back, up_first = lax.optimization_barrier((back, up_first))
-            start = lax.axis_index("head") * (SPB * HPD) + position * HPD
-            sink_sum = lax.dynamic_update_slice(
-                jnp.zeros((HEADS,), jnp.float32), jnp.concatenate(sink_heads), (start,)
-            )
-            sink_sum = lax.psum(sink_sum, ("dp", "head"))
-        pools.append(pool_parts(index[h], back, sink_sum))
+        pools.append(pool_parts(index[h], back))
         if h == 0:
             up_far = shift_groups(pools[0][2], 1)
             down_near = shift_groups(pools[0][3], -1)
@@ -309,17 +325,12 @@
     down_last = shift_groups(onward, -1)
     first = add_rounded(pools[0][0], up_first, down_near)
     second = add_rounded(pools[1][0][:main], up_near[:main], down_last[:main])
-    terms = [arr[main : main + 1] for arr in (pools[1][0], up_near, down_far, down_last)]
-    terms = jnp.concatenate(terms + [jnp.zeros((EXTRA - ZG, DH), jnp.bfloat16)])
-    pooled = jnp.concatenate(
-        [arr.reshape(XS * SPB, 2 * FRAG, DH) for arr in (first, second)]
-        + [jnp.broadcast_to(terms[None], (XS * SPB, EXTRA, DH))],
-        axis=1,
-    )
-    homed = swap_spread(pooled)
-    terms = homed[:, HPD * 2 * FRAG :, : 3 * HEADS].astype(jnp.float32)
-    grad_sink = jnp.sum(terms.reshape(-1, HEADS), axis=0)
-    homed = homed[:, : HPD * 2 * FRAG]
+    terms = jnp.stack([arr[main] for arr in (pools[1][0], up_near, down_far, down_last)])
+    terms = jnp.sum(terms[:, : 3 * HEADS].astype(jnp.float32).reshape(-1, HEADS), axis=0)
+    grad_sink = lax.psum(terms, "ctx", axis_index_groups=PART_GROUPS)
+    grad_sink = lax.psum(grad_sink, ("dp", "head"))
+    pooled = jnp.stack([arr.reshape(XS * SPB, 2 * FRAG, DH) for arr in (first, second)], axis=1)
+    homed = swap_spread(pooled.reshape(XS * SPB, HPD * 2 * FRAG, DH))
     totals = jnp.transpose(homed.reshape(XS, SPB, HPD, 2, FRAG, DH), (3, 0, 4, 1, 2, 5))
     grad_key = totals[0].reshape(key.shape)
     grad_value = totals[1].reshape(value.shape)

time: 288 us -> 289 us (level)
  blocking collectives: 49.1 us -> 32.7 us
  starting transfers between devices: 104 us -> 120 us
  waiting for transfers between devices: 95.8 us -> 102 us
    all_to_all x1 -> x0, blocking collectives: 36.3 us -> none  [swap_spread(): lax.all_to_all(arr, 'ctx', 0, 0, axis_index_groups=SPREAD_GROUPS, tiled=T...]
    psum x1 -> x2, blocking collectives: 12.8 us -> 32.7 us  [the longest x1 20.5 us: body(): grad_sink = lax.psum(grad_sink, ('dp', 'head'))]
    all_to_all x1 -> x2, starting transfers between devices: 8.47 us -> 21.5 us  [swap_spread(): lax.all_to_all(arr, 'ctx', 0, 0, axis_index_groups=SPREAD_GROUPS, tiled=T...]
    ppermute x12, waiting for transfers between devices: 60.6 us -> 67.2 us  [shift_groups(): return lax.ppermute(arr, 'ctx', pairs)]
    all_to_all x1 -> x2, waiting for transfers between devices: 16.1 us -> 16.1 us  [swap_spread(): lax.all_to_all(arr, 'ctx', 0, 0, axis_index_groups=SPREAD_GROUPS, tiled=T...]
  transfers between devices with their start and end apart: 19 -> 20, of which waited for: 12 -> 12; matrix products, arithmetic and copies ran while one was open for 2% -> 1% of each run, Pallas kernels for 5% -> 5%
where the time goes in v8:
time: 289 us; the launch traced here: 286 us
  starting transfers between devices  120 us (42%)
  waiting for transfers between devices  102 us (35%)
  blocking collectives  32.7 us (11%)
  Pallas kernels  18.7 us (6%)
  local copies, waits for them, and re-layouts  8.83 us (3%)
  other arithmetic  3.14 us (1%)
    ppermute x12, starting transfers between devices, shift_groups(): return lax.ppermute(arr, 'ctx', pairs)  74.2 us
    ppermute x12, waiting for transfers between devices, shift_groups(): return lax.ppermute(arr, 'ctx', pairs)  67.2 us
    all_to_all x6, starting transfers between devices, swap_x(): lax.all_to_all(arr, 'ctx', 0, 0, axis_index_groups=X_GROUPS, tiled=True)  23.8 us
    all_to_all x2, starting transfers between devices, swap_spread(): lax.all_to_all(arr, 'ctx', 0, 0, axis_index_groups=SPREAD_GROUPS, tiled=T...  21.5 us
    psum x1, blocking collectives, body(): grad_sink = lax.psum(grad_sink, ('dp', 'head'))  20.5 us
    all_to_all x6, waiting for transfers between devices, swap_x(): lax.all_to_all(arr, 'ctx', 0, 0, axis_index_groups=X_GROUPS, tiled=True)  19.1 us
    all_to_all x2, waiting for transfers between devices, swap_spread(): lax.all_to_all(arr, 'ctx', 0, 0, axis_index_groups=SPREAD_GROUPS, tiled=T...  16.1 us
    pallas_call x2, Pallas kernels, attend(): pl.pallas_call(attend_kernel, name='attend_head%d' % head, grid=(1,), in_...  13 us
  transfers between devices with their start and end apart: 20, of which 12 were waited for; matrix products, arithmetic and copies ran while one was open for 1% of the time, Pallas kernels for 5%

profile of v8, /device:TPU:24, one launch (start us, length us, event | category | flops | bytes accessed | tf_op | source)
XLA Modules:
  0.0 286.5 jit_solution(13225346769916145667)
XLA Ops:
  0.6 1.1 reshape.114
  1.8 1.1 reshape.115
  2.9 0.7 pad_maximum_fusion
  3.7 0.9 copy.28
  4.6 8.5 %all-to-all-start = ((bf16[16,128,128]{2,1,0:T(8,128)(2,1)}), bf16[16,128,128]{2,1,0:T(8,128)(2,1)S(1)}, u32[]{:S(2)}, u32[]{:S(2)}) async-start(bf16[16,128,128]{2,1,0:T(8,128)(2,1)} %bitcast.9), calls=%async_computation | async-start | bytes 1048576 | tf_op jit(solution)/shard_map/all_to_all | solution.py:41
  13.5 16.1 %all-to-all-done = bf16[16,128,128]{2,1,0:T(8,128)(2,1)S(1)} async-done(((bf16[16,128,128]{2,1,0:T(8,128)(2,1)}), bf16[16,128,128]{2,1,0:T(8,128)(2,1)S(1)}, u32[]{:S(2)}, u32[]{:S(2)}) %all-to-all-start) | async-done | bytes 524320 | tf_op jit(solution)/shard_map/all_to_all | solution.py:41
  29.6 0.8 fusion.10
  30.4 9.1 %collective-permute-start = (bf16[4,256,128]{2,1,0:T(8,128)(2,1)}, bf16[4,256,128]{2,1,0:T(8,128)(2,1)S(1)}, u32[]{:S(2)}, u32[]{:S(2)}) collective-permute-start(bf16[4,256,128]{2,1,0:T(8,128)(2,1)} %bitcast.12.refs_0_), channel_id=1, source_target_pairs={{0,16},{4,20},{8,24},{12,28},{16,32},{20,36},{24,40},{28,44},{32,4... | collective-permute-start | bytes 786440 | tf_op jit(solution)/shard_map/ppermute | solution.py:37
  40.0 3.4 %all-to-all-start.1 = ((bf16[4,256,128]{2,1,0:T(8,128)(2,1)}), bf16[4,256,128]{2,1,0:T(8,128)(2,1)S(1)}, u32[]{:S(2)}, u32[]{:S(2)}) async-start(bf16[4,256,128]{2,1,0:T(8,128)(2,1)} %bitcast.12.refs_0_), calls=%async_computation.1 | async-start | bytes 524288 | tf_op jit(solution)/shard_map/all_to_all | solution.py:45
  43.4 2.9 collective-permute-start.2
  46.3 16.7 %collective-permute-done.refs_3_ = bf16[4,256,128]{2,1,0:T(8,128)(2,1)S(1)} collective-permute-done((bf16[4,256,128]{2,1,0:T(8,128)(2,1)}, bf16[4,256,128]{2,1,0:T(8,128)(2,1)S(1)}, u32[]{:S(2)}, u32[]{:S(2)}) %collective-permute-start) | collective-permute-done | bytes 262176 | tf_op jit(solution)/shard_map/ppermute | solution.py:37
  62.9 6.9 %collective-permute-start.1 = (bf16[4,256,128]{2,1,0:T(8,128)(2,1)}, bf16[4,256,128]{2,1,0:T(8,128)(2,1)S(1)}, u32[]{:S(2)}, u32[]{:S(2)}) collective-permute-start(bf16[4,256,128]{2,1,0:T(8,128)(2,1)} %bitcast.14.refs_0_), channel_id=1, source_target_pairs={{0,48},{4,52},{8,56},{12,60},{16,0},{20,4},{24,8},{28,12},{32,16},... | collective-permute-start | bytes 786440 | tf_op jit(solution)/shard_map/ppermute | solution.py:37
  69.8 2.9 %collective-permute-start.3 = (bf16[4,256,128]{2,1,0:T(8,128)(2,1)S(1)}, bf16[4,256,128]{2,1,0:T(8,128)(2,1)S(1)}, u32[]{:S(2)}, u32[]{:S(2)}) collective-permute-start(bf16[4,256,128]{2,1,0:T(8,128)(2,1)S(1)} %collective-permute-done.refs_3_), channel_id=1, source_target_pairs={{0,16},{4,20},{8,24},{12,28},{16,32},{20,36},{24,40},{28,44},{32,4... | collective-permute-start | bytes 786440 | tf_op jit(solution)/shard_map/ppermute | solution.py:37
  72.8 3.4 %all-to-all-start.2 = ((bf16[4,256,128]{2,1,0:T(8,128)(2,1)}), bf16[4,256,128]{2,1,0:T(8,128)(2,1)S(1)}, u32[]{:S(2)}, u32[]{:S(2)}) async-start(bf16[4,256,128]{2,1,0:T(8,128)(2,1)} %bitcast.14.refs_0_), calls=%async_computation.2 | async-start | bytes 524288 | tf_op jit(solution)/shard_map/all_to_all | solution.py:45
  76.4 6.5 %all-to-all-done.2 = bf16[4,256,128]{2,1,0:T(8,128)(2,1)S(1)} async-done(((bf16[4,256,128]{2,1,0:T(8,128)(2,1)}), bf16[4,256,128]{2,1,0:T(8,128)(2,1)S(1)}, u32[]{:S(2)}, u32[]{:S(2)}) %all-to-all-start.2) | async-done | bytes 262176 | tf_op jit(solution)/shard_map/all_to_all | solution.py:45
  82.8 5.9 %collective-permute-done.1.refs_1_ = bf16[4,256,128]{2,1,0:T(8,128)(2,1)S(1)} collective-permute-done((bf16[4,256,128]{2,1,0:T(8,128)(2,1)}, bf16[4,256,128]{2,1,0:T(8,128)(2,1)S(1)}, u32[]{:S(2)}, u32[]{:S(2)}) %collective-permute-start.1) | collective-permute-done | bytes 262176 | tf_op jit(solution)/shard_map/ppermute | solution.py:37
  88.7 2.3 collective-permute-done.3.refs_2_
  91.0 2.0 gather_picks.2
  93.0 3.6 %all-to-all-start.3 = ((bf16[4,768,128]{2,1,0:T(8,128)(2,1)}), bf16[4,768,128]{2,1,0:T(8,128)(2,1)S(1)}, u32[]{:S(2)}, u32[]{:S(2)}) async-start(bf16[4,768,128]{2,1,0:T(8,128)(2,1)} %bitcast.21), calls=%async_computation.3 | async-start | bytes 1572864 | tf_op jit(solution)/shard_map/all_to_all | solution.py:45
  97.6 4.4 %collective-permute-start.4 = (bf16[4,256,128]{2,1,0:T(8,128)(2,1)}, bf16[4,256,128]{2,1,0:T(8,128)(2,1)S(1)}, u32[]{:S(2)}, u32[]{:S(2)}) collective-permute-start(bf16[4,256,128]{2,1,0:T(8,128)(2,1)} %bitcast.14.refs_0_), channel_id=1, source_target_pairs={{0,16},{4,20},{8,24},{12,28},{16,32},{20,36},{24,40},{28,44},{32,4... | collective-permute-start | bytes 786440 | tf_op jit(solution)/shard_map/ppermute | solution.py:37
  101.9 5.4 %collective-permute-start.5 = (bf16[4,256,128]{2,1,0:T(8,128)(2,1)S(1)}, bf16[4,256,128]{2,1,0:T(8,128)(2,1)S(1)}, u32[]{:S(2)}, u32[]{:S(2)}) collective-permute-start(bf16[4,256,128]{2,1,0:T(8,128)(2,1)S(1)} %collective-permute-done.1.refs_1_), channel_id=1, source_target_pairs={{0,48},{4,52},{8,56},{12,60},{16,0},{20,4},{24,8},{28,12},{32,16},... | collective-permute-start | bytes 786440 | tf_op jit(solution)/shard_map/ppermute | solution.py:37
  107.4 2.0 all-to-all-done.3
  109.4 6.5 %attend_head0.1 = (bf16[512,256]{1,0:T(8,128)(2,1)}, bf16[512,256]{1,0:T(8,128)(2,1)}, bf16[4,1024,128]{2,1,0:T(8,128)(2,1)}, f32[8,128]{1,0:T(8,128)S(1)}) custom-call(s32[4]{0:T(128)S(1)} %pad_add_fusion.1.use_ref, f32[1]{0:T(128)} %get-tuple-element.77.sink_ref, bf16[512,256]{1,0:T(8,128)(2,1)S(1)} %bitcast.62, bf16[512,256]{1,0:T(8,128)(2,1)S(1)} %bitcast.64, ...), custom_call_target="tpu_custom_call" | custom-call | flops 2684354560 | bytes 8388608 | tf_op jit(solution)/shard_map/attend_head0/pallas_call | solution.py:156
  115.8 4.9 %collective-permute-done.5.refs_2_ = bf16[4,256,128]{2,1,0:T(8,128)(2,1)S(1)} collective-permute-done((bf16[4,256,128]{2,1,0:T(8,128)(2,1)S(1)}, bf16[4,256,128]{2,1,0:T(8,128)(2,1)S(1)}, u32[]{:S(2)}, u32[]{:S(2)}) %collective-permute-start.5) | collective-permute-done | bytes 262176 | tf_op jit(solution)/shard_map/ppermute | solution.py:37
  120.8 5.1 %all-to-all-start.4 = ((bf16[4,1024,128]{2,1,0:T(8,128)(2,1)}), bf16[4,1024,128]{2,1,0:T(8,128)(2,1)S(1)}, u32[]{:S(2)}, u32[]{:S(2)}) async-start(bf16[4,1024,128]{2,1,0:T(8,128)(2,1)} %get-tuple-element.43), calls=%async_computation.4 | async-start | bytes 2097152 | tf_op jit(solution)/shard_map/all_to_all | solution.py:45
  126.1 10.7 %all-to-all-done.4.part_ref = bf16[4,1024,128]{2,1,0:T(8,128)(2,1)S(1)} async-done(((bf16[4,1024,128]{2,1,0:T(8,128)(2,1)}), bf16[4,1024,128]{2,1,0:T(8,128)(2,1)S(1)}, u32[]{:S(2)}, u32[]{:S(2)}) %all-to-all-start.4) | async-done | bytes 1048608 | tf_op jit(solution)/shard_map/all_to_all | solution.py:45
  136.8 0.9 pool_parts.2
  138.4 2.0 gather_picks.3
  140.4 3.6 %all-to-all-start.5 = ((bf16[4,768,128]{2,1,0:T(8,128)(2,1)}), bf16[4,768,128]{2,1,0:T(8,128)(2,1)S(1)}, u32[]{:S(2)}, u32[]{:S(2)}) async-start(bf16[4,768,128]{2,1,0:T(8,128)(2,1)} %bitcast.23), calls=%async_computation.5 | async-start | bytes 1572864 | tf_op jit(solution)/shard_map/all_to_all | solution.py:45
  144.0 16.3 %collective-permute-start.6 = (bf16[1024,128]{1,0:T(8,128)(2,1)S(1)}, bf16[1024,128]{1,0:T(8,128)(2,1)S(1)}, u32[]{:S(2)}, u32[]{:S(2)}) collective-permute-start(bf16[1024,128]{1,0:T(8,128)(2,1)S(1)} %copy-done.4), channel_id=1, source_target_pairs={{0,16},{4,20},{8,24},{12,28},{16,32},{20,36},{24,40},{28,44},{32,4... | collective-permute-start | bytes 786440 | tf_op jit(solution)/shard_map/ppermute | solution.py:37
  160.3 2.1 collective-permute-start.7
  162.5 6.5 %attend_head1.1 = (bf16[512,256]{1,0:T(8,128)(2,1)}, bf16[512,256]{1,0:T(8,128)(2,1)}, bf16[4,1032,128]{2,1,0:T(8,128)(2,1)}, f32[8,128]{1,0:T(8,128)}) custom-call(s32[4]{0:T(128)S(1)} %pad_add_fusion.use_ref, f32[1]{0:T(128)} %get-tuple-element.78.sink_ref, bf16[512,256]{1,0:T(8,128)(2,1)S(1)} %bitcast.63, ...), custom_call_target="tpu_custom_call", output_to_operand_aliasing={{0}: (6, {}), {1}: (7, {})} | custom-call | flops 2684354560 | bytes 8388608 | tf_op jit(solution)/shard_map/attend_head1/pallas_call | solution.py:156
  169.0 9.9 %collective-permute-done.6 = bf16[1024,128]{1,0:T(8,128)(2,1)S(1)} collective-permute-done((bf16[1024,128]{1,0:T(8,128)(2,1)S(1)}, bf16[1024,128]{1,0:T(8,128)(2,1)S(1)}, u32[]{:S(2)}, u32[]{:S(2)}) %collective-permute-start.6) | collective-permute-done | bytes 262176 | tf_op jit(solution)/shard_map/ppermute | solution.py:37
  179.6 4.7 %all-to-all-start.6 = ((bf16[4,1032,128]{2,1,0:T(8,128)(2,1)}), bf16[4,1032,128]{2,1,0:T(8,128)(2,1)S(1)}, u32[]{:S(2)}, u32[]{:S(2)}) async-start(bf16[4,1032,128]{2,1,0:T(8,128)(2,1)} %get-tuple-element.58), calls=%async_computation.6 | async-start | bytes 2113536 | tf_op jit(solution)/shard_map/all_to_all | solution.py:45
  184.3 8.4 %collective-permute-start.8 = (bf16[1024,128]{1,0:T(8,128)(2,1)S(1)}, bf16[1024,128]{1,0:T(8,128)(2,1)S(1)}, u32[]{:S(2)}, u32[]{:S(2)}) collective-permute-start(bf16[1024,128]{1,0:T(8,128)(2,1)S(1)} %add_convert_fusion.3), channel_id=1, source_target_pairs={{0,16},{4,20},{8,24},{12,28},{16,32},{20,36},{24,40},{28,44},{32,4... | collective-permute-start | bytes 786440 | tf_op jit(solution)/shard_map/ppermute | solution.py:37
  192.8 15.9 %collective-permute-done.8 = bf16[1024,128]{1,0:T(8,128)(2,1)S(1)} collective-permute-done((bf16[1024,128]{1,0:T(8,128)(2,1)S(1)}, bf16[1024,128]{1,0:T(8,128)(2,1)S(1)}, u32[]{:S(2)}, u32[]{:S(2)}) %collective-permute-start.8) | collective-permute-done | bytes 262176 | tf_op jit(solution)/shard_map/ppermute | solution.py:37
  208.7 0.9 pool_parts.3
  209.6 2.9 collective-permute-start.10
  212.5 6.9 %collective-permute-start.9 = (bf16[1032,128]{1,0:T(8,128)(2,1)S(1)}, bf16[1032,128]{1,0:T(8,128)(2,1)S(1)}, u32[]{:S(2)}, u32[]{:S(2)}) collective-permute-start(bf16[1032,128]{1,0:T(8,128)(2,1)S(1)} %get-tuple-element.64), channel_id=1, source_target_pairs={{0,16},{4,20},{8,24},{12,28},{16,32},{20,36},{24,40},{28,44},{32,4... | collective-permute-start | bytes 792584 | tf_op jit(solution)/shard_map/ppermute | solution.py:37
  219.4 4.7 %collective-permute-done.10 = bf16[1032,128]{1,0:T(8,128)(2,1)S(1)} collective-permute-done((bf16[1032,128]{1,0:T(8,128)(2,1)S(1)}, bf16[1032,128]{1,0:T(8,128)(2,1)S(1)}, u32[]{:S(2)}, u32[]{:S(2)}) %collective-permute-start.10) | collective-permute-done | bytes 264224 | tf_op jit(solution)/shard_map/ppermute | solution.py:37
  224.2 6.2 %collective-permute-start.11 = (bf16[1032,128]{1,0:T(8,128)(2,1)S(1)}, bf16[1032,128]{1,0:T(8,128)(2,1)S(1)}, u32[]{:S(2)}, u32[]{:S(2)}) collective-permute-start(bf16[1032,128]{1,0:T(8,128)(2,1)S(1)} %pad_maximum_fusion.2), channel_id=1, source_target_pairs={{0,48},{4,52},{8,56},{12,60},{16,0},{20,4},{24,8},{28,12},{32,16},... | collective-permute-start | bytes 792584 | tf_op jit(solution)/shard_map/ppermute | solution.py:37
  230.5 6.8 %collective-permute-done.11 = bf16[1032,128]{1,0:T(8,128)(2,1)S(1)} collective-permute-done((bf16[1032,128]{1,0:T(8,128)(2,1)S(1)}, bf16[1032,128]{1,0:T(8,128)(2,1)S(1)}, u32[]{:S(2)}, u32[]{:S(2)}) %collective-permute-start.11) | collective-permute-done | bytes 264224 | tf_op jit(solution)/shard_map/ppermute | solution.py:37
  237.5 0.9 pad_maximum_fusion.1
  238.3 13.1 %all-to-all-start.7 = ((bf16[16,128,128]{2,1,0:T(8,128)(2,1)}), bf16[16,128,128]{2,1,0:T(8,128)(2,1)S(1)}, u32[]{:S(2)}, u32[]{:S(2)}) async-start(bf16[16,128,128]{2,1,0:T(8,128)(2,1)} %bitcast.31), calls=%async_computation.7 | async-start | bytes 1048576 | tf_op jit(solution)/shard_map/all_to_all | solution.py:41
  251.6 12.2 %psum.14 = f32[32]{0:T(128)S(1)} all-reduce(f32[32]{0:T(128)S(1)} %reduce_sum.62), channel_id=1, replica_groups={{0,4,8,12},{16,20,24,28},{32,36,40,44},{48,52,56,60},{64,68,72,76},{80,..., use_global_device_ids=true, to_apply=%region_6.7 | all-reduce | flops 32 | bytes 256 | tf_op jit(solution)/shard_map/psum | solution.py:330
  263.7 20.5 %psum.15 = f32[32]{0:T(128)} all-reduce(f32[32]{0:T(128)S(1)} %psum.14), channel_id=1, replica_groups=mesh['dp'=2,'ctx'=64,'head'=4] {'dp','head'}, use_global_device_ids=true, to_apply=%region_7.8 | all-reduce | flops 32 | bytes 256 | tf_op jit(solution)/shard_map/psum | solution.py:331
  284.5 0.9 reshape_squeeze.15
  285.6 0.9 reshape_squeeze.14
  (64 shorter events, 4.7 us)
Async XLA Ops:
  0.6 38.9 %copy-start = (s32[1,16,8,3]{1,2,3,0:T(8,128)S(1)}, s32[1,16,8,3]{1,2,3,0:T(8,128)}, u32[]{:S(2)}) copy-start(s32[1,16,8,3]{1,2,3,0:T(8,128)} %param.11) | copy-start | bytes 4612
  3.6 9.5 %copy-start.7 = (s32[16]{0:T(128)S(1)}, s32[16]{0:T(128)}, u32[]{:S(2)}) copy-start(s32[16]{0:T(128)} %param.12) | copy-start | bytes 196
  4.6 25.0 %all-to-all-start = ((bf16[16,128,128]{2,1,0:T(8,128)(2,1)}), bf16[16,128,128]{2,1,0:T(8,128)(2,1)S(1)}, u32[]{:S(2)}, u32[]{:S(2)}) async-start(bf16[16,128,128]{2,1,0:T(8,128)(2,1)} %bitcast.9), calls=%async_computation | async-start | bytes 1048576 | tf_op jit(solution)/shard_map/all_to_all | solution.py:41
  30.4 32.5 %collective-permute-start = (bf16[4,256,128]{2,1,0:T(8,128)(2,1)}, bf16[4,256,128]{2,1,0:T(8,128)(2,1)S(1)}, u32[]{:S(2)}, u32[]{:S(2)}) collective-permute-start(bf16[4,256,128]{2,1,0:T(8,128)(2,1)} %bitcast.12.refs_0_), channel_id=1, source_target_pairs={{0,16},{4,20},{8,24},{12,28},{16,32},{20,36},{24,40},{28,44},{32,4... | collective-permute-start | bytes 786440 | tf_op jit(solution)/shard_map/ppermute | solution.py:37
  40.0 32.8 %all-to-all-start.1 = ((bf16[4,256,128]{2,1,0:T(8,128)(2,1)}), bf16[4,256,128]{2,1,0:T(8,128)(2,1)S(1)}, u32[]{:S(2)}, u32[]{:S(2)}) async-start(bf16[4,256,128]{2,1,0:T(8,128)(2,1)} %bitcast.12.refs_0_), calls=%async_computation.1 | async-start | bytes 524288 | tf_op jit(solution)/shard_map/all_to_all | solution.py:45
  43.4 47.6 %collective-permute-start.2 = (bf16[4,256,128]{2,1,0:T(8,128)(2,1)}, bf16[4,256,128]{2,1,0:T(8,128)(2,1)S(1)}, u32[]{:S(2)}, u32[]{:S(2)}) collective-permute-start(bf16[4,256,128]{2,1,0:T(8,128)(2,1)} %bitcast.12.refs_0_), channel_id=1, source_target_pairs={{0,48},{4,52},{8,56},{12,60},{16,0},{20,4},{24,8},{28,12},{32,16},... | collective-permute-start | bytes 786440 | tf_op jit(solution)/shard_map/ppermute | solution.py:37
  62.9 25.8 %collective-permute-start.1 = (bf16[4,256,128]{2,1,0:T(8,128)(2,1)}, bf16[4,256,128]{2,1,0:T(8,128)(2,1)S(1)}, u32[]{:S(2)}, u32[]{:S(2)}) collective-permute-start(bf16[4,256,128]{2,1,0:T(8,128)(2,1)} %bitcast.14.refs_0_), channel_id=1, source_target_pairs={{0,48},{4,52},{8,56},{12,60},{16,0},{20,4},{24,8},{28,12},{32,16},... | collective-permute-start | bytes 786440 | tf_op jit(solution)/shard_map/ppermute | solution.py:37
  69.8 21.2 %collective-permute-start.3 = (bf16[4,256,128]{2,1,0:T(8,128)(2,1)S(1)}, bf16[4,256,128]{2,1,0:T(8,128)(2,1)S(1)}, u32[]{:S(2)}, u32[]{:S(2)}) collective-permute-start(bf16[4,256,128]{2,1,0:T(8,128)(2,1)S(1)} %collective-permute-done.refs_3_), channel_id=1, source_target_pairs={{0,16},{4,20},{8,24},{12,28},{16,32},{20,36},{24,40},{28,44},{32,4... | collective-permute-start | bytes 786440 | tf_op jit(solution)/shard_map/ppermute | solution.py:37
  72.8 10.1 %all-to-all-start.2 = ((bf16[4,256,128]{2,1,0:T(8,128)(2,1)}), bf16[4,256,128]{2,1,0:T(8,128)(2,1)S(1)}, u32[]{:S(2)}, u32[]{:S(2)}) async-start(bf16[4,256,128]{2,1,0:T(8,128)(2,1)} %bitcast.14.refs_0_), calls=%async_computation.2 | async-start | bytes 524288 | tf_op jit(solution)/shard_map/all_to_all | solution.py:45
  93.0 3.7 %copy-start.8 = (f32[8]{0:T(128)S(1)}, f32[8]{0:T(128)}, u32[]{:S(2)}) copy-start(f32[8]{0:T(128)} %param.13) | copy-start | bytes 100
  93.0 16.4 %copy-start.1 = (bf16[1,1,1,512,256]{4,3,2,1,0:T(8,128)(2,1)S(1)}, bf16[1,1,1,512,256]{4,3,2,1,0:T(8,128)(2,1)}, u32[]{:S(2)}) copy-start(bf16[1,1,1,512,256]{4,3,2,1,0:T(8,128)(2,1)} %param.7) | copy-start | bytes 786436
  93.0 16.4 %copy-start.2 = (bf16[1,1,1,512,256]{4,3,2,1,0:T(8,128)(2,1)S(1)}, bf16[1,1,1,512,256]{4,3,2,1,0:T(8,128)(2,1)}, u32[]{:S(2)}) copy-start(bf16[1,1,1,512,256]{4,3,2,1,0:T(8,128)(2,1)} %param.10) | copy-start | bytes 786436
  93.0 16.3 %all-to-all-start.3 = ((bf16[4,768,128]{2,1,0:T(8,128)(2,1)}), bf16[4,768,128]{2,1,0:T(8,128)(2,1)S(1)}, u32[]{:S(2)}, u32[]{:S(2)}) async-start(bf16[4,768,128]{2,1,0:T(8,128)(2,1)} %bitcast.21), calls=%async_computation.3 | async-start | bytes 1572864 | tf_op jit(solution)/shard_map/all_to_all | solution.py:45
  97.6 23.2 %collective-permute-start.4 = (bf16[4,256,128]{2,1,0:T(8,128)(2,1)}, bf16[4,256,128]{2,1,0:T(8,128)(2,1)S(1)}, u32[]{:S(2)}, u32[]{:S(2)}) collective-permute-start(bf16[4,256,128]{2,1,0:T(8,128)(2,1)} %bitcast.14.refs_0_), channel_id=1, source_target_pairs={{0,16},{4,20},{8,24},{12,28},{16,32},{20,36},{24,40},{28,44},{32,4... | collective-permute-start | bytes 786440 | tf_op jit(solution)/shard_map/ppermute | solution.py:37
  101.9 18.9 %collective-permute-start.5 = (bf16[4,256,128]{2,1,0:T(8,128)(2,1)S(1)}, bf16[4,256,128]{2,1,0:T(8,128)(2,1)S(1)}, u32[]{:S(2)}, u32[]{:S(2)}) collective-permute-start(bf16[4,256,128]{2,1,0:T(8,128)(2,1)S(1)} %collective-permute-done.1.refs_1_), channel_id=1, source_target_pairs={{0,48},{4,52},{8,56},{12,60},{16,0},{20,4},{24,8},{28,12},{32,16},... | collective-permute-start | bytes 786440 | tf_op jit(solution)/shard_map/ppermute | solution.py:37
  120.8 16.0 %all-to-all-start.4 = ((bf16[4,1024,128]{2,1,0:T(8,128)(2,1)}), bf16[4,1024,128]{2,1,0:T(8,128)(2,1)S(1)}, u32[]{:S(2)}, u32[]{:S(2)}) async-start(bf16[4,1024,128]{2,1,0:T(8,128)(2,1)} %get-tuple-element.43), calls=%async_computation.4 | async-start | bytes 2097152 | tf_op jit(solution)/shard_map/all_to_all | solution.py:45
  137.7 0.7 copy-start.3
  140.4 3.6 %copy-start.4 = (bf16[1024,128]{1,0:T(8,128)(2,1)S(1)}, bf16[1024,128]{1,0:T(8,128)(2,1)}, u32[]{:S(2)}) copy-start(bf16[1024,128]{1,0:T(8,128)(2,1)} %copy-done.3) | copy-start | bytes 786436
  140.4 22.1 %all-to-all-start.5 = ((bf16[4,768,128]{2,1,0:T(8,128)(2,1)}), bf16[4,768,128]{2,1,0:T(8,128)(2,1)S(1)}, u32[]{:S(2)}, u32[]{:S(2)}) async-start(bf16[4,768,128]{2,1,0:T(8,128)(2,1)} %bitcast.23), calls=%async_computation.5 | async-start | bytes 1572864 | tf_op jit(solution)/shard_map/all_to_all | solution.py:45
  144.0 34.8 %collective-permute-start.6 = (bf16[1024,128]{1,0:T(8,128)(2,1)S(1)}, bf16[1024,128]{1,0:T(8,128)(2,1)S(1)}, u32[]{:S(2)}, u32[]{:S(2)}) collective-permute-start(bf16[1024,128]{1,0:T(8,128)(2,1)S(1)} %copy-done.4), channel_id=1, source_target_pairs={{0,16},{4,20},{8,24},{12,28},{16,32},{20,36},{24,40},{28,44},{32,4... | collective-permute-start | bytes 786440 | tf_op jit(solution)/shard_map/ppermute | solution.py:37
  160.3 18.6 %collective-permute-start.7 = (bf16[1024,128]{1,0:T(8,128)(2,1)S(1)}, bf16[1024,128]{1,0:T(8,128)(2,1)S(1)}, u32[]{:S(2)}, u32[]{:S(2)}) collective-permute-start(bf16[1024,128]{1,0:T(8,128)(2,1)S(1)} %get-tuple-element.47), channel_id=1, source_target_pairs={{0,48},{4,52},{8,56},{12,60},{16,0},{20,4},{24,8},{28,12},{32,16},... | collective-permute-start | bytes 786440 | tf_op jit(solution)/shard_map/ppermute | solution.py:37
  178.9 0.7 copy-start.5
  179.6 29.1 %all-to-all-start.6 = ((bf16[4,1032,128]{2,1,0:T(8,128)(2,1)}), bf16[4,1032,128]{2,1,0:T(8,128)(2,1)S(1)}, u32[]{:S(2)}, u32[]{:S(2)}) async-start(bf16[4,1032,128]{2,1,0:T(8,128)(2,1)} %get-tuple-element.58), calls=%async_computation.6 | async-start | bytes 2113536 | tf_op jit(solution)/shard_map/all_to_all | solution.py:45
  184.3 46.1 %copy-start.6 = (bf16[1024,128]{1,0:T(8,128)(2,1)S(1)}, bf16[1024,128]{1,0:T(8,128)(2,1)}, u32[]{:S(2)}) copy-start(bf16[1024,128]{1,0:T(8,128)(2,1)} %copy-done.5) | copy-start | bytes 786436
  184.3 24.4 %collective-permute-start.8 = (bf16[1024,128]{1,0:T(8,128)(2,1)S(1)}, bf16[1024,128]{1,0:T(8,128)(2,1)S(1)}, u32[]{:S(2)}, u32[]{:S(2)}) collective-permute-start(bf16[1024,128]{1,0:T(8,128)(2,1)S(1)} %add_convert_fusion.3), channel_id=1, source_target_pairs={{0,16},{4,20},{8,24},{12,28},{16,32},{20,36},{24,40},{28,44},{32,4... | collective-permute-start | bytes 786440 | tf_op jit(solution)/shard_map/ppermute | solution.py:37
  209.6 14.5 %collective-permute-start.10 = (bf16[1032,128]{1,0:T(8,128)(2,1)S(1)}, bf16[1032,128]{1,0:T(8,128)(2,1)S(1)}, u32[]{:S(2)}, u32[]{:S(2)}) collective-permute-start(bf16[1032,128]{1,0:T(8,128)(2,1)S(1)} %get-tuple-element.66), channel_id=1, source_target_pairs={{0,48},{4,52},{8,56},{12,60},{16,0},{20,4},{24,8},{28,12},{32,16},... | collective-permute-start | bytes 792584 | tf_op jit(solution)/shard_map/ppermute | solution.py:37
  212.5 18.0 %collective-permute-start.9 = (bf16[1032,128]{1,0:T(8,128)(2,1)S(1)}, bf16[1032,128]{1,0:T(8,128)(2,1)S(1)}, u32[]{:S(2)}, u32[]{:S(2)}) collective-permute-start(bf16[1032,128]{1,0:T(8,128)(2,1)S(1)} %get-tuple-element.64), channel_id=1, source_target_pairs={{0,16},{4,20},{8,24},{12,28},{16,32},{20,36},{24,40},{28,44},{32,4... | collective-permute-start | bytes 792584 | tf_op jit(solution)/shard_map/ppermute | solution.py:37
  224.2 13.1 %collective-permute-start.11 = (bf16[1032,128]{1,0:T(8,128)(2,1)S(1)}, bf16[1032,128]{1,0:T(8,128)(2,1)S(1)}, u32[]{:S(2)}, u32[]{:S(2)}) collective-permute-start(bf16[1032,128]{1,0:T(8,128)(2,1)S(1)} %pad_maximum_fusion.2), channel_id=1, source_target_pairs={{0,48},{4,52},{8,56},{12,60},{16,0},{20,4},{24,8},{28,12},{32,16},... | collective-permute-start | bytes 792584 | tf_op jit(solution)/shard_map/ppermute | solution.py:37
  238.3 46.0 %all-to-all-start.7 = ((bf16[16,128,128]{2,1,0:T(8,128)(2,1)}), bf16[16,128,128]{2,1,0:T(8,128)(2,1)S(1)}, u32[]{:S(2)}, u32[]{:S(2)}) async-start(bf16[16,128,128]{2,1,0:T(8,128)(2,1)} %bitcast.31), calls=%async_computation.7 | async-start | bytes 1048576 | tf_op jit(solution)/shard_map/all_to_all | solution.py:41

commit v9 on v7

--- a/solution.py
+++ b/solution.py
@@ -290,7 +290,6 @@
         back = swap_x(part.reshape(XS, KINDS * ROWS, DH)).reshape(XS, KINDS, ROWS, DH)
         if h > 0:
             up_first = shift_groups(add_rounded(pools[0][1], up_far), 1)
-            back, up_first = lax.optimization_barrier((back, up_first))
             start = lax.axis_index("head") * (SPB * HPD) + position * HPD
             sink_sum = lax.dynamic_update_slice(
                 jnp.zeros((HEADS,), jnp.float32), jnp.concatenate(sink_heads), (start,)
@@ -305,21 +304,16 @@
     main = XS * ROWS
     down_far = shift_groups(pools[1][2], -1)
     up_near = shift_groups(pools[1][1], 1)
+    down_far, up_first = lax.optimization_barrier((down_far, up_first))
     onward = jnp.concatenate([add_rounded(pools[1][3][:main], down_far[:main]), down_far[main:]])
     down_last = shift_groups(onward, -1)
     first = add_rounded(pools[0][0], up_first, down_near)
     second = add_rounded(pools[1][0][:main], up_near[:main], down_last[:main])
-    terms = [arr[main : main + 1] for arr in (pools[1][0], up_near, down_far, down_last)]
-    terms = jnp.concatenate(terms + [jnp.zeros((EXTRA - ZG, DH), jnp.bfloat16)])
-    pooled = jnp.concatenate(
-        [arr.reshape(XS * SPB, 2 * FRAG, DH) for arr in (first, second)]
-        + [jnp.broadcast_to(terms[None], (XS * SPB, EXTRA, DH))],
-        axis=1,
-    )
-    homed = swap_spread(pooled)
-    terms = homed[:, HPD * 2 * FRAG :, : 3 * HEADS].astype(jnp.float32)
-    grad_sink = jnp.sum(terms.reshape(-1, HEADS), axis=0)
-    homed = homed[:, : HPD * 2 * FRAG]
+    terms = jnp.stack([arr[main] for arr in (pools[1][0], up_near, down_far, down_last)])
+    terms = jnp.sum(terms[:, : 3 * HEADS].astype(jnp.float32).reshape(-1, HEADS), axis=0)
+    grad_sink = lax.psum(terms, "ctx", axis_index_groups=SPREAD_GROUPS)
+    pooled = jnp.stack([arr.reshape(XS * SPB, 2 * FRAG, DH) for arr in (first, second)], axis=1)
+    homed = swap_spread(pooled.reshape(XS * SPB, HPD * 2 * FRAG, DH))
     totals = jnp.transpose(homed.reshape(XS, SPB, HPD, 2, FRAG, DH), (3, 0, 4, 1, 2, 5))
     grad_key = totals[0].reshape(key.shape)
     grad_value = totals[1].reshape(value.shape)

time: 288 us -> 319 us (1.11)
  waiting for transfers between devices: 95.8 us -> 114 us
  blocking collectives: 49.1 us -> 57.5 us
  starting transfers between devices: 104 us -> 108 us
    psum x0 -> x1, blocking collectives: none -> 44.4 us  [body(): grad_sink = lax.psum(terms, 'ctx', axis_index_groups=SPREAD_GROUPS)]
    all_to_all x1 -> x0, blocking collectives: 36.3 us -> none  [swap_spread(): lax.all_to_all(arr, 'ctx', 0, 0, axis_index_groups=SPREAD_GROUPS, tiled=T...]
    ppermute x12, waiting for transfers between devices: 60.6 us -> 80.2 us  [shift_groups(): return lax.ppermute(arr, 'ctx', pairs)]
    all_to_all x1 -> x2, starting transfers between devices: 8.47 us -> 13 us  [swap_spread(): lax.all_to_all(arr, 'ctx', 0, 0, axis_index_groups=SPREAD_GROUPS, tiled=T...]
    all_to_all x1 -> x2, waiting for transfers between devices: 16.1 us -> 15.4 us  [swap_spread(): lax.all_to_all(arr, 'ctx', 0, 0, axis_index_groups=SPREAD_GROUPS, tiled=T...]
  transfers between devices with their start and end apart: 19 -> 20, of which waited for: 12 -> 13; matrix products, arithmetic and copies ran while one was open for 2% -> 2% of each run, Pallas kernels for 5% -> 4%
where the time goes in v9:
time: 319 us; the launch traced here: 314 us
  waiting for transfers between devices  114 us (36%)
  starting transfers between devices  108 us (34%)
  blocking collectives  57.5 us (18%)
  Pallas kernels  18.7 us (6%)
  local copies, waits for them, and re-layouts  10.3 us (3%)
  other arithmetic  4.46 us (1%)
    ppermute x12, waiting for transfers between devices, shift_groups(): return lax.ppermute(arr, 'ctx', pairs)  80.2 us
    ppermute x12, starting transfers between devices, shift_groups(): return lax.ppermute(arr, 'ctx', pairs)  70.9 us
    psum x1, blocking collectives, body(): grad_sink = lax.psum(terms, 'ctx', axis_index_groups=SPREAD_GROUPS)  44.4 us
    all_to_all x6, starting transfers between devices, swap_x(): lax.all_to_all(arr, 'ctx', 0, 0, axis_index_groups=X_GROUPS, tiled=True)  23.8 us
    all_to_all x6, waiting for transfers between devices, swap_x(): lax.all_to_all(arr, 'ctx', 0, 0, axis_index_groups=X_GROUPS, tiled=True)  18.6 us
    all_to_all x2, waiting for transfers between devices, swap_spread(): lax.all_to_all(arr, 'ctx', 0, 0, axis_index_groups=SPREAD_GROUPS, tiled=T...  15.4 us
    psum x1, blocking collectives, body(): sink_sum = lax.psum(sink_sum, ('dp', 'head'))  13.1 us
    all_to_all x2, starting transfers between devices, swap_spread(): lax.all_to_all(arr, 'ctx', 0, 0, axis_index_groups=SPREAD_GROUPS, tiled=T...  13 us
  transfers between devices with their start and end apart: 20, of which 13 were waited for; matrix products, arithmetic and copies ran while one was open for 2% of the time, Pallas kernels for 4%

profile of v9, /device:TPU:24, one launch (start us, length us, event | category | flops | bytes accessed | tf_op | source)
XLA Modules:
  0.0 314.0 jit_solution(15081420711957227109)
XLA Ops:
  0.7 1.2 reshape.122
  2.0 0.7 pad_maximum_fusion
  2.8 0.9 copy.28
  3.7 8.5 %all-to-all-start = ((bf16[16,128,128]{2,1,0:T(8,128)(2,1)}), bf16[16,128,128]{2,1,0:T(8,128)(2,1)S(1)}, u32[]{:S(2)}, u32[]{:S(2)}) async-start(bf16[16,128,128]{2,1,0:T(8,128)(2,1)} %bitcast.8), calls=%async_computation | async-start | bytes 1048576 | tf_op jit(solution)/shard_map/all_to_all | solution.py:40
  13.2 15.4 %all-to-all-done = bf16[16,128,128]{2,1,0:T(8,128)(2,1)S(1)} async-done(((bf16[16,128,128]{2,1,0:T(8,128)(2,1)}), bf16[16,128,128]{2,1,0:T(8,128)(2,1)S(1)}, u32[]{:S(2)}, u32[]{:S(2)}) %all-to-all-start) | async-done | bytes 524320 | tf_op jit(solution)/shard_map/all_to_all | solution.py:40
  28.7 0.8 fusion.10
  29.5 9.1 %collective-permute-start = (bf16[4,256,128]{2,1,0:T(8,128)(2,1)}, bf16[4,256,128]{2,1,0:T(8,128)(2,1)S(1)}, u32[]{:S(2)}, u32[]{:S(2)}) collective-permute-start(bf16[4,256,128]{2,1,0:T(8,128)(2,1)} %bitcast.11.refs_0_), channel_id=1, source_target_pairs={{0,16},{4,20},{8,24},{12,28},{16,32},{20,36},{24,40},{28,44},{32,4... | collective-permute-start | bytes 786440 | tf_op jit(solution)/shard_map/ppermute | solution.py:36
  39.1 3.4 %all-to-all-start.1 = ((bf16[4,256,128]{2,1,0:T(8,128)(2,1)}), bf16[4,256,128]{2,1,0:T(8,128)(2,1)S(1)}, u32[]{:S(2)}, u32[]{:S(2)}) async-start(bf16[4,256,128]{2,1,0:T(8,128)(2,1)} %bitcast.11.refs_0_), calls=%async_computation.1 | async-start | bytes 524288 | tf_op jit(solution)/shard_map/all_to_all | solution.py:44
  42.5 2.9 collective-permute-start.2
  45.4 16.7 %collective-permute-done.refs_3_ = bf16[4,256,128]{2,1,0:T(8,128)(2,1)S(1)} collective-permute-done((bf16[4,256,128]{2,1,0:T(8,128)(2,1)}, bf16[4,256,128]{2,1,0:T(8,128)(2,1)S(1)}, u32[]{:S(2)}, u32[]{:S(2)}) %collective-permute-start) | collective-permute-done | bytes 262176 | tf_op jit(solution)/shard_map/ppermute | solution.py:36
  62.1 6.9 %collective-permute-start.1 = (bf16[4,256,128]{2,1,0:T(8,128)(2,1)}, bf16[4,256,128]{2,1,0:T(8,128)(2,1)S(1)}, u32[]{:S(2)}, u32[]{:S(2)}) collective-permute-start(bf16[4,256,128]{2,1,0:T(8,128)(2,1)} %bitcast.13.refs_0_), channel_id=1, source_target_pairs={{0,48},{4,52},{8,56},{12,60},{16,0},{20,4},{24,8},{28,12},{32,16},... | collective-permute-start | bytes 786440 | tf_op jit(solution)/shard_map/ppermute | solution.py:36
  68.9 2.9 collective-permute-start.3
  71.8 3.4 %all-to-all-start.2 = ((bf16[4,256,128]{2,1,0:T(8,128)(2,1)}), bf16[4,256,128]{2,1,0:T(8,128)(2,1)S(1)}, u32[]{:S(2)}, u32[]{:S(2)}) async-start(bf16[4,256,128]{2,1,0:T(8,128)(2,1)} %bitcast.13.refs_0_), calls=%async_computation.2 | async-start | bytes 524288 | tf_op jit(solution)/shard_map/all_to_all | solution.py:44
  75.5 6.5 %all-to-all-done.2 = bf16[4,256,128]{2,1,0:T(8,128)(2,1)S(1)} async-done(((bf16[4,256,128]{2,1,0:T(8,128)(2,1)}), bf16[4,256,128]{2,1,0:T(8,128)(2,1)S(1)}, u32[]{:S(2)}, u32[]{:S(2)}) %all-to-all-start.2) | async-done | bytes 262176 | tf_op jit(solution)/shard_map/all_to_all | solution.py:44
  81.9 5.9 %collective-permute-done.1.refs_1_ = bf16[4,256,128]{2,1,0:T(8,128)(2,1)S(1)} collective-permute-done((bf16[4,256,128]{2,1,0:T(8,128)(2,1)}, bf16[4,256,128]{2,1,0:T(8,128)(2,1)S(1)}, u32[]{:S(2)}, u32[]{:S(2)}) %collective-permute-start.1) | collective-permute-done | bytes 262176 | tf_op jit(solution)/shard_map/ppermute | solution.py:36
  87.8 2.3 collective-permute-done.3.refs_2_
  90.1 2.0 gather_picks.2
  92.1 3.6 %all-to-all-start.3 = ((bf16[4,768,128]{2,1,0:T(8,128)(2,1)}), bf16[4,768,128]{2,1,0:T(8,128)(2,1)S(1)}, u32[]{:S(2)}, u32[]{:S(2)}) async-start(bf16[4,768,128]{2,1,0:T(8,128)(2,1)} %bitcast.19), calls=%async_computation.3 | async-start | bytes 1572864 | tf_op jit(solution)/shard_map/all_to_all | solution.py:44
  96.6 4.4 %collective-permute-start.4 = (bf16[4,256,128]{2,1,0:T(8,128)(2,1)}, bf16[4,256,128]{2,1,0:T(8,128)(2,1)S(1)}, u32[]{:S(2)}, u32[]{:S(2)}) collective-permute-start(bf16[4,256,128]{2,1,0:T(8,128)(2,1)} %bitcast.13.refs_0_), channel_id=1, source_target_pairs={{0,16},{4,20},{8,24},{12,28},{16,32},{20,36},{24,40},{28,44},{32,4... | collective-permute-start | bytes 786440 | tf_op jit(solution)/shard_map/ppermute | solution.py:36
  101.0 5.4 %collective-permute-start.5 = (bf16[4,256,128]{2,1,0:T(8,128)(2,1)S(1)}, bf16[4,256,128]{2,1,0:T(8,128)(2,1)S(1)}, u32[]{:S(2)}, u32[]{:S(2)}) collective-permute-start(bf16[4,256,128]{2,1,0:T(8,128)(2,1)S(1)} %collective-permute-done.1.refs_1_), channel_id=1, source_target_pairs={{0,48},{4,52},{8,56},{12,60},{16,0},{20,4},{24,8},{28,12},{32,16},... | collective-permute-start | bytes 786440 | tf_op jit(solution)/shard_map/ppermute | solution.py:36
  107.1 1.4 all-to-all-done.3
  108.5 6.5 %attend_head0.1 = (bf16[512,256]{1,0:T(8,128)(2,1)}, bf16[512,256]{1,0:T(8,128)(2,1)}, bf16[4,4,4,2,32,128]{5,4,3,2,1,0:T(8,128)(2,1)}, f32[8,128]{1,0:T(8,128)S(1)}) custom-call(s32[3]{0:T(128)S(1)} %get-tuple-element.77.use_ref, f32[1]{0:T(128)} %get-tuple-element.79.sink_ref, bf16[512,256]{1,0:T(8,128)(2,1)S(1)} %bitcast.68, ...), custom_call_target="tpu_custom_call" | custom-call | flops 2684354560 | bytes 8388608 | tf_op jit(solution)/shard_map/attend_head0/pallas_call | solution.py:131
  114.9 4.9 %collective-permute-done.5.refs_2_ = bf16[4,256,128]{2,1,0:T(8,128)(2,1)S(1)} collective-permute-done((bf16[4,256,128]{2,1,0:T(8,128)(2,1)S(1)}, bf16[4,256,128]{2,1,0:T(8,128)(2,1)S(1)}, u32[]{:S(2)}, u32[]{:S(2)}) %collective-permute-start.5) | collective-permute-done | bytes 262176 | tf_op jit(solution)/shard_map/ppermute | solution.py:36
  119.9 5.1 %all-to-all-start.4 = ((bf16[4,1024,128]{2,1,0:T(8,128)(2,1)}), bf16[4,1024,128]{2,1,0:T(8,128)(2,1)S(1)}, u32[]{:S(2)}, u32[]{:S(2)}) async-start(bf16[4,1024,128]{2,1,0:T(8,128)(2,1)} %bitcast.21), calls=%async_computation.4 | async-start | bytes 2097152 | tf_op jit(solution)/shard_map/all_to_all | solution.py:44
  125.1 10.7 %all-to-all-done.4 = bf16[4,1024,128]{2,1,0:T(8,128)(2,1)S(1)} async-done(((bf16[4,1024,128]{2,1,0:T(8,128)(2,1)}), bf16[4,1024,128]{2,1,0:T(8,128)(2,1)S(1)}, u32[]{:S(2)}, u32[]{:S(2)}) %all-to-all-start.4) | async-done | bytes 1048608 | tf_op jit(solution)/shard_map/all_to_all | solution.py:44
  135.9 0.9 pool_parts.2
  137.5 2.0 gather_picks.3
  139.5 3.6 %all-to-all-start.5 = ((bf16[4,768,128]{2,1,0:T(8,128)(2,1)}), bf16[4,768,128]{2,1,0:T(8,128)(2,1)S(1)}, u32[]{:S(2)}, u32[]{:S(2)}) async-start(bf16[4,768,128]{2,1,0:T(8,128)(2,1)} %bitcast.23), calls=%async_computation.5 | async-start | bytes 1572864 | tf_op jit(solution)/shard_map/all_to_all | solution.py:44
  143.1 16.5 %collective-permute-start.6 = (bf16[1024,128]{1,0:T(8,128)(2,1)S(1)}, bf16[1024,128]{1,0:T(8,128)(2,1)S(1)}, u32[]{:S(2)}, u32[]{:S(2)}) collective-permute-start(bf16[1024,128]{1,0:T(8,128)(2,1)S(1)} %copy-done.4), channel_id=1, source_target_pairs={{0,16},{4,20},{8,24},{12,28},{16,32},{20,36},{24,40},{28,44},{32,4... | collective-permute-start | bytes 786440 | tf_op jit(solution)/shard_map/ppermute | solution.py:36
  159.7 2.1 collective-permute-start.7
  161.8 6.5 %attend_head1.1 = (bf16[512,256]{1,0:T(8,128)(2,1)}, bf16[512,256]{1,0:T(8,128)(2,1)}, bf16[4,4,4,2,32,128]{5,4,3,2,1,0:T(8,128)(2,1)}, f32[8,128]{1,0:T(8,128)S(1)}) custom-call(s32[3]{0:T(128)S(1)} %get-tuple-element.78.use_ref, f32[1]{0:T(128)} %get-tuple-element.80.sink_ref, ...), custom_call_target="tpu_custom_call", output_to_operand_aliasing={{0}: (6, {}), {1}: (7, {})} | custom-call | flops 2684354560 | bytes 8388608 | tf_op jit(solution)/shard_map/attend_head1/pallas_call | solution.py:131
  168.3 6.1 %collective-permute-done.7 = bf16[1024,128]{1,0:T(8,128)(2,1)S(1)} collective-permute-done((bf16[1024,128]{1,0:T(8,128)(2,1)S(1)}, bf16[1024,128]{1,0:T(8,128)(2,1)S(1)}, u32[]{:S(2)}, u32[]{:S(2)}) %collective-permute-start.7) | collective-permute-done | bytes 262176 | tf_op jit(solution)/shard_map/ppermute | solution.py:36
  175.1 4.7 %all-to-all-start.6 = ((bf16[4,1024,128]{2,1,0:T(8,128)(2,1)}), bf16[4,1024,128]{2,1,0:T(8,128)(2,1)S(1)}, u32[]{:S(2)}, u32[]{:S(2)}) async-start(bf16[4,1024,128]{2,1,0:T(8,128)(2,1)} %bitcast.27), calls=%async_computation.6 | async-start | bytes 2097152 | tf_op jit(solution)/shard_map/all_to_all | solution.py:44
  180.8 1.5 maximum_dynamic-update-slice_fusion
  182.3 13.1 %psum.14 = f32[32]{0:T(128)S(1)} all-reduce(f32[32]{0:T(128)S(1)} %maximum_dynamic-update-slice_fusion), channel_id=1, replica_groups=mesh['dp'=2,'ctx'=64,'head'=4] {'dp','head'}, use_global_device_ids=true, to_apply=%region_5.6 | all-reduce | flops 32 | bytes 256 | tf_op jit(solution)/shard_map/psum | solution.py:297
  195.5 0.9 pool_parts.3
  196.4 5.0 %collective-permute-start.8 = (bf16[1032,128]{1,0:T(8,128)(2,1)S(1)}, bf16[1032,128]{1,0:T(8,128)(2,1)S(1)}, u32[]{:S(2)}, u32[]{:S(2)}) collective-permute-start(bf16[1032,128]{1,0:T(8,128)(2,1)S(1)} %get-tuple-element.61), channel_id=1, source_target_pairs={{0,48},{4,52},{8,56},{12,60},{16,0},{20,4},{24,8},{28,12},{32,16},... | collective-permute-start | bytes 792584 | tf_op jit(solution)/shard_map/ppermute | solution.py:36
  201.5 4.8 %collective-permute-start.9 = (bf16[1024,128]{1,0:T(8,128)(2,1)S(1)}, bf16[1024,128]{1,0:T(8,128)(2,1)S(1)}, u32[]{:S(2)}, u32[]{:S(2)}) collective-permute-start(bf16[1024,128]{1,0:T(8,128)(2,1)S(1)} %add_convert_fusion.3), channel_id=1, source_target_pairs={{0,16},{4,20},{8,24},{12,28},{16,32},{20,36},{24,40},{28,44},{32,4... | collective-permute-start | bytes 786440 | tf_op jit(solution)/shard_map/ppermute | solution.py:36
  206.3 7.6 %collective-permute-start.10 = (bf16[1032,128]{1,0:T(8,128)(2,1)S(1)}, bf16[1032,128]{1,0:T(8,128)(2,1)S(1)}, u32[]{:S(2)}, u32[]{:S(2)}) collective-permute-start(bf16[1032,128]{1,0:T(8,128)(2,1)S(1)} %get-tuple-element.66), channel_id=1, source_target_pairs={{0,16},{4,20},{8,24},{12,28},{16,32},{20,36},{24,40},{28,44},{32,4... | collective-permute-start | bytes 792584 | tf_op jit(solution)/shard_map/ppermute | solution.py:36
  213.9 34.3 %collective-permute-done.9 = bf16[1024,128]{1,0:T(8,128)(2,1)S(1)} collective-permute-done((bf16[1024,128]{1,0:T(8,128)(2,1)S(1)}, bf16[1024,128]{1,0:T(8,128)(2,1)S(1)}, u32[]{:S(2)}, u32[]{:S(2)}) %collective-permute-start.9) | collective-permute-done | bytes 262176 | tf_op jit(solution)/shard_map/ppermute | solution.py:36
  248.4 3.4 %collective-permute-start.11 = (bf16[1032,128]{1,0:T(8,128)(2,1)S(1)}, bf16[1032,128]{1,0:T(8,128)(2,1)S(1)}, u32[]{:S(2)}, u32[]{:S(2)}) collective-permute-start(bf16[1032,128]{1,0:T(8,128)(2,1)S(1)} %pad_maximum_fusion.2), channel_id=1, source_target_pairs={{0,48},{4,52},{8,56},{12,60},{16,0},{20,4},{24,8},{28,12},{32,16},... | collective-permute-start | bytes 792584 | tf_op jit(solution)/shard_map/ppermute | solution.py:36
  251.9 1.5 collective-permute-done.10
  253.5 8.3 %collective-permute-done.11 = bf16[1032,128]{1,0:T(8,128)(2,1)S(1)} collective-permute-done((bf16[1032,128]{1,0:T(8,128)(2,1)S(1)}, bf16[1032,128]{1,0:T(8,128)(2,1)S(1)}, u32[]{:S(2)}, u32[]{:S(2)}) %collective-permute-start.11) | collective-permute-done | bytes 264224 | tf_op jit(solution)/shard_map/ppermute | solution.py:36
  261.9 0.9 pad_maximum_fusion.1
  262.7 4.5 %all-to-all-start.7 = ((bf16[16,128,128]{2,1,0:T(8,128)(2,1)}), bf16[16,128,128]{2,1,0:T(8,128)(2,1)S(1)}, u32[]{:S(2)}, u32[]{:S(2)}) async-start(bf16[16,128,128]{2,1,0:T(8,128)(2,1)} %bitcast.35), calls=%async_computation.7 | async-start | bytes 1048576 | tf_op jit(solution)/shard_map/all_to_all | solution.py:40
  267.4 44.4 %psum.15 = f32[32]{0:T(128)} all-reduce(f32[32]{0:T(128)S(1)} %reduce_sum.62), channel_id=1, replica_groups={{0,4,8,12,64,68,72,76,128,132,136,140,192,196,200,204},{16,20,24,28,80,..., use_global_device_ids=true, to_apply=%region_7.8 | all-reduce | flops 32 | bytes 256 | tf_op jit(solution)/shard_map/psum | solution.py:314
  312.1 0.9 reshape_squeeze.15
  313.1 0.9 reshape_squeeze.14
  (71 shorter events, 7.1 us)
Async XLA Ops:
  0.6 38.0 %copy-start = (s32[1,16,8,3]{1,2,3,0:T(8,128)S(1)}, s32[1,16,8,3]{1,2,3,0:T(8,128)}, u32[]{:S(2)}) copy-start(s32[1,16,8,3]{1,2,3,0:T(8,128)} %param.11) | copy-start | bytes 4612
  0.6 1.2 copy-start.5
  3.7 25.0 %all-to-all-start = ((bf16[16,128,128]{2,1,0:T(8,128)(2,1)}), bf16[16,128,128]{2,1,0:T(8,128)(2,1)S(1)}, u32[]{:S(2)}, u32[]{:S(2)}) async-start(bf16[16,128,128]{2,1,0:T(8,128)(2,1)} %bitcast.8), calls=%async_computation | async-start | bytes 1048576 | tf_op jit(solution)/shard_map/all_to_all | solution.py:40
  12.2 0.7 copy-start.8
  29.5 32.5 %collective-permute-start = (bf16[4,256,128]{2,1,0:T(8,128)(2,1)}, bf16[4,256,128]{2,1,0:T(8,128)(2,1)S(1)}, u32[]{:S(2)}, u32[]{:S(2)}) collective-permute-start(bf16[4,256,128]{2,1,0:T(8,128)(2,1)} %bitcast.11.refs_0_), channel_id=1, source_target_pairs={{0,16},{4,20},{8,24},{12,28},{16,32},{20,36},{24,40},{28,44},{32,4... | collective-permute-start | bytes 786440 | tf_op jit(solution)/shard_map/ppermute | solution.py:36
  39.1 32.8 %all-to-all-start.1 = ((bf16[4,256,128]{2,1,0:T(8,128)(2,1)}), bf16[4,256,128]{2,1,0:T(8,128)(2,1)S(1)}, u32[]{:S(2)}, u32[]{:S(2)}) async-start(bf16[4,256,128]{2,1,0:T(8,128)(2,1)} %bitcast.11.refs_0_), calls=%async_computation.1 | async-start | bytes 524288 | tf_op jit(solution)/shard_map/all_to_all | solution.py:44
  42.5 47.6 %collective-permute-start.2 = (bf16[4,256,128]{2,1,0:T(8,128)(2,1)}, bf16[4,256,128]{2,1,0:T(8,128)(2,1)S(1)}, u32[]{:S(2)}, u32[]{:S(2)}) collective-permute-start(bf16[4,256,128]{2,1,0:T(8,128)(2,1)} %bitcast.11.refs_0_), channel_id=1, source_target_pairs={{0,48},{4,52},{8,56},{12,60},{16,0},{20,4},{24,8},{28,12},{32,16},... | collective-permute-start | bytes 786440 | tf_op jit(solution)/shard_map/ppermute | solution.py:36
  62.1 25.8 %collective-permute-start.1 = (bf16[4,256,128]{2,1,0:T(8,128)(2,1)}, bf16[4,256,128]{2,1,0:T(8,128)(2,1)S(1)}, u32[]{:S(2)}, u32[]{:S(2)}) collective-permute-start(bf16[4,256,128]{2,1,0:T(8,128)(2,1)} %bitcast.13.refs_0_), channel_id=1, source_target_pairs={{0,48},{4,52},{8,56},{12,60},{16,0},{20,4},{24,8},{28,12},{32,16},... | collective-permute-start | bytes 786440 | tf_op jit(solution)/shard_map/ppermute | solution.py:36
  68.9 21.2 %collective-permute-start.3 = (bf16[4,256,128]{2,1,0:T(8,128)(2,1)S(1)}, bf16[4,256,128]{2,1,0:T(8,128)(2,1)S(1)}, u32[]{:S(2)}, u32[]{:S(2)}) collective-permute-start(bf16[4,256,128]{2,1,0:T(8,128)(2,1)S(1)} %collective-permute-done.refs_3_), channel_id=1, source_target_pairs={{0,16},{4,20},{8,24},{12,28},{16,32},{20,36},{24,40},{28,44},{32,4... | collective-permute-start | bytes 786440 | tf_op jit(solution)/shard_map/ppermute | solution.py:36
  71.8 10.1 %all-to-all-start.2 = ((bf16[4,256,128]{2,1,0:T(8,128)(2,1)}), bf16[4,256,128]{2,1,0:T(8,128)(2,1)S(1)}, u32[]{:S(2)}, u32[]{:S(2)}) async-start(bf16[4,256,128]{2,1,0:T(8,128)(2,1)} %bitcast.13.refs_0_), calls=%async_computation.2 | async-start | bytes 524288 | tf_op jit(solution)/shard_map/all_to_all | solution.py:44
  92.1 16.4 %copy-start.1 = (bf16[1,1,1,512,256]{4,3,2,1,0:T(8,128)(2,1)S(1)}, bf16[1,1,1,512,256]{4,3,2,1,0:T(8,128)(2,1)}, u32[]{:S(2)}) copy-start(bf16[1,1,1,512,256]{4,3,2,1,0:T(8,128)(2,1)} %param.7) | copy-start | bytes 786436
  92.1 16.4 %copy-start.2 = (bf16[1,1,1,512,256]{4,3,2,1,0:T(8,128)(2,1)S(1)}, bf16[1,1,1,512,256]{4,3,2,1,0:T(8,128)(2,1)}, u32[]{:S(2)}) copy-start(bf16[1,1,1,512,256]{4,3,2,1,0:T(8,128)(2,1)} %param.10) | copy-start | bytes 786436
  92.1 16.3 %all-to-all-start.3 = ((bf16[4,768,128]{2,1,0:T(8,128)(2,1)}), bf16[4,768,128]{2,1,0:T(8,128)(2,1)S(1)}, u32[]{:S(2)}, u32[]{:S(2)}) async-start(bf16[4,768,128]{2,1,0:T(8,128)(2,1)} %bitcast.19), calls=%async_computation.3 | async-start | bytes 1572864 | tf_op jit(solution)/shard_map/all_to_all | solution.py:44
  95.7 0.7 copy-start.9
  96.6 23.2 %collective-permute-start.4 = (bf16[4,256,128]{2,1,0:T(8,128)(2,1)}, bf16[4,256,128]{2,1,0:T(8,128)(2,1)S(1)}, u32[]{:S(2)}, u32[]{:S(2)}) collective-permute-start(bf16[4,256,128]{2,1,0:T(8,128)(2,1)} %bitcast.13.refs_0_), channel_id=1, source_target_pairs={{0,16},{4,20},{8,24},{12,28},{16,32},{20,36},{24,40},{28,44},{32,4... | collective-permute-start | bytes 786440 | tf_op jit(solution)/shard_map/ppermute | solution.py:36
  101.0 18.9 %collective-permute-start.5 = (bf16[4,256,128]{2,1,0:T(8,128)(2,1)S(1)}, bf16[4,256,128]{2,1,0:T(8,128)(2,1)S(1)}, u32[]{:S(2)}, u32[]{:S(2)}) collective-permute-start(bf16[4,256,128]{2,1,0:T(8,128)(2,1)S(1)} %collective-permute-done.1.refs_1_), channel_id=1, source_target_pairs={{0,48},{4,52},{8,56},{12,60},{16,0},{20,4},{24,8},{28,12},{32,16},... | collective-permute-start | bytes 786440 | tf_op jit(solution)/shard_map/ppermute | solution.py:36
  119.9 16.0 %all-to-all-start.4 = ((bf16[4,1024,128]{2,1,0:T(8,128)(2,1)}), bf16[4,1024,128]{2,1,0:T(8,128)(2,1)S(1)}, u32[]{:S(2)}, u32[]{:S(2)}) async-start(bf16[4,1024,128]{2,1,0:T(8,128)(2,1)} %bitcast.21), calls=%async_computation.4 | async-start | bytes 2097152 | tf_op jit(solution)/shard_map/all_to_all | solution.py:44
  136.8 0.7 copy-start.3
  139.5 3.6 %copy-start.4 = (bf16[1024,128]{1,0:T(8,128)(2,1)S(1)}, bf16[1024,128]{1,0:T(8,128)(2,1)}, u32[]{:S(2)}) copy-start(bf16[1024,128]{1,0:T(8,128)(2,1)} %copy-done.3) | copy-start | bytes 786436
  139.5 22.3 %all-to-all-start.5 = ((bf16[4,768,128]{2,1,0:T(8,128)(2,1)}), bf16[4,768,128]{2,1,0:T(8,128)(2,1)S(1)}, u32[]{:S(2)}, u32[]{:S(2)}) async-start(bf16[4,768,128]{2,1,0:T(8,128)(2,1)} %bitcast.23), calls=%async_computation.5 | async-start | bytes 1572864 | tf_op jit(solution)/shard_map/all_to_all | solution.py:44
  143.1 25.2 %collective-permute-start.6 = (bf16[1024,128]{1,0:T(8,128)(2,1)S(1)}, bf16[1024,128]{1,0:T(8,128)(2,1)S(1)}, u32[]{:S(2)}, u32[]{:S(2)}) collective-permute-start(bf16[1024,128]{1,0:T(8,128)(2,1)S(1)} %copy-done.4), channel_id=1, source_target_pairs={{0,16},{4,20},{8,24},{12,28},{16,32},{20,36},{24,40},{28,44},{32,4... | collective-permute-start | bytes 786440 | tf_op jit(solution)/shard_map/ppermute | solution.py:36
  159.7 14.8 %collective-permute-start.7 = (bf16[1024,128]{1,0:T(8,128)(2,1)S(1)}, bf16[1024,128]{1,0:T(8,128)(2,1)S(1)}, u32[]{:S(2)}, u32[]{:S(2)}) collective-permute-start(bf16[1024,128]{1,0:T(8,128)(2,1)S(1)} %get-tuple-element.48), channel_id=1, source_target_pairs={{0,48},{4,52},{8,56},{12,60},{16,0},{20,4},{24,8},{28,12},{32,16},... | collective-permute-start | bytes 786440 | tf_op jit(solution)/shard_map/ppermute | solution.py:36
  174.4 0.7 copy-start.6
  175.1 20.4 %all-to-all-start.6 = ((bf16[4,1024,128]{2,1,0:T(8,128)(2,1)}), bf16[4,1024,128]{2,1,0:T(8,128)(2,1)S(1)}, u32[]{:S(2)}, u32[]{:S(2)}) async-start(bf16[4,1024,128]{2,1,0:T(8,128)(2,1)} %bitcast.27), calls=%async_computation.6 | async-start | bytes 2097152 | tf_op jit(solution)/shard_map/all_to_all | solution.py:44
  196.4 51.8 %collective-permute-start.8 = (bf16[1032,128]{1,0:T(8,128)(2,1)S(1)}, bf16[1032,128]{1,0:T(8,128)(2,1)S(1)}, u32[]{:S(2)}, u32[]{:S(2)}) collective-permute-start(bf16[1032,128]{1,0:T(8,128)(2,1)S(1)} %get-tuple-element.61), channel_id=1, source_target_pairs={{0,48},{4,52},{8,56},{12,60},{16,0},{20,4},{24,8},{28,12},{32,16},... | collective-permute-start | bytes 792584 | tf_op jit(solution)/shard_map/ppermute | solution.py:36
  201.5 46.7 %collective-permute-start.9 = (bf16[1024,128]{1,0:T(8,128)(2,1)S(1)}, bf16[1024,128]{1,0:T(8,128)(2,1)S(1)}, u32[]{:S(2)}, u32[]{:S(2)}) collective-permute-start(bf16[1024,128]{1,0:T(8,128)(2,1)S(1)} %add_convert_fusion.3), channel_id=1, source_target_pairs={{0,16},{4,20},{8,24},{12,28},{16,32},{20,36},{24,40},{28,44},{32,4... | collective-permute-start | bytes 786440 | tf_op jit(solution)/shard_map/ppermute | solution.py:36
  206.3 47.2 %collective-permute-start.10 = (bf16[1032,128]{1,0:T(8,128)(2,1)S(1)}, bf16[1032,128]{1,0:T(8,128)(2,1)S(1)}, u32[]{:S(2)}, u32[]{:S(2)}) collective-permute-start(bf16[1032,128]{1,0:T(8,128)(2,1)S(1)} %get-tuple-element.66), channel_id=1, source_target_pairs={{0,16},{4,20},{8,24},{12,28},{16,32},{20,36},{24,40},{28,44},{32,4... | collective-permute-start | bytes 792584 | tf_op jit(solution)/shard_map/ppermute | solution.py:36
  248.3 3.5 %copy-start.7 = (bf16[1024,128]{1,0:T(8,128)(2,1)S(1)}, bf16[1024,128]{1,0:T(8,128)(2,1)}, u32[]{:S(2)}) copy-start(bf16[1024,128]{1,0:T(8,128)(2,1)} %copy-done.6) | copy-start | bytes 786436
  248.4 13.4 %collective-permute-start.11 = (bf16[1032,128]{1,0:T(8,128)(2,1)S(1)}, bf16[1032,128]{1,0:T(8,128)(2,1)S(1)}, u32[]{:S(2)}, u32[]{:S(2)}) collective-permute-start(bf16[1032,128]{1,0:T(8,128)(2,1)S(1)} %pad_maximum_fusion.2), channel_id=1, source_target_pairs={{0,48},{4,52},{8,56},{12,60},{16,0},{20,4},{24,8},{28,12},{32,16},... | collective-permute-start | bytes 792584 | tf_op jit(solution)/shard_map/ppermute | solution.py:36
  262.7 49.1 %all-to-all-start.7 = ((bf16[16,128,128]{2,1,0:T(8,128)(2,1)}), bf16[16,128,128]{2,1,0:T(8,128)(2,1)S(1)}, u32[]{:S(2)}, u32[]{:S(2)}) async-start(bf16[16,128,128]{2,1,0:T(8,128)(2,1)} %bitcast.35), calls=%async_computation.7 | async-start | bytes 1048576 | tf_op jit(solution)/shard_map/all_to_all | solution.py:40

commit v10 on v8

--- a/solution.py
+++ b/solution.py
@@ -285,45 +285,43 @@
     query_rows = query.reshape(BLOCK, HPD * DH)
     grad_rows = grad_out.reshape(BLOCK, HPD * DH)
     own = [swap_x(arr) for arr in held]
-    below = [shift_groups(held[0], 1), None]
-    above = [shift_groups(held[0], -1), None]
-    down, _ = lax.optimization_barrier((held[1], below[0]))
-    above[1] = shift_groups(down, -1)
-    far = [shift_groups(below[0], 1), None]
-    up, far[0] = lax.optimization_barrier((held[1], far[0]))
-    below[1] = shift_groups(up, 1)
-    far[1] = shift_groups(above[1], -1)
-    ready, above[1], own = lax.optimization_barrier((held[0], above[1], own))
-    sources = [(ready, above[0], far[0], below[0]), None]
+    below = [shift_groups(arr, 1) for arr in held]
+    above = [shift_groups(arr, -1) for arr in held]
+    far = [shift_groups(below[0], 1), shift_groups(above[1], -1)]
+    ready, below[1], above[1], far[1] = lax.optimization_barrier(
+        (held[0], below[1], above[1], far[1])
+    )
+    picks = [
+        swap_x(gather_picks(index[h], sources).reshape(XS, TOPK * ROWS, DH))
+        for h, sources in enumerate(
+            ((ready, above[0], far[0], below[0]), (held[1], above[1], far[1], below[1]))
+        )
+    ]
     start = lax.axis_index("head") * (SPB * HPD) + position * HPD
     earlier = ()
     pools = []
     for h in range(HPD):
-        picks = swap_x(gather_picks(index[h], sources[h]).reshape(XS, TOPK * ROWS, DH))
         att, dq, part, sink_sum = attend(
-            h, jnp.append(use[h], start + h), sink_mine[h : h + 1], query_rows, grad_rows, own[h], picks, earlier
+            h,
+            jnp.append(use[h], start + h),
+            sink_mine[h : h + 1],
+            query_rows,
+            grad_rows,
+            own[h],
+            picks[h],
+            earlier,
         )
         earlier = (att, dq, sink_sum)
-        if h == 0:
-            part, below[1], far[1] = lax.optimization_barrier((part, below[1], far[1]))
-        else:
-            part, up_far, down_near = lax.optimization_barrier((part, up_far, down_near))
-        back = swap_x(part)
-        if h > 0:
-            up_first = shift_groups(add_rounded(pools[0][1], up_far), 1)
-            back, up_first = lax.optimization_barrier((back, up_first))
-        pools.append(pool_parts(index[h], back))
-        if h == 0:
-            up_far = shift_groups(pools[0][2], 1)
-            down_near = shift_groups(pools[0][3], -1)
-            late, _ = lax.optimization_barrier((held[1], pools[0]))
-            sources[1] = (late, above[1], far[1], below[1])
+        pools.append(pool_parts(index[h], swap_x(part)))
     main = XS * ROWS
+    up_far = shift_groups(pools[0][2], 1)
+    down_near = shift_groups(pools[0][3], -1)
     down_far = shift_groups(pools[1][2], -1)
     up_near = shift_groups(pools[1][1], 1)
+    up_last = shift_groups(add_rounded(pools[0][1], up_far), 1)
     onward = jnp.concatenate([add_rounded(pools[1][3][:main], down_far[:main]), down_far[main:]])
     down_last = shift_groups(onward, -1)
-    first = add_rounded(pools[0][0], up_first, down_near)
+    first = add_rounded(pools[0][0], up_last, down_near)
     second = add_rounded(pools[1][0][:main], up_near[:main], down_last[:main])
     terms = jnp.stack([arr[main] for arr in (pools[1][0], up_near, down_far, down_last)])
     terms = jnp.sum(terms[:, : 3 * HEADS].astype(jnp.float32).reshape(-1, HEADS), axis=0)

time: 289 us -> 285 us (0.986)
  blocking collectives: 32.7 us -> 27.4 us
    all_to_all x6, waiting for transfers between devices: 19.1 us -> 32.1 us  [swap_x(): lax.all_to_all(arr, 'ctx', 0, 0, axis_index_groups=X_GROUPS, tiled=True)]
    ppermute x12, waiting for transfers between devices: 67.2 us -> 54.4 us  [shift_groups(): return lax.ppermute(arr, 'ctx', pairs)]
    ppermute x12, starting transfers between devices: 74.2 us -> 84.7 us  [shift_groups(): return lax.ppermute(arr, 'ctx', pairs)]
    all_to_all x2, starting transfers between devices: 21.5 us -> 12 us  [swap_spread(): lax.all_to_all(arr, 'ctx', 0, 0, axis_index_groups=SPREAD_GROUPS, tiled=T...]
    psum x1, blocking collectives: 20.5 us -> 13.3 us  [body(): grad_sink = lax.psum(grad_sink, ('dp', 'head'))]
  transfers between devices with their start and end apart: 20 -> 20, of which waited for: 12 -> 12; matrix products, arithmetic and copies ran while one was open for 1% -> 2% of each run, Pallas kernels for 5% -> 7%
where the time goes in v10:
time: 285 us; the launch traced here: 280 us
  starting transfers between devices  118 us (41%)
  waiting for transfers between devices  103 us (36%)
  blocking collectives  27.4 us (10%)
  Pallas kernels  18.8 us (7%)
  local copies, waits for them, and re-layouts  8.03 us (3%)
  other arithmetic  4.09 us (1%)
    ppermute x12, starting transfers between devices, shift_groups(): return lax.ppermute(arr, 'ctx', pairs)  84.7 us
    ppermute x12, waiting for transfers between devices, shift_groups(): return lax.ppermute(arr, 'ctx', pairs)  54.4 us
    all_to_all x6, waiting for transfers between devices, swap_x(): lax.all_to_all(arr, 'ctx', 0, 0, axis_index_groups=X_GROUPS, tiled=True)  32.1 us
    all_to_all x6, starting transfers between devices, swap_x(): lax.all_to_all(arr, 'ctx', 0, 0, axis_index_groups=X_GROUPS, tiled=True)  21.2 us
    all_to_all x2, waiting for transfers between devices, swap_spread(): lax.all_to_all(arr, 'ctx', 0, 0, axis_index_groups=SPREAD_GROUPS, tiled=T...  16.1 us
    psum x1, blocking collectives, body(): grad_sink = lax.psum(terms, 'ctx', axis_index_groups=PART_GROUPS)  14.1 us
    psum x1, blocking collectives, body(): grad_sink = lax.psum(grad_sink, ('dp', 'head'))  13.3 us
    pallas_call x2, Pallas kernels, attend(): pl.pallas_call(attend_kernel, name='attend_head%d' % head, grid=(1,), in_...  13 us
  transfers between devices with their start and end apart: 20, of which 12 were waited for; matrix products, arithmetic and copies ran while one was open for 2% of the time, Pallas kernels for 7%

profile of v10, /device:TPU:24, one launch (start us, length us, event | category | flops | bytes accessed | tf_op | source)
XLA Modules:
  0.0 279.9 jit_solution(7662536128643629869)
XLA Ops:
  0.6 1.1 reshape.114
  1.8 1.1 reshape.115
  3.7 0.9 copy.28
  4.6 8.5 %all-to-all-start = ((bf16[16,128,128]{2,1,0:T(8,128)(2,1)}), bf16[16,128,128]{2,1,0:T(8,128)(2,1)S(1)}, u32[]{:S(2)}, u32[]{:S(2)}) async-start(bf16[16,128,128]{2,1,0:T(8,128)(2,1)} %bitcast.9), calls=%async_computation | async-start | bytes 1048576 | tf_op jit(solution)/shard_map/all_to_all | solution.py:41
  13.5 16.1 %all-to-all-done = bf16[16,128,128]{2,1,0:T(8,128)(2,1)S(1)} async-done(((bf16[16,128,128]{2,1,0:T(8,128)(2,1)}), bf16[16,128,128]{2,1,0:T(8,128)(2,1)S(1)}, u32[]{:S(2)}, u32[]{:S(2)}) %all-to-all-start) | async-done | bytes 524320 | tf_op jit(solution)/shard_map/all_to_all | solution.py:41
  29.6 0.8 fusion.10
  30.4 10.0 %collective-permute-start.1 = (bf16[4,256,128]{2,1,0:T(8,128)(2,1)}, bf16[4,256,128]{2,1,0:T(8,128)(2,1)S(1)}, u32[]{:S(2)}, u32[]{:S(2)}) collective-permute-start(bf16[4,256,128]{2,1,0:T(8,128)(2,1)} %bitcast.12.refs_0_), channel_id=1, source_target_pairs={{0,48},{4,52},{8,56},{12,60},{16,0},{20,4},{24,8},{28,12},{32,16},... | collective-permute-start | bytes 786440 | tf_op jit(solution)/shard_map/ppermute | solution.py:37
  40.4 1.9 collective-permute-start.4
  42.8 3.4 %all-to-all-start.1 = ((bf16[4,256,128]{2,1,0:T(8,128)(2,1)}), bf16[4,256,128]{2,1,0:T(8,128)(2,1)S(1)}, u32[]{:S(2)}, u32[]{:S(2)}) async-start(bf16[4,256,128]{2,1,0:T(8,128)(2,1)} %bitcast.12.refs_0_), calls=%async_computation.1 | async-start | bytes 524288 | tf_op jit(solution)/shard_map/all_to_all | solution.py:45
  46.2 6.9 %collective-permute-start = (bf16[4,256,128]{2,1,0:T(8,128)(2,1)}, bf16[4,256,128]{2,1,0:T(8,128)(2,1)S(1)}, u32[]{:S(2)}, u32[]{:S(2)}) collective-permute-start(bf16[4,256,128]{2,1,0:T(8,128)(2,1)} %bitcast.12.refs_0_), channel_id=1, source_target_pairs={{0,16},{4,20},{8,24},{12,28},{16,32},{20,36},{24,40},{28,44},{32,4... | collective-permute-start | bytes 786440 | tf_op jit(solution)/shard_map/ppermute | solution.py:37
  53.1 2.9 %collective-permute-start.3 = (bf16[4,256,128]{2,1,0:T(8,128)(2,1)}, bf16[4,256,128]{2,1,0:T(8,128)(2,1)S(1)}, u32[]{:S(2)}, u32[]{:S(2)}) collective-permute-start(bf16[4,256,128]{2,1,0:T(8,128)(2,1)} %bitcast.17.refs_0_), channel_id=1, source_target_pairs={{0,48},{4,52},{8,56},{12,60},{16,0},{20,4},{24,8},{28,12},{32,16},... | collective-permute-start | bytes 786440 | tf_op jit(solution)/shard_map/ppermute | solution.py:37
  56.0 7.7 %collective-permute-done.1.refs_1_ = bf16[4,256,128]{2,1,0:T(8,128)(2,1)S(1)} collective-permute-done((bf16[4,256,128]{2,1,0:T(8,128)(2,1)}, bf16[4,256,128]{2,1,0:T(8,128)(2,1)S(1)}, u32[]{:S(2)}, u32[]{:S(2)}) %collective-permute-start.1) | collective-permute-done | bytes 262176 | tf_op jit(solution)/shard_map/ppermute | solution.py:37
  63.7 7.5 %collective-permute-start.2 = (bf16[4,256,128]{2,1,0:T(8,128)(2,1)S(1)}, bf16[4,256,128]{2,1,0:T(8,128)(2,1)S(1)}, u32[]{:S(2)}, u32[]{:S(2)}) collective-permute-start(bf16[4,256,128]{2,1,0:T(8,128)(2,1)S(1)} %collective-permute-done.1.refs_1_), channel_id=1, source_target_pairs={{0,48},{4,52},{8,56},{12,60},{16,0},{20,4},{24,8},{28,12},{32,16},... | collective-permute-start | bytes 786440 | tf_op jit(solution)/shard_map/ppermute | solution.py:37
  71.2 10.8 %collective-permute-done.4.refs_3_ = bf16[4,256,128]{2,1,0:T(8,128)(2,1)S(1)} collective-permute-done((bf16[4,256,128]{2,1,0:T(8,128)(2,1)}, bf16[4,256,128]{2,1,0:T(8,128)(2,1)S(1)}, u32[]{:S(2)}, u32[]{:S(2)}) %collective-permute-start.4) | collective-permute-done | bytes 262176 | tf_op jit(solution)/shard_map/ppermute | solution.py:37
  82.0 7.4 %collective-permute-start.5 = (bf16[4,256,128]{2,1,0:T(8,128)(2,1)S(1)}, bf16[4,256,128]{2,1,0:T(8,128)(2,1)S(1)}, u32[]{:S(2)}, u32[]{:S(2)}) collective-permute-start(bf16[4,256,128]{2,1,0:T(8,128)(2,1)S(1)} %collective-permute-done.4.refs_3_), channel_id=1, source_target_pairs={{0,16},{4,20},{8,24},{12,28},{16,32},{20,36},{24,40},{28,44},{32,4... | collective-permute-start | bytes 786440 | tf_op jit(solution)/shard_map/ppermute | solution.py:37
  89.4 3.4 %all-to-all-start.3 = ((bf16[4,256,128]{2,1,0:T(8,128)(2,1)}), bf16[4,256,128]{2,1,0:T(8,128)(2,1)S(1)}, u32[]{:S(2)}, u32[]{:S(2)}) async-start(bf16[4,256,128]{2,1,0:T(8,128)(2,1)} %bitcast.17.refs_0_), calls=%async_computation.3 | async-start | bytes 524288 | tf_op jit(solution)/shard_map/all_to_all | solution.py:45
  93.1 12.4 %collective-permute-done.refs_3_ = bf16[4,256,128]{2,1,0:T(8,128)(2,1)S(1)} collective-permute-done((bf16[4,256,128]{2,1,0:T(8,128)(2,1)}, bf16[4,256,128]{2,1,0:T(8,128)(2,1)S(1)}, u32[]{:S(2)}, u32[]{:S(2)}) %collective-permute-start) | collective-permute-done | bytes 262176 | tf_op jit(solution)/shard_map/ppermute | solution.py:37
  105.5 8.5 %collective-permute-done.5.refs_2_ = bf16[4,256,128]{2,1,0:T(8,128)(2,1)S(1)} collective-permute-done((bf16[4,256,128]{2,1,0:T(8,128)(2,1)S(1)}, bf16[4,256,128]{2,1,0:T(8,128)(2,1)S(1)}, u32[]{:S(2)}, u32[]{:S(2)}) %collective-permute-start.5) | collective-permute-done | bytes 262176 | tf_op jit(solution)/shard_map/ppermute | solution.py:37
  114.0 2.0 gather_picks.3
  116.0 3.6 %all-to-all-start.4 = ((bf16[4,768,128]{2,1,0:T(8,128)(2,1)}), bf16[4,768,128]{2,1,0:T(8,128)(2,1)S(1)}, u32[]{:S(2)}, u32[]{:S(2)}) async-start(bf16[4,768,128]{2,1,0:T(8,128)(2,1)} %bitcast.23), calls=%async_computation.4 | async-start | bytes 1572864 | tf_op jit(solution)/shard_map/all_to_all | solution.py:45
  120.1 2.0 gather_picks.2
  122.1 10.3 %all-to-all-done.4 = bf16[4,768,128]{2,1,0:T(8,128)(2,1)S(1)} async-done(((bf16[4,768,128]{2,1,0:T(8,128)(2,1)}), bf16[4,768,128]{2,1,0:T(8,128)(2,1)S(1)}, u32[]{:S(2)}, u32[]{:S(2)}) %all-to-all-start.4) | async-done | bytes 786464 | tf_op jit(solution)/shard_map/all_to_all | solution.py:45
  132.4 3.5 %all-to-all-start.2 = ((bf16[4,768,128]{2,1,0:T(8,128)(2,1)}), bf16[4,768,128]{2,1,0:T(8,128)(2,1)S(1)}, u32[]{:S(2)}, u32[]{:S(2)}) async-start(bf16[4,768,128]{2,1,0:T(8,128)(2,1)} %bitcast.18), calls=%async_computation.2 | async-start | bytes 1572864 | tf_op jit(solution)/shard_map/all_to_all | solution.py:45
  136.5 6.5 %attend_head0.1 = (bf16[512,256]{1,0:T(8,128)(2,1)}, bf16[512,256]{1,0:T(8,128)(2,1)}, bf16[4,1024,128]{2,1,0:T(8,128)(2,1)}, f32[8,128]{1,0:T(8,128)S(1)}) custom-call(s32[4]{0:T(128)S(1)} %pad_add_fusion.1.use_ref, f32[1]{0:T(128)} %get-tuple-element.53.sink_ref, bf16[512,256]{1,0:T(8,128)(2,1)S(1)} %bitcast.62, bf16[512,256]{1,0:T(8,128)(2,1)S(1)} %bitcast.64, ...), custom_call_target="tpu_custom_call" | custom-call | flops 2684354560 | bytes 8388608 | tf_op jit(solution)/shard_map/attend_head0/pallas_call | solution.py:156
  143.0 4.7 %all-to-all-done.2 = bf16[4,768,128]{2,1,0:T(8,128)(2,1)S(1)} async-done(((bf16[4,768,128]{2,1,0:T(8,128)(2,1)}), bf16[4,768,128]{2,1,0:T(8,128)(2,1)S(1)}, u32[]{:S(2)}, u32[]{:S(2)}) %all-to-all-start.2) | async-done | bytes 786464 | tf_op jit(solution)/shard_map/all_to_all | solution.py:45
  147.7 3.5 %all-to-all-start.5 = ((bf16[4,1024,128]{2,1,0:T(8,128)(2,1)}), bf16[4,1024,128]{2,1,0:T(8,128)(2,1)S(1)}, u32[]{:S(2)}, u32[]{:S(2)}) async-start(bf16[4,1024,128]{2,1,0:T(8,128)(2,1)} %get-tuple-element.33), calls=%async_computation.5 | async-start | bytes 2097152 | tf_op jit(solution)/shard_map/all_to_all | solution.py:45
  151.3 6.5 %attend_head1.1 = (bf16[512,256]{1,0:T(8,128)(2,1)}, bf16[512,256]{1,0:T(8,128)(2,1)}, bf16[4,1032,128]{2,1,0:T(8,128)(2,1)}, f32[8,128]{1,0:T(8,128)}) custom-call(s32[4]{0:T(128)S(1)} %pad_add_fusion.use_ref, f32[1]{0:T(128)} %get-tuple-element.54.sink_ref, bf16[512,256]{1,0:T(8,128)(2,1)S(1)} %bitcast.63, ...), custom_call_target="tpu_custom_call", output_to_operand_aliasing={{0}: (6, {}), {1}: (7, {})} | custom-call | flops 2684354560 | bytes 8388608 | tf_op jit(solution)/shard_map/attend_head1/pallas_call | solution.py:156
  157.8 7.2 %all-to-all-done.5.part_ref = bf16[4,1024,128]{2,1,0:T(8,128)(2,1)S(1)} async-done(((bf16[4,1024,128]{2,1,0:T(8,128)(2,1)}), bf16[4,1024,128]{2,1,0:T(8,128)(2,1)S(1)}, u32[]{:S(2)}, u32[]{:S(2)}) %all-to-all-start.5) | async-done | bytes 1048608 | tf_op jit(solution)/shard_map/all_to_all | solution.py:45
  165.0 3.7 %all-to-all-start.6 = ((bf16[4,1032,128]{2,1,0:T(8,128)(2,1)}), bf16[4,1032,128]{2,1,0:T(8,128)(2,1)S(1)}, u32[]{:S(2)}, u32[]{:S(2)}) async-start(bf16[4,1032,128]{2,1,0:T(8,128)(2,1)} %get-tuple-element.38), calls=%async_computation.6 | async-start | bytes 2113536 | tf_op jit(solution)/shard_map/all_to_all | solution.py:45
  168.7 0.9 pool_parts.2
  169.6 1.9 collective-permute-start.6
  171.6 9.9 %all-to-all-done.6.part_ref = bf16[4,1032,128]{2,1,0:T(8,128)(2,1)S(1)} async-done(((bf16[4,1032,128]{2,1,0:T(8,128)(2,1)}), bf16[4,1032,128]{2,1,0:T(8,128)(2,1)S(1)}, u32[]{:S(2)}, u32[]{:S(2)}) %all-to-all-start.6) | async-done | bytes 1056800 | tf_op jit(solution)/shard_map/all_to_all | solution.py:45
  181.5 0.9 pool_parts.3
  182.4 1.9 collective-permute-start.10
  184.3 1.9 collective-permute-start.8
  186.2 7.8 %collective-permute-start.9 = (bf16[1032,128]{1,0:T(8,128)(2,1)S(1)}, bf16[1032,128]{1,0:T(8,128)(2,1)S(1)}, u32[]{:S(2)}, u32[]{:S(2)}) collective-permute-start(bf16[1032,128]{1,0:T(8,128)(2,1)S(1)} %get-tuple-element.40), channel_id=1, source_target_pairs={{0,16},{4,20},{8,24},{12,28},{16,32},{20,36},{24,40},{28,44},{32,4... | collective-permute-start | bytes 792584 | tf_op jit(solution)/shard_map/ppermute | solution.py:37
  194.1 1.0 add_convert_fusion.3
  195.1 7.8 %collective-permute-start.7 = (bf16[1024,128]{1,0:T(8,128)(2,1)S(1)}, bf16[1024,128]{1,0:T(8,128)(2,1)S(1)}, u32[]{:S(2)}, u32[]{:S(2)}) collective-permute-start(bf16[1024,128]{1,0:T(8,128)(2,1)S(1)} %add_convert_fusion.3), channel_id=1, source_target_pairs={{0,16},{4,20},{8,24},{12,28},{16,32},{20,36},{24,40},{28,44},{32,4... | collective-permute-start | bytes 786440 | tf_op jit(solution)/shard_map/ppermute | solution.py:37
  203.0 1.8 collective-permute-done.10
  204.9 26.7 %collective-permute-start.11 = (bf16[1032,128]{1,0:T(8,128)(2,1)S(1)}, bf16[1032,128]{1,0:T(8,128)(2,1)S(1)}, u32[]{:S(2)}, u32[]{:S(2)}) collective-permute-start(bf16[1032,128]{1,0:T(8,128)(2,1)S(1)} %pad_maximum_fusion.2), channel_id=1, source_target_pairs={{0,48},{4,52},{8,56},{12,60},{16,0},{20,4},{24,8},{28,12},{32,16},... | collective-permute-start | bytes 792584 | tf_op jit(solution)/shard_map/ppermute | solution.py:37
  231.6 6.6 %collective-permute-done.8 = bf16[1024,128]{1,0:T(8,128)(2,1)S(1)} collective-permute-done((bf16[1024,128]{1,0:T(8,128)(2,1)S(1)}, bf16[1024,128]{1,0:T(8,128)(2,1)S(1)}, u32[]{:S(2)}, u32[]{:S(2)}) %collective-permute-start.8) | collective-permute-done | bytes 262176 | tf_op jit(solution)/shard_map/ppermute | solution.py:37
  238.3 6.6 %collective-permute-done.11 = bf16[1032,128]{1,0:T(8,128)(2,1)S(1)} collective-permute-done((bf16[1032,128]{1,0:T(8,128)(2,1)S(1)}, bf16[1032,128]{1,0:T(8,128)(2,1)S(1)}, u32[]{:S(2)}, u32[]{:S(2)}) %collective-permute-start.11) | collective-permute-done | bytes 264224 | tf_op jit(solution)/shard_map/ppermute | solution.py:37
  245.0 0.8 pad_maximum_fusion.1
  245.8 3.6 %all-to-all-start.7 = ((bf16[16,128,128]{2,1,0:T(8,128)(2,1)}), bf16[16,128,128]{2,1,0:T(8,128)(2,1)S(1)}, u32[]{:S(2)}, u32[]{:S(2)}) async-start(bf16[16,128,128]{2,1,0:T(8,128)(2,1)} %bitcast.31), calls=%async_computation.7 | async-start | bytes 1048576 | tf_op jit(solution)/shard_map/all_to_all | solution.py:41
  250.2 14.1 %psum.14 = f32[32]{0:T(128)S(1)} all-reduce(f32[32]{0:T(128)S(1)} %reduce_sum.62), channel_id=1, replica_groups={{0,4,8,12},{16,20,24,28},{32,36,40,44},{48,52,56,60},{64,68,72,76},{80,..., use_global_device_ids=true, to_apply=%region_6.7 | all-reduce | flops 32 | bytes 256 | tf_op jit(solution)/shard_map/psum | solution.py:328
  264.3 13.3 %psum.15 = f32[32]{0:T(128)} all-reduce(f32[32]{0:T(128)S(1)} %psum.14), channel_id=1, replica_groups=mesh['dp'=2,'ctx'=64,'head'=4] {'dp','head'}, use_global_device_ids=true, to_apply=%region_7.8 | all-reduce | flops 32 | bytes 256 | tf_op jit(solution)/shard_map/psum | solution.py:329
  277.9 0.9 reshape_squeeze.15
  279.0 0.9 reshape_squeeze.14
  (58 shorter events, 4.5 us)
Async XLA Ops:
  0.6 41.7 %copy-start = (s32[1,16,8,3]{1,2,3,0:T(8,128)S(1)}, s32[1,16,8,3]{1,2,3,0:T(8,128)}, u32[]{:S(2)}) copy-start(s32[1,16,8,3]{1,2,3,0:T(8,128)} %param.11) | copy-start | bytes 4612
  3.6 9.5 %copy-start.4 = (s32[16]{0:T(128)S(1)}, s32[16]{0:T(128)}, u32[]{:S(2)}) copy-start(s32[16]{0:T(128)} %param.12) | copy-start | bytes 196
  4.6 25.0 %all-to-all-start = ((bf16[16,128,128]{2,1,0:T(8,128)(2,1)}), bf16[16,128,128]{2,1,0:T(8,128)(2,1)S(1)}, u32[]{:S(2)}, u32[]{:S(2)}) async-start(bf16[16,128,128]{2,1,0:T(8,128)(2,1)} %bitcast.9), calls=%async_computation | async-start | bytes 1048576 | tf_op jit(solution)/shard_map/all_to_all | solution.py:41
  30.4 33.3 %collective-permute-start.1 = (bf16[4,256,128]{2,1,0:T(8,128)(2,1)}, bf16[4,256,128]{2,1,0:T(8,128)(2,1)S(1)}, u32[]{:S(2)}, u32[]{:S(2)}) collective-permute-start(bf16[4,256,128]{2,1,0:T(8,128)(2,1)} %bitcast.12.refs_0_), channel_id=1, source_target_pairs={{0,48},{4,52},{8,56},{12,60},{16,0},{20,4},{24,8},{28,12},{32,16},... | collective-permute-start | bytes 786440 | tf_op jit(solution)/shard_map/ppermute | solution.py:37
  40.4 41.6 %collective-permute-start.4 = (bf16[4,256,128]{2,1,0:T(8,128)(2,1)}, bf16[4,256,128]{2,1,0:T(8,128)(2,1)S(1)}, u32[]{:S(2)}, u32[]{:S(2)}) collective-permute-start(bf16[4,256,128]{2,1,0:T(8,128)(2,1)} %bitcast.17.refs_0_), channel_id=1, source_target_pairs={{0,16},{4,20},{8,24},{12,28},{16,32},{20,36},{24,40},{28,44},{32,4... | collective-permute-start | bytes 786440 | tf_op jit(solution)/shard_map/ppermute | solution.py:37
  42.8 46.6 %all-to-all-start.1 = ((bf16[4,256,128]{2,1,0:T(8,128)(2,1)}), bf16[4,256,128]{2,1,0:T(8,128)(2,1)S(1)}, u32[]{:S(2)}, u32[]{:S(2)}) async-start(bf16[4,256,128]{2,1,0:T(8,128)(2,1)} %bitcast.12.refs_0_), calls=%async_computation.1 | async-start | bytes 524288 | tf_op jit(solution)/shard_map/all_to_all | solution.py:45
  46.2 59.2 %collective-permute-start = (bf16[4,256,128]{2,1,0:T(8,128)(2,1)}, bf16[4,256,128]{2,1,0:T(8,128)(2,1)S(1)}, u32[]{:S(2)}, u32[]{:S(2)}) collective-permute-start(bf16[4,256,128]{2,1,0:T(8,128)(2,1)} %bitcast.12.refs_0_), channel_id=1, source_target_pairs={{0,16},{4,20},{8,24},{12,28},{16,32},{20,36},{24,40},{28,44},{32,4... | collective-permute-start | bytes 786440 | tf_op jit(solution)/shard_map/ppermute | solution.py:37
  53.1 52.4 %collective-permute-start.3 = (bf16[4,256,128]{2,1,0:T(8,128)(2,1)}, bf16[4,256,128]{2,1,0:T(8,128)(2,1)S(1)}, u32[]{:S(2)}, u32[]{:S(2)}) collective-permute-start(bf16[4,256,128]{2,1,0:T(8,128)(2,1)} %bitcast.17.refs_0_), channel_id=1, source_target_pairs={{0,48},{4,52},{8,56},{12,60},{16,0},{20,4},{24,8},{28,12},{32,16},... | collective-permute-start | bytes 786440 | tf_op jit(solution)/shard_map/ppermute | solution.py:37
  63.7 41.8 %collective-permute-start.2 = (bf16[4,256,128]{2,1,0:T(8,128)(2,1)S(1)}, bf16[4,256,128]{2,1,0:T(8,128)(2,1)S(1)}, u32[]{:S(2)}, u32[]{:S(2)}) collective-permute-start(bf16[4,256,128]{2,1,0:T(8,128)(2,1)S(1)} %collective-permute-done.1.refs_1_), channel_id=1, source_target_pairs={{0,48},{4,52},{8,56},{12,60},{16,0},{20,4},{24,8},{28,12},{32,16},... | collective-permute-start | bytes 786440 | tf_op jit(solution)/shard_map/ppermute | solution.py:37
  82.0 32.0 %collective-permute-start.5 = (bf16[4,256,128]{2,1,0:T(8,128)(2,1)S(1)}, bf16[4,256,128]{2,1,0:T(8,128)(2,1)S(1)}, u32[]{:S(2)}, u32[]{:S(2)}) collective-permute-start(bf16[4,256,128]{2,1,0:T(8,128)(2,1)S(1)} %collective-permute-done.4.refs_3_), channel_id=1, source_target_pairs={{0,16},{4,20},{8,24},{12,28},{16,32},{20,36},{24,40},{28,44},{32,4... | collective-permute-start | bytes 786440 | tf_op jit(solution)/shard_map/ppermute | solution.py:37
  89.4 26.6 %all-to-all-start.3 = ((bf16[4,256,128]{2,1,0:T(8,128)(2,1)}), bf16[4,256,128]{2,1,0:T(8,128)(2,1)S(1)}, u32[]{:S(2)}, u32[]{:S(2)}) async-start(bf16[4,256,128]{2,1,0:T(8,128)(2,1)} %bitcast.17.refs_0_), calls=%async_computation.3 | async-start | bytes 524288 | tf_op jit(solution)/shard_map/all_to_all | solution.py:45
  116.0 3.7 %copy-start.5 = (f32[8]{0:T(128)S(1)}, f32[8]{0:T(128)}, u32[]{:S(2)}) copy-start(f32[8]{0:T(128)} %param.13) | copy-start | bytes 100
  116.0 16.3 %all-to-all-start.4 = ((bf16[4,768,128]{2,1,0:T(8,128)(2,1)}), bf16[4,768,128]{2,1,0:T(8,128)(2,1)S(1)}, u32[]{:S(2)}, u32[]{:S(2)}) async-start(bf16[4,768,128]{2,1,0:T(8,128)(2,1)} %bitcast.23), calls=%async_computation.4 | async-start | bytes 1572864 | tf_op jit(solution)/shard_map/all_to_all | solution.py:45
  122.1 14.5 %copy-start.1 = (bf16[1,1,1,512,256]{4,3,2,1,0:T(8,128)(2,1)S(1)}, bf16[1,1,1,512,256]{4,3,2,1,0:T(8,128)(2,1)}, u32[]{:S(2)}) copy-start(bf16[1,1,1,512,256]{4,3,2,1,0:T(8,128)(2,1)} %param.7) | copy-start | bytes 786436
  122.1 14.5 %copy-start.2 = (bf16[1,1,1,512,256]{4,3,2,1,0:T(8,128)(2,1)S(1)}, bf16[1,1,1,512,256]{4,3,2,1,0:T(8,128)(2,1)}, u32[]{:S(2)}) copy-start(bf16[1,1,1,512,256]{4,3,2,1,0:T(8,128)(2,1)} %param.10) | copy-start | bytes 786436
  132.4 15.4 %all-to-all-start.2 = ((bf16[4,768,128]{2,1,0:T(8,128)(2,1)}), bf16[4,768,128]{2,1,0:T(8,128)(2,1)S(1)}, u32[]{:S(2)}, u32[]{:S(2)}) async-start(bf16[4,768,128]{2,1,0:T(8,128)(2,1)} %bitcast.18), calls=%async_computation.2 | async-start | bytes 1572864 | tf_op jit(solution)/shard_map/all_to_all | solution.py:45
  147.7 17.3 %all-to-all-start.5 = ((bf16[4,1024,128]{2,1,0:T(8,128)(2,1)}), bf16[4,1024,128]{2,1,0:T(8,128)(2,1)S(1)}, u32[]{:S(2)}, u32[]{:S(2)}) async-start(bf16[4,1024,128]{2,1,0:T(8,128)(2,1)} %get-tuple-element.33), calls=%async_computation.5 | async-start | bytes 2097152 | tf_op jit(solution)/shard_map/all_to_all | solution.py:45
  165.0 16.4 %all-to-all-start.6 = ((bf16[4,1032,128]{2,1,0:T(8,128)(2,1)}), bf16[4,1032,128]{2,1,0:T(8,128)(2,1)S(1)}, u32[]{:S(2)}, u32[]{:S(2)}) async-start(bf16[4,1032,128]{2,1,0:T(8,128)(2,1)} %get-tuple-element.38), calls=%async_computation.6 | async-start | bytes 2113536 | tf_op jit(solution)/shard_map/all_to_all | solution.py:45
  169.6 24.4 %collective-permute-start.6 = (bf16[1024,128]{1,0:T(8,128)(2,1)S(1)}, bf16[1024,128]{1,0:T(8,128)(2,1)}, u32[]{:S(2)}, u32[]{:S(2)}) collective-permute-start(bf16[1024,128]{1,0:T(8,128)(2,1)S(1)} %get-tuple-element.36), channel_id=1, source_target_pairs={{0,16},{4,20},{8,24},{12,28},{16,32},{20,36},{24,40},{28,44},{32,4... | collective-permute-start | bytes 786440 | tf_op jit(solution)/shard_map/ppermute | solution.py:37
  182.4 22.4 %collective-permute-start.10 = (bf16[1032,128]{1,0:T(8,128)(2,1)S(1)}, bf16[1032,128]{1,0:T(8,128)(2,1)S(1)}, u32[]{:S(2)}, u32[]{:S(2)}) collective-permute-start(bf16[1032,128]{1,0:T(8,128)(2,1)S(1)} %get-tuple-element.42), channel_id=1, source_target_pairs={{0,48},{4,52},{8,56},{12,60},{16,0},{20,4},{24,8},{28,12},{32,16},... | collective-permute-start | bytes 792584 | tf_op jit(solution)/shard_map/ppermute | solution.py:37
  184.3 53.9 %collective-permute-start.8 = (bf16[1024,128]{1,0:T(8,128)(2,1)S(1)}, bf16[1024,128]{1,0:T(8,128)(2,1)S(1)}, u32[]{:S(2)}, u32[]{:S(2)}) collective-permute-start(bf16[1024,128]{1,0:T(8,128)(2,1)S(1)} %get-tuple-element.37), channel_id=1, source_target_pairs={{0,48},{4,52},{8,56},{12,60},{16,0},{20,4},{24,8},{28,12},{32,16},... | collective-permute-start | bytes 786440 | tf_op jit(solution)/shard_map/ppermute | solution.py:37
  186.2 52.0 %collective-permute-start.9 = (bf16[1032,128]{1,0:T(8,128)(2,1)S(1)}, bf16[1032,128]{1,0:T(8,128)(2,1)S(1)}, u32[]{:S(2)}, u32[]{:S(2)}) collective-permute-start(bf16[1032,128]{1,0:T(8,128)(2,1)S(1)} %get-tuple-element.40), channel_id=1, source_target_pairs={{0,16},{4,20},{8,24},{12,28},{16,32},{20,36},{24,40},{28,44},{32,4... | collective-permute-start | bytes 792584 | tf_op jit(solution)/shard_map/ppermute | solution.py:37
  195.1 43.1 %collective-permute-start.7 = (bf16[1024,128]{1,0:T(8,128)(2,1)S(1)}, bf16[1024,128]{1,0:T(8,128)(2,1)S(1)}, u32[]{:S(2)}, u32[]{:S(2)}) collective-permute-start(bf16[1024,128]{1,0:T(8,128)(2,1)S(1)} %add_convert_fusion.3), channel_id=1, source_target_pairs={{0,16},{4,20},{8,24},{12,28},{16,32},{20,36},{24,40},{28,44},{32,4... | collective-permute-start | bytes 786440 | tf_op jit(solution)/shard_map/ppermute | solution.py:37
  204.9 40.0 %collective-permute-start.11 = (bf16[1032,128]{1,0:T(8,128)(2,1)S(1)}, bf16[1032,128]{1,0:T(8,128)(2,1)S(1)}, u32[]{:S(2)}, u32[]{:S(2)}) collective-permute-start(bf16[1032,128]{1,0:T(8,128)(2,1)S(1)} %pad_maximum_fusion.2), channel_id=1, source_target_pairs={{0,48},{4,52},{8,56},{12,60},{16,0},{20,4},{24,8},{28,12},{32,16},... | collective-permute-start | bytes 792584 | tf_op jit(solution)/shard_map/ppermute | solution.py:37
  238.3 7.5 %copy-start.3 = (bf16[1032,128]{1,0:T(8,128)(2,1)}, bf16[1032,128]{1,0:T(8,128)(2,1)S(1)}, u32[]{:S(2)}) copy-start(bf16[1032,128]{1,0:T(8,128)(2,1)S(1)} %collective-permute-done.9) | copy-start | bytes 792580
  245.8 31.8 %all-to-all-start.7 = ((bf16[16,128,128]{2,1,0:T(8,128)(2,1)}), bf16[16,128,128]{2,1,0:T(8,128)(2,1)S(1)}, u32[]{:S(2)}, u32[]{:S(2)}) async-start(bf16[16,128,128]{2,1,0:T(8,128)(2,1)} %bitcast.31), calls=%async_computation.7 | async-start | bytes 1048576 | tf_op jit(solution)/shard_map/all_to_all | solution.py:41

commit v11 on v10

--- a/solution.py
+++ b/solution.py
@@ -25,6 +25,7 @@
 NEG = -1e30
 
 SPREAD_GROUPS = [[x * ZS + g * SPB + r for x in range(XS) for r in range(SPB)] for g in range(ZG)]
+FAR_GROUPS = [[x * ZS + g * SPB + r for g in range(ZG)] for x in range(XS) for r in range(SPB)]
 PART_GROUPS = [[s * SPB + r for r in range(SPB)] for s in range(XS * ZG)]
 X_GROUPS = [[x * ZS + z for x in range(XS)] for z in range(ZS)]
 
@@ -223,18 +224,19 @@
         total = terms
         for term in range(1, 4):
             total = total + pltpu.roll(terms, term * HEADS, 1)
-        for ref in out_refs:
-            ref[XS * ROWS :] = split_terms(total)
+        refs[ZG][...] = total
 
 
 def pool_parts(index, parts):
-    shape = (XS * ROWS + parts.shape[1] - KINDS * ROWS, DH)
+    shapes = [jax.ShapeDtypeStruct((XS * ROWS, DH), jnp.bfloat16)] * ZG
+    if parts.shape[1] > KINDS * ROWS:
+        shapes = shapes + [jax.ShapeDtypeStruct((EXTRA, 128), jnp.float32)]
     return pl.pallas_call(
         pool_kernel,
         name="pool_parts",
         in_specs=[pl.BlockSpec(memory_space=pltpu.SMEM), pl.BlockSpec(memory_space=pltpu.VMEM)],
-        out_specs=tuple(pl.BlockSpec(memory_space=pltpu.VMEM) for _ in range(ZG)),
-        out_shape=tuple(jax.ShapeDtypeStruct(shape, jnp.bfloat16) for _ in range(ZG)),
+        out_specs=[pl.BlockSpec(memory_space=pltpu.VMEM)] * len(shapes),
+        out_shape=shapes,
         scratch_shapes=[pltpu.VMEM((ZG * XS, ROWS, DH), jnp.float32)],
         compiler_params=pltpu.CompilerParams(vmem_limit_bytes=16 << 20),
         cost_estimate=pl.CostEstimate(flops=1 << 20, transcendentals=0, bytes_accessed=4 << 20),
@@ -313,20 +315,18 @@
         )
         earlier = (att, dq, sink_sum)
         pools.append(pool_parts(index[h], swap_x(part)))
-    main = XS * ROWS
     up_far = shift_groups(pools[0][2], 1)
     down_near = shift_groups(pools[0][3], -1)
     down_far = shift_groups(pools[1][2], -1)
     up_near = shift_groups(pools[1][1], 1)
     up_last = shift_groups(add_rounded(pools[0][1], up_far), 1)
-    onward = jnp.concatenate([add_rounded(pools[1][3][:main], down_far[:main]), down_far[main:]])
-    down_last = shift_groups(onward, -1)
+    down_last = shift_groups(add_rounded(pools[1][3], down_far), -1)
     first = add_rounded(pools[0][0], up_last, down_near)
-    second = add_rounded(pools[1][0][:main], up_near[:main], down_last[:main])
-    terms = jnp.stack([arr[main] for arr in (pools[1][0], up_near, down_far, down_last)])
-    terms = jnp.sum(terms[:, : 3 * HEADS].astype(jnp.float32).reshape(-1, HEADS), axis=0)
-    grad_sink = lax.psum(terms, "ctx", axis_index_groups=PART_GROUPS)
-    grad_sink = lax.psum(grad_sink, ("dp", "head"))
+    second = add_rounded(pools[1][0], up_near, down_last)
+    grad_sink = lax.psum(pools[1][ZG][0, :HEADS], ("dp", "head"))
+    grad_sink = lax.psum(grad_sink, "ctx", axis_index_groups=PART_GROUPS)
+    second, grad_sink = lax.optimization_barrier((second, grad_sink))
+    grad_sink = lax.psum(grad_sink, "ctx", axis_index_groups=FAR_GROUPS)
     pooled = jnp.stack([arr.reshape(XS * SPB, 2 * FRAG, DH) for arr in (first, second)], axis=1)
     homed = swap_spread(pooled.reshape(XS * SPB, HPD * 2 * FRAG, DH))
     totals = jnp.transpose(homed.reshape(XS, SPB, HPD, 2, FRAG, DH), (3, 0, 4, 1, 2, 5))

time: 285 us -> 287 us (level)
  waiting for transfers between devices: 103 us -> 90.3 us
  blocking collectives: 27.4 us -> 38.3 us
  starting transfers between devices: 118 us -> 123 us
    ppermute x12, starting transfers between devices: 84.7 us -> 69 us  [shift_groups(): return lax.ppermute(arr, 'ctx', pairs)]
    all_to_all x6, starting transfers between devices: 21.2 us -> 36.6 us  [swap_x(): lax.all_to_all(arr, 'ctx', 0, 0, axis_index_groups=X_GROUPS, tiled=True)]
    psum x2 -> x3, blocking collectives: 27.4 us -> 38.3 us  [the longest x1 16.9 us: body(): grad_sink = lax.psum(grad_sink, 'ctx', axis_index_groups=FAR_GROUPS)]
    all_to_all x6, waiting for transfers between devices: 32.1 us -> 24.7 us  [swap_x(): lax.all_to_all(arr, 'ctx', 0, 0, axis_index_groups=X_GROUPS, tiled=True)]
    all_to_all x2, starting transfers between devices: 12 us -> 17.7 us  [swap_spread(): lax.all_to_all(arr, 'ctx', 0, 0, axis_index_groups=SPREAD_GROUPS, tiled=T...]
    ppermute x12, waiting for transfers between devices: 54.4 us -> 49.5 us  [shift_groups(): return lax.ppermute(arr, 'ctx', pairs)]
  transfers between devices with their start and end apart: 20 -> 20, of which waited for: 12 -> 10; matrix products, arithmetic and copies ran while one was open for 2% -> 1% of each run, Pallas kernels for 7% -> 7%
where the time goes in v11:
time: 287 us; the launch traced here: 282 us
  starting transfers between devices  123 us (43%)
  waiting for transfers between devices  90.3 us (31%)
  blocking collectives  38.3 us (13%)
  Pallas kernels  18.8 us (7%)
  local copies, waits for them, and re-layouts  7.25 us (3%)
  other arithmetic  3.08 us (1%)
    ppermute x12, starting transfers between devices, shift_groups(): return lax.ppermute(arr, 'ctx', pairs)  69 us
    ppermute x12, waiting for transfers between devices, shift_groups(): return lax.ppermute(arr, 'ctx', pairs)  49.5 us
    all_to_all x6, starting transfers between devices, swap_x(): lax.all_to_all(arr, 'ctx', 0, 0, axis_index_groups=X_GROUPS, tiled=True)  36.6 us
    all_to_all x6, waiting for transfers between devices, swap_x(): lax.all_to_all(arr, 'ctx', 0, 0, axis_index_groups=X_GROUPS, tiled=True)  24.7 us
    all_to_all x2, starting transfers between devices, swap_spread(): lax.all_to_all(arr, 'ctx', 0, 0, axis_index_groups=SPREAD_GROUPS, tiled=T...  17.7 us
    psum x1, blocking collectives, body(): grad_sink = lax.psum(grad_sink, 'ctx', axis_index_groups=FAR_GROUPS)  16.9 us
    all_to_all x2, waiting for transfers between devices, swap_spread(): lax.all_to_all(arr, 'ctx', 0, 0, axis_index_groups=SPREAD_GROUPS, tiled=T...  16.1 us
    psum x1, blocking collectives, body(): grad_sink = lax.psum(pools[1][ZG][0, :HEADS], ('dp', 'head'))  13.1 us
  transfers between devices with their start and end apart: 20, of which 10 were waited for; matrix products, arithmetic and copies ran while one was open for 1% of the time, Pallas kernels for 7%

profile of v11, /device:TPU:24, one launch (start us, length us, event | category | flops | bytes accessed | tf_op | source)
XLA Modules:
  0.0 282.0 jit_solution(8129427136678918787)
XLA Ops:
  0.6 1.1 reshape.108
  1.8 1.1 reshape.109
  2.9 0.7 pad_maximum_fusion
  3.7 0.9 copy.28
  4.6 8.5 %all-to-all-start = ((bf16[16,128,128]{2,1,0:T(8,128)(2,1)}), bf16[16,128,128]{2,1,0:T(8,128)(2,1)S(1)}, u32[]{:S(2)}, u32[]{:S(2)}) async-start(bf16[16,128,128]{2,1,0:T(8,128)(2,1)} %bitcast.9), calls=%async_computation | async-start | bytes 1048576 | tf_op jit(solution)/shard_map/all_to_all | solution.py:42
  13.5 16.1 %all-to-all-done = bf16[16,128,128]{2,1,0:T(8,128)(2,1)S(1)} async-done(((bf16[16,128,128]{2,1,0:T(8,128)(2,1)}), bf16[16,128,128]{2,1,0:T(8,128)(2,1)S(1)}, u32[]{:S(2)}, u32[]{:S(2)}) %all-to-all-start) | async-done | bytes 524320 | tf_op jit(solution)/shard_map/all_to_all | solution.py:42
  29.6 0.8 fusion.10
  30.4 10.0 %collective-permute-start.1 = (bf16[4,256,128]{2,1,0:T(8,128)(2,1)}, bf16[4,256,128]{2,1,0:T(8,128)(2,1)S(1)}, u32[]{:S(2)}, u32[]{:S(2)}) collective-permute-start(bf16[4,256,128]{2,1,0:T(8,128)(2,1)} %bitcast.12.refs_0_), channel_id=1, source_target_pairs={{0,48},{4,52},{8,56},{12,60},{16,0},{20,4},{24,8},{28,12},{32,16},... | collective-permute-start | bytes 786440 | tf_op jit(solution)/shard_map/ppermute | solution.py:38
  40.4 1.9 collective-permute-start.4
  42.8 6.9 %collective-permute-start = (bf16[4,256,128]{2,1,0:T(8,128)(2,1)}, bf16[4,256,128]{2,1,0:T(8,128)(2,1)S(1)}, u32[]{:S(2)}, u32[]{:S(2)}) collective-permute-start(bf16[4,256,128]{2,1,0:T(8,128)(2,1)} %bitcast.12.refs_0_), channel_id=1, source_target_pairs={{0,16},{4,20},{8,24},{12,28},{16,32},{20,36},{24,40},{28,44},{32,4... | collective-permute-start | bytes 786440 | tf_op jit(solution)/shard_map/ppermute | solution.py:38
  49.7 2.9 %collective-permute-start.3 = (bf16[4,256,128]{2,1,0:T(8,128)(2,1)}, bf16[4,256,128]{2,1,0:T(8,128)(2,1)S(1)}, u32[]{:S(2)}, u32[]{:S(2)}) collective-permute-start(bf16[4,256,128]{2,1,0:T(8,128)(2,1)} %bitcast.17.refs_0_), channel_id=1, source_target_pairs={{0,48},{4,52},{8,56},{12,60},{16,0},{20,4},{24,8},{28,12},{32,16},... | collective-permute-start | bytes 786440 | tf_op jit(solution)/shard_map/ppermute | solution.py:38
  52.6 3.4 %all-to-all-start.3 = ((bf16[4,256,128]{2,1,0:T(8,128)(2,1)}), bf16[4,256,128]{2,1,0:T(8,128)(2,1)S(1)}, u32[]{:S(2)}, u32[]{:S(2)}) async-start(bf16[4,256,128]{2,1,0:T(8,128)(2,1)} %bitcast.17.refs_0_), calls=%async_computation.3 | async-start | bytes 524288 | tf_op jit(solution)/shard_map/all_to_all | solution.py:46
  56.0 11.6 %collective-permute-done.1.refs_1_ = bf16[4,256,128]{2,1,0:T(8,128)(2,1)S(1)} collective-permute-done((bf16[4,256,128]{2,1,0:T(8,128)(2,1)}, bf16[4,256,128]{2,1,0:T(8,128)(2,1)S(1)}, u32[]{:S(2)}, u32[]{:S(2)}) %collective-permute-start.1) | collective-permute-done | bytes 262176 | tf_op jit(solution)/shard_map/ppermute | solution.py:38
  67.6 7.4 %collective-permute-start.2 = (bf16[4,256,128]{2,1,0:T(8,128)(2,1)S(1)}, bf16[4,256,128]{2,1,0:T(8,128)(2,1)S(1)}, u32[]{:S(2)}, u32[]{:S(2)}) collective-permute-start(bf16[4,256,128]{2,1,0:T(8,128)(2,1)S(1)} %collective-permute-done.1.refs_1_), channel_id=1, source_target_pairs={{0,48},{4,52},{8,56},{12,60},{16,0},{20,4},{24,8},{28,12},{32,16},... | collective-permute-start | bytes 786440 | tf_op jit(solution)/shard_map/ppermute | solution.py:38
  75.1 6.9 %collective-permute-done.4.refs_3_ = bf16[4,256,128]{2,1,0:T(8,128)(2,1)S(1)} collective-permute-done((bf16[4,256,128]{2,1,0:T(8,128)(2,1)}, bf16[4,256,128]{2,1,0:T(8,128)(2,1)S(1)}, u32[]{:S(2)}, u32[]{:S(2)}) %collective-permute-start.4) | collective-permute-done | bytes 262176 | tf_op jit(solution)/shard_map/ppermute | solution.py:38
  82.0 7.3 %collective-permute-start.5 = (bf16[4,256,128]{2,1,0:T(8,128)(2,1)S(1)}, bf16[4,256,128]{2,1,0:T(8,128)(2,1)S(1)}, u32[]{:S(2)}, u32[]{:S(2)}) collective-permute-start(bf16[4,256,128]{2,1,0:T(8,128)(2,1)S(1)} %collective-permute-done.4.refs_3_), channel_id=1, source_target_pairs={{0,16},{4,20},{8,24},{12,28},{16,32},{20,36},{24,40},{28,44},{32,4... | collective-permute-start | bytes 786440 | tf_op jit(solution)/shard_map/ppermute | solution.py:38
  89.4 10.3 %all-to-all-start.1 = ((bf16[4,256,128]{2,1,0:T(8,128)(2,1)}), bf16[4,256,128]{2,1,0:T(8,128)(2,1)S(1)}, u32[]{:S(2)}, u32[]{:S(2)}) async-start(bf16[4,256,128]{2,1,0:T(8,128)(2,1)} %bitcast.12.refs_0_), calls=%async_computation.1 | async-start | bytes 524288 | tf_op jit(solution)/shard_map/all_to_all | solution.py:46
  99.8 1.4 collective-permute-done.refs_3_
  101.2 5.6 %collective-permute-done.5.refs_2_ = bf16[4,256,128]{2,1,0:T(8,128)(2,1)S(1)} collective-permute-done((bf16[4,256,128]{2,1,0:T(8,128)(2,1)S(1)}, bf16[4,256,128]{2,1,0:T(8,128)(2,1)S(1)}, u32[]{:S(2)}, u32[]{:S(2)}) %collective-permute-start.5) | collective-permute-done | bytes 262176 | tf_op jit(solution)/shard_map/ppermute | solution.py:38
  106.8 2.0 gather_picks.3
  108.8 12.0 %all-to-all-start.4 = ((bf16[4,768,128]{2,1,0:T(8,128)(2,1)}), bf16[4,768,128]{2,1,0:T(8,128)(2,1)S(1)}, u32[]{:S(2)}, u32[]{:S(2)}) async-start(bf16[4,768,128]{2,1,0:T(8,128)(2,1)} %bitcast.23), calls=%async_computation.4 | async-start | bytes 1572864 | tf_op jit(solution)/shard_map/all_to_all | solution.py:46
  121.2 2.0 gather_picks.2
  123.2 9.7 %all-to-all-done.4 = bf16[4,768,128]{2,1,0:T(8,128)(2,1)S(1)} async-done(((bf16[4,768,128]{2,1,0:T(8,128)(2,1)}), bf16[4,768,128]{2,1,0:T(8,128)(2,1)S(1)}, u32[]{:S(2)}, u32[]{:S(2)}) %all-to-all-start.4) | async-done | bytes 786464 | tf_op jit(solution)/shard_map/all_to_all | solution.py:46
  132.9 3.5 %all-to-all-start.2 = ((bf16[4,768,128]{2,1,0:T(8,128)(2,1)}), bf16[4,768,128]{2,1,0:T(8,128)(2,1)S(1)}, u32[]{:S(2)}, u32[]{:S(2)}) async-start(bf16[4,768,128]{2,1,0:T(8,128)(2,1)} %bitcast.18), calls=%async_computation.2 | async-start | bytes 1572864 | tf_op jit(solution)/shard_map/all_to_all | solution.py:46
  136.5 0.6 fusion.12
  137.0 6.5 %attend_head0.1 = (bf16[512,256]{1,0:T(8,128)(2,1)}, bf16[512,256]{1,0:T(8,128)(2,1)}, bf16[4,1024,128]{2,1,0:T(8,128)(2,1)}, f32[8,128]{1,0:T(8,128)S(1)}) custom-call(s32[4]{0:T(128)S(1)} %pad_add_fusion.1.use_ref, f32[1]{0:T(128)} %get-tuple-element.59.sink_ref, bf16[512,256]{1,0:T(8,128)(2,1)S(1)} %bitcast.64, bf16[512,256]{1,0:T(8,128)(2,1)S(1)} %bitcast.66, ...), custom_call_target="tpu_custom_call" | custom-call | flops 2684354560 | bytes 8388608 | tf_op jit(solution)/shard_map/attend_head0/pallas_call | solution.py:157
  143.5 4.0 %all-to-all-done.2 = bf16[4,768,128]{2,1,0:T(8,128)(2,1)S(1)} async-done(((bf16[4,768,128]{2,1,0:T(8,128)(2,1)}), bf16[4,768,128]{2,1,0:T(8,128)(2,1)S(1)}, u32[]{:S(2)}, u32[]{:S(2)}) %all-to-all-start.2) | async-done | bytes 786464 | tf_op jit(solution)/shard_map/all_to_all | solution.py:46
  147.5 3.6 %all-to-all-start.5 = ((bf16[4,1024,128]{2,1,0:T(8,128)(2,1)}), bf16[4,1024,128]{2,1,0:T(8,128)(2,1)S(1)}, u32[]{:S(2)}, u32[]{:S(2)}) async-start(bf16[4,1024,128]{2,1,0:T(8,128)(2,1)} %get-tuple-element.36), calls=%async_computation.5 | async-start | bytes 2097152 | tf_op jit(solution)/shard_map/all_to_all | solution.py:46
  151.2 6.5 %attend_head1.1 = (bf16[512,256]{1,0:T(8,128)(2,1)}, bf16[512,256]{1,0:T(8,128)(2,1)}, bf16[4,1032,128]{2,1,0:T(8,128)(2,1)}, f32[8,128]{1,0:T(8,128)}) custom-call(s32[4]{0:T(128)S(1)} %pad_add_fusion.use_ref, f32[1]{0:T(128)} %get-tuple-element.60.sink_ref, bf16[512,256]{1,0:T(8,128)(2,1)S(1)} %bitcast.65, ...), custom_call_target="tpu_custom_call", output_to_operand_aliasing={{0}: (6, {}), {1}: (7, {})} | custom-call | flops 2684354560 | bytes 8388608 | tf_op jit(solution)/shard_map/attend_head1/pallas_call | solution.py:157
  157.7 6.1 %all-to-all-done.5.part_ref = bf16[4,1024,128]{2,1,0:T(8,128)(2,1)S(1)} async-done(((bf16[4,1024,128]{2,1,0:T(8,128)(2,1)}), bf16[4,1024,128]{2,1,0:T(8,128)(2,1)S(1)}, u32[]{:S(2)}, u32[]{:S(2)}) %all-to-all-start.5) | async-done | bytes 1048608 | tf_op jit(solution)/shard_map/all_to_all | solution.py:46
  163.8 3.7 %all-to-all-start.6 = ((bf16[4,1032,128]{2,1,0:T(8,128)(2,1)}), bf16[4,1032,128]{2,1,0:T(8,128)(2,1)S(1)}, u32[]{:S(2)}, u32[]{:S(2)}) async-start(bf16[4,1032,128]{2,1,0:T(8,128)(2,1)} %get-tuple-element.41), calls=%async_computation.6 | async-start | bytes 2113536 | tf_op jit(solution)/shard_map/all_to_all | solution.py:46
  167.6 0.9 pool_parts.2
  168.5 5.6 %collective-permute-start.6 = (bf16[1024,128]{1,0:T(8,128)(2,1)S(1)}, bf16[1024,128]{1,0:T(8,128)(2,1)S(1)}, u32[]{:S(2)}, u32[]{:S(2)}) collective-permute-start(bf16[1024,128]{1,0:T(8,128)(2,1)S(1)} %get-tuple-element.39), channel_id=1, source_target_pairs={{0,16},{4,20},{8,24},{12,28},{16,32},{20,36},{24,40},{28,44},{32,4... | collective-permute-start | bytes 786440 | tf_op jit(solution)/shard_map/ppermute | solution.py:38
  174.1 4.9 %all-to-all-done.6.part_ref = bf16[4,1032,128]{2,1,0:T(8,128)(2,1)S(1)} async-done(((bf16[4,1032,128]{2,1,0:T(8,128)(2,1)}), bf16[4,1032,128]{2,1,0:T(8,128)(2,1)S(1)}, u32[]{:S(2)}, u32[]{:S(2)}) %all-to-all-start.6) | async-done | bytes 1056800 | tf_op jit(solution)/shard_map/all_to_all | solution.py:46
  178.9 0.9 pool_parts.3
  179.9 5.4 %collective-permute-start.10 = (bf16[1024,128]{1,0:T(8,128)(2,1)S(1)}, bf16[1024,128]{1,0:T(8,128)(2,1)S(1)}, u32[]{:S(2)}, u32[]{:S(2)}) collective-permute-start(bf16[1024,128]{1,0:T(8,128)(2,1)S(1)} %get-tuple-element.45), channel_id=1, source_target_pairs={{0,48},{4,52},{8,56},{12,60},{16,0},{20,4},{24,8},{28,12},{32,16},... | collective-permute-start | bytes 786440 | tf_op jit(solution)/shard_map/ppermute | solution.py:38
  185.3 1.9 collective-permute-start.8
  187.3 7.8 %collective-permute-start.9 = (bf16[1024,128]{1,0:T(8,128)(2,1)S(1)}, bf16[1024,128]{1,0:T(8,128)(2,1)S(1)}, u32[]{:S(2)}, u32[]{:S(2)}) collective-permute-start(bf16[1024,128]{1,0:T(8,128)(2,1)S(1)} %get-tuple-element.43), channel_id=1, source_target_pairs={{0,16},{4,20},{8,24},{12,28},{16,32},{20,36},{24,40},{28,44},{32,4... | collective-permute-start | bytes 786440 | tf_op jit(solution)/shard_map/ppermute | solution.py:38
  195.2 4.3 %collective-permute-start.7 = (bf16[1024,128]{1,0:T(8,128)(2,1)S(1)}, bf16[1024,128]{1,0:T(8,128)(2,1)S(1)}, u32[]{:S(2)}, u32[]{:S(2)}) collective-permute-start(bf16[1024,128]{1,0:T(8,128)(2,1)S(1)} %add_convert_fusion.3), channel_id=1, source_target_pairs={{0,16},{4,20},{8,24},{12,28},{16,32},{20,36},{24,40},{28,44},{32,4... | collective-permute-start | bytes 786440 | tf_op jit(solution)/shard_map/ppermute | solution.py:38
  199.5 24.1 %collective-permute-done.10 = bf16[1024,128]{1,0:T(8,128)(2,1)S(1)} collective-permute-done((bf16[1024,128]{1,0:T(8,128)(2,1)S(1)}, bf16[1024,128]{1,0:T(8,128)(2,1)S(1)}, u32[]{:S(2)}, u32[]{:S(2)}) %collective-permute-start.10) | collective-permute-done | bytes 262176 | tf_op jit(solution)/shard_map/ppermute | solution.py:38
  223.6 7.5 %collective-permute-start.11 = (bf16[1024,128]{1,0:T(8,128)(2,1)S(1)}, bf16[1024,128]{1,0:T(8,128)(2,1)S(1)}, u32[]{:S(2)}, u32[]{:S(2)}) collective-permute-start(bf16[1024,128]{1,0:T(8,128)(2,1)S(1)} %add_convert_fusion.1), channel_id=1, source_target_pairs={{0,48},{4,52},{8,56},{12,60},{16,0},{20,4},{24,8},{28,12},{32,16},... | collective-permute-start | bytes 786440 | tf_op jit(solution)/shard_map/ppermute | solution.py:38
  231.1 13.1 %psum.21 = f32[32]{0:T(128)S(1)} all-reduce(f32[32]{0:T(128)S(1)} %slice_bitcast_fusion), channel_id=1, replica_groups=mesh['dp'=2,'ctx'=64,'head'=4] {'dp','head'}, use_global_device_ids=true, to_apply=%region_5.6 | all-reduce | flops 32 | bytes 256 | tf_op jit(solution)/shard_map/psum | solution.py:326
  244.3 8.4 %psum.22 = f32[32]{0:T(128)S(1)} all-reduce(f32[32]{0:T(128)S(1)} %psum.21), channel_id=1, replica_groups={{0,4,8,12},{16,20,24,28},{32,36,40,44},{48,52,56,60},{64,68,72,76},{80,..., use_global_device_ids=true, to_apply=%region_6.7 | all-reduce | flops 32 | bytes 256 | tf_op jit(solution)/shard_map/psum | solution.py:327
  252.9 0.8 pad_maximum_fusion.1
  253.7 9.2 %all-to-all-start.7 = ((bf16[16,128,128]{2,1,0:T(8,128)(2,1)}), bf16[16,128,128]{2,1,0:T(8,128)(2,1)S(1)}, u32[]{:S(2)}, u32[]{:S(2)}) async-start(bf16[16,128,128]{2,1,0:T(8,128)(2,1)} %bitcast.32), calls=%async_computation.7 | async-start | bytes 1048576 | tf_op jit(solution)/shard_map/all_to_all | solution.py:42
  263.0 16.9 %psum.23 = f32[32]{0:T(128)} all-reduce(f32[32]{0:T(128)S(1)} %psum.22), channel_id=1, replica_groups={{0,16,32,48},{4,20,36,52},{8,24,40,56},{12,28,44,60},{64,80,96,112},{68..., use_global_device_ids=true, to_apply=%region_7.8 | all-reduce | flops 32 | bytes 256 | tf_op jit(solution)/shard_map/psum | solution.py:329
  280.1 0.9 reshape_squeeze.14
  281.2 0.9 reshape_squeeze.15
  (50 shorter events, 2.5 us)
Async XLA Ops:
  0.6 41.7 %copy-start = (s32[1,16,8,3]{1,2,3,0:T(8,128)S(1)}, s32[1,16,8,3]{1,2,3,0:T(8,128)}, u32[]{:S(2)}) copy-start(s32[1,16,8,3]{1,2,3,0:T(8,128)} %param.11) | copy-start | bytes 4612
  3.6 9.5 %copy-start.4 = (s32[16]{0:T(128)S(1)}, s32[16]{0:T(128)}, u32[]{:S(2)}) copy-start(s32[16]{0:T(128)} %param.12) | copy-start | bytes 196
  4.6 25.0 %all-to-all-start = ((bf16[16,128,128]{2,1,0:T(8,128)(2,1)}), bf16[16,128,128]{2,1,0:T(8,128)(2,1)S(1)}, u32[]{:S(2)}, u32[]{:S(2)}) async-start(bf16[16,128,128]{2,1,0:T(8,128)(2,1)} %bitcast.9), calls=%async_computation | async-start | bytes 1048576 | tf_op jit(solution)/shard_map/all_to_all | solution.py:42
  30.4 37.2 %collective-permute-start.1 = (bf16[4,256,128]{2,1,0:T(8,128)(2,1)}, bf16[4,256,128]{2,1,0:T(8,128)(2,1)S(1)}, u32[]{:S(2)}, u32[]{:S(2)}) collective-permute-start(bf16[4,256,128]{2,1,0:T(8,128)(2,1)} %bitcast.12.refs_0_), channel_id=1, source_target_pairs={{0,48},{4,52},{8,56},{12,60},{16,0},{20,4},{24,8},{28,12},{32,16},... | collective-permute-start | bytes 786440 | tf_op jit(solution)/shard_map/ppermute | solution.py:38
  40.4 41.6 %collective-permute-start.4 = (bf16[4,256,128]{2,1,0:T(8,128)(2,1)}, bf16[4,256,128]{2,1,0:T(8,128)(2,1)S(1)}, u32[]{:S(2)}, u32[]{:S(2)}) collective-permute-start(bf16[4,256,128]{2,1,0:T(8,128)(2,1)} %bitcast.17.refs_0_), channel_id=1, source_target_pairs={{0,16},{4,20},{8,24},{12,28},{16,32},{20,36},{24,40},{28,44},{32,4... | collective-permute-start | bytes 786440 | tf_op jit(solution)/shard_map/ppermute | solution.py:38
  42.8 58.4 %collective-permute-start = (bf16[4,256,128]{2,1,0:T(8,128)(2,1)}, bf16[4,256,128]{2,1,0:T(8,128)(2,1)S(1)}, u32[]{:S(2)}, u32[]{:S(2)}) collective-permute-start(bf16[4,256,128]{2,1,0:T(8,128)(2,1)} %bitcast.12.refs_0_), channel_id=1, source_target_pairs={{0,16},{4,20},{8,24},{12,28},{16,32},{20,36},{24,40},{28,44},{32,4... | collective-permute-start | bytes 786440 | tf_op jit(solution)/shard_map/ppermute | solution.py:38
  49.7 51.5 %collective-permute-start.3 = (bf16[4,256,128]{2,1,0:T(8,128)(2,1)}, bf16[4,256,128]{2,1,0:T(8,128)(2,1)S(1)}, u32[]{:S(2)}, u32[]{:S(2)}) collective-permute-start(bf16[4,256,128]{2,1,0:T(8,128)(2,1)} %bitcast.17.refs_0_), channel_id=1, source_target_pairs={{0,48},{4,52},{8,56},{12,60},{16,0},{20,4},{24,8},{28,12},{32,16},... | collective-permute-start | bytes 786440 | tf_op jit(solution)/shard_map/ppermute | solution.py:38
  52.6 36.8 %all-to-all-start.3 = ((bf16[4,256,128]{2,1,0:T(8,128)(2,1)}), bf16[4,256,128]{2,1,0:T(8,128)(2,1)S(1)}, u32[]{:S(2)}, u32[]{:S(2)}) async-start(bf16[4,256,128]{2,1,0:T(8,128)(2,1)} %bitcast.17.refs_0_), calls=%async_computation.3 | async-start | bytes 524288 | tf_op jit(solution)/shard_map/all_to_all | solution.py:46
  67.6 33.6 %collective-permute-start.2 = (bf16[4,256,128]{2,1,0:T(8,128)(2,1)S(1)}, bf16[4,256,128]{2,1,0:T(8,128)(2,1)S(1)}, u32[]{:S(2)}, u32[]{:S(2)}) collective-permute-start(bf16[4,256,128]{2,1,0:T(8,128)(2,1)S(1)} %collective-permute-done.1.refs_1_), channel_id=1, source_target_pairs={{0,48},{4,52},{8,56},{12,60},{16,0},{20,4},{24,8},{28,12},{32,16},... | collective-permute-start | bytes 786440 | tf_op jit(solution)/shard_map/ppermute | solution.py:38
  82.0 24.8 %collective-permute-start.5 = (bf16[4,256,128]{2,1,0:T(8,128)(2,1)S(1)}, bf16[4,256,128]{2,1,0:T(8,128)(2,1)S(1)}, u32[]{:S(2)}, u32[]{:S(2)}) collective-permute-start(bf16[4,256,128]{2,1,0:T(8,128)(2,1)S(1)} %collective-permute-done.4.refs_3_), channel_id=1, source_target_pairs={{0,16},{4,20},{8,24},{12,28},{16,32},{20,36},{24,40},{28,44},{32,4... | collective-permute-start | bytes 786440 | tf_op jit(solution)/shard_map/ppermute | solution.py:38
  89.4 19.4 %all-to-all-start.1 = ((bf16[4,256,128]{2,1,0:T(8,128)(2,1)}), bf16[4,256,128]{2,1,0:T(8,128)(2,1)S(1)}, u32[]{:S(2)}, u32[]{:S(2)}) async-start(bf16[4,256,128]{2,1,0:T(8,128)(2,1)} %bitcast.12.refs_0_), calls=%async_computation.1 | async-start | bytes 524288 | tf_op jit(solution)/shard_map/all_to_all | solution.py:46
  108.8 12.0 %copy-start.5 = (f32[8]{0:T(128)S(1)}, f32[8]{0:T(128)}, u32[]{:S(2)}) copy-start(f32[8]{0:T(128)} %param.13) | copy-start | bytes 100
  108.8 24.1 %all-to-all-start.4 = ((bf16[4,768,128]{2,1,0:T(8,128)(2,1)}), bf16[4,768,128]{2,1,0:T(8,128)(2,1)S(1)}, u32[]{:S(2)}, u32[]{:S(2)}) async-start(bf16[4,768,128]{2,1,0:T(8,128)(2,1)} %bitcast.23), calls=%async_computation.4 | async-start | bytes 1572864 | tf_op jit(solution)/shard_map/all_to_all | solution.py:46
  123.2 13.9 %copy-start.1 = (bf16[1,1,1,512,256]{4,3,2,1,0:T(8,128)(2,1)S(1)}, bf16[1,1,1,512,256]{4,3,2,1,0:T(8,128)(2,1)}, u32[]{:S(2)}) copy-start(bf16[1,1,1,512,256]{4,3,2,1,0:T(8,128)(2,1)} %param.7) | copy-start | bytes 786436
  123.2 13.9 %copy-start.2 = (bf16[1,1,1,512,256]{4,3,2,1,0:T(8,128)(2,1)S(1)}, bf16[1,1,1,512,256]{4,3,2,1,0:T(8,128)(2,1)}, u32[]{:S(2)}) copy-start(bf16[1,1,1,512,256]{4,3,2,1,0:T(8,128)(2,1)} %param.10) | copy-start | bytes 786436
  132.9 14.6 %all-to-all-start.2 = ((bf16[4,768,128]{2,1,0:T(8,128)(2,1)}), bf16[4,768,128]{2,1,0:T(8,128)(2,1)S(1)}, u32[]{:S(2)}, u32[]{:S(2)}) async-start(bf16[4,768,128]{2,1,0:T(8,128)(2,1)} %bitcast.18), calls=%async_computation.2 | async-start | bytes 1572864 | tf_op jit(solution)/shard_map/all_to_all | solution.py:46
  147.5 3.7 %copy-start.3 = (bf16[1,1,1,512,256]{4,3,2,1,0:T(8,128)(2,1)S(1)}, bf16[1,1,1,512,256]{4,3,2,1,0:T(8,128)(2,1)}, u32[]{:S(2)}) copy-start(bf16[1,1,1,512,256]{4,3,2,1,0:T(8,128)(2,1)} %param.10) | copy-start | bytes 786436
  147.5 16.4 %all-to-all-start.5 = ((bf16[4,1024,128]{2,1,0:T(8,128)(2,1)}), bf16[4,1024,128]{2,1,0:T(8,128)(2,1)S(1)}, u32[]{:S(2)}, u32[]{:S(2)}) async-start(bf16[4,1024,128]{2,1,0:T(8,128)(2,1)} %get-tuple-element.36), calls=%async_computation.5 | async-start | bytes 2097152 | tf_op jit(solution)/shard_map/all_to_all | solution.py:46
  163.8 15.1 %all-to-all-start.6 = ((bf16[4,1032,128]{2,1,0:T(8,128)(2,1)}), bf16[4,1032,128]{2,1,0:T(8,128)(2,1)S(1)}, u32[]{:S(2)}, u32[]{:S(2)}) async-start(bf16[4,1032,128]{2,1,0:T(8,128)(2,1)} %get-tuple-element.41), calls=%async_computation.6 | async-start | bytes 2113536 | tf_op jit(solution)/shard_map/all_to_all | solution.py:46
  168.5 26.6 %collective-permute-start.6 = (bf16[1024,128]{1,0:T(8,128)(2,1)S(1)}, bf16[1024,128]{1,0:T(8,128)(2,1)S(1)}, u32[]{:S(2)}, u32[]{:S(2)}) collective-permute-start(bf16[1024,128]{1,0:T(8,128)(2,1)S(1)} %get-tuple-element.39), channel_id=1, source_target_pairs={{0,16},{4,20},{8,24},{12,28},{16,32},{20,36},{24,40},{28,44},{32,4... | collective-permute-start | bytes 786440 | tf_op jit(solution)/shard_map/ppermute | solution.py:38
  179.9 43.7 %collective-permute-start.10 = (bf16[1024,128]{1,0:T(8,128)(2,1)S(1)}, bf16[1024,128]{1,0:T(8,128)(2,1)S(1)}, u32[]{:S(2)}, u32[]{:S(2)}) collective-permute-start(bf16[1024,128]{1,0:T(8,128)(2,1)S(1)} %get-tuple-element.45), channel_id=1, source_target_pairs={{0,48},{4,52},{8,56},{12,60},{16,0},{20,4},{24,8},{28,12},{32,16},... | collective-permute-start | bytes 786440 | tf_op jit(solution)/shard_map/ppermute | solution.py:38
  185.3 67.3 %collective-permute-start.8 = (bf16[1024,128]{1,0:T(8,128)(2,1)S(1)}, bf16[1024,128]{1,0:T(8,128)(2,1)S(1)}, u32[]{:S(2)}, u32[]{:S(2)}) collective-permute-start(bf16[1024,128]{1,0:T(8,128)(2,1)S(1)} %get-tuple-element.40), channel_id=1, source_target_pairs={{0,48},{4,52},{8,56},{12,60},{16,0},{20,4},{24,8},{28,12},{32,16},... | collective-permute-start | bytes 786440 | tf_op jit(solution)/shard_map/ppermute | solution.py:38
  187.3 65.5 %collective-permute-start.9 = (bf16[1024,128]{1,0:T(8,128)(2,1)S(1)}, bf16[1024,128]{1,0:T(8,128)(2,1)S(1)}, u32[]{:S(2)}, u32[]{:S(2)}) collective-permute-start(bf16[1024,128]{1,0:T(8,128)(2,1)S(1)} %get-tuple-element.43), channel_id=1, source_target_pairs={{0,16},{4,20},{8,24},{12,28},{16,32},{20,36},{24,40},{28,44},{32,4... | collective-permute-start | bytes 786440 | tf_op jit(solution)/shard_map/ppermute | solution.py:38
  195.2 57.4 %collective-permute-start.7 = (bf16[1024,128]{1,0:T(8,128)(2,1)S(1)}, bf16[1024,128]{1,0:T(8,128)(2,1)S(1)}, u32[]{:S(2)}, u32[]{:S(2)}) collective-permute-start(bf16[1024,128]{1,0:T(8,128)(2,1)S(1)} %add_convert_fusion.3), channel_id=1, source_target_pairs={{0,16},{4,20},{8,24},{12,28},{16,32},{20,36},{24,40},{28,44},{32,4... | collective-permute-start | bytes 786440 | tf_op jit(solution)/shard_map/ppermute | solution.py:38
  223.6 29.1 %collective-permute-start.11 = (bf16[1024,128]{1,0:T(8,128)(2,1)S(1)}, bf16[1024,128]{1,0:T(8,128)(2,1)S(1)}, u32[]{:S(2)}, u32[]{:S(2)}) collective-permute-start(bf16[1024,128]{1,0:T(8,128)(2,1)S(1)} %add_convert_fusion.1), channel_id=1, source_target_pairs={{0,48},{4,52},{8,56},{12,60},{16,0},{20,4},{24,8},{28,12},{32,16},... | collective-permute-start | bytes 786440 | tf_op jit(solution)/shard_map/ppermute | solution.py:38
  253.7 26.1 %all-to-all-start.7 = ((bf16[16,128,128]{2,1,0:T(8,128)(2,1)}), bf16[16,128,128]{2,1,0:T(8,128)(2,1)S(1)}, u32[]{:S(2)}, u32[]{:S(2)}) async-start(bf16[16,128,128]{2,1,0:T(8,128)(2,1)} %bitcast.32), calls=%async_computation.7 | async-start | bytes 1048576 | tf_op jit(solution)/shard_map/all_to_all | solution.py:42

commit v12 on v11

--- a/solution.py
+++ b/solution.py
@@ -25,8 +25,7 @@
 NEG = -1e30
 
 SPREAD_GROUPS = [[x * ZS + g * SPB + r for x in range(XS) for r in range(SPB)] for g in range(ZG)]
-FAR_GROUPS = [[x * ZS + g * SPB + r for g in range(ZG)] for x in range(XS) for r in range(SPB)]
-PART_GROUPS = [[s * SPB + r for r in range(SPB)] for s in range(XS * ZG)]
+Z_GROUPS = [[x * ZS + z for z in range(ZS)] for x in range(XS)]
 X_GROUPS = [[x * ZS + z for x in range(XS)] for z in range(ZS)]
 
 
@@ -44,6 +43,16 @@
 
 def swap_x(arr):
     return lax.all_to_all(arr, "ctx", 0, 0, axis_index_groups=X_GROUPS, tiled=True)
+
+
+def swap_sink(vals, axes, groups, after=None):
+    count = 8 if groups is None else len(groups[0])
+    vals = vals.reshape(1, -1)
+    size = vals.shape[1]
+    rows = jnp.broadcast_to(jnp.pad(vals, ((0, 0), (0, 128 - size))), (count, 128))
+    if after is not None:
+        rows, _ = lax.optimization_barrier((rows, after))
+    return lax.all_to_all(rows, axes, 0, 0, axis_index_groups=groups, tiled=True)[:, :size]
 
 
 def dot(left, right, left_dim, right_dim):
@@ -323,10 +332,10 @@
     down_last = shift_groups(add_rounded(pools[1][3], down_far), -1)
     first = add_rounded(pools[0][0], up_last, down_near)
     second = add_rounded(pools[1][0], up_near, down_last)
-    grad_sink = lax.psum(pools[1][ZG][0, :HEADS], ("dp", "head"))
-    grad_sink = lax.psum(grad_sink, "ctx", axis_index_groups=PART_GROUPS)
-    second, grad_sink = lax.optimization_barrier((second, grad_sink))
-    grad_sink = lax.psum(grad_sink, "ctx", axis_index_groups=FAR_GROUPS)
+    sink_all = swap_sink(pools[1][ZG][0, :HEADS], "ctx", Z_GROUPS, after=up_far)
+    sink_all = swap_sink(jnp.sum(sink_all.reshape(-1, HEADS), axis=0), ("dp", "head"), None)
+    grad_sink = jnp.sum(sink_all.reshape(-1, HEADS), axis=0)
+    first, grad_sink = lax.optimization_barrier((first, grad_sink))
     pooled = jnp.stack([arr.reshape(XS * SPB, 2 * FRAG, DH) for arr in (first, second)], axis=1)
     homed = swap_spread(pooled.reshape(XS * SPB, HPD * 2 * FRAG, DH))
     totals = jnp.transpose(homed.reshape(XS, SPB, HPD, 2, FRAG, DH), (3, 0, 4, 1, 2, 5))

time: 287 us -> 286 us (level); the launches traced: 282 us -> 284 us
  waiting for transfers between devices: 90.3 us -> 124 us
  starting transfers between devices: 123 us -> 105 us
  blocking collectives: 38.3 us -> 23.5 us
    psum x3 -> x0, blocking collectives: 38.3 us -> none  [the longest x1 16.9 us: body(): grad_sink = lax.psum(grad_sink, 'ctx', axis_index_groups=FAR_GROUPS)]
    ppermute x12, waiting for transfers between devices: 49.5 us -> 78.7 us  [shift_groups(): return lax.ppermute(arr, 'ctx', pairs)]
    all_to_all x0 -> x1, blocking collectives: none -> 23.5 us  [swap_spread(): lax.all_to_all(arr, 'ctx', 0, 0, axis_index_groups=SPREAD_GROUPS, tiled=T...]
    all_to_all x6, starting transfers between devices: 36.6 us -> 21.2 us  [swap_x(): lax.all_to_all(arr, 'ctx', 0, 0, axis_index_groups=X_GROUPS, tiled=True)]
    all_to_all x2 -> x1, starting transfers between devices: 17.7 us -> 8.47 us  [swap_spread(): lax.all_to_all(arr, 'ctx', 0, 0, axis_index_groups=SPREAD_GROUPS, tiled=T...]
    all_to_all x0 -> x2, starting transfers between devices: none -> 8.49 us  [swap_sink(): lax.all_to_all(rows, axes, 0, 0, axis_index_groups=groups, tiled=True)]
    all_to_all x0 -> x2, waiting for transfers between devices: none -> 5.25 us  [swap_sink(): lax.all_to_all(rows, axes, 0, 0, axis_index_groups=groups, tiled=True)]
    all_to_all x2 -> x1, waiting for transfers between devices: 16.1 us -> 16.1 us  [swap_spread(): lax.all_to_all(arr, 'ctx', 0, 0, axis_index_groups=SPREAD_GROUPS, tiled=T...]
  transfers between devices with their start and end apart: 20 -> 21, of which waited for: 10 -> 13; matrix products, arithmetic and copies ran while one was open for 1% -> 2% of each run, Pallas kernels for 7% -> 7%
where the time goes in v12:
time: 286 us; the launch traced here: 284 us
  waiting for transfers between devices  124 us (43%)
  starting transfers between devices  105 us (37%)
  blocking collectives  23.5 us (8%)
  Pallas kernels  18.8 us (7%)
  local copies, waits for them, and re-layouts  8.48 us (3%)
  other arithmetic  3.79 us (1%)
    ppermute x12, waiting for transfers between devices, shift_groups(): return lax.ppermute(arr, 'ctx', pairs)  78.7 us
    ppermute x12, starting transfers between devices, shift_groups(): return lax.ppermute(arr, 'ctx', pairs)  66.4 us
    all_to_all x6, waiting for transfers between devices, swap_x(): lax.all_to_all(arr, 'ctx', 0, 0, axis_index_groups=X_GROUPS, tiled=True)  24.3 us
    all_to_all x1, blocking collectives, swap_spread(): lax.all_to_all(arr, 'ctx', 0, 0, axis_index_groups=SPREAD_GROUPS, tiled=T...  23.5 us
    all_to_all x6, starting transfers between devices, swap_x(): lax.all_to_all(arr, 'ctx', 0, 0, axis_index_groups=X_GROUPS, tiled=True)  21.2 us
    all_to_all x1, waiting for transfers between devices, swap_spread(): lax.all_to_all(arr, 'ctx', 0, 0, axis_index_groups=SPREAD_GROUPS, tiled=T...  16.1 us
    pallas_call x2, Pallas kernels, attend(): pl.pallas_call(attend_kernel, name='attend_head%d' % head, grid=(1,), in_...  13 us
    all_to_all x2, starting transfers between devices, swap_sink(): lax.all_to_all(rows, axes, 0, 0, axis_index_groups=groups, tiled=True)  8.49 us
  transfers between devices with their start and end apart: 21, of which 13 were waited for; matrix products, arithmetic and copies ran while one was open for 2% of the time, Pallas kernels for 7%

profile of v12, /device:TPU:24, one launch (start us, length us, event | category | flops | bytes accessed | tf_op | source)
XLA Modules:
  0.0 284.5 jit_solution(16699834012311088928)
XLA Ops:
  0.6 1.1 reshape.119
  1.8 1.1 reshape.120
  2.9 0.7 pad_maximum_fusion
  3.7 0.9 copy.43
  4.6 8.5 %all-to-all-start = ((bf16[16,128,128]{2,1,0:T(8,128)(2,1)}), bf16[16,128,128]{2,1,0:T(8,128)(2,1)S(1)}, u32[]{:S(2)}, u32[]{:S(2)}) async-start(bf16[16,128,128]{2,1,0:T(8,128)(2,1)} %bitcast.9), calls=%async_computation | async-start | bytes 1048576 | tf_op jit(solution)/shard_map/all_to_all | solution.py:41
  13.5 16.1 %all-to-all-done = bf16[16,128,128]{2,1,0:T(8,128)(2,1)S(1)} async-done(((bf16[16,128,128]{2,1,0:T(8,128)(2,1)}), bf16[16,128,128]{2,1,0:T(8,128)(2,1)S(1)}, u32[]{:S(2)}, u32[]{:S(2)}) %all-to-all-start) | async-done | bytes 524320 | tf_op jit(solution)/shard_map/all_to_all | solution.py:41
  29.6 0.8 fusion.10
  30.4 10.0 %collective-permute-start.1 = (bf16[4,256,128]{2,1,0:T(8,128)(2,1)}, bf16[4,256,128]{2,1,0:T(8,128)(2,1)S(1)}, u32[]{:S(2)}, u32[]{:S(2)}) collective-permute-start(bf16[4,256,128]{2,1,0:T(8,128)(2,1)} %bitcast.12.refs_0_), channel_id=1, source_target_pairs={{0,48},{4,52},{8,56},{12,60},{16,0},{20,4},{24,8},{28,12},{32,16},... | collective-permute-start | bytes 786440 | tf_op jit(solution)/shard_map/ppermute | solution.py:37
  40.4 1.9 collective-permute-start.4
  42.8 3.4 %all-to-all-start.1 = ((bf16[4,256,128]{2,1,0:T(8,128)(2,1)}), bf16[4,256,128]{2,1,0:T(8,128)(2,1)S(1)}, u32[]{:S(2)}, u32[]{:S(2)}) async-start(bf16[4,256,128]{2,1,0:T(8,128)(2,1)} %bitcast.12.refs_0_), calls=%async_computation.1 | async-start | bytes 524288 | tf_op jit(solution)/shard_map/all_to_all | solution.py:45
  46.3 6.9 %collective-permute-start = (bf16[4,256,128]{2,1,0:T(8,128)(2,1)}, bf16[4,256,128]{2,1,0:T(8,128)(2,1)S(1)}, u32[]{:S(2)}, u32[]{:S(2)}) collective-permute-start(bf16[4,256,128]{2,1,0:T(8,128)(2,1)} %bitcast.12.refs_0_), channel_id=1, source_target_pairs={{0,16},{4,20},{8,24},{12,28},{16,32},{20,36},{24,40},{28,44},{32,4... | collective-permute-start | bytes 786440 | tf_op jit(solution)/shard_map/ppermute | solution.py:37
  53.2 2.9 %collective-permute-start.3 = (bf16[4,256,128]{2,1,0:T(8,128)(2,1)}, bf16[4,256,128]{2,1,0:T(8,128)(2,1)S(1)}, u32[]{:S(2)}, u32[]{:S(2)}) collective-permute-start(bf16[4,256,128]{2,1,0:T(8,128)(2,1)} %bitcast.17.refs_0_), channel_id=1, source_target_pairs={{0,48},{4,52},{8,56},{12,60},{16,0},{20,4},{24,8},{28,12},{32,16},... | collective-permute-start | bytes 786440 | tf_op jit(solution)/shard_map/ppermute | solution.py:37
  56.0 7.7 %collective-permute-done.1.refs_1_ = bf16[4,256,128]{2,1,0:T(8,128)(2,1)S(1)} collective-permute-done((bf16[4,256,128]{2,1,0:T(8,128)(2,1)}, bf16[4,256,128]{2,1,0:T(8,128)(2,1)S(1)}, u32[]{:S(2)}, u32[]{:S(2)}) %collective-permute-start.1) | collective-permute-done | bytes 262176 | tf_op jit(solution)/shard_map/ppermute | solution.py:37
  63.7 7.5 %collective-permute-start.2 = (bf16[4,256,128]{2,1,0:T(8,128)(2,1)S(1)}, bf16[4,256,128]{2,1,0:T(8,128)(2,1)S(1)}, u32[]{:S(2)}, u32[]{:S(2)}) collective-permute-start(bf16[4,256,128]{2,1,0:T(8,128)(2,1)S(1)} %collective-permute-done.1.refs_1_), channel_id=1, source_target_pairs={{0,48},{4,52},{8,56},{12,60},{16,0},{20,4},{24,8},{28,12},{32,16},... | collective-permute-start | bytes 786440 | tf_op jit(solution)/shard_map/ppermute | solution.py:37
  71.2 10.8 %collective-permute-done.4.refs_3_ = bf16[4,256,128]{2,1,0:T(8,128)(2,1)S(1)} collective-permute-done((bf16[4,256,128]{2,1,0:T(8,128)(2,1)}, bf16[4,256,128]{2,1,0:T(8,128)(2,1)S(1)}, u32[]{:S(2)}, u32[]{:S(2)}) %collective-permute-start.4) | collective-permute-done | bytes 262176 | tf_op jit(solution)/shard_map/ppermute | solution.py:37
  82.0 7.4 %collective-permute-start.5 = (bf16[4,256,128]{2,1,0:T(8,128)(2,1)S(1)}, bf16[4,256,128]{2,1,0:T(8,128)(2,1)S(1)}, u32[]{:S(2)}, u32[]{:S(2)}) collective-permute-start(bf16[4,256,128]{2,1,0:T(8,128)(2,1)S(1)} %collective-permute-done.4.refs_3_), channel_id=1, source_target_pairs={{0,16},{4,20},{8,24},{12,28},{16,32},{20,36},{24,40},{28,44},{32,4... | collective-permute-start | bytes 786440 | tf_op jit(solution)/shard_map/ppermute | solution.py:37
  89.5 3.4 %all-to-all-start.3 = ((bf16[4,256,128]{2,1,0:T(8,128)(2,1)}), bf16[4,256,128]{2,1,0:T(8,128)(2,1)S(1)}, u32[]{:S(2)}, u32[]{:S(2)}) async-start(bf16[4,256,128]{2,1,0:T(8,128)(2,1)} %bitcast.17.refs_0_), calls=%async_computation.3 | async-start | bytes 524288 | tf_op jit(solution)/shard_map/all_to_all | solution.py:45
  93.1 12.4 %collective-permute-done.refs_3_ = bf16[4,256,128]{2,1,0:T(8,128)(2,1)S(1)} collective-permute-done((bf16[4,256,128]{2,1,0:T(8,128)(2,1)}, bf16[4,256,128]{2,1,0:T(8,128)(2,1)S(1)}, u32[]{:S(2)}, u32[]{:S(2)}) %collective-permute-start) | collective-permute-done | bytes 262176 | tf_op jit(solution)/shard_map/ppermute | solution.py:37
  105.5 8.5 %collective-permute-done.5.refs_2_ = bf16[4,256,128]{2,1,0:T(8,128)(2,1)S(1)} collective-permute-done((bf16[4,256,128]{2,1,0:T(8,128)(2,1)S(1)}, bf16[4,256,128]{2,1,0:T(8,128)(2,1)S(1)}, u32[]{:S(2)}, u32[]{:S(2)}) %collective-permute-start.5) | collective-permute-done | bytes 262176 | tf_op jit(solution)/shard_map/ppermute | solution.py:37
  114.0 2.0 gather_picks.3
  116.0 3.6 %all-to-all-start.4 = ((bf16[4,768,128]{2,1,0:T(8,128)(2,1)}), bf16[4,768,128]{2,1,0:T(8,128)(2,1)S(1)}, u32[]{:S(2)}, u32[]{:S(2)}) async-start(bf16[4,768,128]{2,1,0:T(8,128)(2,1)} %bitcast.23), calls=%async_computation.4 | async-start | bytes 1572864 | tf_op jit(solution)/shard_map/all_to_all | solution.py:45
  120.1 2.0 gather_picks.2
  122.1 10.3 %all-to-all-done.4 = bf16[4,768,128]{2,1,0:T(8,128)(2,1)S(1)} async-done(((bf16[4,768,128]{2,1,0:T(8,128)(2,1)}), bf16[4,768,128]{2,1,0:T(8,128)(2,1)S(1)}, u32[]{:S(2)}, u32[]{:S(2)}) %all-to-all-start.4) | async-done | bytes 786464 | tf_op jit(solution)/shard_map/all_to_all | solution.py:45
  132.4 3.5 %all-to-all-start.2 = ((bf16[4,768,128]{2,1,0:T(8,128)(2,1)}), bf16[4,768,128]{2,1,0:T(8,128)(2,1)S(1)}, u32[]{:S(2)}, u32[]{:S(2)}) async-start(bf16[4,768,128]{2,1,0:T(8,128)(2,1)} %bitcast.18), calls=%async_computation.2 | async-start | bytes 1572864 | tf_op jit(solution)/shard_map/all_to_all | solution.py:45
  136.6 6.5 %attend_head0.1 = (bf16[512,256]{1,0:T(8,128)(2,1)}, bf16[512,256]{1,0:T(8,128)(2,1)}, bf16[4,1024,128]{2,1,0:T(8,128)(2,1)}, f32[8,128]{1,0:T(8,128)S(1)}) custom-call(s32[4]{0:T(128)S(1)} %pad_add_fusion.1.use_ref, f32[1]{0:T(128)} %get-tuple-element.61.sink_ref, bf16[512,256]{1,0:T(8,128)(2,1)S(1)} %bitcast.70, bf16[512,256]{1,0:T(8,128)(2,1)S(1)} %bitcast.72, ...), custom_call_target="tpu_custom_call" | custom-call | flops 2684354560 | bytes 8388608 | tf_op jit(solution)/shard_map/attend_head0/pallas_call | solution.py:166
  143.0 4.7 %all-to-all-done.2 = bf16[4,768,128]{2,1,0:T(8,128)(2,1)S(1)} async-done(((bf16[4,768,128]{2,1,0:T(8,128)(2,1)}), bf16[4,768,128]{2,1,0:T(8,128)(2,1)S(1)}, u32[]{:S(2)}, u32[]{:S(2)}) %all-to-all-start.2) | async-done | bytes 786464 | tf_op jit(solution)/shard_map/all_to_all | solution.py:45
  147.8 3.5 %all-to-all-start.5 = ((bf16[4,1024,128]{2,1,0:T(8,128)(2,1)}), bf16[4,1024,128]{2,1,0:T(8,128)(2,1)S(1)}, u32[]{:S(2)}, u32[]{:S(2)}) async-start(bf16[4,1024,128]{2,1,0:T(8,128)(2,1)} %get-tuple-element.37), calls=%async_computation.5 | async-start | bytes 2097152 | tf_op jit(solution)/shard_map/all_to_all | solution.py:45
  151.4 6.5 %attend_head1.1 = (bf16[512,256]{1,0:T(8,128)(2,1)}, bf16[512,256]{1,0:T(8,128)(2,1)}, bf16[4,1032,128]{2,1,0:T(8,128)(2,1)}, f32[8,128]{1,0:T(8,128)}) custom-call(s32[4]{0:T(128)S(1)} %pad_add_fusion.use_ref, f32[1]{0:T(128)} %get-tuple-element.62.sink_ref, bf16[512,256]{1,0:T(8,128)(2,1)S(1)} %bitcast.71, ...), custom_call_target="tpu_custom_call", output_to_operand_aliasing={{0}: (6, {}), {1}: (7, {})} | custom-call | flops 2684354560 | bytes 8388608 | tf_op jit(solution)/shard_map/attend_head1/pallas_call | solution.py:166
  157.9 7.2 %all-to-all-done.5.part_ref = bf16[4,1024,128]{2,1,0:T(8,128)(2,1)S(1)} async-done(((bf16[4,1024,128]{2,1,0:T(8,128)(2,1)}), bf16[4,1024,128]{2,1,0:T(8,128)(2,1)S(1)}, u32[]{:S(2)}, u32[]{:S(2)}) %all-to-all-start.5) | async-done | bytes 1048608 | tf_op jit(solution)/shard_map/all_to_all | solution.py:45
  165.0 3.7 %all-to-all-start.6 = ((bf16[4,1032,128]{2,1,0:T(8,128)(2,1)}), bf16[4,1032,128]{2,1,0:T(8,128)(2,1)S(1)}, u32[]{:S(2)}, u32[]{:S(2)}) async-start(bf16[4,1032,128]{2,1,0:T(8,128)(2,1)} %get-tuple-element.42), calls=%async_computation.6 | async-start | bytes 2113536 | tf_op jit(solution)/shard_map/all_to_all | solution.py:45
  168.7 0.9 pool_parts.2
  169.7 1.9 collective-permute-start.6
  171.6 7.8 %collective-permute-start.8 = (bf16[1024,128]{1,0:T(8,128)(2,1)S(1)}, bf16[1024,128]{1,0:T(8,128)(2,1)}, u32[]{:S(2)}, u32[]{:S(2)}) collective-permute-start(bf16[1024,128]{1,0:T(8,128)(2,1)S(1)} %get-tuple-element.41), channel_id=1, source_target_pairs={{0,48},{4,52},{8,56},{12,60},{16,0},{20,4},{24,8},{28,12},{32,16},... | collective-permute-start | bytes 786440 | tf_op jit(solution)/shard_map/ppermute | solution.py:37
  179.4 2.0 all-to-all-done.6.part_ref
  181.5 0.9 pool_parts.3
  182.4 1.9 collective-permute-start.9
  184.4 7.8 %collective-permute-start.10 = (bf16[1024,128]{1,0:T(8,128)(2,1)S(1)}, bf16[1024,128]{1,0:T(8,128)(2,1)S(1)}, u32[]{:S(2)}, u32[]{:S(2)}) collective-permute-start(bf16[1024,128]{1,0:T(8,128)(2,1)S(1)} %get-tuple-element.49), channel_id=1, source_target_pairs={{0,48},{4,52},{8,56},{12,60},{16,0},{20,4},{24,8},{28,12},{32,16},... | collective-permute-start | bytes 786440 | tf_op jit(solution)/shard_map/ppermute | solution.py:37
  192.2 14.9 %collective-permute-done.6 = bf16[1024,128]{1,0:T(8,128)(2,1)S(1)} collective-permute-done((bf16[1024,128]{1,0:T(8,128)(2,1)S(1)}, bf16[1024,128]{1,0:T(8,128)(2,1)S(1)}, u32[]{:S(2)}, u32[]{:S(2)}) %collective-permute-start.6) | collective-permute-done | bytes 262176 | tf_op jit(solution)/shard_map/ppermute | solution.py:37
  207.7 3.8 %all-to-all-start.7 = ((f32[16,1,128]{2,1,0:T(1,128)}), f32[16,1,128]{2,1,0:T(1,128)S(1)}, u32[]{:S(2)}, u32[]{:S(2)}) async-start(f32[16,1,128]{2,1,0:T(1,128)} %bitcast.28), calls=%async_computation.7 | async-start | bytes 16384 | tf_op jit(solution)/shard_map/all_to_all | solution.py:55
  211.6 7.7 %collective-permute-start.7 = (bf16[1024,128]{1,0:T(8,128)(2,1)S(1)}, bf16[1024,128]{1,0:T(8,128)(2,1)S(1)}, u32[]{:S(2)}, u32[]{:S(2)}) collective-permute-start(bf16[1024,128]{1,0:T(8,128)(2,1)S(1)} %add_convert_fusion.3), channel_id=1, source_target_pairs={{0,16},{4,20},{8,24},{12,28},{16,32},{20,36},{24,40},{28,44},{32,4... | collective-permute-start | bytes 786440 | tf_op jit(solution)/shard_map/ppermute | solution.py:37
  219.3 4.8 %all-to-all-done.7 = f32[16,1,128]{2,1,0:T(1,128)S(1)} async-done(((f32[16,1,128]{2,1,0:T(1,128)}), f32[16,1,128]{2,1,0:T(1,128)S(1)}, u32[]{:S(2)}, u32[]{:S(2)}) %all-to-all-start.7) | async-done | bytes 8224 | tf_op jit(solution)/shard_map/all_to_all | solution.py:55
  224.8 4.7 %all-to-all-start.8 = ((f32[8,1,128]{2,1,0:T(1,128)}), f32[8,1,128]{2,1,0:T(1,128)S(1)}, u32[]{:S(2)}, u32[]{:S(2)}) async-start(f32[8,1,128]{2,1,0:T(1,128)} %broadcast_in_dim.111), calls=%async_computation.8 | async-start | bytes 8192 | tf_op jit(solution)/shard_map/all_to_all | solution.py:55
  229.5 2.6 collective-permute-start.11
  233.1 1.1 add_convert_fusion.2
  234.2 24.4 %collective-permute-done.11 = bf16[1024,128]{1,0:T(8,128)(2,1)S(1)} collective-permute-done((bf16[1024,128]{1,0:T(8,128)(2,1)S(1)}, bf16[1024,128]{1,0:T(8,128)(2,1)S(1)}, u32[]{:S(2)}, u32[]{:S(2)}) %collective-permute-start.11) | collective-permute-done | bytes 262176 | tf_op jit(solution)/shard_map/ppermute | solution.py:37
  258.8 23.5 %all_to_all.61 = bf16[16,128,128]{2,1,0:T(8,128)(2,1)S(1)} all-to-all(bf16[16,128,128]{2,1,0:T(8,128)(2,1)S(1)} %bitcast.76), channel_id=1, replica_groups={{0,4,8,12,64,68,72,76,128,132,136,140,192,196,200,204},{16,20,24,28,80,..., dimensions={0} | all-to-all | bytes 1048576 | tf_op jit(solution)/shard_map/all_to_all | solution.py:41
  282.5 0.9 reshape_squeeze.15
  283.6 0.9 reshape_squeeze.14
  (54 shorter events, 5.2 us)
Async XLA Ops:
  0.6 41.7 %copy-start = (s32[1,16,8,3]{1,2,3,0:T(8,128)S(1)}, s32[1,16,8,3]{1,2,3,0:T(8,128)}, u32[]{:S(2)}) copy-start(s32[1,16,8,3]{1,2,3,0:T(8,128)} %param.11) | copy-start | bytes 4612
  3.6 9.5 %copy-start.3 = (s32[16]{0:T(128)S(1)}, s32[16]{0:T(128)}, u32[]{:S(2)}) copy-start(s32[16]{0:T(128)} %param.12) | copy-start | bytes 196
  4.6 25.0 %all-to-all-start = ((bf16[16,128,128]{2,1,0:T(8,128)(2,1)}), bf16[16,128,128]{2,1,0:T(8,128)(2,1)S(1)}, u32[]{:S(2)}, u32[]{:S(2)}) async-start(bf16[16,128,128]{2,1,0:T(8,128)(2,1)} %bitcast.9), calls=%async_computation | async-start | bytes 1048576 | tf_op jit(solution)/shard_map/all_to_all | solution.py:41
  30.4 33.3 %collective-permute-start.1 = (bf16[4,256,128]{2,1,0:T(8,128)(2,1)}, bf16[4,256,128]{2,1,0:T(8,128)(2,1)S(1)}, u32[]{:S(2)}, u32[]{:S(2)}) collective-permute-start(bf16[4,256,128]{2,1,0:T(8,128)(2,1)} %bitcast.12.refs_0_), channel_id=1, source_target_pairs={{0,48},{4,52},{8,56},{12,60},{16,0},{20,4},{24,8},{28,12},{32,16},... | collective-permute-start | bytes 786440 | tf_op jit(solution)/shard_map/ppermute | solution.py:37
  40.4 41.6 %collective-permute-start.4 = (bf16[4,256,128]{2,1,0:T(8,128)(2,1)}, bf16[4,256,128]{2,1,0:T(8,128)(2,1)S(1)}, u32[]{:S(2)}, u32[]{:S(2)}) collective-permute-start(bf16[4,256,128]{2,1,0:T(8,128)(2,1)} %bitcast.17.refs_0_), channel_id=1, source_target_pairs={{0,16},{4,20},{8,24},{12,28},{16,32},{20,36},{24,40},{28,44},{32,4... | collective-permute-start | bytes 786440 | tf_op jit(solution)/shard_map/ppermute | solution.py:37
  42.8 46.6 %all-to-all-start.1 = ((bf16[4,256,128]{2,1,0:T(8,128)(2,1)}), bf16[4,256,128]{2,1,0:T(8,128)(2,1)S(1)}, u32[]{:S(2)}, u32[]{:S(2)}) async-start(bf16[4,256,128]{2,1,0:T(8,128)(2,1)} %bitcast.12.refs_0_), calls=%async_computation.1 | async-start | bytes 524288 | tf_op jit(solution)/shard_map/all_to_all | solution.py:45
  46.3 59.2 %collective-permute-start = (bf16[4,256,128]{2,1,0:T(8,128)(2,1)}, bf16[4,256,128]{2,1,0:T(8,128)(2,1)S(1)}, u32[]{:S(2)}, u32[]{:S(2)}) collective-permute-start(bf16[4,256,128]{2,1,0:T(8,128)(2,1)} %bitcast.12.refs_0_), channel_id=1, source_target_pairs={{0,16},{4,20},{8,24},{12,28},{16,32},{20,36},{24,40},{28,44},{32,4... | collective-permute-start | bytes 786440 | tf_op jit(solution)/shard_map/ppermute | solution.py:37
  53.2 52.4 %collective-permute-start.3 = (bf16[4,256,128]{2,1,0:T(8,128)(2,1)}, bf16[4,256,128]{2,1,0:T(8,128)(2,1)S(1)}, u32[]{:S(2)}, u32[]{:S(2)}) collective-permute-start(bf16[4,256,128]{2,1,0:T(8,128)(2,1)} %bitcast.17.refs_0_), channel_id=1, source_target_pairs={{0,48},{4,52},{8,56},{12,60},{16,0},{20,4},{24,8},{28,12},{32,16},... | collective-permute-start | bytes 786440 | tf_op jit(solution)/shard_map/ppermute | solution.py:37
  63.7 41.8 %collective-permute-start.2 = (bf16[4,256,128]{2,1,0:T(8,128)(2,1)S(1)}, bf16[4,256,128]{2,1,0:T(8,128)(2,1)S(1)}, u32[]{:S(2)}, u32[]{:S(2)}) collective-permute-start(bf16[4,256,128]{2,1,0:T(8,128)(2,1)S(1)} %collective-permute-done.1.refs_1_), channel_id=1, source_target_pairs={{0,48},{4,52},{8,56},{12,60},{16,0},{20,4},{24,8},{28,12},{32,16},... | collective-permute-start | bytes 786440 | tf_op jit(solution)/shard_map/ppermute | solution.py:37
  82.0 32.0 %collective-permute-start.5 = (bf16[4,256,128]{2,1,0:T(8,128)(2,1)S(1)}, bf16[4,256,128]{2,1,0:T(8,128)(2,1)S(1)}, u32[]{:S(2)}, u32[]{:S(2)}) collective-permute-start(bf16[4,256,128]{2,1,0:T(8,128)(2,1)S(1)} %collective-permute-done.4.refs_3_), channel_id=1, source_target_pairs={{0,16},{4,20},{8,24},{12,28},{16,32},{20,36},{24,40},{28,44},{32,4... | collective-permute-start | bytes 786440 | tf_op jit(solution)/shard_map/ppermute | solution.py:37
  89.5 26.6 %all-to-all-start.3 = ((bf16[4,256,128]{2,1,0:T(8,128)(2,1)}), bf16[4,256,128]{2,1,0:T(8,128)(2,1)S(1)}, u32[]{:S(2)}, u32[]{:S(2)}) async-start(bf16[4,256,128]{2,1,0:T(8,128)(2,1)} %bitcast.17.refs_0_), calls=%async_computation.3 | async-start | bytes 524288 | tf_op jit(solution)/shard_map/all_to_all | solution.py:45
  116.0 3.7 %copy-start.4 = (f32[8]{0:T(128)S(1)}, f32[8]{0:T(128)}, u32[]{:S(2)}) copy-start(f32[8]{0:T(128)} %param.13) | copy-start | bytes 100
  116.0 16.3 %all-to-all-start.4 = ((bf16[4,768,128]{2,1,0:T(8,128)(2,1)}), bf16[4,768,128]{2,1,0:T(8,128)(2,1)S(1)}, u32[]{:S(2)}, u32[]{:S(2)}) async-start(bf16[4,768,128]{2,1,0:T(8,128)(2,1)} %bitcast.23), calls=%async_computation.4 | async-start | bytes 1572864 | tf_op jit(solution)/shard_map/all_to_all | solution.py:45
  122.1 14.5 %copy-start.1 = (bf16[1,1,1,512,256]{4,3,2,1,0:T(8,128)(2,1)S(1)}, bf16[1,1,1,512,256]{4,3,2,1,0:T(8,128)(2,1)}, u32[]{:S(2)}) copy-start(bf16[1,1,1,512,256]{4,3,2,1,0:T(8,128)(2,1)} %param.7) | copy-start | bytes 786436
  122.1 14.5 %copy-start.2 = (bf16[1,1,1,512,256]{4,3,2,1,0:T(8,128)(2,1)S(1)}, bf16[1,1,1,512,256]{4,3,2,1,0:T(8,128)(2,1)}, u32[]{:S(2)}) copy-start(bf16[1,1,1,512,256]{4,3,2,1,0:T(8,128)(2,1)} %param.10) | copy-start | bytes 786436
  132.4 15.4 %all-to-all-start.2 = ((bf16[4,768,128]{2,1,0:T(8,128)(2,1)}), bf16[4,768,128]{2,1,0:T(8,128)(2,1)S(1)}, u32[]{:S(2)}, u32[]{:S(2)}) async-start(bf16[4,768,128]{2,1,0:T(8,128)(2,1)} %bitcast.18), calls=%async_computation.2 | async-start | bytes 1572864 | tf_op jit(solution)/shard_map/all_to_all | solution.py:45
  147.8 17.3 %all-to-all-start.5 = ((bf16[4,1024,128]{2,1,0:T(8,128)(2,1)}), bf16[4,1024,128]{2,1,0:T(8,128)(2,1)S(1)}, u32[]{:S(2)}, u32[]{:S(2)}) async-start(bf16[4,1024,128]{2,1,0:T(8,128)(2,1)} %get-tuple-element.37), calls=%async_computation.5 | async-start | bytes 2097152 | tf_op jit(solution)/shard_map/all_to_all | solution.py:45
  165.0 16.4 %all-to-all-start.6 = ((bf16[4,1032,128]{2,1,0:T(8,128)(2,1)}), bf16[4,1032,128]{2,1,0:T(8,128)(2,1)S(1)}, u32[]{:S(2)}, u32[]{:S(2)}) async-start(bf16[4,1032,128]{2,1,0:T(8,128)(2,1)} %get-tuple-element.42), calls=%async_computation.6 | async-start | bytes 2113536 | tf_op jit(solution)/shard_map/all_to_all | solution.py:45
  169.7 37.4 %collective-permute-start.6 = (bf16[1024,128]{1,0:T(8,128)(2,1)S(1)}, bf16[1024,128]{1,0:T(8,128)(2,1)S(1)}, u32[]{:S(2)}, u32[]{:S(2)}) collective-permute-start(bf16[1024,128]{1,0:T(8,128)(2,1)S(1)} %get-tuple-element.40), channel_id=1, source_target_pairs={{0,16},{4,20},{8,24},{12,28},{16,32},{20,36},{24,40},{28,44},{32,4... | collective-permute-start | bytes 786440 | tf_op jit(solution)/shard_map/ppermute | solution.py:37
  171.6 61.5 %collective-permute-start.8 = (bf16[1024,128]{1,0:T(8,128)(2,1)S(1)}, bf16[1024,128]{1,0:T(8,128)(2,1)}, u32[]{:S(2)}, u32[]{:S(2)}) collective-permute-start(bf16[1024,128]{1,0:T(8,128)(2,1)S(1)} %get-tuple-element.41), channel_id=1, source_target_pairs={{0,48},{4,52},{8,56},{12,60},{16,0},{20,4},{24,8},{28,12},{32,16},... | collective-permute-start | bytes 786440 | tf_op jit(solution)/shard_map/ppermute | solution.py:37
  182.4 51.7 %collective-permute-start.9 = (bf16[1024,128]{1,0:T(8,128)(2,1)S(1)}, bf16[1024,128]{1,0:T(8,128)(2,1)S(1)}, u32[]{:S(2)}, u32[]{:S(2)}) collective-permute-start(bf16[1024,128]{1,0:T(8,128)(2,1)S(1)} %get-tuple-element.47), channel_id=1, source_target_pairs={{0,16},{4,20},{8,24},{12,28},{16,32},{20,36},{24,40},{28,44},{32,4... | collective-permute-start | bytes 786440 | tf_op jit(solution)/shard_map/ppermute | solution.py:37
  184.4 45.1 %collective-permute-start.10 = (bf16[1024,128]{1,0:T(8,128)(2,1)S(1)}, bf16[1024,128]{1,0:T(8,128)(2,1)S(1)}, u32[]{:S(2)}, u32[]{:S(2)}) collective-permute-start(bf16[1024,128]{1,0:T(8,128)(2,1)S(1)} %get-tuple-element.49), channel_id=1, source_target_pairs={{0,48},{4,52},{8,56},{12,60},{16,0},{20,4},{24,8},{28,12},{32,16},... | collective-permute-start | bytes 786440 | tf_op jit(solution)/shard_map/ppermute | solution.py:37
  207.7 16.4 %all-to-all-start.7 = ((f32[16,1,128]{2,1,0:T(1,128)}), f32[16,1,128]{2,1,0:T(1,128)S(1)}, u32[]{:S(2)}, u32[]{:S(2)}) async-start(f32[16,1,128]{2,1,0:T(1,128)} %bitcast.28), calls=%async_computation.7 | async-start | bytes 16384 | tf_op jit(solution)/shard_map/all_to_all | solution.py:55
  211.6 21.5 %collective-permute-start.7 = (bf16[1024,128]{1,0:T(8,128)(2,1)S(1)}, bf16[1024,128]{1,0:T(8,128)(2,1)S(1)}, u32[]{:S(2)}, u32[]{:S(2)}) collective-permute-start(bf16[1024,128]{1,0:T(8,128)(2,1)S(1)} %add_convert_fusion.3), channel_id=1, source_target_pairs={{0,16},{4,20},{8,24},{12,28},{16,32},{20,36},{24,40},{28,44},{32,4... | collective-permute-start | bytes 786440 | tf_op jit(solution)/shard_map/ppermute | solution.py:37
  224.8 7.8 %all-to-all-start.8 = ((f32[8,1,128]{2,1,0:T(1,128)}), f32[8,1,128]{2,1,0:T(1,128)S(1)}, u32[]{:S(2)}, u32[]{:S(2)}) async-start(f32[8,1,128]{2,1,0:T(1,128)} %broadcast_in_dim.111), calls=%async_computation.8 | async-start | bytes 8192 | tf_op jit(solution)/shard_map/all_to_all | solution.py:55
  229.5 29.1 %collective-permute-start.11 = (bf16[1024,128]{1,0:T(8,128)(2,1)S(1)}, bf16[1024,128]{1,0:T(8,128)(2,1)S(1)}, u32[]{:S(2)}, u32[]{:S(2)}) collective-permute-start(bf16[1024,128]{1,0:T(8,128)(2,1)S(1)} %add_convert_fusion.1), channel_id=1, source_target_pairs={{0,48},{4,52},{8,56},{12,60},{16,0},{20,4},{24,8},{28,12},{32,16},... | collective-permute-start | bytes 786440 | tf_op jit(solution)/shard_map/ppermute | solution.py:37
